TPU v7x, 32 devices: a whole 2x2x4 slice. The times are simulated.
32 devices in a mesh: grp: 4 (over y, core), tok: 8 (over z, x).
Axes of the slice: x: 2, y: 2, z: 4, core: 2. Of those that a mesh axis runs over, the one named last changes fastest.
Arguments:
- tokens: bfloat16 [8192, 960], P(('grp', 'tok')), may hold values from -6 to 6
- w_query: bfloat16 [960, 960], P('tok'), may hold values from -0.1875 to 0.1875
- w_key: bfloat16 [960, 320], P('tok'), may hold values from -0.1875 to 0.1875
- w_value: bfloat16 [960, 320], P('tok'), may hold values from -0.1875 to 0.1875
- w_out: bfloat16 [960, 960], P('tok'), may hold values from -0.75 to 0.75
- w_gate: bfloat16 [960, 2560], P('tok'), may hold values from -0.1875 to 0.1875
- w_up: bfloat16 [960, 2560], P('tok'), may hold values from -0.1875 to 0.1875
- w_down: bfloat16 [2560, 960], P('tok'), may hold values from -0.125 to 0.125
- router: bfloat16 [960, 3], P('tok'), may hold values from -0.1875 to 0.1875
- norm_attn: bfloat16 [960], P('tok'), may hold values from 0.5 to 1.5
- norm_ffn: bfloat16 [960], P('tok'), may hold values from 0.5 to 1.5
- lengths: int32 [4, 2], P('grp'), may hold values from 1 to 1536, 2048 in all within a row
- depths: int32 [8192], P(('grp', 'tok')), may hold values from 1 to 3, as said below
- padding: int32 [8192], P(('grp', 'tok')), may hold values from 0 to 1
- cotangent: bfloat16 [8192, 960], P(('grp', 'tok')), may hold values from -6 to 6
Outputs:
- block_out: bfloat16 [8192, 960], P(('grp', 'tok'))
- grad_tokens: bfloat16 [8192, 960], P(('grp', 'tok'))
- grad_query: float32 [960, 960], P('tok')
- grad_key: float32 [960, 320], P('tok')
- grad_value: float32 [960, 320], P('tok')
- grad_out: float32 [960, 960], P('tok')
- grad_gate: float32 [960, 2560], P('tok')
- grad_up: float32 [960, 2560], P('tok')
- grad_down: float32 [2560, 960], P('tok')
- grad_router: float32 [960, 3], P('tok')
- grad_norm_attn: float32 [960], P('tok')
- grad_norm_ffn: float32 [960], P('tok')
Inputs may be any that keep to these rules, and one draw needn't show every extreme that they name: Each row gives the lengths of the consecutive documents of one group of 2048 tokens and sums to 2048; the longest is at most 1536. `depths`: at most 192 tokens of one pack of 256 have padding 1 and depth 2 or more, and in each group one pack has exactly 192.
All inputs are finite; a program needn't handle non-finite values.
Results may differ from a plain program's by a relative error of at most 0.03.
Values may be sent and summed in bfloat16 or wider, within the bound.
A program may use at most 256 MiB of HBM per device.

v0:
```python
import jax
import jax.numpy as jnp
from jax import lax
from jax.sharding import PartitionSpec as P

HEADS = 15
KV_HEADS = 5
HD = 64
RECS = 3


def for_sending(shard):

    def short(part):
        return part.astype(jnp.bfloat16) if part.dtype == jnp.float32 else part

    return jax.tree.map(short, shard)


def rounders():

    def value_only(v):
        return lax.optimization_barrier(v.astype(jnp.bfloat16)).astype(jnp.float32)

    def value_keep(v):
        return (value_only(v), None)

    def value_pass(kept, grad):
        return (grad,)

    def grad_only(v):
        return v

    def grad_keep(v):
        return (v, None)

    def grad_round(kept, grad):
        return (value_only(grad),)

    round_value = jax.custom_vjp(value_only)
    round_value.defvjp(value_keep, value_pass)
    round_grad = jax.custom_vjp(grad_only)
    round_grad.defvjp(grad_keep, grad_round)
    return (round_value, round_grad)


def positions(length_row, first, count):
    doc_ends = jnp.cumsum(length_row)
    starts = doc_ends - length_row
    indices = first + jnp.arange(count, dtype=jnp.int32)
    doc_ids = jnp.sum((indices[:, None] >= doc_ends[None, :]).astype(jnp.int32), axis=1)
    onehot = doc_ids[:, None] == jnp.arange(length_row.shape[0], dtype=jnp.int32)[None, :]
    begin = jnp.sum(jnp.where(onehot, starts[None, :], 0), axis=1)
    return (indices, doc_ids, indices - begin)


def normalize(state, gain):
    return state * lax.rsqrt(jnp.mean(state * state, axis=-1, keepdims=True) + 1e-05) * gain


def rotate(values, cosine_part, sine_part):
    half = values.shape[-1] // 2
    lower = values[..., :half]
    upper = values[..., half:]
    return jnp.concatenate(
        [lower * cosine_part - upper * sine_part, upper * cosine_part + lower * sine_part], axis=-1
    )


def turning(places):
    freqs = 10000.0 ** (-(jnp.arange(HD // 2, dtype=jnp.float32) * 2.0 / HD))
    angles = places.astype(jnp.float32)[:, None] * freqs[None, :]
    return (jnp.cos(angles)[:, None, :], jnp.sin(angles)[:, None, :])


def project(state, w_query, w_key, w_value, norm_attn, cosine_part, sine_part):
    round_value, round_grad = rounders()
    count = state.shape[0]
    norm_one = round_value(normalize(state, norm_attn))
    query = round_value(
        rotate(
            round_grad(jnp.dot(norm_one, w_query, precision=None)).reshape(count, HEADS, HD),
            cosine_part,
            sine_part,
        )
    )
    keys = round_value(
        rotate(
            round_grad(jnp.dot(norm_one, w_key, precision=None)).reshape(count, KV_HEADS, HD),
            cosine_part,
            sine_part,
        )
    )
    values = round_value(round_grad(jnp.dot(norm_one, w_value, precision=None))).reshape(
        count, KV_HEADS, HD
    )
    return (query, keys, values)


def finish(state, mixed, w_out, w_gate, w_up, w_down, router, norm_ffn, recursion, active):
    round_value, round_grad = rounders()
    attended = round_grad(jnp.dot(mixed, w_out, precision=None))
    middle = state + attended
    norm_two = round_value(normalize(middle, norm_ffn))
    gated = round_grad(jnp.dot(norm_two, w_gate, precision=None))
    upward = round_grad(jnp.dot(norm_two, w_up, precision=None))
    hidden = round_value(jax.nn.silu(gated) * upward)
    fed = round_grad(jnp.dot(hidden, w_down, precision=None))
    gate = jax.nn.sigmoid(jnp.dot(state, router[:, recursion], precision=lax.Precision.HIGHEST))
    scale = active.astype(jnp.float32) * gate
    return state + scale[:, None] * (attended + fed)


def block_width(rows, spread):
    factor = 1
    while rows * factor < 512 and factor < spread:
        factor = factor * 2
    return rows * factor


def permitted(label_block, query_doc, query_order):
    allowed = (
        (query_doc[:, None] == label_block[None, :, 0])
        & (label_block[None, :, 1] <= query_order[:, None])
        & (label_block[None, :, 2] > 0)
    )
    return allowed | (label_block[None, :, 1] == query_order[:, None])


def block_scores(grouped, key_block):
    return jnp.einsum(
        "tkgd,ukd->kgtu", grouped, key_block, preferred_element_type=jnp.float32
    ) * HD ** (-0.5)


def block_probs(grouped, key_block, allowed, largest, total):
    scores = block_scores(grouped, key_block)
    shifted = jnp.where(allowed[None, None], scores - largest[..., None], -1e30)
    return jnp.exp(shifted) / total[..., None]


def attend(grouped, key_blocks, value_blocks, label_blocks, query_doc, query_order):
    rows = grouped.shape[0]
    shares = grouped.shape[2]
    start = (
        jnp.full((KV_HEADS, shares, rows), -1e30, jnp.float32),
        jnp.zeros((KV_HEADS, shares, rows), jnp.float32),
    )

    def measure(carry, block):
        key_block, label_block = block
        allowed = permitted(label_block, query_doc, query_order)

        def visit(inner):
            largest, total = inner
            scores = block_scores(grouped, key_block)
            fresh = jnp.maximum(
                largest, jnp.max(jnp.where(allowed[None, None], scores, -1e30), axis=-1)
            )
            shifted = jnp.where(allowed[None, None], scores - fresh[..., None], -1e30)
            return (fresh, total * jnp.exp(largest - fresh) + jnp.sum(jnp.exp(shifted), axis=-1))

        return (lax.cond(jnp.any(allowed), visit, lambda inner: inner, carry), None)

    (largest, total), unused = lax.scan(measure, start, (key_blocks, label_blocks))

    def collect_values(mixed, block):
        key_block, value_block, label_block = block
        allowed = permitted(label_block, query_doc, query_order)

        def visit(inner):
            probs = block_probs(grouped, key_block, allowed, largest, total).astype(jnp.bfloat16)
            return inner + jnp.einsum(
                "kgtu,ukd->tkgd", probs, value_block, preferred_element_type=jnp.float32
            )

        return (lax.cond(jnp.any(allowed), visit, lambda inner: inner, mixed), None)

    mixed, unused = lax.scan(
        collect_values,
        jnp.zeros((rows, KV_HEADS, shares, HD), jnp.float32),
        (key_blocks, value_blocks, label_blocks),
    )
    return (mixed.reshape(rows, HEADS * HD).astype(jnp.bfloat16), largest, total)


def attend_back(
    grouped,
    upstream_grouped,
    key_blocks,
    value_blocks,
    label_blocks,
    query_doc,
    query_order,
    largest,
    total,
):
    rows = grouped.shape[0]
    shares = grouped.shape[2]

    def measure_delta(delta, block):
        key_block, value_block, label_block = block
        allowed = permitted(label_block, query_doc, query_order)

        def visit(inner):
            probs = block_probs(grouped, key_block, allowed, largest, total)
            upstream = jnp.einsum(
                "tkgd,ukd->kgtu", upstream_grouped, value_block, preferred_element_type=jnp.float32
            )
            return inner + jnp.sum(probs * upstream, axis=-1)

        return (lax.cond(jnp.any(allowed), visit, lambda inner: inner, delta), None)

    delta, unused = lax.scan(
        measure_delta,
        jnp.zeros((KV_HEADS, shares, rows), jnp.float32),
        (key_blocks, value_blocks, label_blocks),
    )

    def spread_back(query_grad, block):
        key_block, value_block, label_block = block
        allowed = permitted(label_block, query_doc, query_order)

        def visit(inner):
            probs = block_probs(grouped, key_block, allowed, largest, total)
            upstream = jnp.einsum(
                "tkgd,ukd->kgtu", upstream_grouped, value_block, preferred_element_type=jnp.float32
            )
            score_grad = (probs * (upstream - delta[..., None])).astype(jnp.bfloat16)
            updated = inner + jnp.einsum(
                "kgtu,ukd->tkgd", score_grad, key_block, preferred_element_type=jnp.float32
            )
            key_grad = jnp.einsum(
                "kgtu,tkgd->ukd", score_grad, grouped, preferred_element_type=jnp.float32
            ) * HD ** (-0.5)
            value_grad = jnp.einsum(
                "kgtu,tkgd->ukd",
                probs.astype(jnp.bfloat16),
                upstream_grouped,
                preferred_element_type=jnp.float32,
            )
            return (updated, key_grad, value_grad)

        def skip(inner):
            return (
                inner,
                jnp.zeros(key_block.shape, jnp.float32),
                jnp.zeros(value_block.shape, jnp.float32),
            )

        updated, key_grad, value_grad = lax.cond(jnp.any(allowed), visit, skip, query_grad)
        return (updated, (key_grad, value_grad))

    query_grad, (key_grads, value_grads) = lax.scan(
        spread_back,
        jnp.zeros((rows, KV_HEADS, shares, HD), jnp.float32),
        (key_blocks, value_blocks, label_blocks),
    )
    count = key_blocks.shape[0] * key_blocks.shape[1]
    return (
        (query_grad * HD ** (-0.5)).reshape(rows, HEADS, HD),
        key_grads.reshape(count, KV_HEADS * HD),
        value_grads.reshape(count, KV_HEADS * HD),
    )


def forward_step(state, weights, recursion, labels, active):
    w_query, w_key, w_value, w_out, w_gate, w_up, w_down, router, norm_attn, norm_ffn = weights
    rows = state.shape[0]
    spread = lax.axis_size("tok")
    cosine_part, sine_part = turning(labels[:, 2])

    def front(inputs, query_matrix, key_matrix, value_matrix, gain):
        return project(inputs, query_matrix, key_matrix, value_matrix, gain, cosine_part, sine_part)

    (query, keys, values), front_pull = jax.vjp(front, state, w_query, w_key, w_value, norm_attn)
    key_labels = jnp.stack([labels[:, 0], labels[:, 1], active.astype(jnp.int32)], axis=1)
    keys_all, values_all, labels_all = (
        lax.all_gather(
            keys.reshape(rows, KV_HEADS * HD).astype(jnp.bfloat16), "tok", axis=0, tiled=True
        ),
        lax.all_gather(
            values.reshape(rows, KV_HEADS * HD).astype(jnp.bfloat16), "tok", axis=0, tiled=True
        ),
        lax.all_gather(key_labels, "tok", axis=0, tiled=True),
    )
    count = keys_all.shape[0]
    width = block_width(rows, spread)
    key_blocks = keys_all.reshape(count // width, width, KV_HEADS, HD)
    value_blocks = values_all.reshape(count // width, width, KV_HEADS, HD)
    label_blocks = labels_all.reshape(count // width, width, 3)
    grouped = query.astype(jnp.bfloat16).reshape(rows, KV_HEADS, HEADS // KV_HEADS, HD)
    mixed, largest, total = attend(
        grouped, key_blocks, value_blocks, label_blocks, labels[:, 0], labels[:, 1]
    )

    def rear(
        inputs, mixed_in, out_matrix, gate_matrix, up_matrix, down_matrix, router_matrix, gain
    ):
        return finish(
            inputs,
            mixed_in,
            out_matrix,
            gate_matrix,
            up_matrix,
            down_matrix,
            router_matrix,
            gain,
            recursion,
            active,
        )

    new_state, rear_pull = jax.vjp(
        rear, state, mixed.astype(jnp.float32), w_out, w_gate, w_up, w_down, router, norm_ffn
    )
    kept = (
        front_pull,
        rear_pull,
        grouped,
        key_blocks,
        value_blocks,
        label_blocks,
        labels[:, 0],
        labels[:, 1],
        largest,
        total,
    )
    return (new_state, kept)


def backward_step(gradient, kept):
    (
        front_pull,
        rear_pull,
        grouped,
        key_blocks,
        value_blocks,
        label_blocks,
        query_doc,
        query_order,
        largest,
        total,
    ) = kept
    rows = grouped.shape[0]
    gradient, mixed_grad, out_grad, gate_grad, up_grad, down_grad, router_grad, ffn_gain_grad = (
        rear_pull(gradient)
    )
    upstream_grouped = mixed_grad.astype(jnp.bfloat16).reshape(
        rows, KV_HEADS, HEADS // KV_HEADS, HD
    )
    query_grad, key_grads, value_grads = attend_back(
        grouped,
        upstream_grouped,
        key_blocks,
        value_blocks,
        label_blocks,
        query_doc,
        query_order,
        largest,
        total,
    )
    key_owned, value_owned = (
        lax.psum_scatter(
            key_grads.astype(jnp.bfloat16), "tok", scatter_dimension=0, tiled=True
        ).astype(jnp.float32),
        lax.psum_scatter(
            value_grads.astype(jnp.bfloat16), "tok", scatter_dimension=0, tiled=True
        ).astype(jnp.float32),
    )
    front_grad, query_matrix_grad, key_matrix_grad, value_matrix_grad, attn_gain_grad = front_pull(
        (query_grad, key_owned.reshape(rows, KV_HEADS, HD), value_owned.reshape(rows, KV_HEADS, HD))
    )
    return (
        gradient + front_grad,
        (
            query_matrix_grad,
            key_matrix_grad,
            value_matrix_grad,
            out_grad,
            gate_grad,
            up_grad,
            down_grad,
            router_grad,
            attn_gain_grad,
            ffn_gain_grad,
        ),
    )


def add_tuples(running, adding):
    return tuple((jnp.add(earlier, latest) for earlier, latest in zip(running, adding)))


def collect(running, grads):
    return grads if running is None else add_tuples(running, grads)


def per_device(
    tokens,
    w_query,
    w_key,
    w_value,
    w_out,
    w_gate,
    w_up,
    w_down,
    router,
    norm_attn,
    norm_ffn,
    lengths,
    depths,
    padding,
    cotangent,
):
    shards = (w_query, w_key, w_value, w_out, w_gate, w_up, w_down, router, norm_attn, norm_ffn)
    gathered = (
        lax.all_gather(shards[0], "tok", axis=0, tiled=True),
        lax.all_gather(shards[1], "tok", axis=0, tiled=True),
        lax.all_gather(shards[2], "tok", axis=0, tiled=True),
        lax.all_gather(shards[3], "tok", axis=0, tiled=True),
        lax.all_gather(shards[4], "tok", axis=0, tiled=True),
        lax.all_gather(shards[5], "tok", axis=0, tiled=True),
        lax.all_gather(shards[6], "tok", axis=0, tiled=True),
        lax.all_gather(shards[7], "tok", axis=0, tiled=True),
        lax.all_gather(shards[8], "tok", axis=0, tiled=True),
        lax.all_gather(shards[9], "tok", axis=0, tiled=True),
    )
    weights = tuple((matrix.astype(jnp.float32) for matrix in gathered))
    rows = tokens.shape[0]
    width_model = tokens.shape[1]
    spread = lax.axis_size("tok")
    orders, doc_ids, places = positions(lengths[0], lax.axis_index("tok") * rows, rows)
    home_labels = jnp.stack([doc_ids, orders, places], axis=1)
    state = tokens.astype(jnp.float32)
    gradient = cotangent.astype(jnp.float32)
    running = None
    state, first_kept = forward_step(state, weights, 0, home_labels, padding > 0)
    eligible = (depths >= 2) & (padding > 0)
    ranking = jnp.cumsum(eligible.astype(jnp.int32)) - 1
    capacity = rows * 3 // 4
    per_peer = capacity // spread
    slots = jnp.where(eligible, ranking % spread * per_peer + ranking // spread, capacity)
    safe_slots = jnp.minimum(slots, capacity - 1)
    home_tile_labels = jnp.concatenate([home_labels, depths[:, None]], axis=1)
    blank = jnp.broadcast_to(jnp.array([-1, -1, 0, 0], jnp.int32), (capacity, 4))
    outgoing = jnp.zeros((capacity, width_model), jnp.float32).at[slots].set(state, mode="drop")
    outgoing_labels = blank.at[slots].set(home_tile_labels, mode="drop")
    tiles, tile_labels = (
        lax.all_to_all(
            outgoing.astype(jnp.bfloat16), "tok", split_axis=0, concat_axis=0, tiled=True
        ).astype(outgoing.dtype),
        lax.all_to_all(outgoing_labels, "tok", split_axis=0, concat_axis=0, tiled=True),
    )
    tile_kept = []
    for recursion in range(1, RECS):
        tiles, kept = forward_step(
            tiles, weights, recursion, tile_labels[:, :3], tile_labels[:, 3] > recursion
        )
        tile_kept.append(kept)
    returned = lax.all_to_all(
        for_sending(tiles), "tok", split_axis=0, concat_axis=0, tiled=True
    ).astype(tiles.dtype)
    final = jnp.where(eligible[:, None], jnp.take(returned, safe_slots, axis=0), state)
    outgoing_grad = (
        jnp.zeros((capacity, width_model), jnp.float32).at[slots].set(gradient, mode="drop")
    )
    tile_grad = lax.all_to_all(
        outgoing_grad.astype(jnp.bfloat16), "tok", split_axis=0, concat_axis=0, tiled=True
    ).astype(outgoing_grad.dtype)
    for kept in reversed(tile_kept):
        tile_grad, grads = backward_step(tile_grad, kept)
        running = collect(running, grads)
    returned_grad = lax.all_to_all(
        tile_grad.astype(jnp.bfloat16), "tok", split_axis=0, concat_axis=0, tiled=True
    ).astype(tile_grad.dtype)
    gradient = jnp.where(eligible[:, None], jnp.take(returned_grad, safe_slots, axis=0), gradient)
    gradient, grads = backward_step(gradient, first_kept)
    running = collect(running, grads)
    running = jax.tree.map(
        lambda part: part.astype(jnp.float32),
        lax.psum_scatter(for_sending(running), "tok", scatter_dimension=0, tiled=True),
    )
    summed = jax.tree.map(
        lambda part: part.astype(jnp.float32), lax.psum(for_sending(running), "grp")
    )
    return (final.astype(jnp.bfloat16), gradient.astype(jnp.bfloat16)) + tuple(summed)


def solution(mesh):
    placed = (
        P(("grp", "tok"), None),
        P("tok", None),
        P("tok", None),
        P("tok", None),
        P("tok", None),
        P("tok", None),
        P("tok", None),
        P("tok", None),
        P("tok", None),
        P("tok"),
        P("tok"),
        P("grp", None),
        P(("grp", "tok")),
        P(("grp", "tok")),
        P(("grp", "tok"), None),
    )
    return jax.shard_map(
        per_device,
        mesh=mesh,
        in_specs=placed,
        out_specs=(
            P(("grp", "tok"), None),
            P(("grp", "tok"), None),
            P("tok", None),
            P("tok", None),
            P("tok", None),
            P("tok", None),
            P("tok", None),
            P("tok", None),
            P("tok", None),
            P("tok", None),
            P("tok"),
            P("tok"),
        ),
        check_vma=False,
    )
```

profile of v0, /device:TPU:17, one launch (start us, length us, event | category | flops | bytes accessed | tf_op | source)
XLA Modules:
  0.0 2095.8 jit_solution(12987282596749066508)
XLA Ops:
  27.4 28.0 %all-gather.1 = bf16[8,120,320]{1,2,0:T(8,128)(2,1)S(1)} all-gather(bf16[1,120,320]{1,2,0:T(8,128)(2,1)} %bitcast.946), channel_id=1, replica_groups=mesh['grp'=4,'tok'=8] {'tok'}, dimensions={0}, use_global_device_ids=true | all-gather | bytes 691200 | tf_op jit(solution)/shard_map/all_gather | solution.py:418
  57.8 26.5 %all-gather.2 = bf16[8,120,320]{1,2,0:T(8,128)(2,1)S(1)} all-gather(bf16[1,120,320]{1,2,0:T(8,128)(2,1)S(1)} %bitcast.947), channel_id=1, replica_groups=mesh['grp'=4,'tok'=8] {'tok'}, dimensions={0}, use_global_device_ids=true | all-gather | bytes 691200 | tf_op jit(solution)/shard_map/all_gather | solution.py:419
  112.5 25.0 %all_gather.58 = s32[2048,3]{0,1:T(4,128)S(1)} all-gather(s32[256,3]{0,1:T(4,128)S(1)} %pad_add_fusion.2), channel_id=1, replica_groups=mesh['grp'=4,'tok'=8] {'tok'}, dimensions={0}, use_global_device_ids=true | all-gather | bytes 27648 | tf_op jit(solution)/shard_map/all_gather | solution.py:285
  163.2 42.4 %all-gather.15.cloned.1.call-done = bf16[960,960]{1,0:T(8,128)(2,1)} async-done(((bf16[120,960]{1,0:T(8,128)(2,1)}), bf16[960,960]{1,0:T(8,128)(2,1)}) %all-gather.15.cloned.1.call-update) | async-done | bytes 1843216 | tf_op jit(solution)/shard_map/all_gather | solution.py:417
  257.1 79.8 %all-gather.21.cloned.1.call-done = bf16[960,2560]{1,0:T(8,128)(2,1)} async-done(((bf16[120,2560]{1,0:T(8,128)(2,1)}), bf16[960,2560]{1,0:T(8,128)(2,1)}) %all-gather.21.cloned.1.call-update) | async-done | bytes 4915216 | tf_op jit(solution)/shard_map/all_gather | solution.py:421
  342.3 77.1 %all-gather.23.cloned.1.call-done = bf16[960,2560]{1,0:T(8,128)(2,1)} async-done(((bf16[120,2560]{1,0:T(8,128)(2,1)}), bf16[960,2560]{1,0:T(8,128)(2,1)}) %all-gather.23.cloned.1.call-update) | async-done | bytes 4915216 | tf_op jit(solution)/shard_map/all_gather | solution.py:422
  426.4 79.7 %all-gather.25.cloned.1.call-done = bf16[2560,960]{1,0:T(8,128)(2,1)} async-done(((bf16[320,960]{1,0:T(8,128)(2,1)}), bf16[2560,960]{1,0:T(8,128)(2,1)}) %all-gather.25.cloned.1.call-update) | async-done | bytes 4915216 | tf_op jit(solution)/shard_map/all_gather | solution.py:423
  524.6 22.9 %all-gather.3 = s32[8,192,3]{1,2,0:T(4,128)S(1)} all-gather(s32[1,192,3]{1,2,0:T(4,128)S(1)} %get-tuple-element.2797), channel_id=1, replica_groups=mesh['grp'=4,'tok'=8] {'tok'}, dimensions={0}, use_global_device_ids=true | all-gather | bytes 20736 | tf_op jit(solution)/shard_map/all_gather | solution.py:285
  547.7 23.8 %all-gather.4 = s32[8,192,3]{1,2,0:T(4,128)S(1)} all-gather(s32[1,192,3]{1,2,0:T(4,128)S(1)} %get-tuple-element.2796), channel_id=1, replica_groups=mesh['grp'=4,'tok'=8] {'tok'}, dimensions={0}, use_global_device_ids=true | all-gather | bytes 20736 | tf_op jit(solution)/shard_map/all_gather | solution.py:285
  585.2 26.4 %all_gather.71 = bf16[1536,320]{1,0:T(8,128)(2,1)S(1)} all-gather(bf16[192,320]{1,0:T(8,128)(2,1)S(1)} %copy.330), channel_id=1, replica_groups=mesh['grp'=4,'tok'=8] {'tok'}, dimensions={0}, use_global_device_ids=true | all-gather | bytes 1105920 | tf_op jit(solution)/shard_map/all_gather | solution.py:279
  631.1 26.3 %all_gather.72 = bf16[1536,320]{1,0:T(8,128)(2,1)S(1)} all-gather(bf16[192,320]{1,0:T(8,128)(2,1)S(1)} %copy-done.147), channel_id=1, replica_groups=mesh['grp'=4,'tok'=8] {'tok'}, dimensions={0}, use_global_device_ids=true | all-gather | bytes 1105920 | tf_op jit(solution)/shard_map/all_gather | solution.py:282
  694.4 26.5 %all_gather.74 = bf16[1536,320]{1,0:T(8,128)(2,1)S(1)} all-gather(bf16[192,320]{1,0:T(8,128)(2,1)S(1)} %copy.341), channel_id=1, replica_groups=mesh['grp'=4,'tok'=8] {'tok'}, dimensions={0}, use_global_device_ids=true | all-gather | bytes 1105920 | tf_op jit(solution)/shard_map/all_gather | solution.py:279
  736.3 28.9 %all_gather.75 = bf16[1536,320]{1,0:T(8,128)(2,1)} all-gather(bf16[192,320]{1,0:T(8,128)(2,1)S(1)} %copy-done.148), channel_id=1, replica_groups=mesh['grp'=4,'tok'=8] {'tok'}, dimensions={0}, use_global_device_ids=true | all-gather | bytes 1105920 | tf_op jit(solution)/shard_map/all_gather | solution.py:282
  813.5 16.4 while.173
  833.0 23.0 %while.174 = (s32[]{:T(128)}, f32[192,5,3,64]{0,3,2,1:T(8,128)S(1)}, bf16[2,768,5,64]{1,3,2,0:T(8,128)(2,1)}, bf16[2,768,5,64]{1,3,2,0:T(8,128)(2,1)}, s32[192,1...) while((s32[]{:T(128)}, f32[192,5,3,64]{0,3,2,1:T(8,128)S(1)}, ...), condition=%wide.region_62.64_spmd, body=%wide.region_58.63_spmd.sunk | while | flops 1434981120 | bytes 55801664 | solution.py:254
  874.7 89.3 %reduce-scatter.39.cloned.1.call-done = bf16[192,320]{1,0:T(8,128)(2,1)} async-done(((bf16[1536,320]{1,0:T(8,128)(2,1)}), bf16[192,320]{1,0:T(8,128)(2,1)}) %reduce-scatter.39.cloned.1.call-update) | async-done | bytes 122896
  965.1 65.5 %reduce-scatter.37.cloned.1.call-done = bf16[192,320]{1,0:T(8,128)(2,1)} async-done(((bf16[1536,320]{1,0:T(8,128)(2,1)}), bf16[192,320]{1,0:T(8,128)(2,1)}) %reduce-scatter.37.cloned.1.call-update) | async-done | bytes 122896
  1047.1 18.7 while.175
  1067.9 26.7 %while.176 = (s32[]{:T(128)}, f32[192,5,3,64]{0,3,2,1:T(8,128)S(1)}, bf16[2,768,5,64]{1,3,2,0:T(8,128)(2,1)}, bf16[2,768,5,64]{1,3,2,0:T(8,128)(2,1)}, s32[192,1...) while((s32[]{:T(128)}, f32[192,5,3,64]{0,3,2,1:T(8,128)S(1)}, ...), condition=%wide.region_78.80_spmd, body=%wide.region_74.79_spmd.sunk | while | flops 1434981120 | bytes 47560704 | solution.py:254
  1108.3 55.6 %reduce-scatter.43.cloned.1.call-done = bf16[192,320]{1,0:T(8,128)(2,1)} async-done(((bf16[1536,320]{1,0:T(8,128)(2,1)}), bf16[192,320]{1,0:T(8,128)(2,1)}) %reduce-scatter.43.cloned.1.call-update) | async-done | bytes 122896
  1165.0 65.9 %reduce-scatter.41.cloned.1.call-done = bf16[192,320]{1,0:T(8,128)(2,1)} async-done(((bf16[1536,320]{1,0:T(8,128)(2,1)}), bf16[192,320]{1,0:T(8,128)(2,1)}) %reduce-scatter.41.cloned.1.call-update) | async-done | bytes 122896
  1273.0 18.7 while.179
  1291.9 30.3 %while.180 = (s32[]{:T(128)}, f32[256,5,3,64]{0,3,2,1:T(8,128)S(1)}, bf16[4,512,5,64]{1,3,2,0:T(8,128)(2,1)}, bf16[4,512,5,64]{1,3,2,0:T(8,128)(2,1)}, s32[256]{...) while((s32[]{:T(128)}, f32[256,5,3,64]{0,3,2,1:T(8,128)S(1)}, ...), condition=%wide.region_94.96_spmd.clone, body=%wide.region_90.95_spmd.clone.sunk | while | flops 1275511552 | bytes 42611968 | solution.py:254
  1333.7 73.1 %reduce-scatter.25.cloned.1.call-done = bf16[256,320]{0,1:T(8,128)(2,1)} async-done(((bf16[2048,320]{0,1:T(8,128)(2,1)}), bf16[256,320]{0,1:T(8,128)(2,1)}) %reduce-scatter.25.cloned.1.call-update) | async-done | bytes 163856 | tf_op jit(solution)/shard_map/reduce_scatter | solution.py:363
  1407.8 66.7 %reduce-scatter.23.cloned.1.call-done = bf16[256,320]{0,1:T(8,128)(2,1)} async-done(((bf16[2048,320]{0,1:T(8,128)(2,1)}), bf16[256,320]{0,1:T(8,128)(2,1)}) %reduce-scatter.23.cloned.1.call-update) | async-done | bytes 163856 | tf_op jit(solution)/shard_map/reduce_scatter | solution.py:366
  1569.5 65.5 %reduce-scatter.29.cloned.1.call-done = bf16[120,960]{1,0:T(8,128)(2,1)} async-done(((bf16[960,960]{1,0:T(8,128)(2,1)}), bf16[120,960]{1,0:T(8,128)(2,1)}) %reduce-scatter.29.cloned.1.call-update) | async-done | bytes 230416 | tf_op jit(solution)/shard_map/reduce_scatter | solution.py:481
  1635.0 68.9 %reduce-scatter.27.cloned.1.call-done = bf16[120,960]{1,0:T(8,128)(2,1)} async-done(((bf16[960,960]{1,0:T(8,128)(2,1)}), bf16[120,960]{1,0:T(8,128)(2,1)}) %reduce-scatter.27.cloned.1.call-update) | async-done | bytes 230416 | tf_op jit(solution)/shard_map/reduce_scatter | solution.py:481
  1703.9 107.4 %reduce-scatter.35.cloned.1.call-done = bf16[320,960]{1,0:T(8,128)(2,1)} async-done(((bf16[2560,960]{1,0:T(8,128)(2,1)}), bf16[320,960]{1,0:T(8,128)(2,1)}) %reduce-scatter.35.cloned.1.call-update) | async-done | bytes 614416 | tf_op jit(solution)/shard_map/reduce_scatter | solution.py:481
  1811.3 102.4 %reduce-scatter.33.cloned.1.call-done = bf16[120,2560]{1,0:T(8,128)(2,1)} async-done(((bf16[960,2560]{1,0:T(8,128)(2,1)}), bf16[120,2560]{1,0:T(8,128)(2,1)}) %reduce-scatter.33.cloned.1.call-update) | async-done | bytes 614416 | tf_op jit(solution)/shard_map/reduce_scatter | solution.py:481
  1913.7 102.1 %reduce-scatter.31.cloned.1.call-done = bf16[120,2560]{1,0:T(8,128)(2,1)} async-done(((bf16[960,2560]{1,0:T(8,128)(2,1)}), bf16[120,2560]{1,0:T(8,128)(2,1)}) %reduce-scatter.31.cloned.1.call-update) | async-done | bytes 614416 | tf_op jit(solution)/shard_map/reduce_scatter | solution.py:481
  2019.0 24.4 %all-reduce.22 = (bf16[960,3]{0,1:T(4,128)(2,1)S(1)}, bf16[960]{0:T(1024)(128)(2,1)S(1)}, bf16[960]{0:T(1024)(128)(2,1)S(1)}) all-reduce(bf16[960,3]{0,1:T(4,128)(2,1)S(1)} %add_convert_fusion.20, bf16[960]{0:T(1024)(128)(2,1)S(1)} %add_convert_fusion.22, ...), channel_id=15, replica_groups=mesh['grp'=4,'tok'=8] {'tok'}, use_global_device_ids=true, to_apply=%region_112.114.clone | all-reduce | flops 4800 | bytes 19200
  2060.6 18.3 all-reduce.32.cloned.1.call-done
  (1149 shorter events, 876.2 us)
Async XLA Ops:
  7.2 134.9 %all-gather.13.cloned.1.call-start = ((), (), s32[]{:S(2)}) async-start(), calls=%async_computation.16 | async-start | bytes 1474560 | tf_op jit(solution)/shard_map/all_gather | solution.py:279
  25.0 666.1 %copy-start.149 = (f32[960]{0:T(1024)}, f32[960]{0:T(1024)S(1)}, u32[]{:S(2)}) copy-start(f32[960]{0:T(1024)S(1)} %convert_element_type.499) | copy-start | bytes 11524
  57.7 98.7 %all-gather.17.cloned.1.call-start = ((), (), s32[]{:S(2)}) async-start(), calls=%async_computation.18 | async-start | bytes 1474560 | tf_op jit(solution)/shard_map/all_gather | solution.py:282
  85.3 606.3 %copy-start.23 = (bf16[960,320]{0,1:T(8,128)(2,1)}, bf16[960,320]{0,1:T(8,128)(2,1)S(1)}, u32[]{:S(2)}) copy-start(bf16[960,320]{0,1:T(8,128)(2,1)S(1)} %reshape.740) | copy-start | bytes 1843204
  86.4 119.2 %all-gather.15.cloned.1.call-start = ((), (), s32[]{:S(2)}) async-start(), calls=%async_computation.17 | async-start | bytes 2211840 | tf_op jit(solution)/shard_map/all_gather | solution.py:417
  87.1 167.2 %all-gather.19.cloned.1.call-start = ((), (), s32[]{:S(2)}) async-start(), calls=%async_computation.19 | async-start | bytes 2211840 | tf_op jit(solution)/shard_map/all_gather | solution.py:420
  87.7 249.2 %all-gather.21.cloned.1.call-start = ((), (), s32[]{:S(2)}) async-start(), calls=%async_computation.20 | async-start | bytes 5529600 | tf_op jit(solution)/shard_map/all_gather | solution.py:421
  88.3 331.1 %all-gather.23.cloned.1.call-start = ((), (), s32[]{:S(2)}) async-start(), calls=%async_computation.21 | async-start | bytes 5529600 | tf_op jit(solution)/shard_map/all_gather | solution.py:422
  92.7 49.3 %all-to-all-start.1 = ((s32[8,24,4]{1,2,0:T(4,128)}), s32[8,24,4]{1,2,0:T(4,128)S(1)}, u32[]{:S(2)}, u32[]{:S(2)}) async-start(s32[8,24,4]{1,2,0:T(4,128)} %copy.326), calls=%async_computation.1 | async-start | bytes 32768 | tf_op jit(solution)/shard_map/all_to_all | solution.py:452
  99.7 406.3 %all-gather.25.cloned.1.call-start = ((), (), s32[]{:S(2)}) async-start(), calls=%async_computation.22 | async-start | bytes 5898240 | tf_op jit(solution)/shard_map/all_gather | solution.py:423
  137.5 672.6 %copy-start.153 = (f32[960]{0:T(1024)}, f32[960]{0:T(1024)S(1)}, u32[]{:S(2)}) copy-start(f32[960]{0:T(1024)S(1)} %convert_element_type.506) | copy-start | bytes 11524
  519.9 51.8 %all-to-all-start = ((bf16[8,24,960]{2,1,0:T(8,128)(2,1)}), bf16[8,24,960]{2,1,0:T(8,128)(2,1)S(1)}, u32[]{:S(2)}, u32[]{:S(2)}) async-start(bf16[8,24,960]{2,1,0:T(8,128)(2,1)} %bitcast.919), calls=%async_computation | async-start | bytes 786432 | tf_op jit(solution)/shard_map/all_to_all | solution.py:449
  571.8 220.5 %all-to-all-start.3 = ((bf16[8,24,960]{2,1,0:T(8,128)(2,1)}), bf16[8,24,960]{2,1,0:T(8,128)(2,1)}, u32[]{:S(2)}, u32[]{:S(2)}) async-start(bf16[8,24,960]{2,1,0:T(8,128)(2,1)} %bitcast.918), calls=%async_computation.3 | async-start | bytes 786432 | tf_op jit(solution)/shard_map/all_to_all | solution.py:467
  580.6 383.4 %reduce-scatter.39.cloned.1.call-start = ((), (), s32[]{:S(2)}) async-start(), calls=%async_computation.31 | async-start | bytes 1327104
  862.1 168.5 %reduce-scatter.37.cloned.1.call-start = ((), (), s32[]{:S(2)}) async-start(), calls=%async_computation.30 | async-start | bytes 1327104
  866.8 297.1 %reduce-scatter.43.cloned.1.call-start = ((), (), s32[]{:S(2)}) async-start(), calls=%async_computation.33 | async-start | bytes 1327104
  1100.4 130.5 %reduce-scatter.41.cloned.1.call-start = ((), (), s32[]{:S(2)}) async-start(), calls=%async_computation.32 | async-start | bytes 1327104
  1237.5 12.7 all-to-all-start.4
  1242.1 164.6 %reduce-scatter.25.cloned.1.call-start = ((), (), s32[]{:S(2)}) async-start(), calls=%async_computation.24 | async-start | bytes 1474560 | tf_op jit(solution)/shard_map/reduce_scatter | solution.py:363
  1326.0 148.5 %reduce-scatter.23.cloned.1.call-start = ((), (), s32[]{:S(2)}) async-start(), calls=%async_computation.23 | async-start | bytes 1474560 | tf_op jit(solution)/shard_map/reduce_scatter | solution.py:366
  1329.9 236.3 %all-reduce.30.cloned.1.call-start = ((), (), s32[]{:S(2)}) async-start(), calls=%async_computation.34 | async-start | bytes 2621440
  1479.7 155.2 %reduce-scatter.29.cloned.1.call-start = ((), (), s32[]{:S(2)}) async-start(), calls=%async_computation.26 | async-start | bytes 2211840 | tf_op jit(solution)/shard_map/reduce_scatter | solution.py:481
  1484.3 219.6 %reduce-scatter.27.cloned.1.call-start = ((), (), s32[]{:S(2)}) async-start(), calls=%async_computation.25 | async-start | bytes 2211840 | tf_op jit(solution)/shard_map/reduce_scatter | solution.py:481
  1488.5 322.8 %reduce-scatter.35.cloned.1.call-start = ((), (), s32[]{:S(2)}) async-start(), calls=%async_computation.29 | async-start | bytes 5898240 | tf_op jit(solution)/shard_map/reduce_scatter | solution.py:481
  1504.2 409.6 %reduce-scatter.33.cloned.1.call-start = ((), (), s32[]{:S(2)}) async-start(), calls=%async_computation.28 | async-start | bytes 5529600 | tf_op jit(solution)/shard_map/reduce_scatter | solution.py:481
  1520.3 495.5 %reduce-scatter.31.cloned.1.call-start = ((), (), s32[]{:S(2)}) async-start(), calls=%async_computation.27 | async-start | bytes 5529600 | tf_op jit(solution)/shard_map/reduce_scatter | solution.py:481
  1536.5 14.7 all-to-all-start.2
  1541.3 537.6 %all-reduce.32.cloned.1.call-start = ((), (), s32[]{:S(2)}) async-start(), calls=%async_computation.35 | async-start | bytes 5079040 | tf_op jit(solution)/shard_map/psum | solution.py:484
  1560.2 497.0 %copy-start.42 = (f32[256,960]{0,1:T(8,128)S(1)}, f32[256,960]{0,1:T(8,128)}, u32[]{:S(2)}) copy-start(f32[256,960]{0,1:T(8,128)} %copy-done.40) | copy-start | bytes 2949124
  1560.2 497.0 %copy-start.58 = (bf16[256,960]{0,1:T(8,128)(2,1)S(1)}, bf16[256,960]{0,1:T(8,128)(2,1)}, u32[]{:S(2)}) copy-start(bf16[256,960]{0,1:T(8,128)(2,1)} %param.80) | copy-start | bytes 1474564
  1560.2 497.0 %copy-start.156 = (f32[960]{0:T(1024)S(1)}, f32[960]{0:T(1024)}, u32[]{:S(2)}) copy-start(f32[960]{0:T(1024)} %copy-done.153) | copy-start | bytes 11524
  1560.2 497.0 %copy-start.170 = (f32[256]{0:T(256)S(1)}, f32[256]{0:T(256)}, u32[]{:S(2)}) copy-start(f32[256]{0:T(256)} %copy-done.168) | copy-start | bytes 3076
  (253 other events, 11658.6 us)
Sparse Core Ops, SparseCore 0:
  57.9 54.9 all-gather.12
  115.5 40.8 all-gather.16
  158.6 47.0 all-gather.14
  207.7 46.6 all-gather.18
  256.3 80.4 all-gather.20
  338.9 80.4 all-gather.22
  421.6 84.4 all-gather.24
  862.2 101.6 reduce-scatter.38
  967.9 62.6 reduce-scatter.36
  1100.5 63.3 reduce-scatter.42
  1167.8 63.0 reduce-scatter.40
  1326.1 80.6 reduce-scatter.24
  1410.2 64.2 reduce-scatter.22
  1479.9 86.2 all-reduce.29
  1569.9 65.0 reduce-scatter.28
  1638.3 65.5 reduce-scatter.26
  1707.8 103.5 reduce-scatter.34
  1815.3 98.3 reduce-scatter.32
  1917.4 98.3 reduce-scatter.30
  2019.4 59.4 all-reduce.31
where the time goes:
time: 2110 us; the launch traced here: 2100 us
  waiting for transfers between devices  1210 us (57%)
  matrix products  310 us (15%)
  blocking collectives  295 us (14%)
  local copies, waits for them, and re-layouts  117 us (6%)
  other arithmetic  92.1 us (4%)
  starting transfers between devices  31.3 us (1%)
  loops' own time  24.7 us (1%)
    reduce_scatter x5, waiting for transfers between devices, per_device(): lax.psum_scatter(for_sending(running), 'tok', scatter_dimension=0, tiled=...  446 us
    unnamed x25, waiting for transfers between devices  284 us
    all_gather x1, waiting for transfers between devices, per_device(): lax.all_gather(shards[4], 'tok', axis=0, tiled=True)  79.8 us
    all_gather x1, waiting for transfers between devices, per_device(): lax.all_gather(shards[6], 'tok', axis=0, tiled=True)  79.7 us
    all_gather x1, waiting for transfers between devices, per_device(): lax.all_gather(shards[5], 'tok', axis=0, tiled=True)  77.1 us
    reduce_scatter x1, waiting for transfers between devices, backward_step(): lax.psum_scatter(key_grads.astype(jnp.bfloat16), 'tok', scatter_dimension...  73.1 us
    all_gather x3, blocking collectives, forward_step(): lax.all_gather(key_labels, 'tok', axis=0, tiled=True)  71.7 us
    reduce_scatter x1, waiting for transfers between devices, backward_step(): lax.psum_scatter(value_grads.astype(jnp.bfloat16), 'tok', scatter_dimensi...  66.7 us
  transfers between devices with their start and end apart: 25, of which 21 were waited for; matrix products, arithmetic and copies ran while one was open for 13% of the time, Pallas kernels for 0%

commit v1 on v0

v1 whole, which is shorter than its diff:
```python
import functools

import jax
import jax.numpy as jnp
from jax import lax
from jax.experimental import pallas as pl
from jax.experimental.pallas import tpu as pltpu
from jax.sharding import PartitionSpec as P

HEADS = 15
KV_HEADS = 5
SHARES = HEADS // KV_HEADS
HD = 64
RECS = 3
EPS = 1e-05
BF = jnp.bfloat16
F32 = jnp.float32
BIG = -1e30
AXES = ("grp", "tok")


class Topo:
    def __init__(self, groups, spread):
        self.G = groups
        self.T = spread
        self.X = spread // groups
        self.Z = groups
        self.Y = groups // 2
        self.bits = {
            "z": self.Z.bit_length() - 1,
            "x": self.X.bit_length() - 1,
            "y": self.Y.bit_length() - 1,
            "c": 1,
        }

    def keys(self, dim):
        return [(dim, k) for k in range(self.bits[dim])]

    def masks(self, key):
        dim, k = key
        if dim == "c":
            return (1, 0)
        if dim == "y":
            return (2 << k, 0)
        if dim == "x":
            return (0, 1 << k)
        return (0, self.X << k)

    def pairs(self, key):
        mg, mt = self.masks(key)
        return [
            (g * self.T + t, (g ^ mg) * self.T + (t ^ mt))
            for g in range(self.G)
            for t in range(self.T)
        ]

    def swap_pairs(self):
        out = []
        for g in range(self.G):
            for t in range(self.T):
                z, x = t // self.X, t % self.X
                out.append((g * self.T + t, z * self.T + g * self.X + x))
        return out

    def bit(self, key):
        mg, mt = self.masks(key)
        if mg:
            return (lax.axis_index("grp") // mg) % 2
        return (lax.axis_index("tok") // mt) % 2


def exchange(topo, arr, key):
    return lax.ppermute(arr, AXES, topo.pairs(key))


def double(topo, arr, key, axis, stack):
    other = exchange(topo, arr, key)
    mine_is_high = topo.bit(key) == 1
    low = jnp.where(mine_is_high, other, arr)
    high = jnp.where(mine_is_high, arr, other)
    if stack:
        return jnp.stack([low, high], axis=axis)
    return jnp.concatenate([low, high], axis=axis)


def halve(topo, arr, key, axis, stack):
    mine_is_high = topo.bit(key) == 1
    if stack:
        low = lax.index_in_dim(arr, 0, axis, keepdims=False)
        high = lax.index_in_dim(arr, 1, axis, keepdims=False)
    else:
        half = arr.shape[axis] // 2
        low = lax.slice_in_dim(arr, 0, half, axis=axis)
        high = lax.slice_in_dim(arr, half, 2 * half, axis=axis)
    send = jnp.where(mine_is_high, low, high).astype(BF)
    keep = jnp.where(mine_is_high, high, low).astype(F32)
    return (keep + exchange(topo, send, key).astype(F32)).astype(BF)


def canonical(topo):
    return list(reversed(topo.keys("z"))) + list(reversed(topo.keys("x")))


def gather_rows(topo, shard, axis, order):
    me = lax.axis_index("grp")
    part = (me % 2) * topo.Y + me // 2
    pieces = jnp.stack(jnp.split(shard, topo.G, axis=axis), axis=0)
    arr = lax.dynamic_index_in_dim(pieces, part, 0, keepdims=False)
    held = []
    names = canonical(topo)
    for key in order:
        if key[0] in ("z", "x"):
            place = sum(1 for h in held if names.index(h) < names.index(key))
            arr = double(topo, arr, key, place, True)
            held.append(key)
        else:
            arr = double(topo, arr, key, axis - 2, False)
    return arr.reshape((topo.T,) + arr.shape[-2:])


def scatter_rows(topo, arr, axis, order):
    names = canonical(topo)
    held = list(names)
    arr = arr.reshape((2,) * len(names) + arr.shape[-2:])
    for key in order:
        if key[0] in ("z", "x"):
            arr = halve(topo, arr, key, held.index(key), True)
            held.remove(key)
        else:
            arr = halve(topo, arr, key, axis - 2, False)
    for key in topo.keys("y") + topo.keys("c"):
        arr = double(topo, arr, key, axis - 2, False)
    return arr


def group_order(topo):
    return list(reversed(topo.keys("y"))) + topo.keys("c") + list(reversed(topo.keys("x")))


def group_gather(topo, arr, order):
    names = group_order(topo)
    held = []
    shape = arr.shape
    for key in order:
        place = sum(1 for h in held if names.index(h) < names.index(key))
        arr = double(topo, arr, key, place, True)
        held.append(key)
    return arr.reshape((topo.T,) + shape)


def group_scatter(topo, arr, order):
    names = group_order(topo)
    held = list(names)
    arr = arr.reshape((2,) * len(names) + arr.shape[1:])
    for key in order:
        arr = halve(topo, arr, key, held.index(key), True)
        held.remove(key)
    return arr


def fill_bias(bias, key_ref, query_ref, rows, first, last):
    def body(t, carry):
        at = pl.ds(pl.multiple_of(t * rows, rows), rows)
        keys = key_ref[at, :]
        live, order = keys[:, 0:1], keys[:, 1:2]
        begin, place = query_ref[0:1, :], query_ref[1:2, :]
        allowed = ((live >= begin) & (live <= place)) | (order == place)
        bias[at, :] = jnp.where(allowed, 0.0, BIG)
        return carry

    lax.fori_loop(first, last, body, 0)


NT = (((1,), (1,)), ((), ()))
TN = (((0,), (0,)), ((), ()))


def attend_kernel(rows, span, key_ref, query_ref, kv_ref, q_ref, out_ref, stat_ref, bias, held):
    first, last = span[0], span[1]

    @pl.when(pl.program_id(0) == 0)
    def _():
        fill_bias(bias, key_ref, query_ref, rows, first, last)

    wide = q_ref.shape[1]
    queries = q_ref[0]

    def scores(t, top):
        at = pl.ds(pl.multiple_of(t * rows, rows), rows)
        s = lax.dot_general(kv_ref[at, :], queries, NT, preferred_element_type=F32) + bias[at, :]
        held[at, :] = s
        return jnp.maximum(top, jnp.max(s.reshape(rows // 8, 8, wide), axis=0))

    top = lax.fori_loop(first, last, scores, jnp.full((8, wide), BIG, F32))
    top = jnp.max(top, axis=0, keepdims=True)

    out_ref[0] = jnp.zeros(out_ref.shape[1:], F32)

    def mix(t, total):
        at = pl.ds(pl.multiple_of(t * rows, rows), rows)
        p = jnp.exp(held[at, :] - top)
        out_ref[0] += lax.dot_general(
            kv_ref[at, :], p.astype(BF), TN, preferred_element_type=F32
        )
        return total + jnp.sum(p.reshape(rows // 8, 8, wide), axis=0)

    total = lax.fori_loop(first, last, mix, jnp.zeros((8, wide), F32))
    total = jnp.sum(total, axis=0, keepdims=True)
    out_ref[0] = out_ref[0] / total
    stat_ref[0] = jnp.broadcast_to(top + jnp.log(total), (8, wide))


def attend(rows, span, key_labels, query_labels, kv_all, q_pad):
    count = kv_all.shape[0]
    wide = q_pad.shape[1]
    fixed = lambda h, s: (0, 0)
    return pl.pallas_call(
        functools.partial(attend_kernel, rows),
        grid_spec=pltpu.PrefetchScalarGridSpec(
            num_scalar_prefetch=1,
            grid=(KV_HEADS,),
            in_specs=[
                pl.BlockSpec((count, 8), fixed),
                pl.BlockSpec((8, wide), fixed),
                pl.BlockSpec((count, 2 * HD), lambda h, s: (0, h)),
                pl.BlockSpec((1, wide, 2 * HD), lambda h, s: (h, 0, 0)),
            ],
            out_specs=[
                pl.BlockSpec((1, 2 * HD, wide), lambda h, s: (h, 0, 0)),
                pl.BlockSpec((1, 8, wide), lambda h, s: (h, 0, 0)),
            ],
            scratch_shapes=[pltpu.VMEM((count, wide), F32), pltpu.VMEM((count, wide), F32)],
        ),
        out_shape=[
            jax.ShapeDtypeStruct((KV_HEADS, 2 * HD, wide), F32),
            jax.ShapeDtypeStruct((KV_HEADS, 8, wide), F32),
        ],
        compiler_params=pltpu.CompilerParams(vmem_limit_bytes=62 << 20),
        cost_estimate=pl.CostEstimate(
            flops=8 * KV_HEADS * wide * count * HD,
            bytes_accessed=2 * count * 2 * HD * KV_HEADS + 8 * KV_HEADS * wide * HD * 2,
            transcendentals=KV_HEADS * wide * count,
        ),
        name="attend",
    )(span, key_labels, query_labels, kv_all, q_pad)


def attend_back_kernel(
    rows, span, key_ref, query_ref, kv_ref, q_ref, stat_ref, delta_ref, dq_ref, dkv_ref, bias
):
    first, last = span[0], span[1]

    @pl.when(pl.program_id(0) == 0)
    def _():
        fill_bias(bias, key_ref, query_ref, rows, first, last)

    queries = q_ref[0]
    stat = stat_ref[0, 0:1, :]
    delta = delta_ref[0, 0:1, :]
    dkv_ref[...] = jnp.zeros(dkv_ref.shape, BF)
    dq_ref[0] = jnp.zeros(dq_ref.shape[1:], F32)
    low = lax.broadcasted_iota(jnp.int32, (rows, 2 * HD), 1) < HD

    def body(t, carry):
        at = pl.ds(pl.multiple_of(t * rows, rows), rows)
        kv = kv_ref[at, :]
        zero = jnp.zeros_like(kv)
        s = lax.dot_general(jnp.where(low, kv, zero), queries, NT, preferred_element_type=F32)
        p = jnp.exp(s + bias[at, :] - stat)
        dp = lax.dot_general(jnp.where(low, zero, kv), queries, NT, preferred_element_type=F32)
        ds = (p * (dp - delta)).astype(BF)
        dk = jnp.dot(ds, queries, preferred_element_type=F32)
        dv = jnp.dot(p.astype(BF), queries, preferred_element_type=F32)
        dkv_ref[at, :] = jnp.where(low, dk, dv).astype(BF)
        dq_ref[0] += lax.dot_general(kv, ds, TN, preferred_element_type=F32)
        return carry

    lax.fori_loop(first, last, body, 0)


def attend_back(rows, span, key_labels, query_labels, kv_all, q_do, stat, delta):
    count = kv_all.shape[0]
    wide = q_do.shape[1]
    fixed = lambda h, s: (0, 0)
    head = lambda h, s: (h, 0, 0)
    return pl.pallas_call(
        functools.partial(attend_back_kernel, rows),
        grid_spec=pltpu.PrefetchScalarGridSpec(
            num_scalar_prefetch=1,
            grid=(KV_HEADS,),
            in_specs=[
                pl.BlockSpec((count, 8), fixed),
                pl.BlockSpec((8, wide), fixed),
                pl.BlockSpec((count, 2 * HD), lambda h, s: (0, h)),
                pl.BlockSpec((1, wide, 2 * HD), head),
                pl.BlockSpec((1, 8, wide), head),
                pl.BlockSpec((1, 8, wide), head),
            ],
            out_specs=[
                pl.BlockSpec((1, 2 * HD, wide), head),
                pl.BlockSpec((count, 2 * HD), lambda h, s: (0, h)),
            ],
            scratch_shapes=[pltpu.VMEM((count, wide), F32)],
        ),
        out_shape=[
            jax.ShapeDtypeStruct((KV_HEADS, 2 * HD, wide), F32),
            jax.ShapeDtypeStruct((count, KV_HEADS * 2 * HD), BF),
        ],
        compiler_params=pltpu.CompilerParams(vmem_limit_bytes=62 << 20),
        cost_estimate=pl.CostEstimate(
            flops=20 * KV_HEADS * wide * count * HD,
            bytes_accessed=4 * count * 2 * HD * KV_HEADS + 8 * KV_HEADS * wide * HD * 2,
            transcendentals=KV_HEADS * wide * count,
        ),
        name="attend_back",
    )(span, key_labels, query_labels, kv_all, q_do, stat, delta)


def mm(a, b):
    return jnp.dot(a, b, preferred_element_type=F32)


def mm_nt(a, b):
    return lax.dot_general(a, b, NT, preferred_element_type=F32)


def mm_tn(a, b):
    return lax.dot_general(a, b, TN, preferred_element_type=F32)


def inverse_rms(v):
    return lax.rsqrt(jnp.mean(v * v, axis=-1, keepdims=True) + EPS)


def norm_back(grad, v, inv, gain):
    scaled = grad * gain
    dot = jnp.mean(scaled * v, axis=-1, keepdims=True)
    return (inv * scaled - v * (inv * inv * inv * dot), jnp.sum(grad * v * inv, axis=0))


def turn(values, cosine, sine):
    half = HD // 2
    lower, upper = values[..., :half], values[..., half:]
    return jnp.concatenate(
        [lower * cosine - upper * sine, upper * cosine + lower * sine], axis=-1
    )


def heads_first(v):
    n = v.shape[0]
    return v.reshape(n, HEADS, HD).transpose(1, 0, 2)


def heads_back(v):
    n = v.shape[-1] // SHARES
    return v.reshape(KV_HEADS, HD, SHARES, n).transpose(3, 0, 2, 1).reshape(n, HEADS, HD)


def pair_up(q, d):
    n = q.shape[1]
    return jnp.concatenate([q, d], axis=-1).reshape(KV_HEADS, SHARES * n, 2 * HD)


def per_device(topo, *args):
    (tokens, w_query, w_key, w_value, w_out, w_gate, w_up, w_down, router, norm_attn, norm_ffn,
     lengths, depths, padding, cotangent) = args
    rows, model = tokens.shape
    kv_cols = w_key.shape[1]
    ff = w_gate.shape[1]
    shard = w_query.shape[0]
    deep_rows = rows * 3 // 4
    zk, xk, yk, ck = (topo.keys(d) for d in "zxyc")
    zdown = list(reversed(zk))

    order_a = zdown + xk + yk + ck
    order_b = zdown + yk + xk if False else zdown + xk + yk + ck
    small = jnp.concatenate(
        [router, norm_attn[:, None], norm_ffn[:, None]], axis=1
    )
    small = jnp.pad(small, ((0, 0), (0, HD - small.shape[1])))
    w_kv = jnp.stack(
        [w_key.reshape(shard, KV_HEADS, HD), w_value.reshape(shard, KV_HEADS, HD)], axis=2
    ).reshape(shard, 2 * kv_cols)
    first = jnp.concatenate([w_query, small, w_kv], axis=1)
    first = jnp.pad(first, ((0, 0), (0, -first.shape[1] % (128 * topo.G))))
    second = jnp.concatenate([w_gate, w_up, w_out], axis=1)
    second = jnp.pad(second, ((0, 0), (0, -second.shape[1] % (128 * topo.G))))
    all_first = gather_rows(topo, first, 1, order_a).reshape(model, -1)

    own = lax.axis_index("tok") * rows + jnp.arange(rows, dtype=jnp.int32)
    eligible = (depths >= 2) & (padding > 0)
    flags = jnp.stack([eligible, ~eligible]).astype(BF)
    upto = (jnp.arange(rows)[:, None] <= jnp.arange(rows)[None, :]).astype(BF)
    counts = mm(flags, upto).astype(jnp.int32)
    slot = jnp.where(eligible, counts[0] - 1, counts[0, -1] + counts[1] - 1)
    chosen = jnp.arange(rows, dtype=jnp.int32)[:, None] == slot[None, :]
    onehot = chosen.astype(BF)
    doc_ends = jnp.cumsum(lengths[0])
    begins = jnp.sum(
        jnp.where(own[:, None] >= doc_ends[None, :], lengths[0][None, :], 0), axis=1
    )
    levels = jnp.where(padding > 0, depths, 0)
    labels = jnp.stack([own, begins, levels])
    labels = jnp.sum(jnp.where(chosen[None], labels[:, None, :], 0), axis=2)
    labels = jnp.pad(labels, ((0, 5), (0, 0)))
    swap = topo.swap_pairs()
    state = lax.ppermute(mm(onehot, tokens).astype(BF), AXES, swap).astype(F32)
    labels = lax.ppermute(labels, AXES, swap)
    gradient = lax.ppermute(mm(onehot, cotangent).astype(BF), AXES, swap).astype(F32)
    order_g = xk + yk + ck
    labels_all = group_gather(topo, labels, order_g)

    all_second = gather_rows(topo, second, 1, order_b).reshape(model, -1)
    all_down = gather_rows(topo, w_down, 0, order_a).reshape(ff, model)
    small = all_first[:, model:model + HD].astype(F32)
    gain_one, gain_two = small[:, RECS], small[:, RECS + 1]
    weight_q = all_first[:, :model]
    weight_kv = all_first[:, model + HD:model + HD + 2 * kv_cols]
    weight_gu = all_second[:, :2 * ff]
    weight_o = all_second[:, 2 * ff:2 * ff + model]
    weight_d = all_down

    pack = (lax.axis_index("grp") * topo.X) + lax.axis_index("tok") % topo.X
    begin_all, level_mine = labels[1], labels[2]
    lowest = jnp.min(labels[1])
    span = jnp.stack([lowest // rows, pack + 1]).astype(jnp.int32)
    places = (labels[0] - labels[1]).astype(F32)
    freqs = 10000.0 ** (-(jnp.arange(HD // 2, dtype=F32) * 2.0 / HD))
    angles = places[:, None] * freqs[None, :]
    cosine, sine = jnp.cos(angles), jnp.sin(angles)

    def forward(state, recursion):
        n = state.shape[0]
        cos_n, sin_n = cosine[:n], sine[:n]
        inv_one = inverse_rms(state)
        n1 = (state * inv_one * gain_one).astype(BF)
        q = heads_first(mm(n1, weight_q))
        q = (turn(q, cos_n, sin_n).astype(BF) * BF(HD ** -0.5)).astype(BF)
        kv = mm(n1, weight_kv).reshape(n, KV_HEADS, 2, HD)
        k = turn(kv[:, :, 0], cos_n[:, None], sin_n[:, None])
        kv = jnp.stack([k, kv[:, :, 1]], axis=2).reshape(n, 2 * kv_cols).astype(BF)
        kv_all = group_gather(topo, kv, order_g).reshape(topo.T * n, 2 * kv_cols)
        live = labels_all[:, 2, :n] > recursion
        order = labels_all[:, 0, :n]
        key_labels = jnp.stack([jnp.where(live, order, -1), order], axis=-1).reshape(-1, 2)
        key_labels = jnp.pad(key_labels, ((0, 0), (0, 6)))
        query_labels = jnp.stack([labels[1, :n], labels[0, :n]])
        query_labels = jnp.pad(jnp.tile(query_labels, (1, SHARES)), ((0, 6), (0, 0)))
        q_pad = pair_up(q, jnp.zeros_like(q))
        out, stat = attend(n, span, key_labels, query_labels, kv_all, q_pad)
        out = heads_back(out[:, HD:])
        mixed = out.reshape(n, HEADS * HD).astype(BF)
        attended = mm(mixed, weight_o)
        middle = state + attended
        inv_two = inverse_rms(middle)
        n2 = (middle * inv_two * gain_two).astype(BF)
        gu = mm(n2, weight_gu)
        gated, upward = gu[:, :ff], gu[:, ff:]
        hidden = (jax.nn.silu(gated) * upward).astype(BF)
        both = attended + mm(hidden, weight_d)
        gate = jax.nn.sigmoid(jnp.sum(state * small[:, recursion], axis=-1, keepdims=True))
        active = (labels[2, :n] > recursion).astype(F32)[:, None]
        new = state + active * gate * both
        kept = (state, inv_one, n1, q, kv_all, key_labels, query_labels, out, stat, mixed, middle,
                inv_two, n2, gu, hidden, both, gate, active)
        return (new, kept)

    def backward(gradient, recursion, kept):
        (state, inv_one, n1, q, kv_all, key_labels, query_labels, out, stat, mixed, middle,
         inv_two, n2, gu, hidden, both, gate, active) = kept
        n = state.shape[0]
        d_both = active * gate * gradient
        d_fed = d_both.astype(BF)
        d_gate = active * gate * (1.0 - gate) * jnp.sum(gradient * both, axis=-1, keepdims=True)
        d_router = jnp.sum(state * d_gate, axis=0)
        gated, upward = gu[:, :ff], gu[:, ff:]
        d_hidden = mm_nt(d_fed, weight_d)
        sig = jax.nn.sigmoid(gated)
        d_up = (d_hidden * gated * sig).astype(BF)
        d_gated = (d_hidden * upward * sig * (1.0 + gated * (1.0 - sig))).astype(BF)
        d_gu = jnp.concatenate([d_gated, d_up], axis=1)
        d_middle, d_gain_two = norm_back(mm_nt(d_gu, weight_gu), middle, inv_two, gain_two)
        d_att = (d_both + d_middle).astype(BF)
        gradient = gradient + d_gate * small[:, recursion] + d_middle
        d_mixed = mm_nt(d_att, weight_o).astype(BF)
        d_heads = heads_first(d_mixed)
        delta = jnp.sum(
            d_heads.astype(F32) * out.transpose(1, 0, 2), axis=-1
        ).reshape(KV_HEADS, 1, SHARES * n)
        delta = jnp.broadcast_to(delta, (KV_HEADS, 8, SHARES * n))
        dq, dkv = attend_back(
            n, span, key_labels, query_labels, kv_all, pair_up(q, d_heads), stat, delta
        )
        dkv = group_scatter(
            topo, dkv.reshape(topo.T, n, 2 * kv_cols), ck + yk + xk
        ).astype(F32).reshape(n, KV_HEADS, 2, HD)
        cos_n, sin_n = cosine[:n, None], sine[:n, None]
        dk = turn(dkv[:, :, 0], cos_n, -sin_n)
        dkv = jnp.stack([dk, dkv[:, :, 1]], axis=2).reshape(n, 2 * kv_cols).astype(BF)
        dq = turn(heads_back(dq[:, :HD]) * HD ** -0.5, cos_n, -sin_n)
        dq = dq.reshape(n, HEADS * HD).astype(BF)
        d_n1 = mm_nt(dq, weight_q) + mm_nt(dkv, weight_kv)
        d_state, d_gain_one = norm_back(d_n1, state, inv_one, gain_one)
        left = (n1, dq, dkv, mixed, d_att, n2, d_gu, hidden, d_fed)
        return (gradient + d_state, left, (d_router, d_gain_one, d_gain_two))

    whole_state, kept = forward(state, 0)
    deep = whole_state[:deep_rows]
    all_kept = [kept]
    for recursion in range(1, RECS):
        deep, kept = forward(deep, recursion)
        all_kept.append(kept)
    final = jnp.concatenate([deep, whole_state[deep_rows:]], axis=0).astype(BF)
    final = lax.ppermute(final, AXES, swap)

    deep_grad = gradient[:deep_rows]
    lefts, smalls = [], []
    for recursion in reversed(range(1, RECS)):
        deep_grad, left, tiny = backward(deep_grad, recursion, all_kept[recursion])
        lefts.append(left)
        smalls.append(tiny)
    gradient = jnp.concatenate([deep_grad, gradient[deep_rows:]], axis=0)
    gradient, left, tiny = backward(gradient, 0, all_kept[0])
    lefts.append(left)
    smalls.append(tiny)
    gradient = lax.ppermute(gradient.astype(BF), AXES, swap)

    n1, dq, dkv, mixed, d_att, n2, d_gu, hidden, d_fed = (
        jnp.concatenate(parts, axis=0) for parts in zip(*lefts)
    )
    spread = topo.T
    ring_a = ck + xk + yk + zk
    ring_b = ck + yk + xk + zk
    cut = lambda g: g.reshape(spread, -1, g.shape[-1])
    grad_down = scatter_rows(topo, cut(mm_tn(hidden, d_fed)), 0, ring_a).astype(F32)
    grad_gu = scatter_rows(topo, cut(mm_tn(n2, d_gu)), 1, ring_b).astype(F32)
    tiny = jnp.stack(
        [smalls[2][0], smalls[1][0], smalls[0][0],
         smalls[0][1] + smalls[1][1] + smalls[2][1],
         smalls[0][2] + smalls[1][2] + smalls[2][2]], axis=1
    )
    tiny = jnp.pad(tiny, ((0, 0), (0, HD - tiny.shape[1])))
    last = jnp.concatenate([mm_tn(n1, dq), tiny, mm_tn(n1, dkv), mm_tn(mixed, d_att)], axis=1)
    last = jnp.pad(last, ((0, 0), (0, -last.shape[1] % (128 * topo.G))))
    last = scatter_rows(topo, cut(last), 1, ring_a).astype(F32)
    grad_query = last[:, :model]
    tiny = last[:, model:model + HD]
    pair = last[:, model + HD:model + HD + 2 * kv_cols].reshape(shard, KV_HEADS, 2, HD)
    grad_key = pair[:, :, 0].reshape(shard, kv_cols)
    grad_value = pair[:, :, 1].reshape(shard, kv_cols)
    grad_out = last[:, model + HD + 2 * kv_cols:2 * model + HD + 2 * kv_cols]

    def unsort(v):
        return mm_tn(onehot, v).astype(BF)

    return (
        unsort(final), unsort(gradient), grad_query, grad_key, grad_value, grad_out,
        grad_gu[:, :ff], grad_gu[:, ff:], grad_down, tiny[:, :RECS], tiny[:, RECS],
        tiny[:, RECS + 1],
    )


def solution(mesh):
    topo = Topo(mesh.shape["grp"], mesh.shape["tok"])
    both = P(("grp", "tok"))
    wide = P(("grp", "tok"), None)
    rows = P("tok", None)
    row = P("tok")
    return jax.shard_map(
        functools.partial(per_device, topo),
        mesh=mesh,
        in_specs=(wide,) + (rows,) * 8 + (row, row, P("grp", None), both, both, wide),
        out_specs=(wide, wide) + (rows,) * 8 + (row, row),
        check_vma=False,
    )
```

time: 2110 us -> 1050 us (0.50)
  waiting for transfers between devices: 1210 us -> 334 us
  blocking collectives: 295 us -> 0 us
  matrix products: 310 us -> 139 us
  starting transfers between devices: 31.3 us -> 120 us
  local copies, waits for them, and re-layouts: 117 us -> 195 us
  Pallas kernels: 0 us -> 75.8 us
  other arithmetic: 92.1 us -> 157 us
  loops' own time: 24.7 us -> 0 us
    reduce_scatter x7 -> x0, waiting for transfers between devices: 586 us -> none  [the longest x5 446 us: per_device(): lax.psum_scatter(for_sending(running), 'tok', scatter_dimension=0, tiled=...]
    ppermute x0 -> x62, waiting for transfers between devices: none -> 334 us  [the longest x57 282 us: exchange(): return lax.ppermute(arr, AXES, topo.pairs(key))]
    all_gather x7 -> x0, waiting for transfers between devices: 302 us -> none  [the longest x1 79.8 us: per_device(): lax.all_gather(shards[4], 'tok', axis=0, tiled=True)]
    unnamed x25 -> x0, waiting for transfers between devices: 284 us -> none
    all_gather x10 -> x0, blocking collectives: 246 us -> none  [the longest x3 71.7 us: forward_step(): lax.all_gather(key_labels, 'tok', axis=0, tiled=True)]
    dot_general x123 -> x40, matrix products: 310 us -> 139 us  [the longest x15 50.3 us: mm_nt(): return lax.dot_general(a, b, NT, preferred_element_type=F32)]
    ppermute x0 -> x62, starting transfers between devices: none -> 120 us  [the longest x57 93.8 us: exchange(): return lax.ppermute(arr, AXES, topo.pairs(key))]
    pallas_call x0 -> x6, Pallas kernels: none -> 75.8 us  [the longest x3 40.9 us: attend_back(): pl.pallas_call(functools.partial(attend_back_kernel, rows), grid_spec=plt...]
  transfers between devices with their start and end apart: 25 -> 62, of which waited for: 21 -> 34; matrix products, arithmetic and copies ran while one was open for 13% -> 28% of each run, Pallas kernels for 0% -> 3%
where the time goes in v1:
time: 1050 us; the launch traced here: 1030 us
  waiting for transfers between devices  334 us (32%)
  local copies, waits for them, and re-layouts  195 us (19%)
  other arithmetic  157 us (15%)
  matrix products  139 us (13%)
  starting transfers between devices  120 us (11%)
  Pallas kernels  75.8 us (7%)
    ppermute x57, waiting for transfers between devices, exchange(): return lax.ppermute(arr, AXES, topo.pairs(key))  282 us
    ppermute x57, starting transfers between devices, exchange(): return lax.ppermute(arr, AXES, topo.pairs(key))  93.8 us
    dot_general x15, matrix products, mm_nt(): return lax.dot_general(a, b, NT, preferred_element_type=F32)  50.3 us
    dot_general x18, matrix products, mm(): return jnp.dot(a, b, preferred_element_type=F32)  50.2 us
    unnamed x475, local copies, waits for them, and re-layouts  41 us
    pallas_call x3, Pallas kernels, attend_back(): pl.pallas_call(functools.partial(attend_back_kernel, rows), grid_spec=plt...  40.9 us
    dot_general x7, matrix products, mm_tn(): return lax.dot_general(a, b, TN, preferred_element_type=F32)  38.1 us
    pallas_call x3, Pallas kernels, attend(): pl.pallas_call(functools.partial(attend_kernel, rows), grid_spec=pltpu.Pr...  34.9 us
  transfers between devices with their start and end apart: 62, of which 34 were waited for; matrix products, arithmetic and copies ran while one was open for 28% of the time, Pallas kernels for 3%

profile of v1, /device:TPU:17, one launch (start us, length us, event | category | flops | bytes accessed | tf_op | source)
XLA Modules:
  0.0 1028.1 jit_solution(6405337246038784304)
XLA Ops:
  17.9 22.8 %collective-permute-done.2 = bf16[120,512]{1,0:T(8,128)(2,1)S(1)} collective-permute-done((bf16[120,512]{1,0:T(8,128)(2,1)S(1)}, bf16[120,512]{1,0:T(8,128)(2,1)S(1)}, u32[]{:S(2)}, u32[]{:S(2)}) %collective-permute-start.2) | collective-permute-done | bytes 122912 | tf_op jit(solution)/shard_map/ppermute | solution.py:73
  40.9 15.2 %collective-permute-done.1 = s32[8,256]{1,0:T(8,128)S(1)} collective-permute-done((s32[8,256]{1,0:T(8,128)S(1)}, s32[8,256]{1,0:T(8,128)S(1)}, u32[]{:S(2)}, u32[]{:S(2)}) %collective-permute-start.1) | collective-permute-done | bytes 8224 | tf_op jit(solution)/shard_map/ppermute | solution.py:408
  76.2 7.2 collective-permute-done.19
  93.5 15.5 %collective-permute-done.15 = bf16[2,2,120,1536]{3,2,1,0:T(8,128)(2,1)S(1)} collective-permute-done((bf16[2,2,120,1536]{3,2,1,0:T(8,128)(2,1)S(1)}, bf16[2,2,120,1536]{3,2,1,0:T(8,128)(2,1)S(1)}, u32[]{:S(2)}, u32[]{:S(2)}) %collective-permute-start.15) | collective-permute-done | bytes 1474592 | tf_op jit(solution)/shard_map/ppermute | solution.py:73
  111.3 10.1 collective-permute-done.20
  128.2 74.9 %collective-permute-done.8 = s32[2,8,256]{2,1,0:T(8,128)S(1)} collective-permute-done((s32[2,8,256]{2,1,0:T(8,128)S(1)}, s32[2,8,256]{2,1,0:T(8,128)S(1)}, u32[]{:S(2)}, u32[]{:S(2)}) %collective-permute-start.8) | collective-permute-done | bytes 16416 | tf_op jit(solution)/shard_map/ppermute | solution.py:73
  236.6 13.5 %collective-permute-done.11 = bf16[2,256,640]{1,2,0:T(8,128)(2,1)} collective-permute-done((bf16[2,256,640]{1,2,0:T(8,128)(2,1)S(1)}, bf16[2,256,640]{1,2,0:T(8,128)(2,1)}, u32[]{:S(2)}, u32[]{:S(2)}) %collective-permute-start.11) | collective-permute-done | bytes 655392 | tf_op jit(solution)/shard_map/ppermute | solution.py:73
  274.2 12.6 %attend.3 = (f32[5,128,768]{2,1,0:T(8,128)}, f32[5,8,768]{2,1,0:T(8,128)}) custom-call(s32[2]{0:T(128)} %pad_add_fusion.9.span, s32[2048,8]{1,0:T(8,128)} %pad.50.key_ref, s32[8,768]{1,0:T(8,128)} %pad.51.query_ref, bf16[2048,640]{1,0:T(8,128)(2,1)} %bitcast.554, bf16[5,768,128]{2,1,0:T(8,128)(2,1)} %bitcast.577), custom_call_target="tpu_custom_call" | custom-call | flops 4026531840 | bytes 6553600 | tf_op jit(solution)/shard_map/attend/pallas_call | solution.py:217
  359.4 11.2 %attend.4 = (f32[5,128,576]{2,1,0:T(8,128)}, f32[5,8,576]{2,1,0:T(8,128)}) custom-call(s32[2]{0:T(128)} %pad_add_fusion.9.span, s32[1536,8]{1,0:T(8,128)} %pad.53.key_ref, s32[8,576]{1,0:T(8,128)} %pad.54.query_ref, bf16[1536,640]{1,0:T(8,128)(2,1)} %bitcast.557, bf16[5,576,128]{2,1,0:T(8,128)(2,1)} %bitcast.583), custom_call_target="tpu_custom_call" | custom-call | flops 2264924160 | bytes 4915200 | tf_op jit(solution)/shard_map/attend/pallas_call | solution.py:217
  407.5 14.8 %collective-permute-done.30 = bf16[256,960]{0,1:T(8,128)(2,1)} collective-permute-done((bf16[256,960]{0,1:T(8,128)(2,1)}, bf16[256,960]{0,1:T(8,128)(2,1)}, u32[]{:S(2)}, u32[]{:S(2)}) %collective-permute-start.30) | collective-permute-done | bytes 491552 | tf_op jit(solution)/shard_map/ppermute | solution.py:409
  452.2 11.2 %attend.5 = (f32[5,128,576]{2,1,0:T(8,128)}, f32[5,8,576]{2,1,0:T(8,128)}) custom-call(s32[2]{0:T(128)} %pad_add_fusion.9.span, s32[1536,8]{1,0:T(8,128)} %pad.55.key_ref, s32[8,576]{1,0:T(8,128)} %pad.54.query_ref, bf16[1536,640]{1,0:T(8,128)(2,1)} %bitcast.559, bf16[5,576,128]{2,1,0:T(8,128)(2,1)} %bitcast.582), custom_call_target="tpu_custom_call" | custom-call | flops 2264924160 | bytes 4915200 | tf_op jit(solution)/shard_map/attend/pallas_call | solution.py:217
  506.5 13.1 %attend_back.3 = (f32[5,128,576]{2,1,0:T(8,128)}, bf16[1536,640]{1,0:T(8,128)(2,1)}) custom-call(s32[2]{0:T(128)} %pad_add_fusion.9.span, s32[1536,8]{1,0:T(8,128)} %pad.55.key_ref, s32[8,576]{1,0:T(8,128)} %pad.54.query_ref, bf16[1536,640]{1,0:T(8,128)(2,1)} %bitcast.560, bf16[5,576,128]{2,1,0:T(8,128)(2,1)} %bitcast.585, ...), custom_call_target="tpu_custom_call" | custom-call | flops 5662310400 | bytes 6881280 | tf_op jit(solution)/shard_map/attend_back/pallas_call | solution.py:286
  541.2 8.8 collective-permute-start.32
  594.5 12.7 %attend_back.4 = (f32[5,128,576]{2,1,0:T(8,128)}, bf16[1536,640]{1,0:T(8,128)(2,1)}) custom-call(s32[2]{0:T(128)} %pad_add_fusion.9.span, s32[1536,8]{1,0:T(8,128)} %pad.53.key_ref, s32[8,576]{1,0:T(8,128)} %pad.54.query_ref, bf16[1536,640]{1,0:T(8,128)(2,1)} %bitcast.558, bf16[5,576,128]{2,1,0:T(8,128)(2,1)} %bitcast.584, ...), custom_call_target="tpu_custom_call" | custom-call | flops 5662310400 | bytes 6881280 | tf_op jit(solution)/shard_map/attend_back/pallas_call | solution.py:286
  637.6 7.5 collective-permute-start.35
  648.7 7.8 collective-permute-done.35
  679.9 7.2 fusion.24
  687.1 15.9 %fusion = f32[960,5120]{1,0:T(8,128)} fusion(bf16[256,2560]{1,0:T(8,128)(2,1)} %get-tuple-element.182, bf16[256,2560]{1,0:T(8,128)(2,1)} %get-tuple-element.181, bf16[192,2560]{1,0:T(8,128)(2,1)} %copy-done.208, bf16[192,2560]{1,0:T(8,128)(2,1)} %copy-done.207, bf16[192,2560]{1,0:T(8,128)(2,1)} %get-tuple-element.186, ...), kind=kOutput, calls=%fused_computation.3 | convolution fusion | flops 6334464000 | bytes 27443200 | tf_op jit(solution)/shard_map/dot_general | solution.py:328
  703.0 8.2 multiply_reduce_fusion
  718.0 15.2 %attend_back.5 = (f32[5,128,768]{2,1,0:T(8,128)}, bf16[2048,640]{1,0:T(8,128)(2,1)}) custom-call(s32[2]{0:T(128)} %pad_add_fusion.9.span, s32[2048,8]{1,0:T(8,128)} %pad.50.key_ref, s32[8,768]{1,0:T(8,128)} %pad.51.query_ref, bf16[2048,640]{1,0:T(8,128)(2,1)} %bitcast.555, bf16[5,768,128]{2,1,0:T(8,128)(2,1)} %bitcast.578, ...), custom_call_target="tpu_custom_call" | custom-call | flops 10066329600 | bytes 9175040 | tf_op jit(solution)/shard_map/attend_back/pallas_call | solution.py:286
  752.4 14.6 %fusion.199 = (f32[2,2,2,120,2560]{4,3,2,1,0:T(8,128)}, f32[2,2,2,120,2560]{4,3,2,1,0:T(8,128)}) fusion(f32[2,2,2,120,5120]{4,3,2,1,0:T(8,128)} %bitcast.519), kind=kLoop, calls=%fused_computation.589 | loop fusion | bytes 39321600 | tf_op jit(solution)/shard_map/slice | solution.py:94
  767.0 9.6 select_convert_fusion
  779.1 10.0 collective-permute-start.38
  827.3 12.4 %concatenate.205 = f32[960,2624]{1,0:T(8,128)} concatenate(f32[960,960]{1,0:T(8,128)} %fusion.50, f32[960,64]{1,0:T(8,128)} %pad.56, f32[960,640]{1,0:T(8,128)} %fusion.92, f32[960,960]{1,0:T(8,128)} %fusion.56), dimensions={1} | concatenate | bytes 20152320 | tf_op jit(solution)/shard_map/concatenate | solution.py:543
  839.7 10.0 pad.57
  885.7 8.1 collective-permute-start.40
  897.0 21.5 %collective-permute-done.40 = bf16[256,960]{0,1:T(8,128)(2,1)S(1)} collective-permute-done((bf16[256,960]{0,1:T(8,128)(2,1)S(1)}, bf16[256,960]{0,1:T(8,128)(2,1)S(1)}, u32[]{:S(2)}, u32[]{:S(2)}) %collective-permute-start.40) | collective-permute-done | bytes 491552 | tf_op jit(solution)/shard_map/ppermute | solution.py:526
  922.0 16.1 %collective-permute-done.49 = bf16[2,2,2,120,1280]{4,3,0,1,2:T(8,128)(2,1)} collective-permute-done((bf16[2,2,2,120,1280]{4,3,0,1,2:T(8,128)(2,1)}, bf16[2,2,2,120,1280]{4,3,0,1,2:T(8,128)(2,1)}, u32[]{:S(2)}, u32[]{:S(2)}) %collective-permute-start.49) | collective-permute-done | bytes 2457632 | tf_op jit(solution)/shard_map/ppermute | solution.py:73
  940.6 16.6 %collective-permute-done.43 = bf16[2,2,120,768]{3,2,1,0:T(8,128)(2,1)S(1)} collective-permute-done((bf16[2,2,120,768]{3,2,1,0:T(8,128)(2,1)S(1)}, bf16[2,2,120,768]{3,2,1,0:T(8,128)(2,1)S(1)}, u32[]{:S(2)}, u32[]{:S(2)}) %collective-permute-start.43) | collective-permute-done | bytes 737312 | tf_op jit(solution)/shard_map/ppermute | solution.py:73
  972.2 10.9 %collective-permute-done.50 = bf16[2,2,120,1280]{3,2,0,1:T(8,128)(2,1)S(1)} collective-permute-done((bf16[2,2,120,1280]{3,2,0,1:T(8,128)(2,1)S(1)}, bf16[2,2,120,1280]{3,2,0,1:T(8,128)(2,1)S(1)}, u32[]{:S(2)}, u32[]{:S(2)}) %collective-permute-start.50) | collective-permute-done | bytes 1228832 | tf_op jit(solution)/shard_map/ppermute | solution.py:73
  994.3 7.6 collective-permute-done.52
  1009.0 10.4 %collective-permute-start.54 = (bf16[120,2560]{1,0:T(8,128)(2,1)}, bf16[120,2560]{1,0:T(8,128)(2,1)}, u32[]{:S(2)}, u32[]{:S(2)}) collective-permute-start(bf16[120,2560]{1,0:T(8,128)(2,1)} %pad_maximum_fusion.26), channel_id=1, source_target_pairs={{0,8},{1,9},{2,10},{3,11},{4,12},{5,13},{6,14},{7,15},{8,0},{9,1},... | collective-permute-start | bytes 1843208 | tf_op jit(solution)/shard_map/ppermute | solution.py:73
  (951 shorter events, 567.4 us)
Async XLA Ops:
  2.2 72.6 %collective-permute-start.18 = (bf16[80,960]{1,0:T(8,128)(2,1)S(1)}, bf16[80,960]{1,0:T(8,128)(2,1)S(1)}, u32[]{:S(2)}, u32[]{:S(2)}) collective-permute-start(bf16[80,960]{1,0:T(8,128)(2,1)S(1)} %fusion.157), channel_id=1, source_target_pairs={{0,4},{1,5},{2,6},{3,7},{4,0},{5,1},{6,2},{7,3},{8,12},{9,13},{10,... | collective-permute-start | bytes 460808 | tf_op jit(solution)/shard_map/ppermute | solution.py:73
  3.0 55.2 %collective-permute-start.13 = (bf16[120,1536]{1,0:T(8,128)(2,1)S(1)}, bf16[120,1536]{1,0:T(8,128)(2,1)S(1)}, u32[]{:S(2)}, u32[]{:S(2)}) collective-permute-start(bf16[120,1536]{1,0:T(8,128)(2,1)S(1)} %fusion.144), channel_id=1, source_target_pairs={{0,4},{1,5},{2,6},{3,7},{4,0},{5,1},{6,2},{7,3},{8,12},{9,13},{10,... | collective-permute-start | bytes 1105928 | tf_op jit(solution)/shard_map/ppermute | solution.py:73
  5.9 34.8 %collective-permute-start.2 = (bf16[120,512]{1,0:T(8,128)(2,1)S(1)}, bf16[120,512]{1,0:T(8,128)(2,1)S(1)}, u32[]{:S(2)}, u32[]{:S(2)}) collective-permute-start(bf16[120,512]{1,0:T(8,128)(2,1)S(1)} %bitcast.594), channel_id=1, source_target_pairs={{0,4},{1,5},{2,6},{3,7},{4,0},{5,1},{6,2},{7,3},{8,12},{9,13},{10,... | collective-permute-start | bytes 368648 | tf_op jit(solution)/shard_map/ppermute | solution.py:73
  8.8 213.9 %collective-permute-start = (bf16[256,960]{0,1:T(8,128)(2,1)}, bf16[256,960]{0,1:T(8,128)(2,1)S(1)}, u32[]{:S(2)}, u32[]{:S(2)}) collective-permute-start(bf16[256,960]{0,1:T(8,128)(2,1)} %convolution_convert_fusion.4), channel_id=1, source_target_pairs={{0,0},{1,1},{2,8},{3,9},{4,16},{5,17},{6,24},{7,25},{8,2},{9,3},{1... | collective-permute-start | bytes 1474568 | tf_op jit(solution)/shard_map/ppermute | solution.py:407
  15.9 40.2 %collective-permute-start.1 = (s32[8,256]{1,0:T(8,128)S(1)}, s32[8,256]{1,0:T(8,128)S(1)}, u32[]{:S(2)}, u32[]{:S(2)}) collective-permute-start(s32[8,256]{1,0:T(8,128)S(1)} %pad.47), channel_id=1, source_target_pairs={{0,0},{1,1},{2,8},{3,9},{4,16},{5,17},{6,24},{7,25},{8,2},{9,3},{1... | collective-permute-start | bytes 24584 | tf_op jit(solution)/shard_map/ppermute | solution.py:408
  60.0 64.3 %collective-permute-start.7 = (s32[8,256]{1,0:T(8,128)S(1)}, s32[8,256]{1,0:T(8,128)S(1)}, u32[]{:S(2)}, u32[]{:S(2)}) collective-permute-start(s32[8,256]{1,0:T(8,128)S(1)} %collective-permute-done.1), channel_id=1, source_target_pairs={{0,1},{1,0},{2,3},{3,2},{4,5},{5,4},{6,7},{7,6},{8,9},{9,8},{10,11... | collective-permute-start | bytes 24584 | tf_op jit(solution)/shard_map/ppermute | solution.py:73
  67.5 22.2 %collective-permute-start.5 = (bf16[2,2,2,120,512]{4,3,0,1,2:T(8,128)(2,1)S(1)}, bf16[2,2,2,120,512]{4,3,0,1,2:T(8,128)(2,1)S(1)}, u32[]{:S(2)}, u32[]{:S(2)}) collective-permute-start(bf16[2,2,2,120,512]{4,3,0,1,2:T(8,128)(2,1)S(1)} %pad_maximum_fusion.16), channel_id=1, source_target_pairs={{0,16},{1,17},{2,18},{3,19},{4,20},{5,21},{6,22},{7,23},{8,24},{9,... | collective-permute-start | bytes 2949128 | tf_op jit(solution)/shard_map/ppermute | solution.py:73
  74.6 34.4 %collective-permute-start.15 = (bf16[2,2,120,1536]{3,2,1,0:T(8,128)(2,1)S(1)}, bf16[2,2,120,1536]{3,2,1,0:T(8,128)(2,1)S(1)}, u32[]{:S(2)}, u32[]{:S(2)}) collective-permute-start(bf16[2,2,120,1536]{3,2,1,0:T(8,128)(2,1)S(1)} %pad_maximum_fusion.10), channel_id=1, source_target_pairs={{0,1},{1,0},{2,3},{3,2},{4,5},{5,4},{6,7},{7,6},{8,9},{9,8},{10,11... | collective-permute-start | bytes 4423688 | tf_op jit(solution)/shard_map/ppermute | solution.py:73
  83.5 37.9 %collective-permute-start.20 = (bf16[2,2,80,960]{3,2,1,0:T(8,128)(2,1)S(1)}, bf16[2,2,80,960]{3,2,1,0:T(8,128)(2,1)S(1)}, u32[]{:S(2)}, u32[]{:S(2)}) collective-permute-start(bf16[2,2,80,960]{3,2,1,0:T(8,128)(2,1)S(1)} %pad_maximum_fusion.23), channel_id=1, source_target_pairs={{0,1},{1,0},{2,3},{3,2},{4,5},{5,4},{6,7},{7,6},{8,9},{9,8},{10,11... | collective-permute-start | bytes 1843208 | tf_op jit(solution)/shard_map/ppermute | solution.py:73
  91.4 118.2 %collective-permute-start.6 = (bf16[2,2,2,120,1024]{4,3,0,1,2:T(8,128)(2,1)}, bf16[2,2,2,120,1024]{4,3,0,1,2:T(8,128)(2,1)}, u32[]{:S(2)}, u32[]{:S(2)}) collective-permute-start(bf16[2,2,2,120,1024]{4,3,0,1,2:T(8,128)(2,1)} %pad_maximum_fusion.9), channel_id=1, source_target_pairs={{0,8},{1,9},{2,10},{3,11},{4,12},{5,13},{6,14},{7,15},{8,0},{9,1},... | collective-permute-start | bytes 5898248 | tf_op jit(solution)/shard_map/ppermute | solution.py:73
  111.3 104.2 %collective-permute-start.16 = (bf16[2,2,2,120,1536]{4,3,2,1,0:T(8,128)(2,1)}, bf16[2,2,2,120,1536]{4,3,2,1,0:T(8,128)(2,1)}, u32[]{:S(2)}, u32[]{:S(2)}) collective-permute-start(bf16[2,2,2,120,1536]{4,3,2,1,0:T(8,128)(2,1)} %pad_maximum_fusion.4), channel_id=1, source_target_pairs={{0,16},{1,17},{2,18},{3,19},{4,20},{5,21},{6,22},{7,23},{8,24},{9,... | collective-permute-start | bytes 8847368 | tf_op jit(solution)/shard_map/ppermute | solution.py:73
  123.5 84.1 %collective-permute-start.21 = (bf16[2,2,2,80,960]{4,3,2,1,0:T(8,128)(2,1)}, bf16[2,2,2,80,960]{4,3,2,1,0:T(8,128)(2,1)}, u32[]{:S(2)}, u32[]{:S(2)}) collective-permute-start(bf16[2,2,2,80,960]{4,3,2,1,0:T(8,128)(2,1)} %pad_maximum_fusion.12), channel_id=1, source_target_pairs={{0,16},{1,17},{2,18},{3,19},{4,20},{5,21},{6,22},{7,23},{8,24},{9,... | collective-permute-start | bytes 3686408 | tf_op jit(solution)/shard_map/ppermute | solution.py:73
  124.3 78.8 %collective-permute-start.8 = (s32[2,8,256]{2,1,0:T(8,128)S(1)}, s32[2,8,256]{2,1,0:T(8,128)S(1)}, u32[]{:S(2)}, u32[]{:S(2)}) collective-permute-start(s32[2,8,256]{2,1,0:T(8,128)S(1)} %pad_add_fusion.2), channel_id=1, source_target_pairs={{0,16},{1,17},{2,18},{3,19},{4,20},{5,21},{6,22},{7,23},{8,24},{9,... | collective-permute-start | bytes 49160 | tf_op jit(solution)/shard_map/ppermute | solution.py:73
  222.7 66.4 %collective-permute-start.17 = (bf16[2,2,2,120,3072]{4,3,2,1,0:T(8,128)(2,1)}, bf16[2,2,2,120,3072]{4,3,2,1,0:T(8,128)(2,1)}, u32[]{:S(2)}, u32[]{:S(2)}) collective-permute-start(bf16[2,2,2,120,3072]{4,3,2,1,0:T(8,128)(2,1)} %pad_maximum_fusion.1), channel_id=1, source_target_pairs={{0,8},{1,9},{2,10},{3,11},{4,12},{5,13},{6,14},{7,15},{8,0},{9,1},... | collective-permute-start | bytes 17694728 | tf_op jit(solution)/shard_map/ppermute | solution.py:73
  228.3 32.3 %collective-permute-start.22 = (bf16[2,2,2,160,960]{4,3,2,1,0:T(8,128)(2,1)}, bf16[2,2,2,160,960]{4,3,2,1,0:T(8,128)(2,1)}, u32[]{:S(2)}, u32[]{:S(2)}) collective-permute-start(bf16[2,2,2,160,960]{4,3,2,1,0:T(8,128)(2,1)} %pad_maximum_fusion.6), channel_id=1, source_target_pairs={{0,8},{1,9},{2,10},{3,11},{4,12},{5,13},{6,14},{7,15},{8,0},{9,1},... | collective-permute-start | bytes 7372808 | tf_op jit(solution)/shard_map/ppermute | solution.py:73
  400.1 22.2 %collective-permute-start.30 = (bf16[256,960]{0,1:T(8,128)(2,1)}, bf16[256,960]{0,1:T(8,128)(2,1)}, u32[]{:S(2)}, u32[]{:S(2)}) collective-permute-start(bf16[256,960]{0,1:T(8,128)(2,1)} %convolution_convert_fusion.2), channel_id=1, source_target_pairs={{0,0},{1,1},{2,8},{3,9},{4,16},{5,17},{6,24},{7,25},{8,2},{9,3},{1... | collective-permute-start | bytes 1474568 | tf_op jit(solution)/shard_map/ppermute | solution.py:409
  405.1 21.2 %collective-permute-start.27 = (bf16[2,192,640]{2,1,0:T(8,128)(2,1)}, bf16[2,192,640]{2,1,0:T(8,128)(2,1)}, u32[]{:S(2)}, u32[]{:S(2)}) collective-permute-start(bf16[2,192,640]{2,1,0:T(8,128)(2,1)} %copy.780), channel_id=1, source_target_pairs={{0,16},{1,17},{2,18},{3,19},{4,20},{5,21},{6,22},{7,23},{8,24},{9,... | collective-permute-start | bytes 1474568 | tf_op jit(solution)/shard_map/ppermute | solution.py:73
  541.2 20.4 %collective-permute-start.32 = (bf16[2,192,640]{2,1,0:T(8,128)(2,1)}, bf16[2,192,640]{2,1,0:T(8,128)(2,1)}, u32[]{:S(2)}, u32[]{:S(2)}) collective-permute-start(bf16[2,192,640]{2,1,0:T(8,128)(2,1)} %copy.801), channel_id=1, source_target_pairs={{0,16},{1,17},{2,18},{3,19},{4,20},{5,21},{6,22},{7,23},{8,24},{9,... | collective-permute-start | bytes 1474568 | tf_op jit(solution)/shard_map/ppermute | solution.py:73
  661.1 232.7 %collective-permute-start.29 = (bf16[256,960]{0,1:T(8,128)(2,1)}, bf16[256,960]{0,1:T(8,128)(2,1)}, u32[]{:S(2)}, u32[]{:S(2)}) collective-permute-start(bf16[256,960]{0,1:T(8,128)(2,1)} %pad_maximum_fusion.28), channel_id=1, source_target_pairs={{0,0},{1,1},{2,8},{3,9},{4,16},{5,17},{6,24},{7,25},{8,2},{9,3},{1... | collective-permute-start | bytes 1474568 | tf_op jit(solution)/shard_map/ppermute | solution.py:514
  739.8 37.4 %collective-permute-start.37 = (bf16[2,2,256,640]{2,3,1,0:T(8,128)(2,1)}, bf16[2,2,256,640]{2,3,1,0:T(8,128)(2,1)}, u32[]{:S(2)}, u32[]{:S(2)}) collective-permute-start(bf16[2,2,256,640]{2,3,1,0:T(8,128)(2,1)} %select_bitcast_fusion.3), channel_id=1, source_target_pairs={{0,8},{1,9},{2,10},{3,11},{4,12},{5,13},{6,14},{7,15},{8,0},{9,1},... | collective-permute-start | bytes 3932168 | tf_op jit(solution)/shard_map/ppermute | solution.py:73
  752.4 60.0 %collective-permute-start.55 = (bf16[2,2,2,160,960]{4,3,2,1,0:T(8,128)(2,1)}, bf16[2,2,2,160,960]{4,3,2,1,0:T(8,128)(2,1)}, u32[]{:S(2)}, u32[]{:S(2)}) collective-permute-start(bf16[2,2,2,160,960]{4,3,2,1,0:T(8,128)(2,1)} %select_convert_fusion.2), channel_id=1, source_target_pairs={{0,8},{1,9},{2,10},{3,11},{4,12},{5,13},{6,14},{7,15},{8,0},{9,1},... | collective-permute-start | bytes 7372808 | tf_op jit(solution)/shard_map/ppermute | solution.py:73
  776.6 90.1 %collective-permute-start.48 = (bf16[2,2,2,120,2560]{4,3,0,1,2:T(8,128)(2,1)}, bf16[2,2,2,120,2560]{4,3,0,1,2:T(8,128)(2,1)}, u32[]{:S(2)}, u32[]{:S(2)}) collective-permute-start(bf16[2,2,2,120,2560]{4,3,0,1,2:T(8,128)(2,1)} %select_convert_fusion), channel_id=1, source_target_pairs={{0,8},{1,9},{2,10},{3,11},{4,12},{5,13},{6,14},{7,15},{8,0},{9,1},... | collective-permute-start | bytes 14745608 | tf_op jit(solution)/shard_map/ppermute | solution.py:73
  779.1 24.7 %collective-permute-start.38 = (bf16[2,256,640]{1,2,0:T(8,128)(2,1)S(1)}, bf16[2,256,640]{1,2,0:T(8,128)(2,1)S(1)}, u32[]{:S(2)}, u32[]{:S(2)}) collective-permute-start(bf16[2,256,640]{1,2,0:T(8,128)(2,1)S(1)} %select_bitcast_fusion.15), channel_id=1, source_target_pairs={{0,16},{1,17},{2,18},{3,19},{4,20},{5,21},{6,22},{7,23},{8,24},{9,... | collective-permute-start | bytes 1966088 | tf_op jit(solution)/shard_map/ppermute | solution.py:73
  817.2 32.5 %collective-permute-start.56 = (bf16[2,2,160,960]{3,2,1,0:T(8,128)(2,1)}, bf16[2,2,160,960]{3,2,1,0:T(8,128)(2,1)}, u32[]{:S(2)}, u32[]{:S(2)}) collective-permute-start(bf16[2,2,160,960]{3,2,1,0:T(8,128)(2,1)} %fusion.45), channel_id=1, source_target_pairs={{0,1},{1,0},{2,3},{3,2},{4,5},{5,4},{6,7},{7,6},{8,9},{9,8},{10,11... | collective-permute-start | bytes 3686408 | tf_op jit(solution)/shard_map/ppermute | solution.py:73
  866.7 29.3 %collective-permute-start.58 = (bf16[2,80,960]{2,1,0:T(8,128)(2,1)S(1)}, bf16[2,80,960]{2,1,0:T(8,128)(2,1)S(1)}, u32[]{:S(2)}, u32[]{:S(2)}) collective-permute-start(bf16[2,80,960]{2,1,0:T(8,128)(2,1)S(1)} %fusion.148), channel_id=1, source_target_pairs={{0,2},{1,3},{2,0},{3,1},{4,6},{5,7},{6,4},{7,5},{8,10},{9,11},{10,... | collective-permute-start | bytes 921608 | tf_op jit(solution)/shard_map/ppermute | solution.py:73
  875.2 62.8 %collective-permute-start.49 = (bf16[2,2,2,120,1280]{4,3,0,1,2:T(8,128)(2,1)}, bf16[2,2,2,120,1280]{4,3,0,1,2:T(8,128)(2,1)}, u32[]{:S(2)}, u32[]{:S(2)}) collective-permute-start(bf16[2,2,2,120,1280]{4,3,0,1,2:T(8,128)(2,1)} %broadcast_select_fusion.6), channel_id=1, source_target_pairs={{0,16},{1,17},{2,18},{3,19},{4,20},{5,21},{6,22},{7,23},{8,24},{9,... | collective-permute-start | bytes 7372808 | tf_op jit(solution)/shard_map/ppermute | solution.py:73
  882.8 37.0 %collective-permute-start.42 = (bf16[2,2,120,1536]{3,2,1,0:T(8,128)(2,1)S(1)}, bf16[2,2,120,1536]{3,2,1,0:T(8,128)(2,1)S(1)}, u32[]{:S(2)}, u32[]{:S(2)}) collective-permute-start(bf16[2,2,120,1536]{3,2,1,0:T(8,128)(2,1)S(1)} %select_bitcast_fusion), channel_id=1, source_target_pairs={{0,1},{1,0},{2,3},{3,2},{4,5},{5,4},{6,7},{7,6},{8,9},{9,8},{10,11... | collective-permute-start | bytes 4423688 | tf_op jit(solution)/shard_map/ppermute | solution.py:73
  885.7 32.8 %collective-permute-start.40 = (bf16[256,960]{0,1:T(8,128)(2,1)S(1)}, bf16[256,960]{0,1:T(8,128)(2,1)S(1)}, u32[]{:S(2)}, u32[]{:S(2)}) collective-permute-start(bf16[256,960]{0,1:T(8,128)(2,1)S(1)} %fusion.85), channel_id=1, source_target_pairs={{0,0},{1,1},{2,8},{3,9},{4,16},{5,17},{6,24},{7,25},{8,2},{9,3},{1... | collective-permute-start | bytes 1474568 | tf_op jit(solution)/shard_map/ppermute | solution.py:526
  896.1 23.5 %collective-permute-start.59 = (bf16[80,960]{1,0:T(8,128)(2,1)S(1)}, bf16[80,960]{1,0:T(8,128)(2,1)S(1)}, u32[]{:S(2)}, u32[]{:S(2)}) collective-permute-start(bf16[80,960]{1,0:T(8,128)(2,1)S(1)} %select_bitcast_fusion.46), channel_id=1, source_target_pairs={{0,4},{1,5},{2,6},{3,7},{4,0},{5,1},{6,2},{7,3},{8,12},{9,13},{10,... | collective-permute-start | bytes 460808 | tf_op jit(solution)/shard_map/ppermute | solution.py:73
  919.7 39.2 %collective-permute-start.60 = (bf16[80,960]{1,0:T(8,128)(2,1)S(1)}, bf16[80,960]{1,0:T(8,128)(2,1)S(1)}, u32[]{:S(2)}, u32[]{:S(2)}) collective-permute-start(bf16[80,960]{1,0:T(8,128)(2,1)S(1)} %fusion.150), channel_id=1, source_target_pairs={{0,16},{1,17},{2,18},{3,19},{4,20},{5,21},{6,22},{7,23},{8,24},{9,... | collective-permute-start | bytes 460808 | tf_op jit(solution)/shard_map/ppermute | solution.py:73
  920.5 36.8 %collective-permute-start.43 = (bf16[2,2,120,768]{3,2,1,0:T(8,128)(2,1)S(1)}, bf16[2,2,120,768]{3,2,1,0:T(8,128)(2,1)S(1)}, u32[]{:S(2)}, u32[]{:S(2)}) collective-permute-start(bf16[2,2,120,768]{3,2,1,0:T(8,128)(2,1)S(1)} %broadcast_select_fusion.13), channel_id=1, source_target_pairs={{0,16},{1,17},{2,18},{3,19},{4,20},{5,21},{6,22},{7,23},{8,24},{9,... | collective-permute-start | bytes 2211848 | tf_op jit(solution)/shard_map/ppermute | solution.py:73
  958.9 24.2 %collective-permute-start.50 = (bf16[2,2,120,1280]{3,2,0,1:T(8,128)(2,1)S(1)}, bf16[2,2,120,1280]{3,2,0,1:T(8,128)(2,1)S(1)}, u32[]{:S(2)}, u32[]{:S(2)}) collective-permute-start(bf16[2,2,120,1280]{3,2,0,1:T(8,128)(2,1)S(1)} %select_bitcast_fusion.12), channel_id=1, source_target_pairs={{0,1},{1,0},{2,3},{3,2},{4,5},{5,4},{6,7},{7,6},{8,9},{9,8},{10,11... | collective-permute-start | bytes 3686408 | tf_op jit(solution)/shard_map/ppermute | solution.py:73
  (261 other events, 2078.0 us)

commit v2 on v1

--- a/solution.py
+++ b/solution.py
@@ -131,6 +131,220 @@
     for key in topo.keys("y") + topo.keys("c"):
         arr = double(topo, arr, key, axis - 2, False)
     return arr
+
+
+class Piece:
+    def __init__(self, array, dim, start, size, core, part):
+        self.array, self.dim, self.start, self.size = array, dim, start, size
+        self.core, self.part = core, part
+
+    def of(self, ref):
+        if self.dim == 0:
+            return ref.at[pl.ds(self.start, self.size), :]
+        return ref.at[:, pl.ds(self.start, self.size)]
+
+
+def cut_pieces(shapes):
+    near = lambda v, unit: max(unit, int(round(v / unit)) * unit)
+    wide_a, wide_g, wide_u, tall = shapes[0][1], shapes[1][1], shapes[2][1], shapes[3][0]
+    a = near(wide_a * 0.634, 128)
+    g = near(wide_g * 0.7, 128)
+    u = near(wide_u * 0.65, 128)
+    d = near(tall * 0.3, 8)
+    return [
+        Piece(1, 1, 0, g, 0, 0),
+        Piece(0, 1, a, wide_a - a, 0, 2),
+        Piece(1, 1, g, wide_g - g, 0, 2),
+        Piece(0, 1, 0, a, 0, 1),
+        Piece(2, 1, u, wide_u - u, 1, 0),
+        Piece(3, 0, 0, d, 1, 0),
+        Piece(3, 0, d, tall - d, 1, 2),
+        Piece(2, 1, 0, u, 1, 1),
+    ]
+
+
+def coordinates(topo):
+    g, t = lax.axis_index("grp"), lax.axis_index("tok")
+    return lax.rem(t, topo.X), lax.div(g, 2), lax.div(t, topo.X), lax.rem(g, 2)
+
+
+def gather_kernel(topo, pieces, *refs):
+    shards, outs = refs[:4], refs[4:8]
+    local_sem, recv_sem, z_sem, x_sem, y_sem, c_sem = refs[8:]
+    x, y, z, c = coordinates(topo)
+    X, Z, T = topo.X, topo.Z, topo.T
+    g, me = lax.axis_index("grp"), lax.axis_index("tok")
+    odd = lax.rem(y, 2)
+    over_y = {"grp": g + 2 - 4 * odd, "tok": me}
+    over_c = {"grp": g + 1 - 2 * c, "tok": me}
+
+    def over_z(k):
+        return {"grp": g, "tok": (z + k) * X + x}
+
+    def over_x(k):
+        return {"grp": g, "tok": z * X + lax.rem(x + k, X)}
+
+    barrier = pltpu.get_barrier_semaphore()
+    partners = [over_y, over_c] + [over_x(k) for k in range(1, X)]
+    for partner in partners:
+        pl.semaphore_signal(barrier, inc=1, device_id=partner, device_id_type=pl.DeviceIdType.MESH)
+    below, above = z > 0, z < Z - 1
+
+    def greet(k):
+        pl.semaphore_signal(
+            barrier, inc=1, device_id=over_z(k), device_id_type=pl.DeviceIdType.MESH
+        )
+
+    pl.when(below)(lambda: greet(-1))
+    pl.when(above)(lambda: greet(1))
+    own = [
+        pltpu.make_async_copy(shards[i], outs[i].at[me], local_sem.at[i]) for i in range(4)
+    ]
+    for copy in own:
+        copy.start()
+    pl.semaphore_wait(barrier, len(partners) + below.astype(jnp.int32) + above.astype(jnp.int32))
+
+    def send(p, t, sem, target, mine=False):
+        piece = pieces[p]
+        landing = piece.of(outs[piece.array].at[t])
+        source = piece.of(shards[piece.array]) if mine else landing
+        return pltpu.make_async_remote_copy(
+            src_ref=source, dst_ref=landing, send_sem=sem, recv_sem=recv_sem.at[p, t],
+            device_id=target, device_id_type=pl.DeviceIdType.MESH,
+        )
+
+    def arrived(p, t):
+        send(p, t, c_sem.at[0, 0], over_c).wait_recv()
+
+    def run(core):
+        mine = [p for p in range(len(pieces)) if pieces[p].core == core]
+        theirs = [p for p in range(len(pieces)) if pieces[p].core != core]
+        slot = {p: i for i, p in enumerate(mine)}
+
+        def inside(p, body):
+            part = pieces[p].part
+            if part == 1:
+                body()
+            else:
+                pl.when(odd == part // 2)(body)
+
+        def outside(p, body):
+            if pieces[p].part != 1:
+                pl.when(odd != pieces[p].part // 2)(body)
+
+        def x_copies(p, zz, first):
+            t = zz * X + x
+            return [
+                send(p, t, x_sem.at[slot[p], zz, k - 1], over_x(k), first) for k in range(1, X)
+            ]
+
+        def y_copy(p, t):
+            return send(p, t, y_sem.at[slot[p], t], over_y)
+
+        def c_copy(p, t):
+            return send(p, t, c_sem.at[slot[p], t], over_c)
+
+        def z_copy(p, zz, k, first):
+            return send(p, zz * X + x, z_sem.at[slot[p], zz, (k + 1) // 2], over_z(k), first)
+
+        for p in mine:
+            def begin(p=p):
+                pl.when(below)(lambda: z_copy(p, z, -1, True).start())
+                pl.when(above)(lambda: z_copy(p, z, 1, True).start())
+                for copy in x_copies(p, z, True):
+                    copy.start()
+            inside(p, begin)
+
+        def share(p, t):
+            if pieces[p].part != 1:
+                y_copy(p, t).start()
+            c_copy(p, t).start()
+
+        def relay(p, zz, k):
+            arrived(p, zz * X + x)
+            pl.when(above if k > 0 else below)(lambda: z_copy(p, zz, k, False).start())
+            for copy in x_copies(p, zz, False):
+                copy.start()
+            share(p, zz * X + x)
+
+        def others(p, zz):
+            for j in range(1, X):
+                t = zz * X + lax.rem(x + j, X)
+                arrived(p, t)
+                share(p, t)
+
+        def around(k, carry):
+            low, high = z - k, z + k
+            for p in mine:
+                inside(p, lambda p=p: pl.when(low >= 0)(lambda: relay(p, low, 1)))
+                inside(p, lambda p=p: pl.when(high < Z)(lambda: relay(p, high, -1)))
+            low, high = z - k + 1, z + k - 1
+            for p in mine:
+                inside(p, lambda p=p: pl.when(low >= 0)(lambda: others(p, low)))
+                inside(p, lambda p=p: pl.when((k > 1) & (high < Z))(lambda: others(p, high)))
+            return carry
+
+        lax.fori_loop(1, Z + 1, around, 0)
+
+        def rest(t, carry):
+            @pl.when(t != me)
+            def _():
+                for p in mine:
+                    def forward(p=p):
+                        arrived(p, t)
+                        c_copy(p, t).start()
+                    outside(p, forward)
+            return carry
+
+        lax.fori_loop(0, T, rest, 0)
+
+        def finish(t, carry):
+            @pl.when(t != me)
+            def _():
+                for p in theirs:
+                    arrived(p, t)
+                for p in mine:
+                    c_copy(p, t).wait_send()
+                    if pieces[p].part != 1:
+                        inside(p, lambda p=p: y_copy(p, t).wait_send())
+            return carry
+
+        lax.fori_loop(0, T, finish, 0)
+        for p in mine:
+            def end(p=p):
+                def each(zz, carry):
+                    pl.when((zz <= z) & above)(lambda: z_copy(p, zz, 1, False).wait_send())
+                    pl.when((zz >= z) & below)(lambda: z_copy(p, zz, -1, False).wait_send())
+                    for copy in x_copies(p, zz, False):
+                        copy.wait_send()
+                    return carry
+                lax.fori_loop(0, Z, each, 0)
+            inside(p, end)
+
+    pl.when(c == 0)(lambda: run(0))
+    pl.when(c == 1)(lambda: run(1))
+    for copy in own:
+        copy.wait()
+
+
+def gather_weights(topo, shards):
+    pieces = cut_pieces([s.shape for s in shards])
+    T = topo.T
+    DMA = pltpu.SemaphoreType.DMA
+    hbm = pl.BlockSpec(memory_space=pl.ANY)
+    outs = pl.pallas_call(
+        functools.partial(gather_kernel, topo, pieces),
+        in_specs=[hbm] * 4,
+        out_specs=[hbm] * 4,
+        out_shape=[jax.ShapeDtypeStruct((T,) + s.shape, s.dtype) for s in shards],
+        scratch_shapes=[
+            DMA((4,)), DMA((len(pieces), T)), DMA((4, topo.Z, 2)), DMA((4, topo.Z, topo.X - 1)),
+            DMA((4, T)), DMA((4, T)),
+        ],
+        compiler_params=pltpu.CompilerParams(collective_id=0, has_side_effects=True),
+        name="gather_weights",
+    )(*shards)
+    return [o.reshape(-1, o.shape[-1]) for o in outs]
 
 
 def group_order(topo):
@@ -370,22 +584,16 @@
     shard = w_query.shape[0]
     deep_rows = rows * 3 // 4
     zk, xk, yk, ck = (topo.keys(d) for d in "zxyc")
-    zdown = list(reversed(zk))
-
-    order_a = zdown + xk + yk + ck
-    order_b = zdown + yk + xk if False else zdown + xk + yk + ck
-    small = jnp.concatenate(
-        [router, norm_attn[:, None], norm_ffn[:, None]], axis=1
-    )
+
+    small = jnp.concatenate([router, norm_attn[:, None], norm_ffn[:, None]], axis=1)
     small = jnp.pad(small, ((0, 0), (0, HD - small.shape[1])))
     w_kv = jnp.stack(
         [w_key.reshape(shard, KV_HEADS, HD), w_value.reshape(shard, KV_HEADS, HD)], axis=2
     ).reshape(shard, 2 * kv_cols)
-    first = jnp.concatenate([w_query, small, w_kv], axis=1)
-    first = jnp.pad(first, ((0, 0), (0, -first.shape[1] % (128 * topo.G))))
-    second = jnp.concatenate([w_gate, w_up, w_out], axis=1)
-    second = jnp.pad(second, ((0, 0), (0, -second.shape[1] % (128 * topo.G))))
-    all_first = gather_rows(topo, first, 1, order_a).reshape(model, -1)
+    first = jnp.concatenate([w_query, small, w_kv, w_out], axis=1)
+    all_first, weight_g, weight_u, weight_d = gather_weights(
+        topo, [first, w_gate, w_up, w_down]
+    )
 
     own = lax.axis_index("tok") * rows + jnp.arange(rows, dtype=jnp.int32)
     eligible = (depths >= 2) & (padding > 0)
@@ -410,15 +618,11 @@
     order_g = xk + yk + ck
     labels_all = group_gather(topo, labels, order_g)
 
-    all_second = gather_rows(topo, second, 1, order_b).reshape(model, -1)
-    all_down = gather_rows(topo, w_down, 0, order_a).reshape(ff, model)
     small = all_first[:, model:model + HD].astype(F32)
     gain_one, gain_two = small[:, RECS], small[:, RECS + 1]
     weight_q = all_first[:, :model]
     weight_kv = all_first[:, model + HD:model + HD + 2 * kv_cols]
-    weight_gu = all_second[:, :2 * ff]
-    weight_o = all_second[:, 2 * ff:2 * ff + model]
-    weight_d = all_down
+    weight_o = all_first[:, model + HD + 2 * kv_cols:]
 
     pack = (lax.axis_index("grp") * topo.X) + lax.axis_index("tok") % topo.X
     begin_all, level_mine = labels[1], labels[2]
@@ -454,32 +658,30 @@
         middle = state + attended
         inv_two = inverse_rms(middle)
         n2 = (middle * inv_two * gain_two).astype(BF)
-        gu = mm(n2, weight_gu)
-        gated, upward = gu[:, :ff], gu[:, ff:]
+        gated, upward = mm(n2, weight_g), mm(n2, weight_u)
         hidden = (jax.nn.silu(gated) * upward).astype(BF)
         both = attended + mm(hidden, weight_d)
         gate = jax.nn.sigmoid(jnp.sum(state * small[:, recursion], axis=-1, keepdims=True))
         active = (labels[2, :n] > recursion).astype(F32)[:, None]
         new = state + active * gate * both
         kept = (state, inv_one, n1, q, kv_all, key_labels, query_labels, out, stat, mixed, middle,
-                inv_two, n2, gu, hidden, both, gate, active)
+                inv_two, n2, gated, upward, hidden, both, gate, active)
         return (new, kept)
 
     def backward(gradient, recursion, kept):
         (state, inv_one, n1, q, kv_all, key_labels, query_labels, out, stat, mixed, middle,
-         inv_two, n2, gu, hidden, both, gate, active) = kept
+         inv_two, n2, gated, upward, hidden, both, gate, active) = kept
         n = state.shape[0]
         d_both = active * gate * gradient
         d_fed = d_both.astype(BF)
         d_gate = active * gate * (1.0 - gate) * jnp.sum(gradient * both, axis=-1, keepdims=True)
         d_router = jnp.sum(state * d_gate, axis=0)
-        gated, upward = gu[:, :ff], gu[:, ff:]
         d_hidden = mm_nt(d_fed, weight_d)
         sig = jax.nn.sigmoid(gated)
         d_up = (d_hidden * gated * sig).astype(BF)
         d_gated = (d_hidden * upward * sig * (1.0 + gated * (1.0 - sig))).astype(BF)
-        d_gu = jnp.concatenate([d_gated, d_up], axis=1)
-        d_middle, d_gain_two = norm_back(mm_nt(d_gu, weight_gu), middle, inv_two, gain_two)
+        d_middle, d_gain_two = norm_back(
+            mm_nt(d_gated, weight_g) + mm_nt(d_up, weight_u), middle, inv_two, gain_two)
         d_att = (d_both + d_middle).astype(BF)
         gradient = gradient + d_gate * small[:, recursion] + d_middle
         d_mixed = mm_nt(d_att, weight_o).astype(BF)
@@ -501,7 +703,7 @@
         dq = dq.reshape(n, HEADS * HD).astype(BF)
         d_n1 = mm_nt(dq, weight_q) + mm_nt(dkv, weight_kv)
         d_state, d_gain_one = norm_back(d_n1, state, inv_one, gain_one)
-        left = (n1, dq, dkv, mixed, d_att, n2, d_gu, hidden, d_fed)
+        left = (n1, dq, dkv, mixed, d_att, n2, d_gated, d_up, hidden, d_fed)
         return (gradient + d_state, left, (d_router, d_gain_one, d_gain_two))
 
     whole_state, kept = forward(state, 0)
@@ -525,7 +727,7 @@
     smalls.append(tiny)
     gradient = lax.ppermute(gradient.astype(BF), AXES, swap)
 
-    n1, dq, dkv, mixed, d_att, n2, d_gu, hidden, d_fed = (
+    n1, dq, dkv, mixed, d_att, n2, d_gated, d_up, hidden, d_fed = (
         jnp.concatenate(parts, axis=0) for parts in zip(*lefts)
     )
     spread = topo.T
@@ -533,7 +735,8 @@
     ring_b = ck + yk + xk + zk
     cut = lambda g: g.reshape(spread, -1, g.shape[-1])
     grad_down = scatter_rows(topo, cut(mm_tn(hidden, d_fed)), 0, ring_a).astype(F32)
-    grad_gu = scatter_rows(topo, cut(mm_tn(n2, d_gu)), 1, ring_b).astype(F32)
+    grad_gate = scatter_rows(topo, cut(mm_tn(n2, d_gated)), 1, ring_b).astype(F32)
+    grad_up = scatter_rows(topo, cut(mm_tn(n2, d_up)), 1, ring_b).astype(F32)
     tiny = jnp.stack(
         [smalls[2][0], smalls[1][0], smalls[0][0],
          smalls[0][1] + smalls[1][1] + smalls[2][1],
@@ -555,7 +758,7 @@
 
     return (
         unsort(final), unsort(gradient), grad_query, grad_key, grad_value, grad_out,
-        grad_gu[:, :ff], grad_gu[:, ff:], grad_down, tiny[:, :RECS], tiny[:, RECS],
+        grad_gate, grad_up, grad_down, tiny[:, :RECS], tiny[:, RECS],
         tiny[:, RECS + 1],
     )
 

time: 1050 us -> 923 us (0.88)
  waiting for transfers between devices: 334 us -> 172 us
  Pallas kernels: 75.8 us -> 171 us
  other arithmetic: 157 us -> 121 us
  local copies, waits for them, and re-layouts: 195 us -> 162 us
  starting transfers between devices: 120 us -> 149 us
  matrix products: 139 us -> 127 us
    ppermute x57 -> x49, waiting for transfers between devices: 282 us -> 162 us  [exchange(): return lax.ppermute(arr, AXES, topo.pairs(key))]
    pallas_call x0 -> x1, Pallas kernels: none -> 95.8 us  [gather_weights(): pl.pallas_call(functools.partial(gather_kernel, topo, pieces), in_specs=[...]
    ppermute x57 -> x49, starting transfers between devices: 93.8 us -> 137 us  [exchange(): return lax.ppermute(arr, AXES, topo.pairs(key))]
    ppermute x1, waiting for transfers between devices: 21.5 us -> 0.01 us  [per_device(): gradient = lax.ppermute(gradient.astype(BF), AXES, swap)]
    select_n x12 -> x8, other arithmetic: 17.8 us -> 0.64 us  [double(): low = jnp.where(mine_is_high, other, arr)]
    ppermute x1, waiting for transfers between devices: 15.2 us -> 0.01 us  [per_device(): labels = lax.ppermute(labels, AXES, swap)]
    concatenate x9 -> x4, other arithmetic: 13.2 us -> 0.11 us  [double(): return jnp.concatenate([low, high], axis=axis)]
    dot_general x15 -> x18, matrix products: 50.3 us -> 38.8 us  [mm_nt(): return lax.dot_general(a, b, NT, preferred_element_type=F32)]
  transfers between devices with their start and end apart: 62 -> 54, of which waited for: 34 -> 24; matrix products, arithmetic and copies ran while one was open for 28% -> 20% of each run, Pallas kernels for 3% -> 11%
where the time goes in v2:
time: 923 us; the launch traced here: 911 us
  waiting for transfers between devices  172 us (19%)
  Pallas kernels  171 us (19%)
  local copies, waits for them, and re-layouts  162 us (18%)
  starting transfers between devices  149 us (16%)
  matrix products  127 us (14%)
  other arithmetic  121 us (13%)
    ppermute x49, waiting for transfers between devices, exchange(): return lax.ppermute(arr, AXES, topo.pairs(key))  162 us
    ppermute x49, starting transfers between devices, exchange(): return lax.ppermute(arr, AXES, topo.pairs(key))  137 us
    pallas_call x1, Pallas kernels, gather_weights(): pl.pallas_call(functools.partial(gather_kernel, topo, pieces), in_specs=[...  95.8 us
    dot_general x21, matrix products, mm(): return jnp.dot(a, b, preferred_element_type=F32)  53.7 us
    convert_element_type x29, other arithmetic, halve(): return (keep + exchange(topo, send, key).astype(F32)).astype(BF)  40.6 us
    pallas_call x3, Pallas kernels, attend_back(): pl.pallas_call(functools.partial(attend_back_kernel, rows), grid_spec=plt...  40.4 us
    dot_general x18, matrix products, mm_nt(): return lax.dot_general(a, b, NT, preferred_element_type=F32)  38.8 us
    pallas_call x3, Pallas kernels, attend(): pl.pallas_call(functools.partial(attend_kernel, rows), grid_spec=pltpu.Pr...  35.1 us
  transfers between devices with their start and end apart: 54, of which 24 were waited for; matrix products, arithmetic and copies ran while one was open for 20% of the time, Pallas kernels for 11%

profile of v2, /device:TPU:17, one launch (start us, length us, event | category | flops | bytes accessed | tf_op | source)
XLA Modules:
  0.0 911.1 jit_solution(4091638261325270415)
XLA Ops:
  15.6 95.8 %gather_weights.1 = (bf16[8,120,2624]{2,1,0:T(8,128)(2,1)}, bf16[8,120,2560]{2,1,0:T(8,128)(2,1)}, bf16[8,120,2560]{2,1,0:T(8,128)(2,1)}, bf16[8,320,960]{2,1,0:T(8,128)(2,1)}) custom-call(bf16[120,2624]{1,0:T(8,128)(2,1)} %concatenate.140.refs_0_, bf16[120,2560]{1,0:T(8,128)(2,1)} %refs_1_.1, bf16[120,2560]{1,0:T(8,128)(2,1)} %refs_2_.1, ...), custom_call_target="tpu_custom_call" | custom-call | tf_op jit(solution)/shard_map/gather_weights/pallas_call | solution.py:335
  125.0 7.6 collective-permute-done.5
  135.3 12.3 %collective-permute-done.6 = bf16[2,256,640]{1,2,0:T(8,128)(2,1)S(1)} collective-permute-done((bf16[2,256,640]{1,2,0:T(8,128)(2,1)S(1)}, bf16[2,256,640]{1,2,0:T(8,128)(2,1)S(1)}, u32[]{:S(2)}, u32[]{:S(2)}) %collective-permute-start.6) | collective-permute-done | bytes 655392 | tf_op jit(solution)/shard_map/ppermute | solution.py:73
  162.0 12.7 %attend.3 = (f32[5,128,768]{2,1,0:T(8,128)}, f32[5,8,768]{2,1,0:T(8,128)}) custom-call(s32[2]{0:T(128)} %pad_add_fusion.9.span, s32[2048,8]{1,0:T(8,128)} %pad.41.key_ref, s32[8,768]{1,0:T(8,128)} %pad.42.query_ref, bf16[2048,640]{1,0:T(8,128)(2,1)} %bitcast.541, bf16[5,768,128]{2,1,0:T(8,128)(2,1)} %bitcast.563), custom_call_target="tpu_custom_call" | custom-call | flops 4026531840 | bytes 6553600 | tf_op jit(solution)/shard_map/attend/pallas_call | solution.py:431
  201.4 9.4 %collective-permute-start.9 = (bf16[2,192,640]{2,1,0:T(8,128)(2,1)S(1)}, bf16[2,192,640]{2,1,0:T(8,128)(2,1)S(1)}, u32[]{:S(2)}, u32[]{:S(2)}) collective-permute-start(bf16[2,192,640]{2,1,0:T(8,128)(2,1)S(1)} %copy.740), channel_id=1, source_target_pairs={{0,16},{1,17},{2,18},{3,19},{4,20},{5,21},{6,22},{7,23},{8,24},{9,... | collective-permute-start | bytes 1474568 | tf_op jit(solution)/shard_map/ppermute | solution.py:73
  243.9 11.2 %attend.4 = (f32[5,128,576]{2,1,0:T(8,128)}, f32[5,8,576]{2,1,0:T(8,128)}) custom-call(s32[2]{0:T(128)} %pad_add_fusion.9.span, s32[1536,8]{1,0:T(8,128)} %pad.43.key_ref, s32[8,576]{1,0:T(8,128)} %pad.44.query_ref, bf16[1536,640]{1,0:T(8,128)(2,1)} %bitcast.544, bf16[5,576,128]{2,1,0:T(8,128)(2,1)} %bitcast.569), custom_call_target="tpu_custom_call" | custom-call | flops 2264924160 | bytes 4915200 | tf_op jit(solution)/shard_map/attend/pallas_call | solution.py:431
  286.0 8.0 collective-permute-start.12
  295.2 9.8 %collective-permute-done.15 = bf16[256,960]{0,1:T(8,128)(2,1)S(1)} collective-permute-done((bf16[256,960]{0,1:T(8,128)(2,1)}, bf16[256,960]{0,1:T(8,128)(2,1)S(1)}, u32[]{:S(2)}, u32[]{:S(2)}) %collective-permute-start.15) | collective-permute-done | bytes 491552 | tf_op jit(solution)/shard_map/ppermute | solution.py:617
  333.8 11.2 %attend.5 = (f32[5,128,576]{2,1,0:T(8,128)}, f32[5,8,576]{2,1,0:T(8,128)}) custom-call(s32[2]{0:T(128)} %pad_add_fusion.9.span, s32[1536,8]{1,0:T(8,128)} %pad.45.key_ref, s32[8,576]{1,0:T(8,128)} %pad.44.query_ref, bf16[1536,640]{1,0:T(8,128)(2,1)} %bitcast.546, bf16[5,576,128]{2,1,0:T(8,128)(2,1)} %bitcast.568), custom_call_target="tpu_custom_call" | custom-call | flops 2264924160 | bytes 4915200 | tf_op jit(solution)/shard_map/attend/pallas_call | solution.py:431
  377.9 12.6 %attend_back.3 = (f32[5,128,576]{2,1,0:T(8,128)}, bf16[1536,640]{1,0:T(8,128)(2,1)}) custom-call(s32[2]{0:T(128)} %pad_add_fusion.9.span, s32[1536,8]{1,0:T(8,128)} %pad.45.key_ref, s32[8,576]{1,0:T(8,128)} %pad.44.query_ref, bf16[1536,640]{1,0:T(8,128)(2,1)} %bitcast.547, bf16[5,576,128]{2,1,0:T(8,128)(2,1)} %bitcast.571, ...), custom_call_target="tpu_custom_call" | custom-call | flops 5662310400 | bytes 6881280 | tf_op jit(solution)/shard_map/attend_back/pallas_call | solution.py:500
  412.4 10.8 %collective-permute-start.17 = (bf16[2,192,640]{2,1,0:T(8,128)(2,1)}, bf16[2,192,640]{2,1,0:T(8,128)(2,1)}, u32[]{:S(2)}, u32[]{:S(2)}) collective-permute-start(bf16[2,192,640]{2,1,0:T(8,128)(2,1)} %copy.780), channel_id=1, source_target_pairs={{0,16},{1,17},{2,18},{3,19},{4,20},{5,21},{6,22},{7,23},{8,24},{9,... | collective-permute-start | bytes 1474568 | tf_op jit(solution)/shard_map/ppermute | solution.py:73
  438.5 6.8 collective-permute-start.18
  473.3 12.8 %attend_back.4 = (f32[5,128,576]{2,1,0:T(8,128)}, bf16[1536,640]{1,0:T(8,128)(2,1)}) custom-call(s32[2]{0:T(128)} %pad_add_fusion.9.span, s32[1536,8]{1,0:T(8,128)} %pad.43.key_ref, s32[8,576]{1,0:T(8,128)} %pad.44.query_ref, bf16[1536,640]{1,0:T(8,128)(2,1)} %bitcast.545, bf16[5,576,128]{2,1,0:T(8,128)(2,1)} %bitcast.570, ...), custom_call_target="tpu_custom_call" | custom-call | flops 5662310400 | bytes 6881280 | tf_op jit(solution)/shard_map/attend_back/pallas_call | solution.py:500
  517.5 6.9 collective-permute-start.20
  527.9 13.0 %collective-permute-done.20 = bf16[2,192,640]{2,1,0:T(8,128)(2,1)} collective-permute-done((bf16[2,192,640]{2,1,0:T(8,128)(2,1)}, bf16[2,192,640]{2,1,0:T(8,128)(2,1)}, u32[]{:S(2)}, u32[]{:S(2)}) %collective-permute-start.20) | collective-permute-done | bytes 491552 | tf_op jit(solution)/shard_map/ppermute | solution.py:73
  557.1 7.7 fusion.12
  569.4 6.5 fusion
  576.0 6.8 fusion.6
  591.5 15.0 %attend_back.5 = (f32[5,128,768]{2,1,0:T(8,128)}, bf16[2048,640]{1,0:T(8,128)(2,1)}) custom-call(s32[2]{0:T(128)} %pad_add_fusion.9.span, s32[2048,8]{1,0:T(8,128)} %pad.41.key_ref, s32[8,768]{1,0:T(8,128)} %pad.42.query_ref, bf16[2048,640]{1,0:T(8,128)(2,1)} %bitcast.542, bf16[5,768,128]{2,1,0:T(8,128)(2,1)} %bitcast.564, ...), custom_call_target="tpu_custom_call" | custom-call | flops 10066329600 | bytes 9175040 | tf_op jit(solution)/shard_map/attend_back/pallas_call | solution.py:500
  645.6 6.6 collective-permute-start.23
  659.9 6.9 collective-permute-done.23
  682.4 10.8 %concatenate.166 = f32[960,2624]{1,0:T(8,128)} concatenate(f32[960,960]{1,0:T(8,128)} %fusion.28, f32[960,64]{1,0:T(8,128)S(1)} %pad.46, f32[960,640]{1,0:T(8,128)S(1)} %fusion.66, f32[960,960]{1,0:T(8,128)} %fusion.34), dimensions={1} | concatenate | bytes 20152320 | tf_op jit(solution)/shard_map/concatenate | solution.py:746
  713.7 6.9 add_convert_fusion.2
  735.9 10.5 %collective-permute-start.49 = (bf16[2,2,80,960]{3,2,1,0:T(8,128)(2,1)S(1)}, bf16[2,2,80,960]{3,2,1,0:T(8,128)(2,1)S(1)}, u32[]{:S(2)}, u32[]{:S(2)}) collective-permute-start(bf16[2,2,80,960]{3,2,1,0:T(8,128)(2,1)S(1)} %broadcast_select_fusion.3), channel_id=1, source_target_pairs={{0,16},{1,17},{2,18},{3,19},{4,20},{5,21},{6,22},{7,23},{8,24},{9,... | collective-permute-start | bytes 1843208 | tf_op jit(solution)/shard_map/ppermute | solution.py:73
  750.0 19.3 %collective-permute-done.34 = bf16[2,2,2,120,640]{4,3,0,1,2:T(8,128)(2,1)S(1)} collective-permute-done((bf16[2,2,2,120,640]{4,3,0,1,2:T(8,128)(2,1)S(1)}, bf16[2,2,2,120,640]{4,3,0,1,2:T(8,128)(2,1)S(1)}, u32[]{:S(2)}, u32[]{:S(2)}) %collective-permute-start.34) | collective-permute-done | bytes 1228832 | tf_op jit(solution)/shard_map/ppermute | solution.py:73
  770.2 13.1 %collective-permute-done.49 = bf16[2,2,80,960]{3,2,1,0:T(8,128)(2,1)S(1)} collective-permute-done((bf16[2,2,80,960]{3,2,1,0:T(8,128)(2,1)S(1)}, bf16[2,2,80,960]{3,2,1,0:T(8,128)(2,1)S(1)}, u32[]{:S(2)}, u32[]{:S(2)}) %collective-permute-start.49) | collective-permute-done | bytes 614432 | tf_op jit(solution)/shard_map/ppermute | solution.py:73
  790.2 17.0 %collective-permute-start.51 = (bf16[80,960]{1,0:T(8,128)(2,1)S(1)}, bf16[80,960]{1,0:T(8,128)(2,1)S(1)}, u32[]{:S(2)}, u32[]{:S(2)}) collective-permute-start(bf16[80,960]{1,0:T(8,128)(2,1)S(1)} %select_bitcast_fusion.33), channel_id=1, source_target_pairs={{0,4},{1,5},{2,6},{3,7},{4,0},{5,1},{6,2},{7,3},{8,12},{9,13},{10,... | collective-permute-start | bytes 460808 | tf_op jit(solution)/shard_map/ppermute | solution.py:73
  807.3 8.1 collective-permute-start.44
  815.6 9.8 %collective-permute-start.37 = (bf16[120,640]{1,0:T(8,128)(2,1)S(1)}, bf16[120,640]{1,0:T(8,128)(2,1)S(1)}, u32[]{:S(2)}, u32[]{:S(2)}) collective-permute-start(bf16[120,640]{1,0:T(8,128)(2,1)S(1)} %select_bitcast_fusion.35), channel_id=1, source_target_pairs={{0,4},{1,5},{2,6},{3,7},{4,0},{5,1},{6,2},{7,3},{8,12},{9,13},{10,... | collective-permute-start | bytes 460808 | tf_op jit(solution)/shard_map/ppermute | solution.py:73
  844.4 19.0 %collective-permute-done.27 = bf16[2,2,120,1536]{3,2,1,0:T(8,128)(2,1)S(1)} collective-permute-done((bf16[2,2,120,1536]{3,2,1,0:T(8,128)(2,1)S(1)}, bf16[2,2,120,1536]{3,2,1,0:T(8,128)(2,1)S(1)}, u32[]{:S(2)}, u32[]{:S(2)}) %collective-permute-start.27) | collective-permute-done | bytes 1474592 | tf_op jit(solution)/shard_map/ppermute | solution.py:73
  868.6 10.0 %collective-permute-done.28 = bf16[2,2,120,768]{3,2,1,0:T(8,128)(2,1)S(1)} collective-permute-done((bf16[2,2,120,768]{3,2,1,0:T(8,128)(2,1)S(1)}, bf16[2,2,120,768]{3,2,1,0:T(8,128)(2,1)S(1)}, u32[]{:S(2)}, u32[]{:S(2)}) %collective-permute-start.28) | collective-permute-done | bytes 737312 | tf_op jit(solution)/shard_map/ppermute | solution.py:73
  895.8 10.0 %collective-permute-start.32 = (bf16[120,1536]{1,0:T(8,128)(2,1)S(1)}, bf16[120,1536]{1,0:T(8,128)(2,1)S(1)}, u32[]{:S(2)}, u32[]{:S(2)}) collective-permute-start(bf16[120,1536]{1,0:T(8,128)(2,1)S(1)} %pad_maximum_fusion.23), channel_id=1, source_target_pairs={{0,8},{1,9},{2,10},{3,11},{4,12},{5,13},{6,14},{7,15},{8,0},{9,1},... | collective-permute-start | bytes 1105928 | tf_op jit(solution)/shard_map/ppermute | solution.py:73
  (929 shorter events, 478.3 us)
Async XLA Ops:
  3.3 117.4 %collective-permute-start = (bf16[256,960]{0,1:T(8,128)(2,1)S(1)}, bf16[256,960]{0,1:T(8,128)(2,1)S(1)}, u32[]{:S(2)}, u32[]{:S(2)}) collective-permute-start(bf16[256,960]{0,1:T(8,128)(2,1)S(1)} %convolution_convert_fusion.4), channel_id=1, source_target_pairs={{0,0},{1,1},{2,8},{3,9},{4,16},{5,17},{6,24},{7,25},{8,2},{9,3},{1... | collective-permute-start | bytes 1474568 | tf_op jit(solution)/shard_map/ppermute | solution.py:615
  9.4 103.9 %collective-permute-start.1 = (s32[8,256]{1,0:T(8,128)S(1)}, s32[8,256]{1,0:T(8,128)S(1)}, u32[]{:S(2)}, u32[]{:S(2)}) collective-permute-start(s32[8,256]{1,0:T(8,128)S(1)} %pad.39), channel_id=1, source_target_pairs={{0,0},{1,1},{2,8},{3,9},{4,16},{5,17},{6,24},{7,25},{8,2},{9,3},{1... | collective-permute-start | bytes 24584 | tf_op jit(solution)/shard_map/ppermute | solution.py:616
  132.8 14.8 %collective-permute-start.6 = (bf16[2,256,640]{1,2,0:T(8,128)(2,1)S(1)}, bf16[2,256,640]{1,2,0:T(8,128)(2,1)S(1)}, u32[]{:S(2)}, u32[]{:S(2)}) collective-permute-start(bf16[2,256,640]{1,2,0:T(8,128)(2,1)S(1)} %pad_maximum_fusion.12), channel_id=1, source_target_pairs={{0,16},{1,17},{2,18},{3,19},{4,20},{5,21},{6,22},{7,23},{8,24},{9,... | collective-permute-start | bytes 1966088 | tf_op jit(solution)/shard_map/ppermute | solution.py:73
  201.4 15.6 %collective-permute-start.9 = (bf16[2,192,640]{2,1,0:T(8,128)(2,1)S(1)}, bf16[2,192,640]{2,1,0:T(8,128)(2,1)S(1)}, u32[]{:S(2)}, u32[]{:S(2)}) collective-permute-start(bf16[2,192,640]{2,1,0:T(8,128)(2,1)S(1)} %copy.740), channel_id=1, source_target_pairs={{0,16},{1,17},{2,18},{3,19},{4,20},{5,21},{6,22},{7,23},{8,24},{9,... | collective-permute-start | bytes 1474568 | tf_op jit(solution)/shard_map/ppermute | solution.py:73
  278.8 26.3 %collective-permute-start.15 = (bf16[256,960]{0,1:T(8,128)(2,1)}, bf16[256,960]{0,1:T(8,128)(2,1)S(1)}, u32[]{:S(2)}, u32[]{:S(2)}) collective-permute-start(bf16[256,960]{0,1:T(8,128)(2,1)} %convolution_convert_fusion.2), channel_id=1, source_target_pairs={{0,0},{1,1},{2,8},{3,9},{4,16},{5,17},{6,24},{7,25},{8,2},{9,3},{1... | collective-permute-start | bytes 1474568 | tf_op jit(solution)/shard_map/ppermute | solution.py:617
  286.0 23.3 %collective-permute-start.12 = (bf16[2,192,640]{2,1,0:T(8,128)(2,1)}, bf16[2,192,640]{2,1,0:T(8,128)(2,1)}, u32[]{:S(2)}, u32[]{:S(2)}) collective-permute-start(bf16[2,192,640]{2,1,0:T(8,128)(2,1)} %copy.758), channel_id=1, source_target_pairs={{0,16},{1,17},{2,18},{3,19},{4,20},{5,21},{6,22},{7,23},{8,24},{9,... | collective-permute-start | bytes 1474568 | tf_op jit(solution)/shard_map/ppermute | solution.py:73
  412.4 22.6 %collective-permute-start.17 = (bf16[2,192,640]{2,1,0:T(8,128)(2,1)}, bf16[2,192,640]{2,1,0:T(8,128)(2,1)}, u32[]{:S(2)}, u32[]{:S(2)}) collective-permute-start(bf16[2,192,640]{2,1,0:T(8,128)(2,1)} %copy.780), channel_id=1, source_target_pairs={{0,16},{1,17},{2,18},{3,19},{4,20},{5,21},{6,22},{7,23},{8,24},{9,... | collective-permute-start | bytes 1474568 | tf_op jit(solution)/shard_map/ppermute | solution.py:73
  508.3 36.2 %collective-permute-start.14 = (bf16[256,960]{0,1:T(8,128)(2,1)}, bf16[256,960]{0,1:T(8,128)(2,1)}, u32[]{:S(2)}, u32[]{:S(2)}) collective-permute-start(bf16[256,960]{0,1:T(8,128)(2,1)} %pad_maximum_fusion.15), channel_id=1, source_target_pairs={{0,0},{1,1},{2,8},{3,9},{4,16},{5,17},{6,24},{7,25},{8,2},{9,3},{1... | collective-permute-start | bytes 1474568 | tf_op jit(solution)/shard_map/ppermute | solution.py:716
  517.5 23.4 %collective-permute-start.20 = (bf16[2,192,640]{2,1,0:T(8,128)(2,1)}, bf16[2,192,640]{2,1,0:T(8,128)(2,1)}, u32[]{:S(2)}, u32[]{:S(2)}) collective-permute-start(bf16[2,192,640]{2,1,0:T(8,128)(2,1)} %copy.796), channel_id=1, source_target_pairs={{0,16},{1,17},{2,18},{3,19},{4,20},{5,21},{6,22},{7,23},{8,24},{9,... | collective-permute-start | bytes 1474568 | tf_op jit(solution)/shard_map/ppermute | solution.py:73
  612.9 30.7 %collective-permute-start.22 = (bf16[2,2,256,640]{2,3,1,0:T(8,128)(2,1)}, bf16[2,2,256,640]{2,3,1,0:T(8,128)(2,1)}, u32[]{:S(2)}, u32[]{:S(2)}) collective-permute-start(bf16[2,2,256,640]{2,3,1,0:T(8,128)(2,1)} %select_bitcast_fusion.1), channel_id=1, source_target_pairs={{0,8},{1,9},{2,10},{3,11},{4,12},{5,13},{6,14},{7,15},{8,0},{9,1},... | collective-permute-start | bytes 3932168 | tf_op jit(solution)/shard_map/ppermute | solution.py:73
  625.1 80.5 %collective-permute-start.47 = (bf16[2,2,2,160,960]{4,3,2,1,0:T(8,128)(2,1)}, bf16[2,2,2,160,960]{4,3,2,1,0:T(8,128)(2,1)}, u32[]{:S(2)}, u32[]{:S(2)}) collective-permute-start(bf16[2,2,2,160,960]{4,3,2,1,0:T(8,128)(2,1)} %select_convert_fusion.1), channel_id=1, source_target_pairs={{0,8},{1,9},{2,10},{3,11},{4,12},{5,13},{6,14},{7,15},{8,0},{9,1},... | collective-permute-start | bytes 7372808 | tf_op jit(solution)/shard_map/ppermute | solution.py:73
  634.1 79.6 %collective-permute-start.40 = (bf16[2,2,2,120,1280]{4,3,0,1,2:T(8,128)(2,1)}, bf16[2,2,2,120,1280]{4,3,0,1,2:T(8,128)(2,1)}, u32[]{:S(2)}, u32[]{:S(2)}) collective-permute-start(bf16[2,2,2,120,1280]{4,3,0,1,2:T(8,128)(2,1)} %select_convert_fusion.2), channel_id=1, source_target_pairs={{0,8},{1,9},{2,10},{3,11},{4,12},{5,13},{6,14},{7,15},{8,0},{9,1},... | collective-permute-start | bytes 7372808 | tf_op jit(solution)/shard_map/ppermute | solution.py:73
  643.6 81.0 %collective-permute-start.33 = (bf16[2,2,2,120,1280]{4,3,0,1,2:T(8,128)(2,1)}, bf16[2,2,2,120,1280]{4,3,0,1,2:T(8,128)(2,1)}, u32[]{:S(2)}, u32[]{:S(2)}) collective-permute-start(bf16[2,2,2,120,1280]{4,3,0,1,2:T(8,128)(2,1)} %select_convert_fusion.3), channel_id=1, source_target_pairs={{0,8},{1,9},{2,10},{3,11},{4,12},{5,13},{6,14},{7,15},{8,0},{9,1},... | collective-permute-start | bytes 7372808 | tf_op jit(solution)/shard_map/ppermute | solution.py:73
  645.6 21.3 %collective-permute-start.23 = (bf16[2,256,640]{1,2,0:T(8,128)(2,1)S(1)}, bf16[2,256,640]{1,2,0:T(8,128)(2,1)S(1)}, u32[]{:S(2)}, u32[]{:S(2)}) collective-permute-start(bf16[2,256,640]{1,2,0:T(8,128)(2,1)S(1)} %select_bitcast_fusion.10), channel_id=1, source_target_pairs={{0,16},{1,17},{2,18},{3,19},{4,20},{5,21},{6,22},{7,23},{8,24},{9,... | collective-permute-start | bytes 1966088 | tf_op jit(solution)/shard_map/ppermute | solution.py:73
  700.9 124.5 %collective-permute-start.26 = (bf16[2,2,2,120,1536]{4,3,2,1,0:T(8,128)(2,1)}, bf16[2,2,2,120,1536]{4,3,2,1,0:T(8,128)(2,1)}, u32[]{:S(2)}, u32[]{:S(2)}) collective-permute-start(bf16[2,2,2,120,1536]{4,3,2,1,0:T(8,128)(2,1)} %select_convert_fusion), channel_id=1, source_target_pairs={{0,8},{1,9},{2,10},{3,11},{4,12},{5,13},{6,14},{7,15},{8,0},{9,1},... | collective-permute-start | bytes 8847368 | tf_op jit(solution)/shard_map/ppermute | solution.py:73
  703.5 28.9 %collective-permute-start.25 = (bf16[256,960]{0,1:T(8,128)(2,1)S(1)}, bf16[256,960]{0,1:T(8,128)(2,1)S(1)}, u32[]{:S(2)}, u32[]{:S(2)}) collective-permute-start(bf16[256,960]{0,1:T(8,128)(2,1)S(1)} %fusion.59), channel_id=1, source_target_pairs={{0,0},{1,1},{2,8},{3,9},{4,16},{5,17},{6,24},{7,25},{8,2},{9,3},{1... | collective-permute-start | bytes 1474568 | tf_op jit(solution)/shard_map/ppermute | solution.py:728
  712.2 21.3 %collective-permute-start.48 = (bf16[2,2,160,960]{3,2,1,0:T(8,128)(2,1)S(1)}, bf16[2,2,160,960]{3,2,1,0:T(8,128)(2,1)}, u32[]{:S(2)}, u32[]{:S(2)}) collective-permute-start(bf16[2,2,160,960]{3,2,1,0:T(8,128)(2,1)S(1)} %fusion.23), channel_id=1, source_target_pairs={{0,1},{1,0},{2,3},{3,2},{4,5},{5,4},{6,7},{7,6},{8,9},{9,8},{10,11... | collective-permute-start | bytes 3686408 | tf_op jit(solution)/shard_map/ppermute | solution.py:73
  723.4 23.0 %collective-permute-start.41 = (bf16[2,2,2,120,640]{4,3,0,1,2:T(8,128)(2,1)}, bf16[2,2,2,120,640]{4,3,0,1,2:T(8,128)(2,1)}, u32[]{:S(2)}, u32[]{:S(2)}) collective-permute-start(bf16[2,2,2,120,640]{4,3,0,1,2:T(8,128)(2,1)} %broadcast_select_fusion), channel_id=1, source_target_pairs={{0,16},{1,17},{2,18},{3,19},{4,20},{5,21},{6,22},{7,23},{8,24},{9,... | collective-permute-start | bytes 3686408 | tf_op jit(solution)/shard_map/ppermute | solution.py:73
  732.0 37.3 %collective-permute-start.34 = (bf16[2,2,2,120,640]{4,3,0,1,2:T(8,128)(2,1)S(1)}, bf16[2,2,2,120,640]{4,3,0,1,2:T(8,128)(2,1)S(1)}, u32[]{:S(2)}, u32[]{:S(2)}) collective-permute-start(bf16[2,2,2,120,640]{4,3,0,1,2:T(8,128)(2,1)S(1)} %broadcast_select_fusion.1), channel_id=1, source_target_pairs={{0,16},{1,17},{2,18},{3,19},{4,20},{5,21},{6,22},{7,23},{8,24},{9,... | collective-permute-start | bytes 3686408 | tf_op jit(solution)/shard_map/ppermute | solution.py:73
  735.9 47.4 %collective-permute-start.49 = (bf16[2,2,80,960]{3,2,1,0:T(8,128)(2,1)S(1)}, bf16[2,2,80,960]{3,2,1,0:T(8,128)(2,1)S(1)}, u32[]{:S(2)}, u32[]{:S(2)}) collective-permute-start(bf16[2,2,80,960]{3,2,1,0:T(8,128)(2,1)S(1)} %broadcast_select_fusion.3), channel_id=1, source_target_pairs={{0,16},{1,17},{2,18},{3,19},{4,20},{5,21},{6,22},{7,23},{8,24},{9,... | collective-permute-start | bytes 1843208 | tf_op jit(solution)/shard_map/ppermute | solution.py:73
  748.5 35.3 %collective-permute-start.42 = (bf16[2,2,120,640]{3,2,0,1:T(8,128)(2,1)S(1)}, bf16[2,2,120,640]{3,2,0,1:T(8,128)(2,1)S(1)}, u32[]{:S(2)}, u32[]{:S(2)}) collective-permute-start(bf16[2,2,120,640]{3,2,0,1:T(8,128)(2,1)S(1)} %select_bitcast_fusion.19), channel_id=1, source_target_pairs={{0,1},{1,0},{2,3},{3,2},{4,5},{5,4},{6,7},{7,6},{8,9},{9,8},{10,11... | collective-permute-start | bytes 1843208 | tf_op jit(solution)/shard_map/ppermute | solution.py:73
  769.8 15.8 %collective-permute-start.35 = (bf16[2,2,120,640]{3,2,0,1:T(8,128)(2,1)S(1)}, bf16[2,2,120,640]{3,2,0,1:T(8,128)(2,1)S(1)}, u32[]{:S(2)}, u32[]{:S(2)}) collective-permute-start(bf16[2,2,120,640]{3,2,0,1:T(8,128)(2,1)S(1)} %select_bitcast_fusion.20), channel_id=1, source_target_pairs={{0,1},{1,0},{2,3},{3,2},{4,5},{5,4},{6,7},{7,6},{8,9},{9,8},{10,11... | collective-permute-start | bytes 1843208 | tf_op jit(solution)/shard_map/ppermute | solution.py:73
  784.0 23.1 %collective-permute-start.43 = (bf16[2,120,640]{2,1,0:T(8,128)(2,1)S(1)}, bf16[2,120,640]{2,1,0:T(8,128)(2,1)S(1)}, u32[]{:S(2)}, u32[]{:S(2)}) collective-permute-start(bf16[2,120,640]{2,1,0:T(8,128)(2,1)S(1)} %select_bitcast_fusion.30), channel_id=1, source_target_pairs={{0,2},{1,3},{2,0},{3,1},{4,6},{5,7},{6,4},{7,5},{8,10},{9,11},{10,... | collective-permute-start | bytes 921608 | tf_op jit(solution)/shard_map/ppermute | solution.py:73
  785.8 29.6 %collective-permute-start.36 = (bf16[2,120,640]{2,1,0:T(8,128)(2,1)S(1)}, bf16[2,120,640]{2,1,0:T(8,128)(2,1)S(1)}, u32[]{:S(2)}, u32[]{:S(2)}) collective-permute-start(bf16[2,120,640]{2,1,0:T(8,128)(2,1)S(1)} %select_bitcast_fusion.31), channel_id=1, source_target_pairs={{0,2},{1,3},{2,0},{3,1},{4,6},{5,7},{6,4},{7,5},{8,10},{9,11},{10,... | collective-permute-start | bytes 921608 | tf_op jit(solution)/shard_map/ppermute | solution.py:73
  790.2 42.4 %collective-permute-start.51 = (bf16[80,960]{1,0:T(8,128)(2,1)S(1)}, bf16[80,960]{1,0:T(8,128)(2,1)S(1)}, u32[]{:S(2)}, u32[]{:S(2)}) collective-permute-start(bf16[80,960]{1,0:T(8,128)(2,1)S(1)} %select_bitcast_fusion.33), channel_id=1, source_target_pairs={{0,4},{1,5},{2,6},{3,7},{4,0},{5,1},{6,2},{7,3},{8,12},{9,13},{10,... | collective-permute-start | bytes 460808 | tf_op jit(solution)/shard_map/ppermute | solution.py:73
  807.3 25.5 %collective-permute-start.44 = (bf16[120,640]{1,0:T(8,128)(2,1)S(1)}, bf16[120,640]{1,0:T(8,128)(2,1)S(1)}, u32[]{:S(2)}, u32[]{:S(2)}) collective-permute-start(bf16[120,640]{1,0:T(8,128)(2,1)S(1)} %select_bitcast_fusion.34), channel_id=1, source_target_pairs={{0,4},{1,5},{2,6},{3,7},{4,0},{5,1},{6,2},{7,3},{8,12},{9,13},{10,... | collective-permute-start | bytes 460808 | tf_op jit(solution)/shard_map/ppermute | solution.py:73
  815.6 18.8 %collective-permute-start.37 = (bf16[120,640]{1,0:T(8,128)(2,1)S(1)}, bf16[120,640]{1,0:T(8,128)(2,1)S(1)}, u32[]{:S(2)}, u32[]{:S(2)}) collective-permute-start(bf16[120,640]{1,0:T(8,128)(2,1)S(1)} %select_bitcast_fusion.35), channel_id=1, source_target_pairs={{0,4},{1,5},{2,6},{3,7},{4,0},{5,1},{6,2},{7,3},{8,12},{9,13},{10,... | collective-permute-start | bytes 460808 | tf_op jit(solution)/shard_map/ppermute | solution.py:73
  832.5 31.0 %collective-permute-start.27 = (bf16[2,2,120,1536]{3,2,1,0:T(8,128)(2,1)S(1)}, bf16[2,2,120,1536]{3,2,1,0:T(8,128)(2,1)S(1)}, u32[]{:S(2)}, u32[]{:S(2)}) collective-permute-start(bf16[2,2,120,1536]{3,2,1,0:T(8,128)(2,1)S(1)} %select_bitcast_fusion), channel_id=1, source_target_pairs={{0,1},{1,0},{2,3},{3,2},{4,5},{5,4},{6,7},{7,6},{8,9},{9,8},{10,11... | collective-permute-start | bytes 4423688 | tf_op jit(solution)/shard_map/ppermute | solution.py:73
  834.4 30.0 %collective-permute-start.38 = (bf16[120,640]{1,0:T(8,128)(2,1)S(1)}, bf16[120,640]{1,0:T(8,128)(2,1)S(1)}, u32[]{:S(2)}, u32[]{:S(2)}) collective-permute-start(bf16[120,640]{1,0:T(8,128)(2,1)S(1)} %fusion.116), channel_id=1, source_target_pairs={{0,16},{1,17},{2,18},{3,19},{4,20},{5,21},{6,22},{7,23},{8,24},{9,... | collective-permute-start | bytes 460808 | tf_op jit(solution)/shard_map/ppermute | solution.py:73
  837.0 54.3 %collective-permute-start.53 = (bf16[160,960]{1,0:T(8,128)(2,1)S(1)}, bf16[160,960]{1,0:T(8,128)(2,1)S(1)}, u32[]{:S(2)}, u32[]{:S(2)}) collective-permute-start(bf16[160,960]{1,0:T(8,128)(2,1)S(1)} %pad_maximum_fusion.30), channel_id=1, source_target_pairs={{0,8},{1,9},{2,10},{3,11},{4,12},{5,13},{6,14},{7,15},{8,0},{9,1},... | collective-permute-start | bytes 921608 | tf_op jit(solution)/shard_map/ppermute | solution.py:73
  842.9 25.6 %collective-permute-start.46 = (bf16[120,1280]{1,0:T(8,128)(2,1)S(1)}, bf16[120,1280]{1,0:T(8,128)(2,1)S(1)}, u32[]{:S(2)}, u32[]{:S(2)}) collective-permute-start(bf16[120,1280]{1,0:T(8,128)(2,1)S(1)} %pad_maximum_fusion.32), channel_id=1, source_target_pairs={{0,8},{1,9},{2,10},{3,11},{4,12},{5,13},{6,14},{7,15},{8,0},{9,1},... | collective-permute-start | bytes 921608 | tf_op jit(solution)/shard_map/ppermute | solution.py:73
  864.5 14.5 %collective-permute-start.39 = (bf16[120,1280]{1,0:T(8,128)(2,1)S(1)}, bf16[120,1280]{1,0:T(8,128)(2,1)S(1)}, u32[]{:S(2)}, u32[]{:S(2)}) collective-permute-start(bf16[120,1280]{1,0:T(8,128)(2,1)S(1)} %pad_maximum_fusion.31), channel_id=1, source_target_pairs={{0,8},{1,9},{2,10},{3,11},{4,12},{5,13},{6,14},{7,15},{8,0},{9,1},... | collective-permute-start | bytes 921608 | tf_op jit(solution)/shard_map/ppermute | solution.py:73
  (254 other events, 1803.4 us)

commit v3 on v2

--- a/solution.py
+++ b/solution.py
@@ -95,42 +95,6 @@
     send = jnp.where(mine_is_high, low, high).astype(BF)
     keep = jnp.where(mine_is_high, high, low).astype(F32)
     return (keep + exchange(topo, send, key).astype(F32)).astype(BF)
-
-
-def canonical(topo):
-    return list(reversed(topo.keys("z"))) + list(reversed(topo.keys("x")))
-
-
-def gather_rows(topo, shard, axis, order):
-    me = lax.axis_index("grp")
-    part = (me % 2) * topo.Y + me // 2
-    pieces = jnp.stack(jnp.split(shard, topo.G, axis=axis), axis=0)
-    arr = lax.dynamic_index_in_dim(pieces, part, 0, keepdims=False)
-    held = []
-    names = canonical(topo)
-    for key in order:
-        if key[0] in ("z", "x"):
-            place = sum(1 for h in held if names.index(h) < names.index(key))
-            arr = double(topo, arr, key, place, True)
-            held.append(key)
-        else:
-            arr = double(topo, arr, key, axis - 2, False)
-    return arr.reshape((topo.T,) + arr.shape[-2:])
-
-
-def scatter_rows(topo, arr, axis, order):
-    names = canonical(topo)
-    held = list(names)
-    arr = arr.reshape((2,) * len(names) + arr.shape[-2:])
-    for key in order:
-        if key[0] in ("z", "x"):
-            arr = halve(topo, arr, key, held.index(key), True)
-            held.remove(key)
-        else:
-            arr = halve(topo, arr, key, axis - 2, False)
-    for key in topo.keys("y") + topo.keys("c"):
-        arr = double(topo, arr, key, axis - 2, False)
-    return arr
 
 
 class Piece:
@@ -345,6 +309,333 @@
         name="gather_weights",
     )(*shards)
     return [o.reshape(-1, o.shape[-1]) for o in outs]
+
+
+class Share:
+    def __init__(self, array, start, shape, part):
+        self.array, self.start, self.shape, self.part = array, start, shape, part
+
+    def of(self, ref, core, *lead):
+        rows, columns = self.shape
+        if self.array == 2:
+            return ref.at[(core,) + lead + (slice(None), pl.ds(self.start, columns))]
+        if self.array == 3:
+            at = pl.multiple_of(core * rows, rows)
+            return ref.at[lead + (pl.ds(at, rows), slice(None))]
+        at = pl.multiple_of(core * columns, 128)
+        return ref.at[lead + (slice(None), pl.ds(at, columns))]
+
+
+def cut_shares(shapes):
+    rows, ff = shapes[2][2], shapes[2][3]
+    one = ff * 3 // 20 // 128 * 128
+    two = ff * 33 // 40 // 128 * 128
+    return [
+        Share(2, one, (rows, two - one), 0),
+        Share(3, 0, (shapes[3][1] // 2, shapes[3][2]), 2),
+        Share(2, two, (rows, ff - two), 2),
+        Share(0, 0, (rows, shapes[0][2] // 2), 1),
+        Share(1, 0, (rows, shapes[1][2] // 2), 1),
+        Share(2, 0, (rows, one), 1),
+    ]
+
+
+def reduce_kernel(topo, shares, *refs):
+    grads, outs = refs[:4], refs[4:8]
+    count = len(shares)
+    groups = []
+    at = 8
+    for _ in range(7):
+        groups.append(refs[at:at + count])
+        at += count
+    held, from_c, from_y, from_x, from_low, from_high, from_f = groups
+    (load_sem, c_send, c_recv, y_send, y_recv, x_send, x_recv, z_send, z_recv, f_send, f_recv,
+     o_send, o_recv, o_local) = refs[at:]
+    x, y, z, c = coordinates(topo)
+    X, Z, T = topo.X, topo.Z, topo.T
+    g, me = lax.axis_index("grp"), lax.axis_index("tok")
+    odd = lax.rem(y, 2)
+    below, above = z > 0, z < Z - 1
+    kind = pl.DeviceIdType.MESH
+
+    def over_y(k):
+        high = lax.rem(lax.div(y, 1 << k), 2)
+        return {"grp": g + (2 - 4 * high) * (1 << k), "tok": me}
+
+    over_c = {"grp": g + 1 - 2 * c, "tok": me}
+
+    def over_z(k):
+        return {"grp": g, "tok": (z + k) * X + x}
+
+    def over_x(k):
+        return {"grp": g, "tok": z * X + lax.rem(x + k, X)}
+
+    barrier = pltpu.get_barrier_semaphore()
+    partners = [over_c] + [over_y(k) for k in range(topo.bits["y"])]
+    partners += [over_x(k) for k in range(1, X)]
+
+    def greet(partner):
+        pl.semaphore_signal(barrier, inc=1, device_id=partner, device_id_type=kind)
+
+    for partner in partners:
+        greet(partner)
+    pl.when(below)(lambda: greet(over_z(-1)))
+    pl.when(above)(lambda: greet(over_z(1)))
+    every = range(count)
+
+    def load(p, t):
+        s = shares[p]
+        return pltpu.make_async_copy(
+            s.of(grads[s.array], c, t), held[p].at[t], load_sem.at[p, t]
+        )
+
+    def remote(source, landing, send, recv, target):
+        return pltpu.make_async_remote_copy(
+            src_ref=source, dst_ref=landing, send_sem=send, recv_sem=recv, device_id=target,
+            device_id_type=kind,
+        )
+
+    def c_copy(p, t):
+        s = shares[p]
+        return remote(
+            s.of(grads[s.array], 1 - c, t), from_c[p].at[t], c_send.at[p, t], c_recv.at[p, t],
+            over_c,
+        )
+
+    def y_copy(p, t):
+        return remote(
+            held[p].at[t], from_y[p].at[t], y_send.at[p, t], y_recv.at[p, t], over_y(0)
+        )
+
+    def x_copy(p, zz, k):
+        t = zz * X + lax.rem(x + k, X)
+        return remote(
+            held[p].at[t], from_x[p].at[zz, k - 1], x_send.at[p, zz, k - 1],
+            x_recv.at[p, zz, k - 1], over_x(k),
+        )
+
+    def z_copy(p, zz, k):
+        landing = from_low if k > 0 else from_high
+        way = (k + 1) // 2
+        return remote(
+            held[p].at[zz * X + x], landing[p].at[zz], z_send.at[p, zz, way],
+            z_recv.at[p, zz, way], over_z(k),
+        )
+
+    def f_copy(p, k):
+        return remote(
+            held[p].at[me], from_f[p].at[k], f_send.at[p, k], f_recv.at[p, k], over_y(k)
+        )
+
+    def o_copy(p):
+        s = shares[p]
+        return remote(
+            held[p].at[me], s.of(outs[s.array], c), o_send.at[p], o_recv.at[p], over_c
+        )
+
+    def o_arrived(p):
+        s = shares[p]
+        return remote(
+            held[p].at[me], s.of(outs[s.array], 1 - c), o_send.at[p], o_recv.at[p], over_c
+        )
+
+    def o_keep(p):
+        s = shares[p]
+        return pltpu.make_async_copy(held[p].at[me], s.of(outs[s.array], c), o_local.at[p])
+
+    def add(p, t, other):
+        held[p][t] = held[p][t] + other
+
+    def layers(body):
+        def step(i, carry):
+            k = Z - 1 - i
+            pl.when(z + k < Z)(lambda: body(z + k))
+            pl.when((k > 0) & (z - k >= 0))(lambda: body(z - k))
+            return carry
+        return step
+
+    def inside(p, body):
+        if shares[p].part == 1:
+            body()
+        else:
+            pl.when(odd == shares[p].part // 2)(body)
+
+    def outside(p, body):
+        if shares[p].part != 1:
+            pl.when(odd != shares[p].part // 2)(body)
+
+    def start_loads(zz):
+        def each(j, carry):
+            t = zz * X + lax.rem(x + j, X)
+            for p in every:
+                load(p, t).start()
+            return carry
+        lax.fori_loop(0, X, each, 0)
+
+    lax.fori_loop(0, Z, layers(start_loads), 0)
+    pl.semaphore_wait(barrier, len(partners) + below.astype(jnp.int32) + above.astype(jnp.int32))
+
+    def start_cores(zz):
+        def each(j, carry):
+            t = zz * X + lax.rem(x + j, X)
+            for p in every:
+                c_copy(p, t).start()
+            return carry
+        lax.fori_loop(0, X, each, 0)
+
+    lax.fori_loop(0, Z, layers(start_cores), 0)
+
+    def cores(zz):
+        def each(j, carry):
+            t = zz * X + lax.rem(x + j + 1, X)
+            for p in every:
+                load(p, t).wait()
+                c_copy(p, t).wait_recv()
+                add(p, t, from_c[p][t])
+                outside(p, lambda p=p: y_copy(p, t).start())
+                if shares[p].part == 1:
+                    for k in range(1, X):
+                        pl.when(j + 1 == k)(lambda p=p, k=k: x_copy(p, zz, k).start())
+            return carry
+        lax.fori_loop(0, X, each, 0)
+
+    lax.fori_loop(0, Z, layers(cores), 0)
+
+    def over(zz):
+        def each(j, carry):
+            t = zz * X + lax.rem(x + j + 1, X)
+            for p in every:
+                if shares[p].part != 1:
+                    def body(p=p):
+                        y_copy(p, t).wait_recv()
+                        add(p, t, from_y[p][t])
+                        for k in range(1, X):
+                            pl.when(j + 1 == k)(lambda: x_copy(p, zz, k).start())
+                    inside(p, body)
+            return carry
+        lax.fori_loop(0, X, each, 0)
+
+    def join(p, zz):
+        t = zz * X + x
+        for k in range(1, X):
+            x_copy(p, zz, k).wait_recv()
+            add(p, t, from_x[p][zz, k - 1])
+
+        def low():
+            z_copy(p, zz, 1).wait_recv()
+            add(p, t, from_low[p][zz])
+
+        def high():
+            z_copy(p, zz, -1).wait_recv()
+            add(p, t, from_high[p][zz])
+
+        pl.when((zz >= z) & below)(low)
+        pl.when((zz <= z) & above)(high)
+        pl.when(zz > z)(lambda: z_copy(p, zz, 1).start())
+        pl.when(zz < z)(lambda: z_copy(p, zz, -1).start())
+
+    def first_joins(zz):
+        for p in every:
+            if shares[p].part == 1:
+                join(p, zz)
+
+    def last_joins(zz):
+        for p in every:
+            if shares[p].part != 1:
+                inside(p, lambda p=p: join(p, zz))
+
+    def main(i, carry):
+        @pl.when(i < Z)
+        def _():
+            layers(first_joins)(i, 0)
+            layers(over)(i, 0)
+
+        @pl.when(i > 0)
+        def _():
+            layers(last_joins)(i - 1, 0)
+
+        return carry
+
+    lax.fori_loop(0, Z + 1, main, 0)
+
+    for k in range(1, topo.bits["y"]):
+        for p in every:
+            inside(p, lambda p=p: f_copy(p, k).start())
+        for p in every:
+            def fold(p=p):
+                f_copy(p, k).wait()
+                add(p, me, from_f[p][k])
+            inside(p, fold)
+    for p in every:
+        inside(p, lambda p=p: f_copy(p, 0).start())
+    for p in every:
+        if shares[p].part == 1:
+            f_copy(p, 0).wait()
+            add(p, me, from_f[p][0])
+        else:
+            def take(p=p):
+                f_copy(p, 0).wait_recv()
+                held[p][me] = from_f[p][0]
+            outside(p, lambda p=p: y_copy(p, me).wait_send())
+            outside(p, take)
+        o_copy(p).start()
+        o_keep(p).start()
+
+    def ends(t, carry):
+        for p in every:
+            c_copy(p, t).wait_send()
+            outside(p, lambda p=p: pl.when(t != me)(lambda: y_copy(p, t).wait_send()))
+        return carry
+
+    lax.fori_loop(0, T, ends, 0)
+
+    def z_ends(zz, carry):
+        for p in every:
+            def body(p=p):
+                for k in range(1, X):
+                    x_copy(p, zz, k).wait_send()
+                pl.when(zz > z)(lambda: z_copy(p, zz, 1).wait_send())
+                pl.when(zz < z)(lambda: z_copy(p, zz, -1).wait_send())
+            inside(p, body)
+        return carry
+
+    lax.fori_loop(0, Z, z_ends, 0)
+    for p in every:
+        if shares[p].part != 1:
+            inside(p, lambda p=p: f_copy(p, 0).wait_send())
+        o_copy(p).wait_send()
+        o_arrived(p).wait_recv()
+        o_keep(p).wait()
+
+
+def reduce_gradients(topo, grads):
+    shares = cut_shares([v.shape for v in grads])
+    X, Z, T = topo.X, topo.Z, topo.T
+    n = len(shares)
+    folds = max(1, topo.bits["y"])
+    DMA = pltpu.SemaphoreType.DMA
+    hbm = pl.BlockSpec(memory_space=pl.ANY)
+    lead = [(T,), (T,), (T,), (Z, X - 1), (Z,), (Z,), (folds,)]
+    rooms = [
+        pltpu.VMEM(front + s.shape, BF)
+        for front in lead for s in shares
+    ]
+    outs = [grads[0].shape[1:], grads[1].shape[1:], (2,) + grads[2].shape[2:], grads[3].shape[1:]]
+    return pl.pallas_call(
+        functools.partial(reduce_kernel, topo, shares),
+        in_specs=[hbm] * 4,
+        out_specs=[hbm] * 4,
+        out_shape=[jax.ShapeDtypeStruct(s, BF) for s in outs],
+        scratch_shapes=rooms + [
+            DMA((n, T)), DMA((n, T)), DMA((n, T)), DMA((n, T)), DMA((n, T)),
+            DMA((n, Z, X - 1)), DMA((n, Z, X - 1)), DMA((n, Z, 2)), DMA((n, Z, 2)),
+            DMA((n, folds)), DMA((n, folds)), DMA((n,)), DMA((n,)), DMA((n,)),
+        ],
+        compiler_params=pltpu.CompilerParams(
+            collective_id=1, has_side_effects=True, vmem_limit_bytes=60 << 20
+        ),
+        name="reduce_gradients",
+    )(*grads)
 
 
 def group_order(topo):
@@ -583,7 +874,7 @@
     ff = w_gate.shape[1]
     shard = w_query.shape[0]
     deep_rows = rows * 3 // 4
-    zk, xk, yk, ck = (topo.keys(d) for d in "zxyc")
+    xk, yk, ck = (topo.keys(d) for d in "xyc")
 
     small = jnp.concatenate([router, norm_attn[:, None], norm_ffn[:, None]], axis=1)
     small = jnp.pad(small, ((0, 0), (0, HD - small.shape[1])))
@@ -703,7 +994,10 @@
         dq = dq.reshape(n, HEADS * HD).astype(BF)
         d_n1 = mm_nt(dq, weight_q) + mm_nt(dkv, weight_kv)
         d_state, d_gain_one = norm_back(d_n1, state, inv_one, gain_one)
-        left = (n1, dq, dkv, mixed, d_att, n2, d_gated, d_up, hidden, d_fed)
+        blank = jnp.zeros((n, HD), BF)
+        dqkv = jnp.concatenate([dq, blank, dkv], axis=1)
+        dqkv = jnp.pad(dqkv, ((0, 0), (0, -dqkv.shape[1] % 256)))
+        left = (n1, dqkv, mixed, d_att, n2, d_gated, d_up, hidden, d_fed)
         return (gradient + d_state, left, (d_router, d_gain_one, d_gain_two))
 
     whole_state, kept = forward(state, 0)
@@ -727,31 +1021,32 @@
     smalls.append(tiny)
     gradient = lax.ppermute(gradient.astype(BF), AXES, swap)
 
-    n1, dq, dkv, mixed, d_att, n2, d_gated, d_up, hidden, d_fed = (
+    n1, dqkv, mixed, d_att, n2, d_gated, d_up, hidden, d_fed = (
         jnp.concatenate(parts, axis=0) for parts in zip(*lefts)
     )
-    spread = topo.T
-    ring_a = ck + xk + yk + zk
-    ring_b = ck + yk + xk + zk
-    cut = lambda g: g.reshape(spread, -1, g.shape[-1])
-    grad_down = scatter_rows(topo, cut(mm_tn(hidden, d_fed)), 0, ring_a).astype(F32)
-    grad_gate = scatter_rows(topo, cut(mm_tn(n2, d_gated)), 1, ring_b).astype(F32)
-    grad_up = scatter_rows(topo, cut(mm_tn(n2, d_up)), 1, ring_b).astype(F32)
+    cut = lambda v: v.astype(BF).reshape(topo.T, -1, v.shape[-1])
     tiny = jnp.stack(
         [smalls[2][0], smalls[1][0], smalls[0][0],
          smalls[0][1] + smalls[1][1] + smalls[2][1],
          smalls[0][2] + smalls[1][2] + smalls[2][2]], axis=1
     )
-    tiny = jnp.pad(tiny, ((0, 0), (0, HD - tiny.shape[1])))
-    last = jnp.concatenate([mm_tn(n1, dq), tiny, mm_tn(n1, dkv), mm_tn(mixed, d_att)], axis=1)
-    last = jnp.pad(last, ((0, 0), (0, -last.shape[1] % (128 * topo.G))))
-    last = scatter_rows(topo, cut(last), 1, ring_a).astype(F32)
-    grad_query = last[:, :model]
-    tiny = last[:, model:model + HD]
-    pair = last[:, model + HD:model + HD + 2 * kv_cols].reshape(shard, KV_HEADS, 2, HD)
+    wide_out = -(-(model + tiny.shape[1]) // 256) * 256
+    tiny = jnp.pad(tiny, ((0, 0), (0, wide_out - model - tiny.shape[1])))
+    grad_qkv, grad_o, grad_gu, grad_down = reduce_gradients(topo, [
+        cut(mm_tn(n1, dqkv)),
+        cut(jnp.concatenate([mm_tn(mixed, d_att), tiny], axis=1)),
+        jnp.stack([cut(mm_tn(n2, d_gated)), cut(mm_tn(n2, d_up))]),
+        cut(mm_tn(hidden, d_fed)),
+    ])
+    grad_query = grad_qkv[:, :model].astype(F32)
+    pair = grad_qkv[:, model + HD:model + HD + 2 * kv_cols].astype(F32)
+    pair = pair.reshape(shard, KV_HEADS, 2, HD)
     grad_key = pair[:, :, 0].reshape(shard, kv_cols)
     grad_value = pair[:, :, 1].reshape(shard, kv_cols)
-    grad_out = last[:, model + HD + 2 * kv_cols:2 * model + HD + 2 * kv_cols]
+    grad_out = grad_o[:, :model].astype(F32)
+    tiny = grad_o[:, model:].astype(F32)
+    grad_gate, grad_up = grad_gu[0].astype(F32), grad_gu[1].astype(F32)
+    grad_down = grad_down.astype(F32)
 
     def unsort(v):
         return mm_tn(onehot, v).astype(BF)

time: 923 us -> 856 us (0.927)
  Pallas kernels: 171 us -> 298 us
  starting transfers between devices: 149 us -> 74.5 us
  waiting for transfers between devices: 172 us -> 104 us
  other arithmetic: 121 us -> 92.1 us
  local copies, waits for them, and re-layouts: 162 us -> 146 us
    pallas_call x0 -> x1, Pallas kernels: none -> 126 us  [reduce_gradients(): pl.pallas_call(functools.partial(reduce_kernel, topo, shares), in_specs=[...]
    ppermute x49 -> x21, waiting for transfers between devices: 162 us -> 70.1 us  [exchange(): return lax.ppermute(arr, AXES, topo.pairs(key))]
    ppermute x49 -> x21, starting transfers between devices: 137 us -> 46.9 us  [exchange(): return lax.ppermute(arr, AXES, topo.pairs(key))]
    convert_element_type x29 -> x9, other arithmetic: 40.6 us -> 10.2 us  [halve(): return (keep + exchange(topo, send, key).astype(F32)).astype(BF)]
    ppermute x1, waiting for transfers between devices: 0.01 us -> 20.1 us  [per_device(): gradient = lax.ppermute(gradient.astype(BF), AXES, swap)]
    ppermute x1, starting transfers between devices: 1.91 us -> 16.9 us  [per_device(): final = lax.ppermute(final, AXES, swap)]
    concatenate x1, local copies, waits for them, and re-layouts: 10.8 us -> 0.67 us  [backward(): dqkv = jnp.concatenate([dq, blank, dkv], axis=1)]
    slice x5 -> x1, local copies, waits for them, and re-layouts: 10.3 us -> 0.7 us  [per_device(): tiny[:, RECS + 1]]
  transfers between devices with their start and end apart: 54 -> 26, of which waited for: 24 -> 14; matrix products, arithmetic and copies ran while one was open for 20% -> 14% of each run, Pallas kernels for 11% -> 11%
where the time goes in v3:
time: 856 us; the launch traced here: 847 us
  Pallas kernels  298 us (35%)
  local copies, waits for them, and re-layouts  146 us (17%)
  matrix products  125 us (15%)
  waiting for transfers between devices  104 us (12%)
  other arithmetic  92.1 us (11%)
  starting transfers between devices  74.5 us (9%)
    pallas_call x1, Pallas kernels, reduce_gradients(): pl.pallas_call(functools.partial(reduce_kernel, topo, shares), in_specs=[...  126 us
    pallas_call x1, Pallas kernels, gather_weights(): pl.pallas_call(functools.partial(gather_kernel, topo, pieces), in_specs=[...  95.8 us
    ppermute x21, waiting for transfers between devices, exchange(): return lax.ppermute(arr, AXES, topo.pairs(key))  70.1 us
    dot_general x21, matrix products, mm(): return jnp.dot(a, b, preferred_element_type=F32)  53.5 us
    ppermute x21, starting transfers between devices, exchange(): return lax.ppermute(arr, AXES, topo.pairs(key))  46.9 us
    dot_general x18, matrix products, mm_nt(): return lax.dot_general(a, b, NT, preferred_element_type=F32)  42.8 us
    pallas_call x3, Pallas kernels, attend_back(): pl.pallas_call(functools.partial(attend_back_kernel, rows), grid_spec=plt...  40.4 us
    pallas_call x3, Pallas kernels, attend(): pl.pallas_call(functools.partial(attend_kernel, rows), grid_spec=pltpu.Pr...  35.1 us
  transfers between devices with their start and end apart: 26, of which 14 were waited for; matrix products, arithmetic and copies ran while one was open for 14% of the time, Pallas kernels for 11%

profile of v3, /device:TPU:17, one launch (start us, length us, event | category | flops | bytes accessed | tf_op | source)
XLA Modules:
  0.0 847.2 jit_solution(11235962807565183661)
XLA Ops:
  15.6 95.8 %gather_weights.1 = (bf16[8,120,2624]{2,1,0:T(8,128)(2,1)}, bf16[8,120,2560]{2,1,0:T(8,128)(2,1)}, bf16[8,120,2560]{2,1,0:T(8,128)(2,1)}, bf16[8,320,960]{2,1,0:T(8,128)(2,1)}) custom-call(bf16[120,2624]{1,0:T(8,128)(2,1)} %concatenate.128.refs_0_, bf16[120,2560]{1,0:T(8,128)(2,1)} %refs_1_.1, bf16[120,2560]{1,0:T(8,128)(2,1)} %refs_2_.1, ...), custom_call_target="tpu_custom_call" | custom-call | tf_op jit(solution)/shard_map/gather_weights/pallas_call | solution.py:299
  125.0 7.6 collective-permute-done.5
  135.2 12.3 %collective-permute-done.6 = bf16[2,256,640]{1,2,0:T(8,128)(2,1)S(1)} collective-permute-done((bf16[2,256,640]{1,2,0:T(8,128)(2,1)S(1)}, bf16[2,256,640]{1,2,0:T(8,128)(2,1)S(1)}, u32[]{:S(2)}, u32[]{:S(2)}) %collective-permute-start.6) | collective-permute-done | bytes 655392 | tf_op jit(solution)/shard_map/ppermute | solution.py:73
  162.0 12.7 %attend.3 = (f32[5,128,768]{2,1,0:T(8,128)}, f32[5,8,768]{2,1,0:T(8,128)}) custom-call(s32[2]{0:T(128)} %pad_add_fusion.9.span, s32[2048,8]{1,0:T(8,128)} %pad.49.key_ref, s32[8,768]{1,0:T(8,128)} %pad.50.query_ref, bf16[2048,640]{1,0:T(8,128)(2,1)} %bitcast.431, bf16[5,768,128]{2,1,0:T(8,128)(2,1)} %bitcast.467), custom_call_target="tpu_custom_call" | custom-call | flops 4026531840 | bytes 6553600 | tf_op jit(solution)/shard_map/attend/pallas_call | solution.py:722
  180.5 4.2 fusion.138
  198.3 4.5 collective-permute-done.8
  203.3 4.5 collective-permute-start.9
  240.8 11.2 %attend.4 = (f32[5,128,576]{2,1,0:T(8,128)}, f32[5,8,576]{2,1,0:T(8,128)}) custom-call(s32[2]{0:T(128)} %pad_add_fusion.9.span, s32[1536,8]{1,0:T(8,128)} %pad.51.key_ref, s32[8,576]{1,0:T(8,128)} %pad.52.query_ref, bf16[1536,640]{1,0:T(8,128)(2,1)} %bitcast.438, bf16[5,576,128]{2,1,0:T(8,128)(2,1)} %bitcast.474), custom_call_target="tpu_custom_call" | custom-call | flops 2264924160 | bytes 4915200 | tf_op jit(solution)/shard_map/attend/pallas_call | solution.py:722
  273.7 4.4 collective-permute-start.11
  289.5 13.5 %collective-permute-done.15 = bf16[256,960]{0,1:T(8,128)(2,1)S(1)} collective-permute-done((bf16[256,960]{0,1:T(8,128)(2,1)}, bf16[256,960]{0,1:T(8,128)(2,1)S(1)}, u32[]{:S(2)}, u32[]{:S(2)}) %collective-permute-start.15) | collective-permute-done | bytes 491552 | tf_op jit(solution)/shard_map/ppermute | solution.py:908
  324.3 4.2 copy.553
  328.6 11.2 %attend.5 = (f32[5,128,576]{2,1,0:T(8,128)}, f32[5,8,576]{2,1,0:T(8,128)}) custom-call(s32[2]{0:T(128)} %pad_add_fusion.9.span, s32[1536,8]{1,0:T(8,128)} %pad.53.key_ref, s32[8,576]{1,0:T(8,128)} %pad.52.query_ref, bf16[1536,640]{1,0:T(8,128)(2,1)} %bitcast.441, bf16[5,576,128]{2,1,0:T(8,128)(2,1)} %bitcast.473), custom_call_target="tpu_custom_call" | custom-call | flops 2264924160 | bytes 4915200 | tf_op jit(solution)/shard_map/attend/pallas_call | solution.py:722
  372.7 12.6 %attend_back.3 = (f32[5,128,576]{2,1,0:T(8,128)}, bf16[1536,640]{1,0:T(8,128)(2,1)}) custom-call(s32[2]{0:T(128)} %pad_add_fusion.9.span, s32[1536,8]{1,0:T(8,128)} %pad.53.key_ref, s32[8,576]{1,0:T(8,128)} %pad.52.query_ref, bf16[1536,640]{1,0:T(8,128)(2,1)} %bitcast.442, bf16[5,576,128]{2,1,0:T(8,128)(2,1)} %bitcast.476, ...), custom_call_target="tpu_custom_call" | custom-call | flops 5662310400 | bytes 6881280 | tf_op jit(solution)/shard_map/attend_back/pallas_call | solution.py:791
  407.4 5.1 collective-permute-start.17
  418.9 5.4 collective-permute-done.17
  427.8 6.7 collective-permute-start.18
  437.0 4.9 collective-permute-done.18
  462.5 12.7 %attend_back.4 = (f32[5,128,576]{2,1,0:T(8,128)}, bf16[1536,640]{1,0:T(8,128)(2,1)}) custom-call(s32[2]{0:T(128)} %pad_add_fusion.9.span, s32[1536,8]{1,0:T(8,128)} %pad.51.key_ref, s32[8,576]{1,0:T(8,128)} %pad.52.query_ref, bf16[1536,640]{1,0:T(8,128)(2,1)} %bitcast.439, bf16[5,576,128]{2,1,0:T(8,128)(2,1)} %bitcast.475, ...), custom_call_target="tpu_custom_call" | custom-call | flops 5662310400 | bytes 6881280 | tf_op jit(solution)/shard_map/attend_back/pallas_call | solution.py:791
  498.7 16.9 %collective-permute-start.14 = (bf16[256,960]{0,1:T(8,128)(2,1)}, bf16[256,960]{0,1:T(8,128)(2,1)}, u32[]{:S(2)}, u32[]{:S(2)}) collective-permute-start(bf16[256,960]{0,1:T(8,128)(2,1)} %pad_maximum_fusion.19), channel_id=1, source_target_pairs={{0,0},{1,1},{2,8},{3,9},{4,16},{5,17},{6,24},{7,25},{8,2},{9,3},{1... | collective-permute-start | bytes 1474568 | tf_op jit(solution)/shard_map/ppermute | solution.py:1010
  526.4 15.8 %collective-permute-done.20 = bf16[2,192,640]{2,1,0:T(8,128)(2,1)} collective-permute-done((bf16[2,192,640]{2,1,0:T(8,128)(2,1)}, bf16[2,192,640]{2,1,0:T(8,128)(2,1)}, u32[]{:S(2)}, u32[]{:S(2)}) %collective-permute-start.20) | collective-permute-done | bytes 491552 | tf_op jit(solution)/shard_map/ppermute | solution.py:73
  552.0 5.6 collective-permute-done.21
  563.8 5.8 convolution_convert_fusion
  572.5 6.0 convolution_convert_fusion.2
  589.4 15.0 %attend_back.5 = (f32[5,128,768]{2,1,0:T(8,128)}, bf16[2048,640]{1,0:T(8,128)(2,1)}) custom-call(s32[2]{0:T(128)} %pad_add_fusion.9.span, s32[2048,8]{1,0:T(8,128)} %pad.49.key_ref, s32[8,768]{1,0:T(8,128)} %pad.50.query_ref, bf16[2048,640]{1,0:T(8,128)(2,1)} %bitcast.432, bf16[5,768,128]{2,1,0:T(8,128)(2,1)} %bitcast.468, ...), custom_call_target="tpu_custom_call" | custom-call | flops 10066329600 | bytes 9175040 | tf_op jit(solution)/shard_map/attend_back/pallas_call | solution.py:791
  625.6 6.0 convolution_convert_fusion.1
  638.5 8.6 %pad_maximum_fusion.refs_2_ = bf16[2,8,120,2560]{3,2,1,0:T(8,128)(2,1)} fusion(bf16[1,8,120,2560]{3,2,1,0:T(8,128)(2,1)} %bitcast.402, bf16[1,8,120,2560]{3,2,1,0:T(8,128)(2,1)} %bitcast.401), kind=kLoop, calls=%fused_computation | loop fusion | flops 4915200 | bytes 19660800 | tf_op jit(solution)/shard_map/stack | solution.py:1038
  647.1 6.3 collective-permute-done.23
  655.6 4.8 collective-permute-start.24
  660.5 7.9 copy.600
  678.2 4.8 convolution_convert_fusion.3
  683.0 126.3 %reduce_gradients.1 = (bf16[120,1792]{1,0:T(8,128)(2,1)}, bf16[120,1024]{1,0:T(8,128)(2,1)}, bf16[2,120,2560]{2,1,0:T(8,128)(2,1)}, bf16[320,960]{1,0:T(8,128)(2,1)}) custom-call(bf16[8,120,1792]{2,1,0:T(8,128)(2,1)} %bitcast.411, bf16[8,120,1024]{2,1,0:T(8,128)(2,1)} %pad_maximum_fusion.4.refs_1_, bf16[2,8,120,2560]{3,2,1,0:T(8,128)(2,1)} %pad_maximum_fusion.refs_2_, ...), custom_call_target="tpu_custom_call" | custom-call | tf_op jit(solution)/shard_map/reduce_gradients/pallas_call | solution.py:624
  825.5 20.1 %collective-permute-done.25 = bf16[256,960]{0,1:T(8,128)(2,1)S(1)} collective-permute-done((bf16[256,960]{0,1:T(8,128)(2,1)S(1)}, bf16[256,960]{0,1:T(8,128)(2,1)S(1)}, u32[]{:S(2)}, u32[]{:S(2)}) %collective-permute-start.25) | collective-permute-done | bytes 491552 | tf_op jit(solution)/shard_map/ppermute | solution.py:1022
  (850 shorter events, 355.8 us)
Async XLA Ops:
  3.3 117.4 %collective-permute-start = (bf16[256,960]{0,1:T(8,128)(2,1)S(1)}, bf16[256,960]{0,1:T(8,128)(2,1)S(1)}, u32[]{:S(2)}, u32[]{:S(2)}) collective-permute-start(bf16[256,960]{0,1:T(8,128)(2,1)S(1)} %convolution_convert_fusion.9), channel_id=1, source_target_pairs={{0,0},{1,1},{2,8},{3,9},{4,16},{5,17},{6,24},{7,25},{8,2},{9,3},{1... | collective-permute-start | bytes 1474568 | tf_op jit(solution)/shard_map/ppermute | solution.py:906
  9.4 103.9 %collective-permute-start.1 = (s32[8,256]{1,0:T(8,128)S(1)}, s32[8,256]{1,0:T(8,128)S(1)}, u32[]{:S(2)}, u32[]{:S(2)}) collective-permute-start(s32[8,256]{1,0:T(8,128)S(1)} %pad.47), channel_id=1, source_target_pairs={{0,0},{1,1},{2,8},{3,9},{4,16},{5,17},{6,24},{7,25},{8,2},{9,3},{1... | collective-permute-start | bytes 24584 | tf_op jit(solution)/shard_map/ppermute | solution.py:907
  113.3 67.0 %copy-start.114 = (f32[960,1]{0,1:T(1,128)}, f32[960,1]{0,1:T(1,128)S(1)}, u32[]{:S(2)}) copy-start(f32[960,1]{0,1:T(1,128)S(1)} %get-tuple-element.247) | copy-start | bytes 11524
  113.3 79.1 %copy-start.125 = (f32[960,1]{0,1:T(1,128)}, f32[960,1]{0,1:T(1,128)S(1)}, u32[]{:S(2)}) copy-start(f32[960,1]{0,1:T(1,128)S(1)} %get-tuple-element.249) | copy-start | bytes 11524
  114.8 79.9 %copy-start.86 = (f32[192,32]{0,1:T(8,128)}, f32[192,32]{0,1:T(8,128)S(1)}, u32[]{:S(2)}) copy-start(f32[192,32]{0,1:T(8,128)S(1)} %get-tuple-element.254) | copy-start | bytes 73732
  114.8 5.7 collective-permute-start.2
  120.5 3.5 collective-permute-start.3
  120.6 67.7 %copy-start.2 = (bf16[256,960]{0,1:T(8,128)(2,1)}, bf16[256,960]{0,1:T(8,128)(2,1)S(1)}, u32[]{:S(2)}) copy-start(bf16[256,960]{0,1:T(8,128)(2,1)S(1)} %collective-permute-done) | copy-start | bytes 1474564
  123.9 8.7 %collective-permute-start.5 = (bf16[256,640]{0,1:T(8,128)(2,1)S(1)}, bf16[256,640]{0,1:T(8,128)(2,1)S(1)}, u32[]{:S(2)}, u32[]{:S(2)}) collective-permute-start(bf16[256,640]{0,1:T(8,128)(2,1)S(1)} %bitcast.463), channel_id=1, source_target_pairs={{0,1},{1,0},{2,3},{3,2},{4,5},{5,4},{6,7},{7,6},{8,9},{9,8},{10,11... | collective-permute-start | bytes 983048 | tf_op jit(solution)/shard_map/ppermute | solution.py:73
  124.1 11.1 %collective-permute-start.4 = (s32[2,2,8,256]{3,2,1,0:T(8,128)S(1)}, s32[2,2,8,256]{3,2,1,0:T(8,128)S(1)}, u32[]{:S(2)}, u32[]{:S(2)}) collective-permute-start(s32[2,2,8,256]{3,2,1,0:T(8,128)S(1)} %pad_add_fusion.1), channel_id=1, source_target_pairs={{0,8},{1,9},{2,10},{3,11},{4,12},{5,13},{6,14},{7,15},{8,0},{9,1},... | collective-permute-start | bytes 98312 | tf_op jit(solution)/shard_map/ppermute | solution.py:73
  132.8 14.8 %collective-permute-start.6 = (bf16[2,256,640]{1,2,0:T(8,128)(2,1)S(1)}, bf16[2,256,640]{1,2,0:T(8,128)(2,1)S(1)}, u32[]{:S(2)}, u32[]{:S(2)}) collective-permute-start(bf16[2,256,640]{1,2,0:T(8,128)(2,1)S(1)} %pad_maximum_fusion.16), channel_id=1, source_target_pairs={{0,16},{1,17},{2,18},{3,19},{4,20},{5,21},{6,22},{7,23},{8,24},{9,... | collective-permute-start | bytes 1966088 | tf_op jit(solution)/shard_map/ppermute | solution.py:73
  148.8 8.5 %collective-permute-start.7 = (bf16[2,2,256,640]{2,3,1,0:T(8,128)(2,1)}, bf16[2,2,256,640]{2,3,1,0:T(8,128)(2,1)}, u32[]{:S(2)}, u32[]{:S(2)}) collective-permute-start(bf16[2,2,256,640]{2,3,1,0:T(8,128)(2,1)} %pad_maximum_fusion.5), channel_id=1, source_target_pairs={{0,8},{1,9},{2,10},{3,11},{4,12},{5,13},{6,14},{7,15},{8,0},{9,1},... | collective-permute-start | bytes 3932168 | tf_op jit(solution)/shard_map/ppermute | solution.py:73
  194.9 7.9 collective-permute-start.8
  203.3 10.7 %collective-permute-start.9 = (bf16[2,192,640]{2,1,0:T(8,128)(2,1)S(1)}, bf16[2,192,640]{2,1,0:T(8,128)(2,1)S(1)}, u32[]{:S(2)}, u32[]{:S(2)}) collective-permute-start(bf16[2,192,640]{2,1,0:T(8,128)(2,1)S(1)} %copy.529), channel_id=1, source_target_pairs={{0,16},{1,17},{2,18},{3,19},{4,20},{5,21},{6,22},{7,23},{8,24},{9,... | collective-permute-start | bytes 1474568 | tf_op jit(solution)/shard_map/ppermute | solution.py:73
  220.5 10.1 %collective-permute-start.10 = (bf16[2,2,192,640]{3,2,1,0:T(8,128)(2,1)}, bf16[2,2,192,640]{3,2,1,0:T(8,128)(2,1)}, u32[]{:S(2)}, u32[]{:S(2)}) collective-permute-start(bf16[2,2,192,640]{3,2,1,0:T(8,128)(2,1)} %copy.532), channel_id=1, source_target_pairs={{0,8},{1,9},{2,10},{3,11},{4,12},{5,13},{6,14},{7,15},{8,0},{9,1},... | collective-permute-start | bytes 2949128 | tf_op jit(solution)/shard_map/ppermute | solution.py:73
  270.8 47.5 %copy-start.184 = (f32[192]{0:T(256)}, f32[192]{0:T(256)S(1)}, u32[]{:S(2)}) copy-start(f32[192]{0:T(256)S(1)} %get-tuple-element.150) | copy-start | bytes 2308
  273.7 9.2 %collective-permute-start.11 = (bf16[192,640]{0,1:T(8,128)(2,1)S(1)}, bf16[192,640]{0,1:T(8,128)(2,1)S(1)}, u32[]{:S(2)}, u32[]{:S(2)}) collective-permute-start(bf16[192,640]{0,1:T(8,128)(2,1)S(1)} %bitcast.464), channel_id=1, source_target_pairs={{0,1},{1,0},{2,3},{3,2},{4,5},{5,4},{6,7},{7,6},{8,9},{9,8},{10,11... | collective-permute-start | bytes 737288 | tf_op jit(solution)/shard_map/ppermute | solution.py:73
  279.3 23.8 %collective-permute-start.15 = (bf16[256,960]{0,1:T(8,128)(2,1)}, bf16[256,960]{0,1:T(8,128)(2,1)S(1)}, u32[]{:S(2)}, u32[]{:S(2)}) collective-permute-start(bf16[256,960]{0,1:T(8,128)(2,1)} %convolution_convert_fusion.7), channel_id=1, source_target_pairs={{0,0},{1,1},{2,8},{3,9},{4,16},{5,17},{6,24},{7,25},{8,2},{9,3},{1... | collective-permute-start | bytes 1474568 | tf_op jit(solution)/shard_map/ppermute | solution.py:908
  284.1 19.8 %collective-permute-start.12 = (bf16[2,192,640]{2,1,0:T(8,128)(2,1)}, bf16[2,192,640]{2,1,0:T(8,128)(2,1)}, u32[]{:S(2)}, u32[]{:S(2)}) collective-permute-start(bf16[2,192,640]{2,1,0:T(8,128)(2,1)} %copy.547), channel_id=1, source_target_pairs={{0,16},{1,17},{2,18},{3,19},{4,20},{5,21},{6,22},{7,23},{8,24},{9,... | collective-permute-start | bytes 1474568 | tf_op jit(solution)/shard_map/ppermute | solution.py:73
  312.1 7.0 collective-permute-start.13
  397.9 2.8 collective-permute-start.16
  407.4 16.9 %collective-permute-start.17 = (bf16[2,192,640]{2,1,0:T(8,128)(2,1)}, bf16[2,192,640]{2,1,0:T(8,128)(2,1)}, u32[]{:S(2)}, u32[]{:S(2)}) collective-permute-start(bf16[2,192,640]{2,1,0:T(8,128)(2,1)} %copy.569), channel_id=1, source_target_pairs={{0,16},{1,17},{2,18},{3,19},{4,20},{5,21},{6,22},{7,23},{8,24},{9,... | collective-permute-start | bytes 1474568 | tf_op jit(solution)/shard_map/ppermute | solution.py:73
  427.8 14.1 %collective-permute-start.18 = (bf16[192,640]{0,1:T(8,128)(2,1)S(1)}, bf16[192,640]{0,1:T(8,128)(2,1)S(1)}, u32[]{:S(2)}, u32[]{:S(2)}) collective-permute-start(bf16[192,640]{0,1:T(8,128)(2,1)S(1)} %select_bitcast_fusion.20), channel_id=1, source_target_pairs={{0,1},{1,0},{2,3},{3,2},{4,5},{5,4},{6,7},{7,6},{8,9},{9,8},{10,11... | collective-permute-start | bytes 737288 | tf_op jit(solution)/shard_map/ppermute | solution.py:73
  487.0 29.6 %collective-permute-start.19 = (bf16[2,2,192,640]{3,2,1,0:T(8,128)(2,1)}, bf16[2,2,192,640]{3,2,1,0:T(8,128)(2,1)}, u32[]{:S(2)}, u32[]{:S(2)}) collective-permute-start(bf16[2,2,192,640]{3,2,1,0:T(8,128)(2,1)} %copy.583), channel_id=1, source_target_pairs={{0,8},{1,9},{2,10},{3,11},{4,12},{5,13},{6,14},{7,15},{8,0},{9,1},... | collective-permute-start | bytes 2949128 | tf_op jit(solution)/shard_map/ppermute | solution.py:73
  488.8 72.8 %copy-start.28 = (f32[64,960]{0,1:T(8,128)}, f32[64,960]{0,1:T(8,128)S(1)}, u32[]{:S(2)}) copy-start(f32[64,960]{0,1:T(8,128)S(1)} %slice.492) | copy-start | bytes 737284
  498.7 51.1 %collective-permute-start.14 = (bf16[256,960]{0,1:T(8,128)(2,1)}, bf16[256,960]{0,1:T(8,128)(2,1)}, u32[]{:S(2)}, u32[]{:S(2)}) collective-permute-start(bf16[256,960]{0,1:T(8,128)(2,1)} %pad_maximum_fusion.19), channel_id=1, source_target_pairs={{0,0},{1,1},{2,8},{3,9},{4,16},{5,17},{6,24},{7,25},{8,2},{9,3},{1... | collective-permute-start | bytes 1474568 | tf_op jit(solution)/shard_map/ppermute | solution.py:1010
  522.9 19.2 %collective-permute-start.20 = (bf16[2,192,640]{2,1,0:T(8,128)(2,1)}, bf16[2,192,640]{2,1,0:T(8,128)(2,1)}, u32[]{:S(2)}, u32[]{:S(2)}) collective-permute-start(bf16[2,192,640]{2,1,0:T(8,128)(2,1)} %copy.585), channel_id=1, source_target_pairs={{0,16},{1,17},{2,18},{3,19},{4,20},{5,21},{6,22},{7,23},{8,24},{9,... | collective-permute-start | bytes 1474568 | tf_op jit(solution)/shard_map/ppermute | solution.py:73
  545.6 11.9 %collective-permute-start.21 = (bf16[192,640]{0,1:T(8,128)(2,1)S(1)}, bf16[192,640]{0,1:T(8,128)(2,1)S(1)}, u32[]{:S(2)}, u32[]{:S(2)}) collective-permute-start(bf16[192,640]{0,1:T(8,128)(2,1)S(1)} %select_bitcast_fusion.19), channel_id=1, source_target_pairs={{0,1},{1,0},{2,3},{3,2},{4,5},{5,4},{6,7},{7,6},{8,9},{9,8},{10,11... | collective-permute-start | bytes 737288 | tf_op jit(solution)/shard_map/ppermute | solution.py:73
  614.6 17.0 %collective-permute-start.22 = (bf16[2,2,256,640]{2,3,1,0:T(8,128)(2,1)}, bf16[2,2,256,640]{2,3,1,0:T(8,128)(2,1)}, u32[]{:S(2)}, u32[]{:S(2)}) collective-permute-start(bf16[2,2,256,640]{2,3,1,0:T(8,128)(2,1)} %select_bitcast_fusion), channel_id=1, source_target_pairs={{0,8},{1,9},{2,10},{3,11},{4,12},{5,13},{6,14},{7,15},{8,0},{9,1},... | collective-permute-start | bytes 3932168 | tf_op jit(solution)/shard_map/ppermute | solution.py:73
  635.5 17.9 %collective-permute-start.23 = (bf16[2,256,640]{1,2,0:T(8,128)(2,1)}, bf16[2,256,640]{1,2,0:T(8,128)(2,1)}, u32[]{:S(2)}, u32[]{:S(2)}) collective-permute-start(bf16[2,256,640]{1,2,0:T(8,128)(2,1)} %select_bitcast_fusion.9), channel_id=1, source_target_pairs={{0,16},{1,17},{2,18},{3,19},{4,20},{5,21},{6,22},{7,23},{8,24},{9,... | collective-permute-start | bytes 1966088 | tf_op jit(solution)/shard_map/ppermute | solution.py:73
  655.6 15.1 %collective-permute-start.24 = (bf16[256,640]{0,1:T(8,128)(2,1)S(1)}, bf16[256,640]{0,1:T(8,128)(2,1)S(1)}, u32[]{:S(2)}, u32[]{:S(2)}) collective-permute-start(bf16[256,640]{0,1:T(8,128)(2,1)S(1)} %select_bitcast_fusion.18), channel_id=1, source_target_pairs={{0,1},{1,0},{2,3},{3,2},{4,5},{5,4},{6,7},{7,6},{8,9},{9,8},{10,11... | collective-permute-start | bytes 983048 | tf_op jit(solution)/shard_map/ppermute | solution.py:73
  819.2 26.4 %collective-permute-start.25 = (bf16[256,960]{0,1:T(8,128)(2,1)S(1)}, bf16[256,960]{0,1:T(8,128)(2,1)S(1)}, u32[]{:S(2)}, u32[]{:S(2)}) collective-permute-start(bf16[256,960]{0,1:T(8,128)(2,1)S(1)} %fusion.63), channel_id=1, source_target_pairs={{0,0},{1,1},{2,8},{3,9},{4,16},{5,17},{6,24},{7,25},{8,2},{9,3},{1... | collective-permute-start | bytes 1474568 | tf_op jit(solution)/shard_map/ppermute | solution.py:1022
  (238 other events, 1137.0 us)

commit v4 on v3

--- a/solution.py
+++ b/solution.py
@@ -111,15 +111,14 @@
 def cut_pieces(shapes):
     near = lambda v, unit: max(unit, int(round(v / unit)) * unit)
     wide_a, wide_g, wide_u, tall = shapes[0][1], shapes[1][1], shapes[2][1], shapes[3][0]
-    a = near(wide_a * 0.634, 128)
     g = near(wide_g * 0.7, 128)
     u = near(wide_u * 0.65, 128)
     d = near(tall * 0.3, 8)
     return [
         Piece(1, 1, 0, g, 0, 0),
-        Piece(0, 1, a, wide_a - a, 0, 2),
+        Piece(4, 1, 0, shapes[4][1], 0, 2),
         Piece(1, 1, g, wide_g - g, 0, 2),
-        Piece(0, 1, 0, a, 0, 1),
+        Piece(0, 1, 0, wide_a, 0, 1),
         Piece(2, 1, u, wide_u - u, 1, 0),
         Piece(3, 0, 0, d, 1, 0),
         Piece(3, 0, d, tall - d, 1, 2),
@@ -133,8 +132,8 @@
 
 
 def gather_kernel(topo, pieces, *refs):
-    shards, outs = refs[:4], refs[4:8]
-    local_sem, recv_sem, z_sem, x_sem, y_sem, c_sem = refs[8:]
+    shards, outs = refs[:5], refs[5:10]
+    local_sem, recv_sem, z_sem, x_sem, y_sem, c_sem = refs[10:]
     x, y, z, c = coordinates(topo)
     X, Z, T = topo.X, topo.Z, topo.T
     g, me = lax.axis_index("grp"), lax.axis_index("tok")
@@ -162,7 +161,7 @@
     pl.when(below)(lambda: greet(-1))
     pl.when(above)(lambda: greet(1))
     own = [
-        pltpu.make_async_copy(shards[i], outs[i].at[me], local_sem.at[i]) for i in range(4)
+        pltpu.make_async_copy(shards[i], outs[i].at[me], local_sem.at[i]) for i in range(5)
     ]
     for copy in own:
         copy.start()
@@ -298,11 +297,11 @@
     hbm = pl.BlockSpec(memory_space=pl.ANY)
     outs = pl.pallas_call(
         functools.partial(gather_kernel, topo, pieces),
-        in_specs=[hbm] * 4,
-        out_specs=[hbm] * 4,
+        in_specs=[hbm] * 5,
+        out_specs=[hbm] * 5,
         out_shape=[jax.ShapeDtypeStruct((T,) + s.shape, s.dtype) for s in shards],
         scratch_shapes=[
-            DMA((4,)), DMA((len(pieces), T)), DMA((4, topo.Z, 2)), DMA((4, topo.Z, topo.X - 1)),
+            DMA((5,)), DMA((len(pieces), T)), DMA((4, topo.Z, 2)), DMA((4, topo.Z, topo.X - 1)),
             DMA((4, T)), DMA((4, T)),
         ],
         compiler_params=pltpu.CompilerParams(collective_id=0, has_side_effects=True),
@@ -663,6 +662,248 @@
     return arr
 
 
+def small_layer(topo):
+    return topo.X == 2 and topo.Y == 2
+
+
+class Layer:
+    def __init__(self, topo):
+        self.topo = topo
+        x, y, z, c = coordinates(topo)
+        self.c = c
+        far_x, far_y = 1 - x, 1 - y
+        a = (x + c * (far_x - x), far_y + c * (y - far_y))
+        b = (far_x + c * (x - far_x), y + c * (far_y - y))
+        self.chips = [(x, y), a, b, (far_x, far_y)]
+        self.z = z
+
+    def pack(self, slot, core):
+        x, y = self.chips[slot]
+        return (y * 2 + core) * self.topo.X + x
+
+    def device(self, slot, core):
+        x, y = self.chips[slot]
+        return {"grp": y * 2 + core, "tok": self.z * self.topo.X + x}
+
+    def meet(self):
+        barrier = pltpu.get_barrier_semaphore()
+        for target in (self.device(1, self.c), self.device(2, self.c), self.device(0, 1 - self.c)):
+            pl.semaphore_signal(
+                barrier, inc=1, device_id=target, device_id_type=pl.DeviceIdType.MESH
+            )
+        pl.semaphore_wait(barrier, 3)
+
+
+def remote_copy(source, landing, send, recv, target):
+    return pltpu.make_async_remote_copy(
+        src_ref=source, dst_ref=landing, send_sem=send, recv_sem=recv, device_id=target,
+        device_id_type=pl.DeviceIdType.MESH,
+    )
+
+
+def group_gather_kernel(topo, count, *refs):
+    mine, outs = refs[:count], refs[count:2 * count]
+    local_sem, send_sem, recv_sem = refs[2 * count:]
+    layer = Layer(topo)
+    c = layer.c
+    arrays = range(count)
+    a, b, sibling = layer.device(1, c), layer.device(2, c), layer.device(0, 1 - c)
+    own = layer.pack(0, c)
+
+    def send(i, way, pack, target):
+        landing = outs[i].at[pack]
+        source = mine[i] if way in (0, 1, 3) else landing
+        return remote_copy(source, landing, send_sem.at[i, way], recv_sem.at[i, pack], target)
+
+    ways = [
+        (0, own, a), (1, own, b), (2, layer.pack(1, c), b), (3, own, sibling),
+        (4, layer.pack(1, c), sibling), (5, layer.pack(2, c), sibling),
+        (6, layer.pack(3, c), sibling),
+    ]
+
+    def start(k):
+        for i in arrays:
+            send(i, *ways[k]).start()
+
+    def arrived(pack):
+        for i in arrays:
+            send(i, 2, pack, sibling).wait_recv()
+
+    keep = [pltpu.make_async_copy(mine[i], outs[i].at[own], local_sem.at[i]) for i in arrays]
+    for copy in keep:
+        copy.start()
+    layer.meet()
+    start(0)
+    start(1)
+    start(3)
+    arrived(layer.pack(1, c))
+    start(2)
+    start(4)
+    arrived(layer.pack(2, c))
+    start(5)
+    arrived(layer.pack(3, c))
+    start(6)
+    for slot in range(4):
+        arrived(layer.pack(slot, 1 - c))
+    for way in ways:
+        for i in arrays:
+            send(i, *way).wait_send()
+    for copy in keep:
+        copy.wait()
+
+
+def gather_layer(topo, arrays, ident):
+    DMA = pltpu.SemaphoreType.DMA
+    hbm = pl.BlockSpec(memory_space=pl.ANY)
+    n = len(arrays)
+    return pl.pallas_call(
+        functools.partial(group_gather_kernel, topo, n),
+        in_specs=[hbm] * n,
+        out_specs=[hbm] * n,
+        out_shape=[jax.ShapeDtypeStruct((topo.T,) + v.shape, v.dtype) for v in arrays],
+        scratch_shapes=[DMA((n,)), DMA((n, 7)), DMA((n, topo.T))],
+        compiler_params=pltpu.CompilerParams(collective_id=ident, has_side_effects=True),
+        name="gather_layer",
+    )(*arrays)
+
+
+def group_reduce_kernel(topo, grads, out, held, from_c, from_b, from_a, load_sem, c_send, c_recv,
+                        send_sem, recv_sem):
+    layer = Layer(topo)
+    c = layer.c
+    a, b, sibling = layer.device(1, c), layer.device(2, c), layer.device(0, 1 - c)
+    order = (3, 2, 1, 0)
+
+    def load(slot):
+        return pltpu.make_async_copy(
+            grads.at[layer.pack(slot, c)], held.at[slot], load_sem.at[slot]
+        )
+
+    def c_copy(slot):
+        theirs = (0, 2, 1, 3)[slot]
+        return remote_copy(
+            grads.at[layer.pack(slot, 1 - c)], from_c.at[theirs], c_send.at[theirs],
+            c_recv.at[theirs], sibling,
+        )
+
+    def c_arrived(slot):
+        remote_copy(
+            grads.at[layer.pack(slot, c)], from_c.at[slot], c_send.at[slot], c_recv.at[slot],
+            sibling,
+        ).wait_recv()
+
+    across = remote_copy(held.at[3], from_b.at[1], send_sem.at[0], recv_sem.at[0], b)
+    direct = remote_copy(held.at[2], from_b.at[0], send_sem.at[1], recv_sem.at[1], b)
+    passed = remote_copy(held.at[1], from_a, send_sem.at[2], recv_sem.at[2], a)
+
+    for slot in order:
+        load(slot).start()
+    layer.meet()
+    for slot in (3, 1, 2, 0):
+        c_copy(slot).start()
+    for slot in order:
+        load(slot).wait()
+        c_arrived(slot)
+        held[slot] = held[slot] + from_c[slot]
+        if slot == 3:
+            across.start()
+        if slot == 2:
+            direct.start()
+    across.wait_recv()
+    held[1] = held[1] + from_b[1]
+    passed.start()
+    direct.wait_recv()
+    held[0] = held[0] + from_b[0]
+    passed.wait_recv()
+    out[...] = held[0] + from_a[...]
+    across.wait_send()
+    direct.wait_send()
+    passed.wait_send()
+    for slot in range(4):
+        c_copy(slot).wait_send()
+
+
+def reduce_layer(topo, grads, ident):
+    DMA = pltpu.SemaphoreType.DMA
+    block = grads.shape[1:]
+    return pl.pallas_call(
+        functools.partial(group_reduce_kernel, topo),
+        in_specs=[pl.BlockSpec(memory_space=pl.ANY)],
+        out_specs=pl.BlockSpec(memory_space=pltpu.VMEM),
+        out_shape=jax.ShapeDtypeStruct(block, BF),
+        scratch_shapes=[
+            pltpu.VMEM((4,) + block, BF), pltpu.VMEM((4,) + block, BF),
+            pltpu.VMEM((2,) + block, BF), pltpu.VMEM(block, BF),
+            DMA((4,)), DMA((4,)), DMA((4,)), DMA((3,)), DMA((3,)),
+        ],
+        compiler_params=pltpu.CompilerParams(
+            collective_id=ident, has_side_effects=True, vmem_limit_bytes=32 << 20
+        ),
+        name="reduce_layer",
+    )(grads)
+
+
+NT = (((1,), (1,)), ((), ()))
+TN = (((0,), (0,)), ((), ()))
+LANES = 2 * HD
+CHUNKS = (HEADS + 1) // 2
+ROOM = 60 << 20
+
+
+def lanes_of(rows):
+    return lax.broadcasted_iota(jnp.int32, (rows, LANES), 1)
+
+
+def spin(v):
+    first = lax.rem(lanes_of(v.shape[0]), HD) < HD // 2
+    return jnp.where(first, -pltpu.roll(v, LANES - HD // 2, 1), pltpu.roll(v, HD // 2, 1))
+
+
+def whole(*shape):
+    return pl.BlockSpec(shape, lambda *i: (0,) * len(shape))
+
+
+def normed(v, gain):
+    return v * lax.rsqrt(jnp.mean(v * v, axis=-1, keepdims=True) + EPS) * gain
+
+
+def project_kernel(state_ref, gain_ref, w_ref, turn_ref, n1_ref, q_ref, kv_ref):
+    n1 = normed(state_ref[...], gain_ref[...]).astype(BF)
+    n1_ref[...] = n1
+    cosine, sine = turn_ref[0], turn_ref[1]
+    key = lanes_of(n1.shape[0]) < HD
+    columns = w_ref.shape[1]
+    for start in range(0, columns, 2 * LANES):
+        wide = min(2 * LANES, columns - start)
+        both = jnp.dot(n1, w_ref[:, start:start + wide], preferred_element_type=F32)
+        for half in range(wide // LANES):
+            j = start // LANES + half
+            v = both[:, half * LANES:(half + 1) * LANES]
+            turned = v * cosine + spin(v) * sine
+            if j < CHUNKS:
+                q_ref[j] = (turned * HD ** -0.5).astype(BF)
+            else:
+                j -= CHUNKS
+                kv_ref[:, j * LANES:(j + 1) * LANES] = jnp.where(key, turned, v).astype(BF)
+
+
+def project(state, gain, w, turns):
+    n, model = state.shape
+    return pl.pallas_call(
+        project_kernel,
+        grid=(1,),
+        in_specs=[whole(n, model), whole(1, model), whole(*w.shape), whole(*turns.shape)],
+        out_specs=[whole(n, model), whole(CHUNKS, n, LANES), whole(n, KV_HEADS * LANES)],
+        out_shape=[
+            jax.ShapeDtypeStruct((n, model), BF),
+            jax.ShapeDtypeStruct((CHUNKS, n, LANES), BF),
+            jax.ShapeDtypeStruct((n, KV_HEADS * LANES), BF),
+        ],
+        compiler_params=pltpu.CompilerParams(vmem_limit_bytes=ROOM),
+        name="project",
+    )(state, gain, w, turns)
+
+
 def fill_bias(bias, key_ref, query_ref, rows, first, last):
     def body(t, carry):
         at = pl.ds(pl.multiple_of(t * rows, rows), rows)
@@ -676,19 +917,23 @@
     lax.fori_loop(first, last, body, 0)
 
 
-NT = (((1,), (1,)), ((), ()))
-TN = (((0,), (0,)), ((), ()))
-
-
-def attend_kernel(rows, span, key_ref, query_ref, kv_ref, q_ref, out_ref, stat_ref, bias, held):
+def attend_kernel(rows, span, key_ref, query_ref, kv_ref, q_ref, mixed_ref, out_ref, stat_ref,
+                  bias, held, stacked, mixing, heads):
     first, last = span[0], span[1]
-
-    @pl.when(pl.program_id(0) == 0)
+    group = pl.program_id(0)
+
+    @pl.when(group == 0)
     def _():
         fill_bias(bias, key_ref, query_ref, rows, first, last)
 
-    wide = q_ref.shape[1]
-    queries = q_ref[0]
+    low = lanes_of(rows) < HD
+    for j in range(SHARES):
+        head = group * SHARES + j
+        chunk = q_ref[head // 2].astype(F32)
+        chunk = jnp.where(lax.rem(head, 2) == 1, pltpu.roll(chunk, HD, 1), chunk)
+        stacked[j * rows:(j + 1) * rows, :] = jnp.where(low, chunk, 0.0).astype(BF)
+    wide = stacked.shape[0]
+    queries = stacked[...]
 
     def scores(t, top):
         at = pl.ds(pl.multiple_of(t * rows, rows), rows)
@@ -698,73 +943,101 @@
 
     top = lax.fori_loop(first, last, scores, jnp.full((8, wide), BIG, F32))
     top = jnp.max(top, axis=0, keepdims=True)
-
-    out_ref[0] = jnp.zeros(out_ref.shape[1:], F32)
+    mixing[...] = jnp.zeros(mixing.shape, F32)
 
     def mix(t, total):
         at = pl.ds(pl.multiple_of(t * rows, rows), rows)
         p = jnp.exp(held[at, :] - top)
-        out_ref[0] += lax.dot_general(
+        mixing[...] += lax.dot_general(
             kv_ref[at, :], p.astype(BF), TN, preferred_element_type=F32
         )
         return total + jnp.sum(p.reshape(rows // 8, 8, wide), axis=0)
 
     total = lax.fori_loop(first, last, mix, jnp.zeros((8, wide), F32))
     total = jnp.sum(total, axis=0, keepdims=True)
-    out_ref[0] = out_ref[0] / total
     stat_ref[0] = jnp.broadcast_to(top + jnp.log(total), (8, wide))
-
-
-def attend(rows, span, key_labels, query_labels, kv_all, q_pad):
+    out = jnp.transpose(mixing[...] / total)
+    for j in range(SHARES):
+        heads[group * SHARES + j] = out[j * rows:(j + 1) * rows, :]
+
+    @pl.when(group == KV_HEADS - 1)
+    def _():
+        for j in range(CHUNKS):
+            even = pltpu.roll(heads[2 * j], HD, 1)
+            odd = heads[2 * j + 1] if 2 * j + 1 < HEADS else jnp.zeros((rows, LANES), F32)
+            both = jnp.where(low, even, odd)
+            out_ref[j] = both
+            size = min(LANES, HEADS * HD - j * LANES)
+            mixed_ref[:, j * LANES:j * LANES + size] = both.astype(BF)[:, :size]
+
+
+def attend(rows, span, key_labels, query_labels, kv_all, q):
     count = kv_all.shape[0]
-    wide = q_pad.shape[1]
-    fixed = lambda h, s: (0, 0)
+    wide = SHARES * rows
     return pl.pallas_call(
         functools.partial(attend_kernel, rows),
         grid_spec=pltpu.PrefetchScalarGridSpec(
             num_scalar_prefetch=1,
             grid=(KV_HEADS,),
             in_specs=[
-                pl.BlockSpec((count, 8), fixed),
-                pl.BlockSpec((8, wide), fixed),
-                pl.BlockSpec((count, 2 * HD), lambda h, s: (0, h)),
-                pl.BlockSpec((1, wide, 2 * HD), lambda h, s: (h, 0, 0)),
+                whole(count, 8),
+                whole(8, wide),
+                pl.BlockSpec((count, LANES), lambda h, s: (0, h)),
+                whole(CHUNKS, rows, LANES),
             ],
             out_specs=[
-                pl.BlockSpec((1, 2 * HD, wide), lambda h, s: (h, 0, 0)),
+                whole(rows, HEADS * HD),
+                whole(CHUNKS, rows, LANES),
                 pl.BlockSpec((1, 8, wide), lambda h, s: (h, 0, 0)),
             ],
-            scratch_shapes=[pltpu.VMEM((count, wide), F32), pltpu.VMEM((count, wide), F32)],
+            scratch_shapes=[
+                pltpu.VMEM((count, wide), F32), pltpu.VMEM((count, wide), F32),
+                pltpu.VMEM((wide, LANES), BF), pltpu.VMEM((LANES, wide), F32),
+                pltpu.VMEM((HEADS, rows, LANES), F32),
+            ],
         ),
         out_shape=[
-            jax.ShapeDtypeStruct((KV_HEADS, 2 * HD, wide), F32),
+            jax.ShapeDtypeStruct((rows, HEADS * HD), BF),
+            jax.ShapeDtypeStruct((CHUNKS, rows, LANES), F32),
             jax.ShapeDtypeStruct((KV_HEADS, 8, wide), F32),
         ],
         compiler_params=pltpu.CompilerParams(vmem_limit_bytes=62 << 20),
-        cost_estimate=pl.CostEstimate(
-            flops=8 * KV_HEADS * wide * count * HD,
-            bytes_accessed=2 * count * 2 * HD * KV_HEADS + 8 * KV_HEADS * wide * HD * 2,
-            transcendentals=KV_HEADS * wide * count,
-        ),
         name="attend",
-    )(span, key_labels, query_labels, kv_all, q_pad)
-
-
-def attend_back_kernel(
-    rows, span, key_ref, query_ref, kv_ref, q_ref, stat_ref, delta_ref, dq_ref, dkv_ref, bias
-):
+    )(span, key_labels, query_labels, kv_all, q)
+
+
+def attend_back_kernel(rows, span, key_ref, query_ref, kv_ref, q_ref, d_ref, out_ref, stat_ref,
+                       turn_ref, dq_ref, dkv_ref, bias, stacked, part, mixing, heads):
     first, last = span[0], span[1]
-
-    @pl.when(pl.program_id(0) == 0)
+    group = pl.program_id(0)
+
+    @pl.when(group == 0)
     def _():
         fill_bias(bias, key_ref, query_ref, rows, first, last)
 
-    queries = q_ref[0]
+    low = lanes_of(rows) < HD
+    for j in range(SHARES):
+        head = group * SHARES + j
+        odd = lax.rem(head, 2) == 1
+        mine = low != odd
+        q = q_ref[head // 2].astype(F32)
+        d = d_ref[head // 2].astype(F32)
+        q_low = jnp.where(odd, pltpu.roll(q, HD, 1), q)
+        d_high = jnp.where(odd, d, pltpu.roll(d, HD, 1))
+        at = pl.ds(j * rows, rows)
+        stacked[at, :] = jnp.where(low, q_low, d_high).astype(BF)
+        part[at, :] = jnp.where(mine, d * out_ref[head // 2], 0.0)
+    wide = stacked.shape[0]
+    queries = stacked[...]
+    ones = jnp.ones((8, LANES), BF)
+    coarse = part[...].astype(BF)
+    fine = (part[...] - coarse.astype(F32)).astype(BF)
+    delta = lax.dot_general(ones, coarse, NT, preferred_element_type=F32)
+    delta += lax.dot_general(ones, fine, NT, preferred_element_type=F32)
+    delta = delta[0:1, :]
     stat = stat_ref[0, 0:1, :]
-    delta = delta_ref[0, 0:1, :]
     dkv_ref[...] = jnp.zeros(dkv_ref.shape, BF)
-    dq_ref[0] = jnp.zeros(dq_ref.shape[1:], F32)
-    low = lax.broadcasted_iota(jnp.int32, (rows, 2 * HD), 1) < HD
+    mixing[...] = jnp.zeros(mixing.shape, F32)
 
     def body(t, carry):
         at = pl.ds(pl.multiple_of(t * rows, rows), rows)
@@ -777,48 +1050,188 @@
         dk = jnp.dot(ds, queries, preferred_element_type=F32)
         dv = jnp.dot(p.astype(BF), queries, preferred_element_type=F32)
         dkv_ref[at, :] = jnp.where(low, dk, dv).astype(BF)
-        dq_ref[0] += lax.dot_general(kv, ds, TN, preferred_element_type=F32)
+        mixing[...] += lax.dot_general(kv, ds, TN, preferred_element_type=F32)
         return carry
 
     lax.fori_loop(first, last, body, 0)
-
-
-def attend_back(rows, span, key_labels, query_labels, kv_all, q_do, stat, delta):
+    back = jnp.transpose(mixing[...])
+    for j in range(SHARES):
+        heads[group * SHARES + j] = back[j * rows:(j + 1) * rows, :]
+
+    @pl.when(group == KV_HEADS - 1)
+    def _():
+        cosine, sine = turn_ref[0], turn_ref[1]
+        for j in range(CHUNKS):
+            odd = jnp.zeros((rows, LANES), F32)
+            if 2 * j + 1 < HEADS:
+                odd = pltpu.roll(heads[2 * j + 1], HD, 1)
+            both = jnp.where(low, heads[2 * j], odd) * HD ** -0.5
+            both = both * cosine - spin(both) * sine
+            dq_ref[:, j * LANES:(j + 1) * LANES] = both.astype(BF)
+
+
+def attend_back(rows, span, key_labels, query_labels, kv_all, q, d_mixed, out, stat, turns):
     count = kv_all.shape[0]
-    wide = q_do.shape[1]
-    fixed = lambda h, s: (0, 0)
-    head = lambda h, s: (h, 0, 0)
+    wide = SHARES * rows
     return pl.pallas_call(
         functools.partial(attend_back_kernel, rows),
         grid_spec=pltpu.PrefetchScalarGridSpec(
             num_scalar_prefetch=1,
             grid=(KV_HEADS,),
             in_specs=[
-                pl.BlockSpec((count, 8), fixed),
-                pl.BlockSpec((8, wide), fixed),
-                pl.BlockSpec((count, 2 * HD), lambda h, s: (0, h)),
-                pl.BlockSpec((1, wide, 2 * HD), head),
-                pl.BlockSpec((1, 8, wide), head),
-                pl.BlockSpec((1, 8, wide), head),
+                whole(count, 8),
+                whole(8, wide),
+                pl.BlockSpec((count, LANES), lambda h, s: (0, h)),
+                whole(CHUNKS, rows, LANES),
+                whole(CHUNKS, rows, LANES),
+                whole(CHUNKS, rows, LANES),
+                pl.BlockSpec((1, 8, wide), lambda h, s: (h, 0, 0)),
+                whole(*turns.shape),
             ],
             out_specs=[
-                pl.BlockSpec((1, 2 * HD, wide), head),
-                pl.BlockSpec((count, 2 * HD), lambda h, s: (0, h)),
+                whole(rows, CHUNKS * LANES),
+                pl.BlockSpec((count, LANES), lambda h, s: (0, h)),
             ],
-            scratch_shapes=[pltpu.VMEM((count, wide), F32)],
+            scratch_shapes=[
+                pltpu.VMEM((count, wide), F32), pltpu.VMEM((wide, LANES), BF),
+                pltpu.VMEM((wide, LANES), F32), pltpu.VMEM((LANES, wide), F32),
+                pltpu.VMEM((HEADS, rows, LANES), F32),
+            ],
         ),
         out_shape=[
-            jax.ShapeDtypeStruct((KV_HEADS, 2 * HD, wide), F32),
-            jax.ShapeDtypeStruct((count, KV_HEADS * 2 * HD), BF),
+            jax.ShapeDtypeStruct((rows, CHUNKS * LANES), BF),
+            jax.ShapeDtypeStruct((count, KV_HEADS * LANES), BF),
         ],
         compiler_params=pltpu.CompilerParams(vmem_limit_bytes=62 << 20),
+        name="attend_back",
+    )(span, key_labels, query_labels, kv_all, q, d_mixed, out, stat, turns)
+
+
+def out_back_kernel(d_ref, w_ref, out_ref):
+    d = d_ref[...]
+    for j in range(CHUNKS):
+        size = min(LANES, w_ref.shape[0] - j * LANES)
+        v = lax.dot_general(
+            d, w_ref[j * LANES:j * LANES + size, :], NT, preferred_element_type=F32
+        ).astype(BF)
+        if size < LANES:
+            v = jnp.concatenate([v, jnp.zeros((d.shape[0], LANES - size), BF)], axis=1)
+        out_ref[j] = v
+
+
+def out_back(d_att, w_out):
+    n = d_att.shape[0]
+    return pl.pallas_call(
+        out_back_kernel,
+        grid=(1,),
+        in_specs=[whole(*d_att.shape), whole(*w_out.shape)],
+        out_specs=whole(CHUNKS, n, LANES),
+        out_shape=jax.ShapeDtypeStruct((CHUNKS, n, LANES), BF),
+        compiler_params=pltpu.CompilerParams(vmem_limit_bytes=ROOM),
+        name="out_back",
+    )(d_att, w_out)
+
+
+def project_back_kernel(gradient_ref, state_ref, gain_ref, w_ref, turn_ref, dq_ref, raw_ref,
+                        grad_ref, dkv_ref, dgain_ref):
+    cosine, sine = turn_ref[0], turn_ref[1]
+    key = lanes_of(dq_ref.shape[0]) < HD
+    for j in range(KV_HEADS):
+        v = raw_ref[:, j * LANES:(j + 1) * LANES].astype(F32)
+        turned = v * cosine - spin(v) * sine
+        dkv_ref[:, j * LANES:(j + 1) * LANES] = jnp.where(key, turned, v).astype(BF)
+    split = CHUNKS * LANES
+    d = lax.dot_general(dq_ref[...], w_ref[:, :split], NT, preferred_element_type=F32)
+    d += lax.dot_general(dkv_ref[...], w_ref[:, split:], NT, preferred_element_type=F32)
+    v = state_ref[...]
+    inv = lax.rsqrt(jnp.mean(v * v, axis=-1, keepdims=True) + EPS)
+    scaled = d * gain_ref[...]
+    dot = jnp.mean(scaled * v, axis=-1, keepdims=True)
+    grad_ref[...] = gradient_ref[...] + inv * scaled - v * (inv * inv * inv * dot)
+    dgain_ref[...] = jnp.sum(d * v * inv, axis=0, keepdims=True)
+
+
+def project_back(gradient, state, gain, w, turns, dq, dkv):
+    n, model = state.shape
+    return pl.pallas_call(
+        project_back_kernel,
+        grid=(1,),
+        in_specs=[
+            whole(n, model), whole(n, model), whole(1, model), whole(*w.shape),
+            whole(*turns.shape), whole(*dq.shape), whole(*dkv.shape),
+        ],
+        out_specs=[whole(n, model), whole(*dkv.shape), whole(1, model)],
+        out_shape=[
+            jax.ShapeDtypeStruct((n, model), F32),
+            jax.ShapeDtypeStruct(dkv.shape, BF),
+            jax.ShapeDtypeStruct((1, model), F32),
+        ],
+        compiler_params=pltpu.CompilerParams(vmem_limit_bytes=ROOM),
+        name="project_back",
+    )(gradient, state, gain, w, turns, dq, dkv)
+
+
+def outer_columns_kernel(count, x_ref, *refs):
+    ds, out_ref, turned = refs[:count], refs[count], refs[count + 1]
+
+    @pl.when((pl.program_id(0) == 0) & (pl.program_id(1) == 0))
+    def _():
+        turned[...] = jnp.transpose(x_ref[...])
+
+    for i in range(count):
+        @pl.when(pl.program_id(0) == i)
+        def _(i=i):
+            out_ref[0] = jnp.dot(
+                turned[...], ds[i][...], preferred_element_type=F32
+            ).astype(BF)
+
+
+def outer_columns(x, ds, tile):
+    n, rows = x.shape
+    columns = ds[0].shape[1]
+    count = len(ds)
+
+    def taken(i):
+        return lambda a, j: (0, jnp.where(a == i, j, jnp.where(a < i, 0, columns // tile - 1)))
+
+    return pl.pallas_call(
+        functools.partial(outer_columns_kernel, count),
+        grid=(count, columns // tile),
+        in_specs=[whole(n, rows)] + [pl.BlockSpec((n, tile), taken(i)) for i in range(count)],
+        out_specs=pl.BlockSpec((1, rows, tile), lambda a, j: (a, 0, j)),
+        out_shape=jax.ShapeDtypeStruct((count, rows, columns), BF),
+        scratch_shapes=[pltpu.VMEM((rows, n), BF)],
+        compiler_params=pltpu.CompilerParams(vmem_limit_bytes=ROOM),
         cost_estimate=pl.CostEstimate(
-            flops=20 * KV_HEADS * wide * count * HD,
-            bytes_accessed=4 * count * 2 * HD * KV_HEADS + 8 * KV_HEADS * wide * HD * 2,
-            transcendentals=KV_HEADS * wide * count,
+            flops=2 * n * rows * columns * count, transcendentals=0,
+            bytes_accessed=2 * count * (n * columns + rows * columns) + 2 * n * rows,
         ),
-        name="attend_back",
-    )(span, key_labels, query_labels, kv_all, q_do, stat, delta)
+        name="outer_columns",
+    )(x, *ds)
+
+
+def outer_rows_kernel(x_ref, d_ref, out_ref):
+    out_ref[...] = jnp.dot(
+        jnp.transpose(x_ref[...]), d_ref[...], preferred_element_type=F32
+    ).astype(BF)
+
+
+def outer_rows(x, d, tile):
+    n, rows = x.shape
+    columns = d.shape[1]
+    return pl.pallas_call(
+        outer_rows_kernel,
+        grid=(rows // tile,),
+        in_specs=[pl.BlockSpec((n, tile), lambda i: (0, i)), whole(n, columns)],
+        out_specs=pl.BlockSpec((tile, columns), lambda i: (i, 0)),
+        out_shape=jax.ShapeDtypeStruct((rows, columns), BF),
+        compiler_params=pltpu.CompilerParams(vmem_limit_bytes=ROOM),
+        cost_estimate=pl.CostEstimate(
+            flops=2 * n * rows * columns, transcendentals=0,
+            bytes_accessed=2 * (n * columns + n * rows + rows * columns),
+        ),
+        name="outer_rows",
+    )(x, d)
 
 
 def mm(a, b):
@@ -841,29 +1254,6 @@
     scaled = grad * gain
     dot = jnp.mean(scaled * v, axis=-1, keepdims=True)
     return (inv * scaled - v * (inv * inv * inv * dot), jnp.sum(grad * v * inv, axis=0))
-
-
-def turn(values, cosine, sine):
-    half = HD // 2
-    lower, upper = values[..., :half], values[..., half:]
-    return jnp.concatenate(
-        [lower * cosine - upper * sine, upper * cosine + lower * sine], axis=-1
-    )
-
-
-def heads_first(v):
-    n = v.shape[0]
-    return v.reshape(n, HEADS, HD).transpose(1, 0, 2)
-
-
-def heads_back(v):
-    n = v.shape[-1] // SHARES
-    return v.reshape(KV_HEADS, HD, SHARES, n).transpose(3, 0, 2, 1).reshape(n, HEADS, HD)
-
-
-def pair_up(q, d):
-    n = q.shape[1]
-    return jnp.concatenate([q, d], axis=-1).reshape(KV_HEADS, SHARES * n, 2 * HD)
 
 
 def per_device(topo, *args):
@@ -881,9 +1271,9 @@
     w_kv = jnp.stack(
         [w_key.reshape(shard, KV_HEADS, HD), w_value.reshape(shard, KV_HEADS, HD)], axis=2
     ).reshape(shard, 2 * kv_cols)
-    first = jnp.concatenate([w_query, small, w_kv, w_out], axis=1)
-    all_first, weight_g, weight_u, weight_d = gather_weights(
-        topo, [first, w_gate, w_up, w_down]
+    first = jnp.concatenate([w_query, small, w_kv], axis=1)
+    weight_qkv, weight_g, weight_u, weight_d, weight_o = gather_weights(
+        topo, [first, w_gate, w_up, w_down, w_out]
     )
 
     own = lax.axis_index("tok") * rows + jnp.arange(rows, dtype=jnp.int32)
@@ -905,15 +1295,25 @@
     swap = topo.swap_pairs()
     state = lax.ppermute(mm(onehot, tokens).astype(BF), AXES, swap).astype(F32)
     labels = lax.ppermute(labels, AXES, swap)
-    gradient = lax.ppermute(mm(onehot, cotangent).astype(BF), AXES, swap).astype(F32)
+    gradient, weight_qkv = lax.optimization_barrier(
+        (mm(onehot, cotangent).astype(BF), weight_qkv)
+    )
+    gradient = lax.ppermute(gradient, AXES, swap).astype(F32)
     order_g = xk + yk + ck
-    labels_all = group_gather(topo, labels, order_g)
-
-    small = all_first[:, model:model + HD].astype(F32)
-    gain_one, gain_two = small[:, RECS], small[:, RECS + 1]
-    weight_q = all_first[:, :model]
-    weight_kv = all_first[:, model + HD:model + HD + 2 * kv_cols]
-    weight_o = all_first[:, model + HD + 2 * kv_cols:]
+
+    def collect(arrays, ident):
+        if small_layer(topo):
+            return gather_layer(topo, arrays, ident)
+        return [group_gather(topo, v, order_g) for v in arrays]
+
+    def distribute(grads, ident):
+        if small_layer(topo):
+            return reduce_layer(topo, grads, ident)
+        return group_scatter(topo, grads, ck + yk + xk)
+
+
+    small = weight_qkv[:, model:model + HD].astype(F32)
+    gain_one, gain_two = small[:, RECS][None], small[:, RECS + 1][None]
 
     pack = (lax.axis_index("grp") * topo.X) + lax.axis_index("tok") % topo.X
     begin_all, level_mine = labels[1], labels[2]
@@ -922,29 +1322,24 @@
     places = (labels[0] - labels[1]).astype(F32)
     freqs = 10000.0 ** (-(jnp.arange(HD // 2, dtype=F32) * 2.0 / HD))
     angles = places[:, None] * freqs[None, :]
-    cosine, sine = jnp.cos(angles), jnp.sin(angles)
-
-    def forward(state, recursion):
+    turns = jnp.stack([jnp.cos(angles), jnp.sin(angles)])
+    turns = jnp.tile(turns, (1, 1, LANES * 2 // HD))
+
+    def forward(state, recursion, labels_all=None):
         n = state.shape[0]
-        cos_n, sin_n = cosine[:n], sine[:n]
-        inv_one = inverse_rms(state)
-        n1 = (state * inv_one * gain_one).astype(BF)
-        q = heads_first(mm(n1, weight_q))
-        q = (turn(q, cos_n, sin_n).astype(BF) * BF(HD ** -0.5)).astype(BF)
-        kv = mm(n1, weight_kv).reshape(n, KV_HEADS, 2, HD)
-        k = turn(kv[:, :, 0], cos_n[:, None], sin_n[:, None])
-        kv = jnp.stack([k, kv[:, :, 1]], axis=2).reshape(n, 2 * kv_cols).astype(BF)
-        kv_all = group_gather(topo, kv, order_g).reshape(topo.T * n, 2 * kv_cols)
+        n1, q, kv = project(state, gain_one, weight_qkv, turns[:, :n])
+        if recursion == 0:
+            kv_all, labels_all = collect([kv, labels], 2)
+        else:
+            kv_all, = collect([kv], 3)
+        kv_all = kv_all.reshape(topo.T * n, 2 * kv_cols)
         live = labels_all[:, 2, :n] > recursion
         order = labels_all[:, 0, :n]
         key_labels = jnp.stack([jnp.where(live, order, -1), order], axis=-1).reshape(-1, 2)
         key_labels = jnp.pad(key_labels, ((0, 0), (0, 6)))
         query_labels = jnp.stack([labels[1, :n], labels[0, :n]])
         query_labels = jnp.pad(jnp.tile(query_labels, (1, SHARES)), ((0, 6), (0, 0)))
-        q_pad = pair_up(q, jnp.zeros_like(q))
-        out, stat = attend(n, span, key_labels, query_labels, kv_all, q_pad)
-        out = heads_back(out[:, HD:])
-        mixed = out.reshape(n, HEADS * HD).astype(BF)
+        mixed, out, stat = attend(n, span, key_labels, query_labels, kv_all, q)
         attended = mm(mixed, weight_o)
         middle = state + attended
         inv_two = inverse_rms(middle)
@@ -955,12 +1350,12 @@
         gate = jax.nn.sigmoid(jnp.sum(state * small[:, recursion], axis=-1, keepdims=True))
         active = (labels[2, :n] > recursion).astype(F32)[:, None]
         new = state + active * gate * both
-        kept = (state, inv_one, n1, q, kv_all, key_labels, query_labels, out, stat, mixed, middle,
+        kept = (state, n1, q, kv_all, key_labels, query_labels, out, stat, mixed, middle,
                 inv_two, n2, gated, upward, hidden, both, gate, active)
-        return (new, kept)
+        return (new, kept, labels_all)
 
     def backward(gradient, recursion, kept):
-        (state, inv_one, n1, q, kv_all, key_labels, query_labels, out, stat, mixed, middle,
+        (state, n1, q, kv_all, key_labels, query_labels, out, stat, mixed, middle,
          inv_two, n2, gated, upward, hidden, both, gate, active) = kept
         n = state.shape[0]
         d_both = active * gate * gradient
@@ -975,39 +1370,24 @@
             mm_nt(d_gated, weight_g) + mm_nt(d_up, weight_u), middle, inv_two, gain_two)
         d_att = (d_both + d_middle).astype(BF)
         gradient = gradient + d_gate * small[:, recursion] + d_middle
-        d_mixed = mm_nt(d_att, weight_o).astype(BF)
-        d_heads = heads_first(d_mixed)
-        delta = jnp.sum(
-            d_heads.astype(F32) * out.transpose(1, 0, 2), axis=-1
-        ).reshape(KV_HEADS, 1, SHARES * n)
-        delta = jnp.broadcast_to(delta, (KV_HEADS, 8, SHARES * n))
         dq, dkv = attend_back(
-            n, span, key_labels, query_labels, kv_all, pair_up(q, d_heads), stat, delta
-        )
-        dkv = group_scatter(
-            topo, dkv.reshape(topo.T, n, 2 * kv_cols), ck + yk + xk
-        ).astype(F32).reshape(n, KV_HEADS, 2, HD)
-        cos_n, sin_n = cosine[:n, None], sine[:n, None]
-        dk = turn(dkv[:, :, 0], cos_n, -sin_n)
-        dkv = jnp.stack([dk, dkv[:, :, 1]], axis=2).reshape(n, 2 * kv_cols).astype(BF)
-        dq = turn(heads_back(dq[:, :HD]) * HD ** -0.5, cos_n, -sin_n)
-        dq = dq.reshape(n, HEADS * HD).astype(BF)
-        d_n1 = mm_nt(dq, weight_q) + mm_nt(dkv, weight_kv)
-        d_state, d_gain_one = norm_back(d_n1, state, inv_one, gain_one)
-        blank = jnp.zeros((n, HD), BF)
-        dqkv = jnp.concatenate([dq, blank, dkv], axis=1)
-        dqkv = jnp.pad(dqkv, ((0, 0), (0, -dqkv.shape[1] % 256)))
-        left = (n1, dqkv, mixed, d_att, n2, d_gated, d_up, hidden, d_fed)
-        return (gradient + d_state, left, (d_router, d_gain_one, d_gain_two))
-
-    whole_state, kept = forward(state, 0)
+            n, span, key_labels, query_labels, kv_all, q, out_back(d_att, weight_o), out, stat,
+            turns[:, :n],
+        )
+        dkv = distribute(dkv.reshape(topo.T, n, 2 * kv_cols), 5 if recursion else 4)
+        gradient, dkv, d_gain_one = project_back(
+            gradient, state, gain_one, weight_qkv, turns[:, :n], dq, dkv
+        )
+        left = (n1, dq, dkv, mixed, d_att, n2, d_gated, d_up, hidden, d_fed)
+        return (gradient, left, (d_router, d_gain_one[0], d_gain_two))
+
+    whole_state, kept, labels_all = forward(state, 0)
     deep = whole_state[:deep_rows]
     all_kept = [kept]
     for recursion in range(1, RECS):
-        deep, kept = forward(deep, recursion)
+        deep, kept, _ = forward(deep, recursion, labels_all)
         all_kept.append(kept)
     final = jnp.concatenate([deep, whole_state[deep_rows:]], axis=0).astype(BF)
-    final = lax.ppermute(final, AXES, swap)
 
     deep_grad = gradient[:deep_rows]
     lefts, smalls = [], []
@@ -1019,11 +1399,15 @@
     gradient, left, tiny = backward(gradient, 0, all_kept[0])
     lefts.append(left)
     smalls.append(tiny)
-    gradient = lax.ppermute(gradient.astype(BF), AXES, swap)
-
-    n1, dqkv, mixed, d_att, n2, d_gated, d_up, hidden, d_fed = (
+    final, gradient = lax.optimization_barrier((final, gradient.astype(BF)))
+    final = lax.ppermute(final, AXES, swap)
+    gradient = lax.ppermute(gradient, AXES, swap)
+
+    n1, dq, dkv, mixed, d_att, n2, d_gated, d_up, hidden, d_fed = (
         jnp.concatenate(parts, axis=0) for parts in zip(*lefts)
     )
+    dqkv = jnp.concatenate([dq, dkv], axis=1)
+    dqkv = jnp.pad(dqkv, ((0, 0), (0, -dqkv.shape[1] % 256)))
     cut = lambda v: v.astype(BF).reshape(topo.T, -1, v.shape[-1])
     tiny = jnp.stack(
         [smalls[2][0], smalls[1][0], smalls[0][0],
@@ -1035,8 +1419,8 @@
     grad_qkv, grad_o, grad_gu, grad_down = reduce_gradients(topo, [
         cut(mm_tn(n1, dqkv)),
         cut(jnp.concatenate([mm_tn(mixed, d_att), tiny], axis=1)),
-        jnp.stack([cut(mm_tn(n2, d_gated)), cut(mm_tn(n2, d_up))]),
-        cut(mm_tn(hidden, d_fed)),
+        outer_columns(n2, [d_gated, d_up], 640).reshape(2, topo.T, -1, ff),
+        outer_rows(hidden, d_fed, 640).reshape(topo.T, -1, model),
     ])
     grad_query = grad_qkv[:, :model].astype(F32)
     pair = grad_qkv[:, model + HD:model + HD + 2 * kv_cols].astype(F32)

time: 856 us -> 696 us (0.81)
  Pallas kernels: 298 us -> 502 us
  local copies, waits for them, and re-layouts: 146 us -> 26.7 us
  waiting for transfers between devices: 104 us -> 0.01 us
  other arithmetic: 92.1 us -> 39.1 us
  matrix products: 125 us -> 79.8 us
  starting transfers between devices: 74.5 us -> 35.5 us
    pallas_call x0 -> x17, Pallas kernels: none -> 182 us  [the longest x3 62.5 us: reduce_layer(): pl.pallas_call(functools.partial(group_reduce_kernel, topo), in_specs=[pl...]
    ppermute x23 -> x2, waiting for transfers between devices: 104 us -> 0.01 us  [the longest x1 0.01 us: per_device(): gradient = lax.ppermute(gradient, AXES, swap).astype(F32)]
    ppermute x23 -> x2, starting transfers between devices: 51.2 us -> 3.84 us  [the longest x1 1.92 us: per_device(): gradient = lax.ppermute(gradient, AXES, swap).astype(F32)]
    another operation x52 -> x3, other arithmetic: 27.9 us -> 0.84 us  [the longest x24 16 us: double(): return jnp.stack([low, high], axis=axis)]
    unnamed x502 -> x198, local copies, waits for them, and re-layouts: 32.1 us -> 10.6 us
    dot_general x21 -> x15, matrix products: 53.5 us -> 33.3 us  [mm(): return jnp.dot(a, b, preferred_element_type=F32)]
    another operation x13 -> x2, local copies, waits for them, and re-layouts: 17.9 us -> 0.14 us  [per_device(): turns = jnp.tile(turns, (1, 1, LANES * 2 // HD))]
    ppermute x8 -> x0, local copies, waits for them, and re-layouts: 15.2 us -> none  [exchange(): return lax.ppermute(arr, AXES, topo.pairs(key))]
  transfers between devices with their start and end apart: 26 -> 5, of which waited for: 14 -> 0; matrix products, arithmetic and copies ran while one was open for 14% -> 11% of each run, Pallas kernels for 11% -> 53%
where the time goes in v4:
time: 696 us; the launch traced here: 688 us
  Pallas kernels  502 us (72%)
  matrix products  79.8 us (11%)
  other arithmetic  39.1 us (6%)
  starting transfers between devices  35.5 us (5%)
  local copies, waits for them, and re-layouts  26.7 us (4%)
    pallas_call x1, Pallas kernels, reduce_gradients(): pl.pallas_call(functools.partial(reduce_kernel, topo, shares), in_specs=[...  126 us
    pallas_call x1, Pallas kernels, gather_weights(): pl.pallas_call(functools.partial(gather_kernel, topo, pieces), in_specs=[...  103 us
    pallas_call x3, Pallas kernels, reduce_layer(): pl.pallas_call(functools.partial(group_reduce_kernel, topo), in_specs=[pl...  62.5 us
    pallas_call x3, Pallas kernels, gather_layer(): pl.pallas_call(functools.partial(group_gather_kernel, topo, n), in_specs=...  58.1 us
    pallas_call x3, Pallas kernels, attend_back(): pl.pallas_call(functools.partial(attend_back_kernel, rows), grid_spec=plt...  50.3 us
    pallas_call x3, Pallas kernels, attend(): pl.pallas_call(functools.partial(attend_kernel, rows), grid_spec=pltpu.Pr...  41.4 us
    dot_general x15, matrix products, mm(): return jnp.dot(a, b, preferred_element_type=F32)  33.3 us
    dot_general x9, matrix products, mm_nt(): return lax.dot_general(a, b, NT, preferred_element_type=F32)  29.1 us
  transfers between devices with their start and end apart: 5, of which 0 were waited for; matrix products, arithmetic and copies ran while one was open for 11% of the time, Pallas kernels for 53%

profile of v4, /device:TPU:17, one launch (start us, length us, event | category | flops | bytes accessed | tf_op | source)
XLA Modules:
  0.0 688.3 jit_solution(9762478957765734410)
XLA Ops:
  16.5 102.7 %gather_weights.1 = (bf16[8,120,1664]{2,1,0:T(8,128)(2,1)}, bf16[8,120,2560]{2,1,0:T(8,128)(2,1)}, bf16[8,120,2560]{2,1,0:T(8,128)(2,1)}, bf16[8,320,960]{2,1,0:T(8,128)(2,1)}, bf16[8,120,960]{2,1,0:T(8,128)(2,1)}) custom-call(bf16[120,1664]{1,0:T(8,128)(2,1)} %concatenate.59.refs_0_, bf16[120,2560]{1,0:T(8,128)(2,1)} %refs_1_.1, bf16[120,2560]{1,0:T(8,128)(2,1)} %refs_2_.1, ...), custom_call_target="tpu_custom_call" | custom-call | tf_op jit(solution)/shard_map/gather_weights/pallas_call | solution.py:298
  131.5 4.4 project.3
  135.8 23.2 %gather_layer.3 = (bf16[8,256,640]{2,1,0:T(8,128)(2,1)}, s32[8,8,256]{2,1,0:T(8,128)}) custom-call(bf16[256,640]{1,0:T(8,128)(2,1)} %get-tuple-element.62.refs_0_, s32[8,256]{1,0:T(8,128)} %copy-done.65), custom_call_target="tpu_custom_call" | custom-call | tf_op jit(solution)/shard_map/gather_layer/pallas_call | solution.py:759
  164.0 15.1 %attend.3 = (bf16[256,960]{1,0:T(8,128)(2,1)}, f32[8,256,128]{2,1,0:T(8,128)}, f32[5,8,768]{2,1,0:T(8,128)}) custom-call(s32[2]{0:T(128)} %pad_add_fusion.6.span, s32[2048,8]{1,0:T(8,128)} %pad.39.key_ref, s32[8,768]{1,0:T(8,128)} %pad.40.query_ref, bf16[2048,640]{1,0:T(8,128)(2,1)} %bitcast.157, bf16[8,256,128]{2,1,0:T(8,128)(2,1)} %get-tuple-element.65.q_ref), custom_call_target="tpu_custom_call" | custom-call | tf_op jit(solution)/shard_map/attend/pallas_call | solution.py:977
  182.1 4.7 fusion.61
  197.5 4.0 project.4
  201.5 17.9 %gather_layer.4 = bf16[8,192,640]{2,1,0:T(8,128)(2,1)} custom-call(bf16[192,640]{1,0:T(8,128)(2,1)} %get-tuple-element.71.refs_0_), custom_call_target="tpu_custom_call" | custom-call | tf_op jit(solution)/shard_map/gather_layer/pallas_call | solution.py:759
  219.4 13.2 %attend.4 = (bf16[192,960]{1,0:T(8,128)(2,1)}, f32[8,192,128]{2,1,0:T(8,128)}, f32[5,8,576]{2,1,0:T(8,128)}) custom-call(s32[2]{0:T(128)} %pad_add_fusion.6.span, s32[1536,8]{1,0:T(8,128)} %pad.41.key_ref, s32[8,576]{1,0:T(8,128)} %pad.42.query_ref, bf16[1536,640]{1,0:T(8,128)(2,1)} %bitcast.141, bf16[8,192,128]{2,1,0:T(8,128)(2,1)} %get-tuple-element.72.q_ref), custom_call_target="tpu_custom_call" | custom-call | tf_op jit(solution)/shard_map/attend/pallas_call | solution.py:977
  235.9 3.7 fusion.62
  244.9 4.0 project.5
  248.8 17.0 %gather_layer.5 = bf16[8,192,640]{2,1,0:T(8,128)(2,1)} custom-call(bf16[192,640]{1,0:T(8,128)(2,1)} %get-tuple-element.74.refs_0_), custom_call_target="tpu_custom_call" | custom-call | tf_op jit(solution)/shard_map/gather_layer/pallas_call | solution.py:759
  265.8 13.1 %attend.5 = (bf16[192,960]{1,0:T(8,128)(2,1)}, f32[8,192,128]{2,1,0:T(8,128)}, f32[5,8,576]{2,1,0:T(8,128)}) custom-call(s32[2]{0:T(128)} %pad_add_fusion.6.span, s32[1536,8]{1,0:T(8,128)} %pad.43.key_ref, s32[8,576]{1,0:T(8,128)} %pad.42.query_ref, bf16[1536,640]{1,0:T(8,128)(2,1)} %bitcast.143, bf16[8,192,128]{2,1,0:T(8,128)(2,1)} %get-tuple-element.75.q_ref), custom_call_target="tpu_custom_call" | custom-call | tf_op jit(solution)/shard_map/attend/pallas_call | solution.py:977
  281.0 3.7 fusion.64
  303.4 15.8 %attend_back.3 = (bf16[192,1024]{1,0:T(8,128)(2,1)}, bf16[1536,640]{1,0:T(8,128)(2,1)}) custom-call(s32[2]{0:T(128)} %pad_add_fusion.6.span, s32[1536,8]{1,0:T(8,128)} %pad.43.key_ref, s32[8,576]{1,0:T(8,128)} %pad.42.query_ref, bf16[1536,640]{1,0:T(8,128)(2,1)} %bitcast.144, bf16[8,192,128]{2,1,0:T(8,128)(2,1)} %get-tuple-element.75.q_ref, ...), custom_call_target="tpu_custom_call" | custom-call | tf_op jit(solution)/shard_map/attend_back/pallas_call | solution.py:1076
  320.8 23.0 %reduce_layer.3.raw_ref = bf16[192,640]{1,0:T(8,128)(2,1)S(1)} custom-call(bf16[8,192,640]{2,1,0:T(8,128)(2,1)S(1)} %bitcast.103), custom_call_target="tpu_custom_call" | custom-call | tf_op jit(solution)/shard_map/reduce_layer/pallas_call | solution.py:829
  344.5 5.0 project_back.3
  350.8 5.5 multiply_convert_fusion.3
  358.1 4.3 multiply_reduce_fusion.6
  367.3 15.8 %attend_back.4 = (bf16[192,1024]{1,0:T(8,128)(2,1)}, bf16[1536,640]{1,0:T(8,128)(2,1)}) custom-call(s32[2]{0:T(128)} %pad_add_fusion.6.span, s32[1536,8]{1,0:T(8,128)} %pad.41.key_ref, s32[8,576]{1,0:T(8,128)} %pad.42.query_ref, bf16[1536,640]{1,0:T(8,128)(2,1)} %bitcast.142, bf16[8,192,128]{2,1,0:T(8,128)(2,1)} %get-tuple-element.72.q_ref, ...), custom_call_target="tpu_custom_call" | custom-call | tf_op jit(solution)/shard_map/attend_back/pallas_call | solution.py:1076
  384.6 18.2 %reduce_layer.4.raw_ref = bf16[192,640]{1,0:T(8,128)(2,1)S(1)} custom-call(bf16[8,192,640]{2,1,0:T(8,128)(2,1)S(1)} %bitcast.102), custom_call_target="tpu_custom_call" | custom-call | tf_op jit(solution)/shard_map/reduce_layer/pallas_call | solution.py:829
  403.6 4.9 project_back.4
  410.9 5.9 multiply_convert_fusion
  418.9 4.3 multiply_reduce_fusion
  424.9 3.9 out_back.5.d_ref
  436.4 18.6 %attend_back.5 = (bf16[256,1024]{1,0:T(8,128)(2,1)}, bf16[2048,640]{1,0:T(8,128)(2,1)}) custom-call(s32[2]{0:T(128)} %pad_add_fusion.6.span, s32[2048,8]{1,0:T(8,128)} %pad.39.key_ref, s32[8,768]{1,0:T(8,128)} %pad.40.query_ref, bf16[2048,640]{1,0:T(8,128)(2,1)} %bitcast.158, bf16[8,256,128]{2,1,0:T(8,128)(2,1)} %get-tuple-element.65.q_ref, ...), custom_call_target="tpu_custom_call" | custom-call | tf_op jit(solution)/shard_map/attend_back/pallas_call | solution.py:1076
  456.7 21.4 %reduce_layer.5.raw_ref = bf16[256,640]{1,0:T(8,128)(2,1)S(1)} custom-call(bf16[8,256,640]{2,1,0:T(8,128)(2,1)S(1)} %bitcast.101), custom_call_target="tpu_custom_call" | custom-call | tf_op jit(solution)/shard_map/reduce_layer/pallas_call | solution.py:829
  478.8 5.3 project_back.5
  487.5 25.2 %collective-permute-start.3 = (bf16[256,960]{1,0:T(8,128)(2,1)}, bf16[256,960]{1,0:T(8,128)(2,1)}, u32[]{:S(2)}, u32[]{:S(2)}) collective-permute-start(bf16[256,960]{1,0:T(8,128)(2,1)} %pad_maximum_fusion.7), channel_id=1, source_target_pairs={{0,0},{1,1},{2,8},{3,9},{4,16},{5,17},{6,24},{7,25},{8,2},{9,3},{1... | collective-permute-start | bytes 1474568 | tf_op jit(solution)/shard_map/ppermute | solution.py:1403
  516.1 8.0 %outer_rows.1 = bf16[2560,960]{1,0:T(8,128)(2,1)} custom-call(bf16[640,2560]{1,0:T(8,128)(2,1)} %pad_maximum_fusion.2.x_ref, bf16[640,960]{1,0:T(8,128)(2,1)} %pad_maximum_fusion.5.d_ref), custom_call_target="tpu_custom_call" | custom-call | flops 3145728000 | bytes 9420800 | tf_op jit(solution)/shard_map/outer_rows/pallas_call | solution.py:1222
  524.2 14.7 %outer_columns.1 = bf16[2,960,2560]{2,1,0:T(8,128)(2,1)} custom-call(bf16[640,960]{1,0:T(8,128)(2,1)} %pad_maximum_fusion.4.x_ref, bf16[640,2560]{1,0:T(8,128)(2,1)} %get-tuple-element.255.refs_0_, bf16[640,2560]{1,0:T(8,128)(2,1)} %get-tuple-element.256.refs_1_), custom_call_target="tpu_custom_call" | custom-call | flops 6291456000 | bytes 17612800 | tf_op jit(solution)/shard_map/outer_columns/pallas_call | solution.py:1197
  539.0 9.8 %convolution_convert_fusion = bf16[960,1792]{1,0:T(8,128)(2,1)} fusion(bf16[256,640]{1,0:T(8,128)(2,1)S(1)} %copy-done.74, bf16[256,1024]{1,0:T(8,128)(2,1)S(1)} %copy-done.58, bf16[192,640]{1,0:T(8,128)(2,1)S(1)} %copy-done.76, bf16[192,640]{1,0:T(8,128)(2,1)S(1)} %copy-done.75, bf16[192,1024]{1,0:T(8,128)(2,1)S(1)} %copy-done.61, ...), kind=kOutput, calls=%fused_computation.7 | convolution fusion | flops 2229207040 | bytes 6799360 | tf_op jit(solution)/shard_map/dot_general | solution.py:1246
  548.8 125.8 %reduce_gradients.1 = (bf16[120,1792]{1,0:T(8,128)(2,1)}, bf16[120,1024]{1,0:T(8,128)(2,1)}, bf16[2,120,2560]{2,1,0:T(8,128)(2,1)}, bf16[320,960]{1,0:T(8,128)(2,1)}) custom-call(bf16[8,120,1792]{2,1,0:T(8,128)(2,1)} %bitcast.161, bf16[8,120,1024]{2,1,0:T(8,128)(2,1)} %pad_maximum_fusion.3.refs_1_, bf16[2,8,120,2560]{3,2,1,0:T(8,128)(2,1)} %bitcast.159, ...), custom_call_target="tpu_custom_call" | custom-call | tf_op jit(solution)/shard_map/reduce_gradients/pallas_call | solution.py:623
  (345 shorter events, 120.8 us)
Async XLA Ops:
  0.6 8.4 %copy-start = (bf16[256,960]{0,1:T(8,128)(2,1)S(1)}, bf16[256,960]{0,1:T(8,128)(2,1)}, u32[]{:S(2)}) copy-start(bf16[256,960]{0,1:T(8,128)(2,1)} %param.15) | copy-start | bytes 1474564
  0.7 13.8 %copy-start.59 = (bf16[256,960]{0,1:T(8,128)(2,1)S(1)}, bf16[256,960]{0,1:T(8,128)(2,1)}, u32[]{:S(2)}) copy-start(bf16[256,960]{0,1:T(8,128)(2,1)} %param.29) | copy-start | bytes 1474564
  0.7 15.0 %copy-start.64 = (bf16[120,960]{1,0:T(8,128)(2,1)S(1)}, bf16[120,960]{1,0:T(8,128)(2,1)}, u32[]{:S(2)}) copy-start(bf16[120,960]{1,0:T(8,128)(2,1)} %param.16) | copy-start | bytes 691204
  5.5 118.5 %collective-permute-start.1 = (s32[8,256]{1,0:T(8,128)S(1)}, s32[8,256]{1,0:T(8,128)S(1)}, u32[]{:S(2)}, u32[]{:S(2)}) collective-permute-start(s32[8,256]{1,0:T(8,128)S(1)} %pad.37), channel_id=1, source_target_pairs={{0,0},{1,1},{2,8},{3,9},{4,16},{5,17},{6,24},{7,25},{8,2},{9,3},{1... | collective-permute-start | bytes 24584 | tf_op jit(solution)/shard_map/ppermute | solution.py:1297
  9.6 120.7 %collective-permute-start = (bf16[256,960]{1,0:T(8,128)(2,1)S(1)}, bf16[256,960]{1,0:T(8,128)(2,1)S(1)}, u32[]{:S(2)}, u32[]{:S(2)}) collective-permute-start(bf16[256,960]{1,0:T(8,128)(2,1)S(1)} %copy.113), channel_id=1, source_target_pairs={{0,0},{1,1},{2,8},{3,9},{4,16},{5,17},{6,24},{7,25},{8,2},{9,3},{1... | collective-permute-start | bytes 1474568 | tf_op jit(solution)/shard_map/ppermute | solution.py:1296
  119.2 168.0 %collective-permute-start.2 = (bf16[256,960]{1,0:T(8,128)(2,1)}, bf16[256,960]{1,0:T(8,128)(2,1)}, u32[]{:S(2)}, u32[]{:S(2)}) collective-permute-start(bf16[256,960]{1,0:T(8,128)(2,1)} %convolution_convert_fusion.2), channel_id=1, source_target_pairs={{0,0},{1,1},{2,8},{3,9},{4,16},{5,17},{6,24},{7,25},{8,2},{9,3},{1... | collective-permute-start | bytes 1474568 | tf_op jit(solution)/shard_map/ppermute | solution.py:1301
  124.0 11.9 %copy-start.65 = (s32[8,256]{1,0:T(8,128)}, s32[8,256]{1,0:T(8,128)S(1)}, u32[]{:S(2)}) copy-start(s32[8,256]{1,0:T(8,128)S(1)} %collective-permute-done.1.refs_1_) | copy-start | bytes 24580
  130.3 50.9 %copy-start.69 = (pred[256]{0:T(512)(128)(4,1)}, pred[256]{0:T(512)(128)(4,1)S(1)}, u32[]{:S(2)}) copy-start(pred[256]{0:T(512)(128)(4,1)S(1)} %compare_reduce_fusion.4) | copy-start | bytes 772
  164.0 15.1 %copy-start.8 = (bf16[8,120,960]{2,1,0:T(8,128)(2,1)S(1)}, bf16[8,120,960]{2,1,0:T(8,128)(2,1)}, u32[]{:S(2)}) copy-start(bf16[8,120,960]{2,1,0:T(8,128)(2,1)} %get-tuple-element.67) | copy-start | bytes 5529604
  181.2 5.6 slice-start.12
  182.1 8.0 %slice-start.6 = ((s8[5242880]{0:T(1024)(128)(4,1)}), s8[4194304]{0:T(1024)(128)(4,1)S(1)}, s32[]{:S(2)}) async-start(s8[5242880]{0:T(1024)(128)(4,1)} %bitcast.131), calls=%async_computation.6 | async-start | bytes 8388608
  232.7 7.0 %slice-start.14 = ((s8[4915200]{0:T(1024)(128)(4,1)}), s8[4194304]{0:T(1024)(128)(4,1)S(1)}, s32[]{:S(2)}) async-start(s8[4915200]{0:T(1024)(128)(4,1)} %bitcast.151), calls=%async_computation.14 | async-start | bytes 8388608
  235.9 6.5 slice-start.8
  344.5 6.4 copy-start.32
  344.5 11.9 %slice-start.2 = ((s8[4915200]{0:T(1024)(128)(4,1)}), s8[720896]{0:T(1024)(128)(4,1)S(1)}, s32[]{:S(2)}) async-start(s8[4915200]{0:T(1024)(128)(4,1)} %bitcast.123), calls=%async_computation.2 | async-start | bytes 1441792
  403.6 6.0 copy-start.47
  403.6 13.3 %slice-start.4 = ((s8[4915200]{0:T(1024)(128)(4,1)}), s8[720896]{0:T(1024)(128)(4,1)S(1)}, s32[]{:S(2)}) async-start(s8[4915200]{0:T(1024)(128)(4,1)} %bitcast.126), calls=%async_computation.4 | async-start | bytes 1441792
  410.9 5.9 slice-start.5
  478.8 7.4 %copy-start.33 = (bf16[192,960]{1,0:T(8,128)(2,1)S(1)}, bf16[192,960]{1,0:T(8,128)(2,1)}, u32[]{:S(2)}) copy-start(bf16[192,960]{1,0:T(8,128)(2,1)} %get-tuple-element.214) | copy-start | bytes 1105924
  478.8 7.4 %copy-start.57 = (bf16[64,960]{1,0:T(8,128)(2,1)S(1)}, bf16[64,960]{1,0:T(8,128)(2,1)}, u32[]{:S(2)}) copy-start(bf16[64,960]{1,0:T(8,128)(2,1)} %slice.218) | copy-start | bytes 368644
  487.5 196.0 %collective-permute-start.3 = (bf16[256,960]{1,0:T(8,128)(2,1)}, bf16[256,960]{1,0:T(8,128)(2,1)}, u32[]{:S(2)}, u32[]{:S(2)}) collective-permute-start(bf16[256,960]{1,0:T(8,128)(2,1)} %pad_maximum_fusion.7), channel_id=1, source_target_pairs={{0,0},{1,1},{2,8},{3,9},{4,16},{5,17},{6,24},{7,25},{8,2},{9,3},{1... | collective-permute-start | bytes 1474568 | tf_op jit(solution)/shard_map/ppermute | solution.py:1403
  512.6 173.0 %collective-permute-start.4 = (bf16[256,960]{1,0:T(8,128)(2,1)}, bf16[256,960]{1,0:T(8,128)(2,1)}, u32[]{:S(2)}, u32[]{:S(2)}) collective-permute-start(bf16[256,960]{1,0:T(8,128)(2,1)} %convert_element_type.166), channel_id=1, source_target_pairs={{0,0},{1,1},{2,8},{3,9},{4,16},{5,17},{6,24},{7,25},{8,2},{9,3},{1... | collective-permute-start | bytes 1474568 | tf_op jit(solution)/shard_map/ppermute | solution.py:1404
  524.1 14.8 %copy-start.58 = (bf16[256,1024]{1,0:T(8,128)(2,1)S(1)}, bf16[256,1024]{1,0:T(8,128)(2,1)}, u32[]{:S(2)}) copy-start(bf16[256,1024]{1,0:T(8,128)(2,1)} %get-tuple-element.90.dq_ref) | copy-start | bytes 1572868
  524.1 14.8 %copy-start.60 = (bf16[192,1024]{1,0:T(8,128)(2,1)S(1)}, bf16[192,1024]{1,0:T(8,128)(2,1)}, u32[]{:S(2)}) copy-start(bf16[192,1024]{1,0:T(8,128)(2,1)} %get-tuple-element.80.dq_ref) | copy-start | bytes 1179652
  524.1 14.8 %copy-start.61 = (bf16[192,1024]{1,0:T(8,128)(2,1)S(1)}, bf16[192,1024]{1,0:T(8,128)(2,1)}, u32[]{:S(2)}) copy-start(bf16[192,1024]{1,0:T(8,128)(2,1)} %get-tuple-element.85.dq_ref) | copy-start | bytes 1179652
  524.1 14.8 %copy-start.71 = (bf16[256,960]{1,0:T(8,128)(2,1)S(1)}, bf16[256,960]{1,0:T(8,128)(2,1)}, u32[]{:S(2)}) copy-start(bf16[256,960]{1,0:T(8,128)(2,1)} %get-tuple-element.97) | copy-start | bytes 1474564
  524.1 14.8 %copy-start.72 = (bf16[192,960]{1,0:T(8,128)(2,1)S(1)}, bf16[192,960]{1,0:T(8,128)(2,1)}, u32[]{:S(2)}) copy-start(bf16[192,960]{1,0:T(8,128)(2,1)} %get-tuple-element.96) | copy-start | bytes 1105924
  524.2 14.8 %copy-start.73 = (bf16[192,960]{1,0:T(8,128)(2,1)S(1)}, bf16[192,960]{1,0:T(8,128)(2,1)}, u32[]{:S(2)}) copy-start(bf16[192,960]{1,0:T(8,128)(2,1)} %get-tuple-element.95) | copy-start | bytes 1105924
  524.2 14.8 %copy-start.74 = (bf16[256,640]{1,0:T(8,128)(2,1)S(1)}, bf16[256,640]{1,0:T(8,128)(2,1)}, u32[]{:S(2)}) copy-start(bf16[256,640]{1,0:T(8,128)(2,1)} %get-tuple-element.100) | copy-start | bytes 983044
  524.2 14.8 %copy-start.75 = (bf16[192,640]{1,0:T(8,128)(2,1)S(1)}, bf16[192,640]{1,0:T(8,128)(2,1)}, u32[]{:S(2)}) copy-start(bf16[192,640]{1,0:T(8,128)(2,1)} %get-tuple-element.98) | copy-start | bytes 737284
  524.2 14.8 %copy-start.76 = (bf16[192,640]{1,0:T(8,128)(2,1)S(1)}, bf16[192,640]{1,0:T(8,128)(2,1)}, u32[]{:S(2)}) copy-start(bf16[192,640]{1,0:T(8,128)(2,1)} %get-tuple-element.99) | copy-start | bytes 737284
  680.6 7.2 %copy-start.1 = (bf16[256,960]{0,1:T(8,128)(2,1)S(1)}, bf16[256,960]{0,1:T(8,128)(2,1)}, u32[]{:S(2)}) copy-start(bf16[256,960]{0,1:T(8,128)(2,1)} %param.15) | copy-start | bytes 1474564
  (70 other events, 222.3 us)

commit v5 on v4

--- a/solution.py
+++ b/solution.py
@@ -533,15 +533,23 @@
         pl.when(zz > z)(lambda: z_copy(p, zz, 1).start())
         pl.when(zz < z)(lambda: z_copy(p, zz, -1).start())
 
+    single = topo.bits["y"] == 1
+
     def first_joins(zz):
         for p in every:
             if shares[p].part == 1:
                 join(p, zz)
+                if single:
+                    pl.when(zz == z)(lambda p=p: f_copy(p, 0).start())
 
     def last_joins(zz):
         for p in every:
             if shares[p].part != 1:
-                inside(p, lambda p=p: join(p, zz))
+                def body(p=p):
+                    join(p, zz)
+                    if single:
+                        pl.when(zz == z)(lambda: f_copy(p, 0).start())
+                inside(p, body)
 
     def main(i, carry):
         @pl.when(i < Z)
@@ -565,8 +573,9 @@
                 f_copy(p, k).wait()
                 add(p, me, from_f[p][k])
             inside(p, fold)
-    for p in every:
-        inside(p, lambda p=p: f_copy(p, 0).start())
+    if not single:
+        for p in every:
+            inside(p, lambda p=p: f_copy(p, 0).start())
     for p in every:
         if shares[p].part == 1:
             f_copy(p, 0).wait()
@@ -904,96 +913,100 @@
     )(state, gain, w, turns)
 
 
-def fill_bias(bias, key_ref, query_ref, rows, first, last):
+def attend_kernel(rows, span, key_ref, query_ref, kv_ref, q_ref, mixed_ref, out_ref, stat_ref,
+                  stacked, mixing, tops, sums):
+    low = lanes_of(rows) < HD
+    wide = SHARES * rows
+    for h in range(KV_HEADS):
+        for j in range(SHARES):
+            head = h * SHARES + j
+            chunk = q_ref[head // 2].astype(F32)
+            if head % 2:
+                chunk = pltpu.roll(chunk, HD, 1)
+            stacked[h, j * rows:(j + 1) * rows, :] = jnp.where(low, chunk, 0.0).astype(BF)
+    mixing[...] = jnp.zeros(mixing.shape, F32)
+    sums[...] = jnp.zeros(sums.shape, F32)
+    tops[...] = jnp.full(tops.shape, BIG, F32)
+
     def body(t, carry):
         at = pl.ds(pl.multiple_of(t * rows, rows), rows)
-        keys = key_ref[at, :]
-        live, order = keys[:, 0:1], keys[:, 1:2]
-        begin, place = query_ref[0:1, :], query_ref[1:2, :]
-        allowed = ((live >= begin) & (live <= place)) | (order == place)
-        bias[at, :] = jnp.where(allowed, 0.0, BIG)
+        bias = block_bias(key_ref[at, :], query_ref)
+        def score(h):
+            kv = kv_ref[at, h * LANES:(h + 1) * LANES]
+            return lax.dot_general(kv, stacked[h], NT, preferred_element_type=F32) + bias
+
+        def end(h, p, fade):
+            kv = kv_ref[at, h * LANES:(h + 1) * LANES]
+            mixing[h] = mixing[h] * fade + lax.dot_general(
+                kv[:, HD:], p, TN, preferred_element_type=F32
+            )
+
+        ahead = score(0)
+        before = None
+        for h in range(KV_HEADS):
+            s = ahead
+            if h + 1 < KV_HEADS:
+                ahead = score(h + 1)
+            if before is not None:
+                end(*before)
+            old = tops[h, 0:1, :]
+            top = jnp.max(s.reshape(rows // 8, 8, wide), axis=0)
+            top = jnp.maximum(old, jnp.max(top, axis=0, keepdims=True))
+            p = jnp.exp(s - top)
+            fade = jnp.exp(old - top)
+            sums[h] = sums[h] * fade + jnp.sum(p.reshape(rows // 8, 8, wide), axis=0)
+            tops[h] = jnp.broadcast_to(top, (8, wide))
+            before = (h, p.astype(BF), fade)
+        end(*before)
         return carry
 
-    lax.fori_loop(first, last, body, 0)
-
-
-def attend_kernel(rows, span, key_ref, query_ref, kv_ref, q_ref, mixed_ref, out_ref, stat_ref,
-                  bias, held, stacked, mixing, heads):
-    first, last = span[0], span[1]
-    group = pl.program_id(0)
-
-    @pl.when(group == 0)
-    def _():
-        fill_bias(bias, key_ref, query_ref, rows, first, last)
-
-    low = lanes_of(rows) < HD
-    for j in range(SHARES):
-        head = group * SHARES + j
-        chunk = q_ref[head // 2].astype(F32)
-        chunk = jnp.where(lax.rem(head, 2) == 1, pltpu.roll(chunk, HD, 1), chunk)
-        stacked[j * rows:(j + 1) * rows, :] = jnp.where(low, chunk, 0.0).astype(BF)
-    wide = stacked.shape[0]
-    queries = stacked[...]
-
-    def scores(t, top):
-        at = pl.ds(pl.multiple_of(t * rows, rows), rows)
-        s = lax.dot_general(kv_ref[at, :], queries, NT, preferred_element_type=F32) + bias[at, :]
-        held[at, :] = s
-        return jnp.maximum(top, jnp.max(s.reshape(rows // 8, 8, wide), axis=0))
-
-    top = lax.fori_loop(first, last, scores, jnp.full((8, wide), BIG, F32))
-    top = jnp.max(top, axis=0, keepdims=True)
-    mixing[...] = jnp.zeros(mixing.shape, F32)
-
-    def mix(t, total):
-        at = pl.ds(pl.multiple_of(t * rows, rows), rows)
-        p = jnp.exp(held[at, :] - top)
-        mixing[...] += lax.dot_general(
-            kv_ref[at, :], p.astype(BF), TN, preferred_element_type=F32
-        )
-        return total + jnp.sum(p.reshape(rows // 8, 8, wide), axis=0)
-
-    total = lax.fori_loop(first, last, mix, jnp.zeros((8, wide), F32))
-    total = jnp.sum(total, axis=0, keepdims=True)
-    stat_ref[0] = jnp.broadcast_to(top + jnp.log(total), (8, wide))
-    out = jnp.transpose(mixing[...] / total)
-    for j in range(SHARES):
-        heads[group * SHARES + j] = out[j * rows:(j + 1) * rows, :]
-
-    @pl.when(group == KV_HEADS - 1)
-    def _():
-        for j in range(CHUNKS):
-            even = pltpu.roll(heads[2 * j], HD, 1)
-            odd = heads[2 * j + 1] if 2 * j + 1 < HEADS else jnp.zeros((rows, LANES), F32)
-            both = jnp.where(low, even, odd)
-            out_ref[j] = both
-            size = min(LANES, HEADS * HD - j * LANES)
-            mixed_ref[:, j * LANES:j * LANES + size] = both.astype(BF)[:, :size]
+    lax.fori_loop(span[0], span[1], body, 0)
+    for h in range(KV_HEADS):
+        total = jnp.sum(sums[h], axis=0, keepdims=True)
+        stat_ref[h] = tops[h] + jnp.log(total)
+        mixing[h] = mixing[h] / total
+    for j in range(CHUNKS):
+        both = head_pair(mixing, j, rows)
+        out_ref[j] = both
+        size = min(LANES, HEADS * HD - j * LANES)
+        mixed_ref[:, j * LANES:j * LANES + size] = both.astype(BF)[:, :size]
+
+
+def block_bias(keys, query_ref):
+    live, order = keys[:, 0:1], keys[:, 1:2]
+    begin, place = query_ref[0:1, :], query_ref[1:2, :]
+    allowed = ((live >= begin) & (live <= place)) | (order == place)
+    return jnp.where(allowed, 0.0, BIG)
+
+
+def head_pair(mixing, j, rows):
+    def one(head):
+        if head >= HEADS:
+            return jnp.zeros((HD, rows), F32)
+        at = head % SHARES * rows
+        return mixing[head // SHARES, :, at:at + rows]
+
+    return jnp.transpose(jnp.concatenate([one(2 * j), one(2 * j + 1)], axis=0))
 
 
 def attend(rows, span, key_labels, query_labels, kv_all, q):
-    count = kv_all.shape[0]
+    count, columns = kv_all.shape
     wide = SHARES * rows
     return pl.pallas_call(
         functools.partial(attend_kernel, rows),
         grid_spec=pltpu.PrefetchScalarGridSpec(
             num_scalar_prefetch=1,
-            grid=(KV_HEADS,),
+            grid=(1,),
             in_specs=[
-                whole(count, 8),
-                whole(8, wide),
-                pl.BlockSpec((count, LANES), lambda h, s: (0, h)),
+                whole(count, 8), whole(8, wide), whole(count, columns),
                 whole(CHUNKS, rows, LANES),
             ],
             out_specs=[
-                whole(rows, HEADS * HD),
-                whole(CHUNKS, rows, LANES),
-                pl.BlockSpec((1, 8, wide), lambda h, s: (h, 0, 0)),
+                whole(rows, HEADS * HD), whole(CHUNKS, rows, LANES), whole(KV_HEADS, 8, wide),
             ],
             scratch_shapes=[
-                pltpu.VMEM((count, wide), F32), pltpu.VMEM((count, wide), F32),
-                pltpu.VMEM((wide, LANES), BF), pltpu.VMEM((LANES, wide), F32),
-                pltpu.VMEM((HEADS, rows, LANES), F32),
+                pltpu.VMEM((KV_HEADS, wide, LANES), BF), pltpu.VMEM((KV_HEADS, HD, wide), F32),
+                pltpu.VMEM((KV_HEADS, 8, wide), F32), pltpu.VMEM((KV_HEADS, 8, wide), F32),
             ],
         ),
         out_shape=[
@@ -1007,100 +1020,79 @@
 
 
 def attend_back_kernel(rows, span, key_ref, query_ref, kv_ref, q_ref, d_ref, out_ref, stat_ref,
-                       turn_ref, dq_ref, dkv_ref, bias, stacked, part, mixing, heads):
-    first, last = span[0], span[1]
-    group = pl.program_id(0)
-
-    @pl.when(group == 0)
-    def _():
-        fill_bias(bias, key_ref, query_ref, rows, first, last)
-
+                       turn_ref, dq_ref, dkv_ref, stacked, part, mixing, deltas):
     low = lanes_of(rows) < HD
-    for j in range(SHARES):
-        head = group * SHARES + j
-        odd = lax.rem(head, 2) == 1
-        mine = low != odd
-        q = q_ref[head // 2].astype(F32)
-        d = d_ref[head // 2].astype(F32)
-        q_low = jnp.where(odd, pltpu.roll(q, HD, 1), q)
-        d_high = jnp.where(odd, d, pltpu.roll(d, HD, 1))
-        at = pl.ds(j * rows, rows)
-        stacked[at, :] = jnp.where(low, q_low, d_high).astype(BF)
-        part[at, :] = jnp.where(mine, d * out_ref[head // 2], 0.0)
-    wide = stacked.shape[0]
-    queries = stacked[...]
+    wide = SHARES * rows
     ones = jnp.ones((8, LANES), BF)
-    coarse = part[...].astype(BF)
-    fine = (part[...] - coarse.astype(F32)).astype(BF)
-    delta = lax.dot_general(ones, coarse, NT, preferred_element_type=F32)
-    delta += lax.dot_general(ones, fine, NT, preferred_element_type=F32)
-    delta = delta[0:1, :]
-    stat = stat_ref[0, 0:1, :]
+    for h in range(KV_HEADS):
+        for j in range(SHARES):
+            head = h * SHARES + j
+            q = q_ref[head // 2].astype(F32)
+            d = d_ref[head // 2].astype(F32)
+            if head % 2:
+                q = pltpu.roll(q, HD, 1)
+            product = d * out_ref[head // 2]
+            mine = ~low if head % 2 else low
+            if head % 2 == 0:
+                d = pltpu.roll(d, HD, 1)
+            at = pl.ds(j * rows, rows)
+            stacked[h, at, :] = jnp.where(low, q, d).astype(BF)
+            part[at, :] = jnp.where(mine, product, 0.0)
+        coarse = part[...].astype(BF)
+        fine = (part[...] - coarse.astype(F32)).astype(BF)
+        deltas[h] = lax.dot_general(
+            ones, coarse, NT, preferred_element_type=F32
+        ) + lax.dot_general(ones, fine, NT, preferred_element_type=F32)
     dkv_ref[...] = jnp.zeros(dkv_ref.shape, BF)
     mixing[...] = jnp.zeros(mixing.shape, F32)
 
     def body(t, carry):
         at = pl.ds(pl.multiple_of(t * rows, rows), rows)
-        kv = kv_ref[at, :]
-        zero = jnp.zeros_like(kv)
-        s = lax.dot_general(jnp.where(low, kv, zero), queries, NT, preferred_element_type=F32)
-        p = jnp.exp(s + bias[at, :] - stat)
-        dp = lax.dot_general(jnp.where(low, zero, kv), queries, NT, preferred_element_type=F32)
-        ds = (p * (dp - delta)).astype(BF)
-        dk = jnp.dot(ds, queries, preferred_element_type=F32)
-        dv = jnp.dot(p.astype(BF), queries, preferred_element_type=F32)
-        dkv_ref[at, :] = jnp.where(low, dk, dv).astype(BF)
-        mixing[...] += lax.dot_general(kv, ds, TN, preferred_element_type=F32)
+        bias = block_bias(key_ref[at, :], query_ref)
+        for h in range(KV_HEADS):
+            kv = kv_ref[at, h * LANES:(h + 1) * LANES]
+            zero = jnp.zeros_like(kv)
+            queries = stacked[h]
+            s = lax.dot_general(jnp.where(low, kv, zero), queries, NT, preferred_element_type=F32)
+            p = jnp.exp(s + bias - stat_ref[h, 0:1, :])
+            dp = lax.dot_general(jnp.where(low, zero, kv), queries, NT, preferred_element_type=F32)
+            ds = (p * (dp - deltas[h, 0:1, :])).astype(BF)
+            dk = jnp.dot(ds, queries, preferred_element_type=F32)
+            dv = jnp.dot(p.astype(BF), queries, preferred_element_type=F32)
+            dkv_ref[at, h * LANES:(h + 1) * LANES] = jnp.where(low, dk, dv).astype(BF)
+            mixing[h] += lax.dot_general(kv[:, :HD], ds, TN, preferred_element_type=F32)
         return carry
 
-    lax.fori_loop(first, last, body, 0)
-    back = jnp.transpose(mixing[...])
-    for j in range(SHARES):
-        heads[group * SHARES + j] = back[j * rows:(j + 1) * rows, :]
-
-    @pl.when(group == KV_HEADS - 1)
-    def _():
-        cosine, sine = turn_ref[0], turn_ref[1]
-        for j in range(CHUNKS):
-            odd = jnp.zeros((rows, LANES), F32)
-            if 2 * j + 1 < HEADS:
-                odd = pltpu.roll(heads[2 * j + 1], HD, 1)
-            both = jnp.where(low, heads[2 * j], odd) * HD ** -0.5
-            both = both * cosine - spin(both) * sine
-            dq_ref[:, j * LANES:(j + 1) * LANES] = both.astype(BF)
+    lax.fori_loop(span[0], span[1], body, 0)
+    cosine, sine = turn_ref[0], turn_ref[1]
+    for j in range(CHUNKS):
+        both = head_pair(mixing, j, rows) * HD ** -0.5
+        both = both * cosine - spin(both) * sine
+        dq_ref[:, j * LANES:(j + 1) * LANES] = both.astype(BF)
 
 
 def attend_back(rows, span, key_labels, query_labels, kv_all, q, d_mixed, out, stat, turns):
-    count = kv_all.shape[0]
+    count, columns = kv_all.shape
     wide = SHARES * rows
     return pl.pallas_call(
         functools.partial(attend_back_kernel, rows),
         grid_spec=pltpu.PrefetchScalarGridSpec(
             num_scalar_prefetch=1,
-            grid=(KV_HEADS,),
+            grid=(1,),
             in_specs=[
-                whole(count, 8),
-                whole(8, wide),
-                pl.BlockSpec((count, LANES), lambda h, s: (0, h)),
-                whole(CHUNKS, rows, LANES),
-                whole(CHUNKS, rows, LANES),
-                whole(CHUNKS, rows, LANES),
-                pl.BlockSpec((1, 8, wide), lambda h, s: (h, 0, 0)),
-                whole(*turns.shape),
+                whole(count, 8), whole(8, wide), whole(count, columns),
+                whole(CHUNKS, rows, LANES), whole(CHUNKS, rows, LANES),
+                whole(CHUNKS, rows, LANES), whole(KV_HEADS, 8, wide), whole(*turns.shape),
             ],
-            out_specs=[
-                whole(rows, CHUNKS * LANES),
-                pl.BlockSpec((count, LANES), lambda h, s: (0, h)),
-            ],
+            out_specs=[whole(rows, CHUNKS * LANES), whole(count, columns)],
             scratch_shapes=[
-                pltpu.VMEM((count, wide), F32), pltpu.VMEM((wide, LANES), BF),
-                pltpu.VMEM((wide, LANES), F32), pltpu.VMEM((LANES, wide), F32),
-                pltpu.VMEM((HEADS, rows, LANES), F32),
+                pltpu.VMEM((KV_HEADS, wide, LANES), BF), pltpu.VMEM((wide, LANES), F32),
+                pltpu.VMEM((KV_HEADS, HD, wide), F32), pltpu.VMEM((KV_HEADS, 8, wide), F32),
             ],
         ),
         out_shape=[
             jax.ShapeDtypeStruct((rows, CHUNKS * LANES), BF),
-            jax.ShapeDtypeStruct((count, KV_HEADS * LANES), BF),
+            jax.ShapeDtypeStruct((count, columns), BF),
         ],
         compiler_params=pltpu.CompilerParams(vmem_limit_bytes=62 << 20),
         name="attend_back",
@@ -1295,16 +1287,12 @@
     swap = topo.swap_pairs()
     state = lax.ppermute(mm(onehot, tokens).astype(BF), AXES, swap).astype(F32)
     labels = lax.ppermute(labels, AXES, swap)
-    gradient, weight_qkv = lax.optimization_barrier(
-        (mm(onehot, cotangent).astype(BF), weight_qkv)
-    )
-    gradient = lax.ppermute(gradient, AXES, swap).astype(F32)
-    order_g = xk + yk + ck
+    cotangent = mm(onehot, cotangent).astype(BF)
 
     def collect(arrays, ident):
         if small_layer(topo):
             return gather_layer(topo, arrays, ident)
-        return [group_gather(topo, v, order_g) for v in arrays]
+        return [group_gather(topo, v, xk + yk + ck) for v in arrays]
 
     def distribute(grads, ident):
         if small_layer(topo):
@@ -1327,9 +1315,12 @@
 
     def forward(state, recursion, labels_all=None):
         n = state.shape[0]
+        extra = None
         n1, q, kv = project(state, gain_one, weight_qkv, turns[:, :n])
         if recursion == 0:
             kv_all, labels_all = collect([kv, labels], 2)
+            kv_all, later = lax.optimization_barrier((kv_all, cotangent))
+            extra = (labels_all, lax.ppermute(later, AXES, swap).astype(F32))
         else:
             kv_all, = collect([kv], 3)
         kv_all = kv_all.reshape(topo.T * n, 2 * kv_cols)
@@ -1352,7 +1343,7 @@
         new = state + active * gate * both
         kept = (state, n1, q, kv_all, key_labels, query_labels, out, stat, mixed, middle,
                 inv_two, n2, gated, upward, hidden, both, gate, active)
-        return (new, kept, labels_all)
+        return (new, kept, extra)
 
     def backward(gradient, recursion, kept):
         (state, n1, q, kv_all, key_labels, query_labels, out, stat, mixed, middle,
@@ -1381,7 +1372,7 @@
         left = (n1, dq, dkv, mixed, d_att, n2, d_gated, d_up, hidden, d_fed)
         return (gradient, left, (d_router, d_gain_one[0], d_gain_two))
 
-    whole_state, kept, labels_all = forward(state, 0)
+    whole_state, kept, (labels_all, gradient) = forward(state, 0)
     deep = whole_state[:deep_rows]
     all_kept = [kept]
     for recursion in range(1, RECS):
@@ -1417,9 +1408,9 @@
     wide_out = -(-(model + tiny.shape[1]) // 256) * 256
     tiny = jnp.pad(tiny, ((0, 0), (0, wide_out - model - tiny.shape[1])))
     grad_qkv, grad_o, grad_gu, grad_down = reduce_gradients(topo, [
-        cut(mm_tn(n1, dqkv)),
+        cut(outer_columns(n1, [dqkv], 256)[0]),
         cut(jnp.concatenate([mm_tn(mixed, d_att), tiny], axis=1)),
-        outer_columns(n2, [d_gated, d_up], 640).reshape(2, topo.T, -1, ff),
+        outer_columns(n2, [d_gated, d_up], 512).reshape(2, topo.T, -1, ff),
         outer_rows(hidden, d_fed, 640).reshape(topo.T, -1, model),
     ])
     grad_query = grad_qkv[:, :model].astype(F32)

time: 696 us -> 661 us (0.950)
  Pallas kernels: 502 us -> 469 us
  starting transfers between devices: 35.5 us -> 16.3 us
  waiting for transfers between devices: 0.01 us -> 15.6 us
  matrix products: 79.8 us -> 70.5 us
    ppermute x1, starting transfers between devices: 25.2 us -> 5.81 us  [per_device(): final = lax.ppermute(final, AXES, swap)]
    ppermute x1, waiting for transfers between devices: 0.01 us -> 15.6 us  [forward(): extra = (labels_all, lax.ppermute(later, AXES, swap).astype(F32))]
    pallas_call x3, Pallas kernels: 41.4 us -> 27.6 us  [attend(): pl.pallas_call(functools.partial(attend_kernel, rows), grid_spec=pltpu.Pr...]
    pallas_call x1, Pallas kernels: 126 us -> 113 us  [reduce_gradients(): pl.pallas_call(functools.partial(reduce_kernel, topo, shares), in_specs=[...]
    dot_general x4 -> x3, matrix products: 17.3 us -> 7.49 us  [mm_tn(): return lax.dot_general(a, b, TN, preferred_element_type=F32)]
    pallas_call x3, Pallas kernels: 50.3 us -> 40.5 us  [attend_back(): pl.pallas_call(functools.partial(attend_back_kernel, rows), grid_spec=plt...]
    pallas_call x1 -> x2, Pallas kernels: 14.7 us -> 23.1 us  [outer_columns(): pl.pallas_call(functools.partial(outer_columns_kernel, count), grid=(coun...]
  transfers between devices with their start and end apart: 5 -> 5, of which waited for: 0 -> 1; matrix products, arithmetic and copies ran while one was open for 11% -> 5% of each run, Pallas kernels for 53% -> 38%
where the time goes in v5:
time: 661 us; the launch traced here: 649 us
  Pallas kernels  469 us (71%)
  matrix products  70.5 us (11%)
  other arithmetic  44.4 us (7%)
  local copies, waits for them, and re-layouts  27.8 us (4%)
  starting transfers between devices  16.3 us (2%)
  waiting for transfers between devices  15.6 us (2%)
    pallas_call x1, Pallas kernels, reduce_gradients(): pl.pallas_call(functools.partial(reduce_kernel, topo, shares), in_specs=[...  113 us
    pallas_call x1, Pallas kernels, gather_weights(): pl.pallas_call(functools.partial(gather_kernel, topo, pieces), in_specs=[...  103 us
    pallas_call x3, Pallas kernels, gather_layer(): pl.pallas_call(functools.partial(group_gather_kernel, topo, n), in_specs=...  58.3 us
    pallas_call x3, Pallas kernels, reduce_layer(): pl.pallas_call(functools.partial(group_reduce_kernel, topo), in_specs=[pl...  57.5 us
    pallas_call x3, Pallas kernels, attend_back(): pl.pallas_call(functools.partial(attend_back_kernel, rows), grid_spec=plt...  40.5 us
    dot_general x15, matrix products, mm(): return jnp.dot(a, b, preferred_element_type=F32)  33.8 us
    dot_general x9, matrix products, mm_nt(): return lax.dot_general(a, b, NT, preferred_element_type=F32)  29.1 us
    pallas_call x3, Pallas kernels, attend(): pl.pallas_call(functools.partial(attend_kernel, rows), grid_spec=pltpu.Pr...  27.6 us
  transfers between devices with their start and end apart: 5, of which 1 were waited for; matrix products, arithmetic and copies ran while one was open for 5% of the time, Pallas kernels for 38%

profile of v5, /device:TPU:17, one launch (start us, length us, event | category | flops | bytes accessed | tf_op | source)
XLA Modules:
  0.0 648.9 jit_solution(6079697280438422627)
XLA Ops:
  16.5 102.7 %gather_weights.1 = (bf16[8,120,1664]{2,1,0:T(8,128)(2,1)}, bf16[8,120,2560]{2,1,0:T(8,128)(2,1)}, bf16[8,120,2560]{2,1,0:T(8,128)(2,1)}, bf16[8,320,960]{2,1,0:T(8,128)(2,1)}, bf16[8,120,960]{2,1,0:T(8,128)(2,1)}) custom-call(bf16[120,1664]{1,0:T(8,128)(2,1)} %concatenate.59.refs_0_, bf16[120,2560]{1,0:T(8,128)(2,1)} %refs_1_.1, bf16[120,2560]{1,0:T(8,128)(2,1)} %refs_2_.1, ...), custom_call_target="tpu_custom_call" | custom-call | tf_op jit(solution)/shard_map/gather_weights/pallas_call | solution.py:298
  129.5 4.4 project.3
  133.9 20.1 %gather_layer.3 = (bf16[8,256,640]{2,1,0:T(8,128)(2,1)}, s32[8,8,256]{2,1,0:T(8,128)}) custom-call(bf16[256,640]{1,0:T(8,128)(2,1)} %get-tuple-element.61.refs_0_, s32[8,256]{1,0:T(8,128)} %copy-done.69), custom_call_target="tpu_custom_call" | custom-call | tf_op jit(solution)/shard_map/gather_layer/pallas_call | solution.py:768
  158.9 11.0 %attend.3 = (bf16[256,960]{1,0:T(8,128)(2,1)}, f32[8,256,128]{2,1,0:T(8,128)}, f32[5,8,768]{2,1,0:T(8,128)}) custom-call(s32[2]{0:T(128)} %pad_add_fusion.6.span, s32[2048,8]{1,0:T(8,128)} %pad.39.key_ref, s32[8,768]{1,0:T(8,128)} %pad.40.query_ref, bf16[2048,640]{1,0:T(8,128)(2,1)} %bitcast.157, bf16[8,256,128]{2,1,0:T(8,128)(2,1)} %get-tuple-element.65.q_ref), custom_call_target="tpu_custom_call" | custom-call | tf_op jit(solution)/shard_map/attend/pallas_call | solution.py:995
  173.0 4.7 fusion.39
  188.4 4.0 project.4
  192.3 21.2 %gather_layer.4 = bf16[8,192,640]{2,1,0:T(8,128)(2,1)} custom-call(bf16[192,640]{1,0:T(8,128)(2,1)} %get-tuple-element.71.refs_0_), custom_call_target="tpu_custom_call" | custom-call | tf_op jit(solution)/shard_map/gather_layer/pallas_call | solution.py:768
  213.5 8.5 %attend.4 = (bf16[192,960]{1,0:T(8,128)(2,1)}, f32[8,192,128]{2,1,0:T(8,128)}, f32[5,8,576]{2,1,0:T(8,128)}) custom-call(s32[2]{0:T(128)} %pad_add_fusion.6.span, s32[1536,8]{1,0:T(8,128)} %pad.41.key_ref, s32[8,576]{1,0:T(8,128)} %pad.42.query_ref, bf16[1536,640]{1,0:T(8,128)(2,1)} %bitcast.141, bf16[8,192,128]{2,1,0:T(8,128)(2,1)} %get-tuple-element.72.q_ref), custom_call_target="tpu_custom_call" | custom-call | tf_op jit(solution)/shard_map/attend/pallas_call | solution.py:995
  234.2 4.0 project.5
  238.2 17.0 %gather_layer.5 = bf16[8,192,640]{2,1,0:T(8,128)(2,1)} custom-call(bf16[192,640]{1,0:T(8,128)(2,1)} %get-tuple-element.74.refs_0_), custom_call_target="tpu_custom_call" | custom-call | tf_op jit(solution)/shard_map/gather_layer/pallas_call | solution.py:768
  255.2 8.1 %attend.5 = (bf16[192,960]{1,0:T(8,128)(2,1)}, f32[8,192,128]{2,1,0:T(8,128)}, f32[5,8,576]{2,1,0:T(8,128)}) custom-call(s32[2]{0:T(128)} %pad_add_fusion.6.span, s32[1536,8]{1,0:T(8,128)} %pad.43.key_ref, s32[8,576]{1,0:T(8,128)} %pad.42.query_ref, bf16[1536,640]{1,0:T(8,128)(2,1)} %bitcast.143, bf16[8,192,128]{2,1,0:T(8,128)(2,1)} %get-tuple-element.75.q_ref), custom_call_target="tpu_custom_call" | custom-call | tf_op jit(solution)/shard_map/attend/pallas_call | solution.py:995
  266.9 4.3 fusion.42
  275.7 15.6 %collective-permute-done.2 = bf16[256,960]{1,0:T(8,128)(2,1)S(1)} collective-permute-done((bf16[256,960]{1,0:T(8,128)(2,1)S(1)}, bf16[256,960]{1,0:T(8,128)(2,1)S(1)}, u32[]{:S(2)}, u32[]{:S(2)}) %collective-permute-start.2) | collective-permute-done | bytes 491552 | tf_op jit(solution)/shard_map/ppermute | solution.py:1323
  306.0 12.7 %attend_back.3 = (bf16[192,1024]{1,0:T(8,128)(2,1)}, bf16[1536,640]{1,0:T(8,128)(2,1)}) custom-call(s32[2]{0:T(128)} %pad_add_fusion.6.span, s32[1536,8]{1,0:T(8,128)} %pad.43.key_ref, s32[8,576]{1,0:T(8,128)} %pad.42.query_ref, bf16[1536,640]{1,0:T(8,128)(2,1)} %bitcast.144, bf16[8,192,128]{2,1,0:T(8,128)(2,1)} %get-tuple-element.75.q_ref, ...), custom_call_target="tpu_custom_call" | custom-call | tf_op jit(solution)/shard_map/attend_back/pallas_call | solution.py:1077
  320.2 13.8 %reduce_layer.3.raw_ref = bf16[192,640]{1,0:T(8,128)(2,1)S(1)} custom-call(bf16[8,192,640]{2,1,0:T(8,128)(2,1)S(1)} %bitcast.103), custom_call_target="tpu_custom_call" | custom-call | tf_op jit(solution)/shard_map/reduce_layer/pallas_call | solution.py:838
  334.7 5.0 project_back.3
  341.1 5.5 multiply_convert_fusion.3
  348.4 4.3 multiply_reduce_fusion.6
  357.6 12.9 %attend_back.4 = (bf16[192,1024]{1,0:T(8,128)(2,1)}, bf16[1536,640]{1,0:T(8,128)(2,1)}) custom-call(s32[2]{0:T(128)} %pad_add_fusion.6.span, s32[1536,8]{1,0:T(8,128)} %pad.41.key_ref, s32[8,576]{1,0:T(8,128)} %pad.42.query_ref, bf16[1536,640]{1,0:T(8,128)(2,1)} %bitcast.142, bf16[8,192,128]{2,1,0:T(8,128)(2,1)} %get-tuple-element.72.q_ref, ...), custom_call_target="tpu_custom_call" | custom-call | tf_op jit(solution)/shard_map/attend_back/pallas_call | solution.py:1077
  372.0 20.3 %reduce_layer.4.raw_ref = bf16[192,640]{1,0:T(8,128)(2,1)S(1)} custom-call(bf16[8,192,640]{2,1,0:T(8,128)(2,1)S(1)} %bitcast.102), custom_call_target="tpu_custom_call" | custom-call | tf_op jit(solution)/shard_map/reduce_layer/pallas_call | solution.py:838
  393.0 5.0 project_back.4
  400.0 5.9 multiply_convert_fusion
  407.9 4.3 multiply_reduce_fusion
  425.6 14.9 %attend_back.5 = (bf16[256,1024]{1,0:T(8,128)(2,1)}, bf16[2048,640]{1,0:T(8,128)(2,1)}) custom-call(s32[2]{0:T(128)} %pad_add_fusion.6.span, s32[2048,8]{1,0:T(8,128)} %pad.39.key_ref, s32[8,768]{1,0:T(8,128)} %pad.40.query_ref, bf16[2048,640]{1,0:T(8,128)(2,1)} %bitcast.158, bf16[8,256,128]{2,1,0:T(8,128)(2,1)} %get-tuple-element.65.q_ref, ...), custom_call_target="tpu_custom_call" | custom-call | tf_op jit(solution)/shard_map/attend_back/pallas_call | solution.py:1077
  442.2 23.4 %reduce_layer.5.raw_ref = bf16[256,640]{1,0:T(8,128)(2,1)S(1)} custom-call(bf16[8,256,640]{2,1,0:T(8,128)(2,1)S(1)} %bitcast.101), custom_call_target="tpu_custom_call" | custom-call | tf_op jit(solution)/shard_map/reduce_layer/pallas_call | solution.py:838
  466.3 5.3 project_back.5
  476.7 5.8 collective-permute-start.3
  484.4 5.0 fusion.8.refs_0_
  489.5 8.4 %outer_columns.2 = bf16[1,960,1792]{2,1,0:T(8,128)(2,1)} custom-call(bf16[640,960]{1,0:T(8,128)(2,1)} %pad_maximum_fusion.4.x_ref, bf16[640,1792]{1,0:T(8,128)(2,1)} %fusion.8.refs_0_), custom_call_target="tpu_custom_call" | custom-call | flops 2202009600 | bytes 6963200 | tf_op jit(solution)/shard_map/outer_columns/pallas_call | solution.py:1189
  499.5 8.0 %outer_rows.1 = bf16[2560,960]{1,0:T(8,128)(2,1)} custom-call(bf16[640,2560]{1,0:T(8,128)(2,1)} %pad_maximum_fusion.2.x_ref, bf16[640,960]{1,0:T(8,128)(2,1)} %pad_maximum_fusion.6.d_ref), custom_call_target="tpu_custom_call" | custom-call | flops 3145728000 | bytes 9420800 | tf_op jit(solution)/shard_map/outer_rows/pallas_call | solution.py:1214
  507.5 14.7 %outer_columns.3 = bf16[2,960,2560]{2,1,0:T(8,128)(2,1)} custom-call(bf16[640,960]{1,0:T(8,128)(2,1)} %pad_maximum_fusion.5.x_ref, bf16[640,2560]{1,0:T(8,128)(2,1)} %get-tuple-element.255.refs_0_, bf16[640,2560]{1,0:T(8,128)(2,1)} %get-tuple-element.256.refs_1_), custom_call_target="tpu_custom_call" | custom-call | flops 6291456000 | bytes 17612800 | tf_op jit(solution)/shard_map/outer_columns/pallas_call | solution.py:1189
  522.2 113.4 %reduce_gradients.1 = (bf16[120,1792]{1,0:T(8,128)(2,1)}, bf16[120,1024]{1,0:T(8,128)(2,1)}, bf16[2,120,2560]{2,1,0:T(8,128)(2,1)}, bf16[320,960]{1,0:T(8,128)(2,1)}) custom-call(bf16[8,120,1792]{2,1,0:T(8,128)(2,1)} %bitcast.161, bf16[8,120,1024]{2,1,0:T(8,128)(2,1)} %pad_maximum_fusion.3.refs_1_, bf16[2,8,120,2560]{3,2,1,0:T(8,128)(2,1)} %bitcast.159, ...), custom_call_target="tpu_custom_call" | custom-call | tf_op jit(solution)/shard_map/reduce_gradients/pallas_call | solution.py:632
  (343 shorter events, 129.9 us)
Async XLA Ops:
  0.6 8.4 %copy-start = (bf16[256,960]{0,1:T(8,128)(2,1)S(1)}, bf16[256,960]{0,1:T(8,128)(2,1)}, u32[]{:S(2)}) copy-start(bf16[256,960]{0,1:T(8,128)(2,1)} %param.15) | copy-start | bytes 1474564
  0.7 13.8 %copy-start.63 = (bf16[256,960]{0,1:T(8,128)(2,1)S(1)}, bf16[256,960]{0,1:T(8,128)(2,1)}, u32[]{:S(2)}) copy-start(bf16[256,960]{0,1:T(8,128)(2,1)} %param.29) | copy-start | bytes 1474564
  0.7 15.0 %copy-start.68 = (bf16[120,960]{1,0:T(8,128)(2,1)S(1)}, bf16[120,960]{1,0:T(8,128)(2,1)}, u32[]{:S(2)}) copy-start(bf16[120,960]{1,0:T(8,128)(2,1)} %param.16) | copy-start | bytes 691204
  5.5 116.6 %collective-permute-start.1 = (s32[8,256]{1,0:T(8,128)S(1)}, s32[8,256]{1,0:T(8,128)S(1)}, u32[]{:S(2)}, u32[]{:S(2)}) collective-permute-start(s32[8,256]{1,0:T(8,128)S(1)} %pad.37), channel_id=1, source_target_pairs={{0,0},{1,1},{2,8},{3,9},{4,16},{5,17},{6,24},{7,25},{8,2},{9,3},{1... | collective-permute-start | bytes 24584 | tf_op jit(solution)/shard_map/ppermute | solution.py:1289
  9.6 118.8 %collective-permute-start = (bf16[256,960]{1,0:T(8,128)(2,1)S(1)}, bf16[256,960]{1,0:T(8,128)(2,1)S(1)}, u32[]{:S(2)}, u32[]{:S(2)}) collective-permute-start(bf16[256,960]{1,0:T(8,128)(2,1)S(1)} %copy.113), channel_id=1, source_target_pairs={{0,0},{1,1},{2,8},{3,9},{4,16},{5,17},{6,24},{7,25},{8,2},{9,3},{1... | collective-permute-start | bytes 1474568 | tf_op jit(solution)/shard_map/ppermute | solution.py:1288
  122.1 11.9 %copy-start.69 = (s32[8,256]{1,0:T(8,128)}, s32[8,256]{1,0:T(8,128)S(1)}, u32[]{:S(2)}) copy-start(s32[8,256]{1,0:T(8,128)S(1)} %collective-permute-done.1.refs_1_) | copy-start | bytes 24580
  128.4 43.7 %copy-start.73 = (pred[256]{0:T(512)(128)(4,1)}, pred[256]{0:T(512)(128)(4,1)S(1)}, u32[]{:S(2)}) copy-start(pred[256]{0:T(512)(128)(4,1)S(1)} %compare_reduce_fusion.4) | copy-start | bytes 772
  158.9 11.0 %copy-start.8 = (bf16[8,120,960]{2,1,0:T(8,128)(2,1)S(1)}, bf16[8,120,960]{2,1,0:T(8,128)(2,1)}, u32[]{:S(2)}) copy-start(bf16[8,120,960]{2,1,0:T(8,128)(2,1)} %get-tuple-element.67) | copy-start | bytes 5529604
  172.1 5.7 slice-start.12
  173.0 8.0 %slice-start.6 = ((s8[5242880]{0:T(1024)(128)(4,1)}), s8[4194304]{0:T(1024)(128)(4,1)S(1)}, s32[]{:S(2)}) async-start(s8[5242880]{0:T(1024)(128)(4,1)} %bitcast.131), calls=%async_computation.6 | async-start | bytes 8388608
  222.0 7.0 %slice-start.14 = ((s8[4915200]{0:T(1024)(128)(4,1)}), s8[4194304]{0:T(1024)(128)(4,1)S(1)}, s32[]{:S(2)}) async-start(s8[4915200]{0:T(1024)(128)(4,1)} %bitcast.151), calls=%async_computation.14 | async-start | bytes 8388608
  225.2 6.4 slice-start.8
  265.5 9.0 %slice-start = ((s8[4915200]{0:T(1024)(128)(4,1)}), s8[4194304]{0:T(1024)(128)(4,1)S(1)}, s32[]{:S(2)}) async-start(s8[4915200]{0:T(1024)(128)(4,1)} %bitcast.119), calls=%async_computation | async-start | bytes 8388608
  266.8 6.4 copy-start.60
  266.8 6.4 copy-start.64
  266.8 6.4 copy-start.65
  266.9 7.7 %slice-start.1 = ((s8[4915200]{0:T(1024)(128)(4,1)}), s8[720896]{0:T(1024)(128)(4,1)S(1)}, s32[]{:S(2)}) async-start(s8[4915200]{0:T(1024)(128)(4,1)} %bitcast.119), calls=%async_computation.1 | async-start | bytes 1441792
  271.1 20.2 %collective-permute-start.2 = (bf16[256,960]{1,0:T(8,128)(2,1)S(1)}, bf16[256,960]{1,0:T(8,128)(2,1)S(1)}, u32[]{:S(2)}, u32[]{:S(2)}) collective-permute-start(bf16[256,960]{1,0:T(8,128)(2,1)S(1)} %copy-done.61), channel_id=1, source_target_pairs={{0,0},{1,1},{2,8},{3,9},{4,16},{5,17},{6,24},{7,25},{8,2},{9,3},{1... | collective-permute-start | bytes 1474568 | tf_op jit(solution)/shard_map/ppermute | solution.py:1323
  273.3 18.2 %slice-start.10 = ((s8[5242880]{0:T(1024)(128)(4,1)}), s8[4194304]{0:T(1024)(128)(4,1)S(1)}, s32[]{:S(2)}) async-start(s8[5242880]{0:T(1024)(128)(4,1)} %bitcast.137), calls=%async_computation.10 | async-start | bytes 8388608
  274.5 17.0 %slice-start.11 = ((s8[5242880]{0:T(1024)(128)(4,1)}), s8[1048576]{0:T(1024)(128)(4,1)S(1)}, s32[]{:S(2)}) async-start(s8[5242880]{0:T(1024)(128)(4,1)} %bitcast.137), calls=%async_computation.11 | async-start | bytes 2097152
  334.7 6.4 copy-start.33
  334.7 11.9 %slice-start.2 = ((s8[4915200]{0:T(1024)(128)(4,1)}), s8[720896]{0:T(1024)(128)(4,1)S(1)}, s32[]{:S(2)}) async-start(s8[4915200]{0:T(1024)(128)(4,1)} %bitcast.123), calls=%async_computation.2 | async-start | bytes 1441792
  393.0 12.8 %slice-start.4 = ((s8[4915200]{0:T(1024)(128)(4,1)}), s8[720896]{0:T(1024)(128)(4,1)S(1)}, s32[]{:S(2)}) async-start(s8[4915200]{0:T(1024)(128)(4,1)} %bitcast.126), calls=%async_computation.4 | async-start | bytes 1441792
  400.0 5.9 slice-start.5
  466.3 7.5 %copy-start.36 = (bf16[192,960]{1,0:T(8,128)(2,1)S(1)}, bf16[192,960]{1,0:T(8,128)(2,1)}, u32[]{:S(2)}) copy-start(bf16[192,960]{1,0:T(8,128)(2,1)} %get-tuple-element.214) | copy-start | bytes 1105924
  466.3 7.5 %copy-start.62 = (bf16[64,960]{1,0:T(8,128)(2,1)S(1)}, bf16[64,960]{1,0:T(8,128)(2,1)}, u32[]{:S(2)}) copy-start(bf16[64,960]{1,0:T(8,128)(2,1)} %slice.219) | copy-start | bytes 368644
  471.6 12.8 %copy-start.30 = (bf16[256,1024]{1,0:T(8,128)(2,1)S(1)}, bf16[256,1024]{1,0:T(8,128)(2,1)}, u32[]{:S(2)}) copy-start(bf16[256,1024]{1,0:T(8,128)(2,1)} %get-tuple-element.90.dq_ref) | copy-start | bytes 1572868
  471.6 12.8 %copy-start.34 = (bf16[192,1024]{1,0:T(8,128)(2,1)S(1)}, bf16[192,1024]{1,0:T(8,128)(2,1)}, u32[]{:S(2)}) copy-start(bf16[192,1024]{1,0:T(8,128)(2,1)} %get-tuple-element.80.dq_ref) | copy-start | bytes 1179652
  471.6 12.8 %copy-start.35 = (bf16[192,1024]{1,0:T(8,128)(2,1)S(1)}, bf16[192,1024]{1,0:T(8,128)(2,1)}, u32[]{:S(2)}) copy-start(bf16[192,1024]{1,0:T(8,128)(2,1)} %get-tuple-element.85.dq_ref) | copy-start | bytes 1179652
  476.7 167.7 %collective-permute-start.3 = (bf16[256,960]{1,0:T(8,128)(2,1)}, bf16[256,960]{1,0:T(8,128)(2,1)}, u32[]{:S(2)}, u32[]{:S(2)}) collective-permute-start(bf16[256,960]{1,0:T(8,128)(2,1)} %pad_maximum_fusion.8), channel_id=1, source_target_pairs={{0,0},{1,1},{2,8},{3,9},{4,16},{5,17},{6,24},{7,25},{8,2},{9,3},{1... | collective-permute-start | bytes 1474568 | tf_op jit(solution)/shard_map/ppermute | solution.py:1394
  482.5 164.0 %collective-permute-start.4 = (bf16[256,960]{1,0:T(8,128)(2,1)}, bf16[256,960]{1,0:T(8,128)(2,1)}, u32[]{:S(2)}, u32[]{:S(2)}) collective-permute-start(bf16[256,960]{1,0:T(8,128)(2,1)} %convert_element_type.163), channel_id=1, source_target_pairs={{0,0},{1,1},{2,8},{3,9},{4,16},{5,17},{6,24},{7,25},{8,2},{9,3},{1... | collective-permute-start | bytes 1474568 | tf_op jit(solution)/shard_map/ppermute | solution.py:1395
  641.4 7.2 %copy-start.1 = (bf16[256,960]{0,1:T(8,128)(2,1)S(1)}, bf16[256,960]{0,1:T(8,128)(2,1)}, u32[]{:S(2)}) copy-start(bf16[256,960]{0,1:T(8,128)(2,1)} %param.15) | copy-start | bytes 1474564
  (68 other events, 210.6 us)

commit v6 on v5

--- a/solution.py
+++ b/solution.py
@@ -317,7 +317,7 @@
     def of(self, ref, core, *lead):
         rows, columns = self.shape
         if self.array == 2:
-            return ref.at[(core,) + lead + (slice(None), pl.ds(self.start, columns))]
+            return ref.at[lead + (slice(None), pl.ds(self.start, columns))]
         if self.array == 3:
             at = pl.multiple_of(core * rows, rows)
             return ref.at[lead + (pl.ds(at, rows), slice(None))]
@@ -326,7 +326,7 @@
 
 
 def cut_shares(shapes):
-    rows, ff = shapes[2][2], shapes[2][3]
+    rows, ff = shapes[2][1], shapes[2][2]
     one = ff * 3 // 20 // 128 * 128
     two = ff * 33 // 40 // 128 * 128
     return [
@@ -340,10 +340,10 @@
 
 
 def reduce_kernel(topo, shares, *refs):
-    grads, outs = refs[:4], refs[4:8]
+    grads, outs = refs[:5], refs[5:9]
     count = len(shares)
     groups = []
-    at = 8
+    at = 9
     for _ in range(7):
         groups.append(refs[at:at + count])
         at += count
@@ -382,11 +382,21 @@
     pl.when(above)(lambda: greet(over_z(1)))
     every = range(count)
 
-    def load(p, t):
-        s = shares[p]
+    def source(s, core, t, up):
+        place = {2: 4 if up else 2, 3: 3}.get(s.array, s.array)
+        return s.of(grads[place], core, t)
+
+    def load(p, t, up=False):
         return pltpu.make_async_copy(
-            s.of(grads[s.array], c, t), held[p].at[t], load_sem.at[p, t]
-        )
+            source(shares[p], c, t, up), held[p].at[t], load_sem.at[p, t]
+        )
+
+    def start(p, make, up_core):
+        if shares[p].array == 2:
+            pl.when(c != up_core)(lambda: make(False).start())
+            pl.when(c == up_core)(lambda: make(True).start())
+        else:
+            make(False).start()
 
     def remote(source, landing, send, recv, target):
         return pltpu.make_async_remote_copy(
@@ -394,10 +404,9 @@
             device_id_type=kind,
         )
 
-    def c_copy(p, t):
-        s = shares[p]
+    def c_copy(p, t, up=False):
         return remote(
-            s.of(grads[s.array], 1 - c, t), from_c[p].at[t], c_send.at[p, t], c_recv.at[p, t],
+            source(shares[p], 1 - c, t, up), from_c[p].at[t], c_send.at[p, t], c_recv.at[p, t],
             over_c,
         )
 
@@ -426,21 +435,26 @@
             held[p].at[me], from_f[p].at[k], f_send.at[p, k], f_recv.at[p, k], over_y(k)
         )
 
+    def result(s, core):
+        if s.array == 2:
+            return outs[2].at[core, :, pl.ds(s.start, s.shape[1])]
+        return s.of(outs[s.array], core)
+
     def o_copy(p):
         s = shares[p]
         return remote(
-            held[p].at[me], s.of(outs[s.array], c), o_send.at[p], o_recv.at[p], over_c
+            held[p].at[me], result(s, c), o_send.at[p], o_recv.at[p], over_c
         )
 
     def o_arrived(p):
         s = shares[p]
         return remote(
-            held[p].at[me], s.of(outs[s.array], 1 - c), o_send.at[p], o_recv.at[p], over_c
+            held[p].at[me], result(s, 1 - c), o_send.at[p], o_recv.at[p], over_c
         )
 
     def o_keep(p):
         s = shares[p]
-        return pltpu.make_async_copy(held[p].at[me], s.of(outs[s.array], c), o_local.at[p])
+        return pltpu.make_async_copy(held[p].at[me], result(s, c), o_local.at[p])
 
     def add(p, t, other):
         held[p][t] = held[p][t] + other
@@ -467,7 +481,7 @@
         def each(j, carry):
             t = zz * X + lax.rem(x + j, X)
             for p in every:
-                load(p, t).start()
+                start(p, lambda up, p=p: load(p, t, up), 1)
             return carry
         lax.fori_loop(0, X, each, 0)
 
@@ -478,7 +492,7 @@
         def each(j, carry):
             t = zz * X + lax.rem(x + j, X)
             for p in every:
-                c_copy(p, t).start()
+                start(p, lambda up, p=p: c_copy(p, t, up), 0)
             return carry
         lax.fori_loop(0, X, each, 0)
 
@@ -628,10 +642,10 @@
         pltpu.VMEM(front + s.shape, BF)
         for front in lead for s in shares
     ]
-    outs = [grads[0].shape[1:], grads[1].shape[1:], (2,) + grads[2].shape[2:], grads[3].shape[1:]]
+    outs = [grads[0].shape[1:], grads[1].shape[1:], (2,) + grads[2].shape[1:], grads[3].shape[1:]]
     return pl.pallas_call(
         functools.partial(reduce_kernel, topo, shares),
-        in_specs=[hbm] * 4,
+        in_specs=[hbm] * 5,
         out_specs=[hbm] * 4,
         out_shape=[jax.ShapeDtypeStruct(s, BF) for s in outs],
         scratch_shapes=rooms + [
@@ -877,23 +891,7 @@
 
 
 def project_kernel(state_ref, gain_ref, w_ref, turn_ref, n1_ref, q_ref, kv_ref):
-    n1 = normed(state_ref[...], gain_ref[...]).astype(BF)
-    n1_ref[...] = n1
-    cosine, sine = turn_ref[0], turn_ref[1]
-    key = lanes_of(n1.shape[0]) < HD
-    columns = w_ref.shape[1]
-    for start in range(0, columns, 2 * LANES):
-        wide = min(2 * LANES, columns - start)
-        both = jnp.dot(n1, w_ref[:, start:start + wide], preferred_element_type=F32)
-        for half in range(wide // LANES):
-            j = start // LANES + half
-            v = both[:, half * LANES:(half + 1) * LANES]
-            turned = v * cosine + spin(v) * sine
-            if j < CHUNKS:
-                q_ref[j] = (turned * HD ** -0.5).astype(BF)
-            else:
-                j -= CHUNKS
-                kv_ref[:, j * LANES:(j + 1) * LANES] = jnp.where(key, turned, v).astype(BF)
+    project_into(state_ref[...], gain_ref[...], w_ref, turn_ref, n1_ref, q_ref, kv_ref)
 
 
 def project(state, gain, w, turns):
@@ -1015,6 +1013,10 @@
             jax.ShapeDtypeStruct((KV_HEADS, 8, wide), F32),
         ],
         compiler_params=pltpu.CompilerParams(vmem_limit_bytes=62 << 20),
+        cost_estimate=pl.CostEstimate(
+            flops=16 * KV_HEADS * wide * count * HD, bytes_accessed=4 * count * columns,
+            transcendentals=KV_HEADS * wide * count,
+        ),
         name="attend",
     )(span, key_labels, query_labels, kv_all, q)
 
@@ -1111,30 +1113,20 @@
         out_ref[j] = v
 
 
-def out_back(d_att, w_out):
-    n = d_att.shape[0]
-    return pl.pallas_call(
-        out_back_kernel,
-        grid=(1,),
-        in_specs=[whole(*d_att.shape), whole(*w_out.shape)],
-        out_specs=whole(CHUNKS, n, LANES),
-        out_shape=jax.ShapeDtypeStruct((CHUNKS, n, LANES), BF),
-        compiler_params=pltpu.CompilerParams(vmem_limit_bytes=ROOM),
-        name="out_back",
-    )(d_att, w_out)
-
-
 def project_back_kernel(gradient_ref, state_ref, gain_ref, w_ref, turn_ref, dq_ref, raw_ref,
-                        grad_ref, dkv_ref, dgain_ref):
+                        grad_ref, joint_ref, dgain_ref):
     cosine, sine = turn_ref[0], turn_ref[1]
     key = lanes_of(dq_ref.shape[0]) < HD
     for j in range(KV_HEADS):
         v = raw_ref[:, j * LANES:(j + 1) * LANES].astype(F32)
         turned = v * cosine - spin(v) * sine
-        dkv_ref[:, j * LANES:(j + 1) * LANES] = jnp.where(key, turned, v).astype(BF)
-    split = CHUNKS * LANES
-    d = lax.dot_general(dq_ref[...], w_ref[:, :split], NT, preferred_element_type=F32)
-    d += lax.dot_general(dkv_ref[...], w_ref[:, split:], NT, preferred_element_type=F32)
+        at = (CHUNKS + j) * LANES
+        joint_ref[:, at:at + LANES] = jnp.where(key, turned, v).astype(BF)
+    split, full = CHUNKS * LANES, w_ref.shape[1]
+    joint_ref[:, :split] = dq_ref[...]
+    if joint_ref.shape[1] > full:
+        joint_ref[:, full:] = jnp.zeros((key.shape[0], joint_ref.shape[1] - full), BF)
+    d = lax.dot_general(joint_ref[:, :full], w_ref[...], NT, preferred_element_type=F32)
     v = state_ref[...]
     inv = lax.rsqrt(jnp.mean(v * v, axis=-1, keepdims=True) + EPS)
     scaled = d * gain_ref[...]
@@ -1145,6 +1137,7 @@
 
 def project_back(gradient, state, gain, w, turns, dq, dkv):
     n, model = state.shape
+    joint = -(-w.shape[1] // 256) * 256
     return pl.pallas_call(
         project_back_kernel,
         grid=(1,),
@@ -1152,10 +1145,10 @@
             whole(n, model), whole(n, model), whole(1, model), whole(*w.shape),
             whole(*turns.shape), whole(*dq.shape), whole(*dkv.shape),
         ],
-        out_specs=[whole(n, model), whole(*dkv.shape), whole(1, model)],
+        out_specs=[whole(n, model), whole(n, joint), whole(1, model)],
         out_shape=[
             jax.ShapeDtypeStruct((n, model), F32),
-            jax.ShapeDtypeStruct(dkv.shape, BF),
+            jax.ShapeDtypeStruct((n, joint), BF),
             jax.ShapeDtypeStruct((1, model), F32),
         ],
         compiler_params=pltpu.CompilerParams(vmem_limit_bytes=ROOM),
@@ -1163,89 +1156,209 @@
     )(gradient, state, gain, w, turns, dq, dkv)
 
 
-def outer_columns_kernel(count, x_ref, *refs):
-    ds, out_ref, turned = refs[:count], refs[count], refs[count + 1]
-
-    @pl.when((pl.program_id(0) == 0) & (pl.program_id(1) == 0))
+def project_into(state, gain, w_ref, turn_ref, n1_ref, q_ref, kv_ref):
+    n1 = normed(state, gain).astype(BF)
+    n1_ref[...] = n1
+    rows = n1.shape[0]
+    cosine, sine = turn_ref[0, :rows], turn_ref[1, :rows]
+    key = lanes_of(rows) < HD
+    columns = w_ref.shape[1]
+    for start in range(0, columns, 2 * LANES):
+        wide = min(2 * LANES, columns - start)
+        both = jnp.dot(n1, w_ref[:, start:start + wide], preferred_element_type=F32)
+        for half in range(wide // LANES):
+            j = start // LANES + half
+            v = both[:, half * LANES:(half + 1) * LANES]
+            turned = v * cosine + spin(v) * sine
+            if j < CHUNKS:
+                q_ref[j] = (turned * HD ** -0.5).astype(BF)
+            else:
+                j -= CHUNKS
+                kv_ref[:, j * LANES:(j + 1) * LANES] = jnp.where(key, turned, v).astype(BF)
+
+
+def feed_kernel(following, mixed_ref, state_ref, w_out_ref, gain_ref, router_ref, active_ref,
+                w_gate_ref, w_up_ref, w_down_ref, *refs):
+    if following:
+        next_gain_ref, w_ref, turn_ref = refs[:3]
+        refs = refs[3:]
+    (new_ref, middle_ref, n2_ref, gated_ref, up_ref, hidden_ref, both_ref, gate_ref) = refs[:8]
+    step = pl.program_id(0)
+
+    @pl.when(step == 0)
     def _():
-        turned[...] = jnp.transpose(x_ref[...])
-
-    for i in range(count):
-        @pl.when(pl.program_id(0) == i)
-        def _(i=i):
-            out_ref[0] = jnp.dot(
-                turned[...], ds[i][...], preferred_element_type=F32
-            ).astype(BF)
-
-
-def outer_columns(x, ds, tile):
-    n, rows = x.shape
-    columns = ds[0].shape[1]
-    count = len(ds)
-
-    def taken(i):
-        return lambda a, j: (0, jnp.where(a == i, j, jnp.where(a < i, 0, columns // tile - 1)))
-
+        att = jnp.dot(mixed_ref[...], w_out_ref[...], preferred_element_type=F32)
+        middle = state_ref[...] + att
+        middle_ref[...] = middle
+        n2_ref[...] = normed(middle, gain_ref[...]).astype(BF)
+        both_ref[...] = att
+
+    n2 = n2_ref[...]
+    gated = jnp.dot(n2, w_gate_ref[...], preferred_element_type=F32)
+    upward = jnp.dot(n2, w_up_ref[...], preferred_element_type=F32)
+    hidden = (gated * jax.nn.sigmoid(gated) * upward).astype(BF)
+    gated_ref[...] = gated.astype(BF)
+    up_ref[...] = upward.astype(BF)
+    hidden_ref[...] = hidden
+    both_ref[...] += jnp.dot(hidden, w_down_ref[...], preferred_element_type=F32)
+
+    @pl.when(step == pl.num_programs(0) - 1)
+    def _():
+        state = state_ref[...]
+        gate = jax.nn.sigmoid(jnp.sum(state * router_ref[...], axis=-1, keepdims=True))
+        gate_ref[...] = gate
+        new_ref[...] = state + active_ref[...] * gate * both_ref[...]
+        if following:
+            project_into(
+                new_ref[:following, :], next_gain_ref[...], w_ref, turn_ref, *refs[8:11]
+            )
+
+
+def feed(mixed, state, w_out, gain, router, active, w_gate, w_up, w_down, following, then=()):
+    n, model = state.shape
+    ff = w_gate.shape[1]
+    tile = 512 if ff % 512 == 0 else ff
+    across = pl.BlockSpec((model, tile), lambda i: (0, i))
+    made = pl.BlockSpec((n, tile), lambda i: (0, i))
+    out_specs = [
+        whole(n, model), whole(n, model), whole(n, model), made, made, made, whole(n, model),
+        whole(n, 1),
+    ]
+    wide = lambda dtype: jax.ShapeDtypeStruct((n, model), dtype)
+    tall = jax.ShapeDtypeStruct((n, ff), BF)
+    out_shape = [
+        wide(F32), wide(F32), wide(BF), tall, tall, tall, wide(F32),
+        jax.ShapeDtypeStruct((n, 1), F32),
+    ]
+    if following:
+        shapes = [(following, model), (CHUNKS, following, LANES), (following, KV_HEADS * LANES)]
+        out_specs += [whole(*s) for s in shapes]
+        out_shape += [jax.ShapeDtypeStruct(s, BF) for s in shapes]
     return pl.pallas_call(
-        functools.partial(outer_columns_kernel, count),
-        grid=(count, columns // tile),
-        in_specs=[whole(n, rows)] + [pl.BlockSpec((n, tile), taken(i)) for i in range(count)],
-        out_specs=pl.BlockSpec((1, rows, tile), lambda a, j: (a, 0, j)),
-        out_shape=jax.ShapeDtypeStruct((count, rows, columns), BF),
-        scratch_shapes=[pltpu.VMEM((rows, n), BF)],
+        functools.partial(feed_kernel, following),
+        grid=(ff // tile,),
+        in_specs=[
+            whole(n, model), whole(n, model), whole(*w_out.shape), whole(1, model),
+            whole(1, model), whole(n, 1), across, across,
+            pl.BlockSpec((tile, model), lambda i: (i, 0)),
+        ] + [whole(*v.shape) for v in then],
+        out_specs=out_specs,
+        out_shape=out_shape,
         compiler_params=pltpu.CompilerParams(vmem_limit_bytes=ROOM),
-        cost_estimate=pl.CostEstimate(
-            flops=2 * n * rows * columns * count, transcendentals=0,
-            bytes_accessed=2 * count * (n * columns + rows * columns) + 2 * n * rows,
-        ),
-        name="outer_columns",
-    )(x, *ds)
-
-
-def outer_rows_kernel(x_ref, d_ref, out_ref):
-    out_ref[...] = jnp.dot(
-        jnp.transpose(x_ref[...]), d_ref[...], preferred_element_type=F32
-    ).astype(BF)
-
-
-def outer_rows(x, d, tile):
-    n, rows = x.shape
-    columns = d.shape[1]
+        name="feed",
+    )(mixed, state, w_out, gain, router, active, w_gate, w_up, w_down, *then)
+
+
+def feed_back_kernel(gradient_ref, both_ref, gate_ref, active_ref, state_ref, router_ref,
+                     middle_ref, gain_ref, w_out_ref, gated_ref, up_ref, w_gate_ref, w_up_ref,
+                     w_down_ref, d_fed_ref, d_gated_ref, d_up_ref, d_att_ref, grad_ref,
+                     d_mixed_ref, d_router_ref, d_gain_ref, total):
+    step = pl.program_id(0)
+
+    @pl.when(step == 0)
+    def _():
+        d_fed_ref[...] = (active_ref[...] * gate_ref[...] * gradient_ref[...]).astype(BF)
+        total[...] = jnp.zeros(total.shape, F32)
+
+    d_hidden = lax.dot_general(d_fed_ref[...], w_down_ref[...], NT, preferred_element_type=F32)
+    gated, upward = gated_ref[...].astype(F32), up_ref[...].astype(F32)
+    sig = jax.nn.sigmoid(gated)
+    part = d_hidden * sig
+    d_up = (part * gated).astype(BF)
+    d_gated = (part * upward * (1.0 + gated * (1.0 - sig))).astype(BF)
+    d_up_ref[...] = d_up
+    d_gated_ref[...] = d_gated
+    total[...] += lax.dot_general(
+        d_gated, w_gate_ref[...], NT, preferred_element_type=F32
+    ) + lax.dot_general(d_up, w_up_ref[...], NT, preferred_element_type=F32)
+
+    @pl.when(step == pl.num_programs(0) - 1)
+    def _():
+        gradient, gate, active = gradient_ref[...], gate_ref[...], active_ref[...]
+        d = total[...]
+        v = middle_ref[...]
+        inv = lax.rsqrt(jnp.mean(v * v, axis=-1, keepdims=True) + EPS)
+        d_gain_ref[...] = jnp.sum(d * v * inv, axis=0, keepdims=True)
+        scaled = d * gain_ref[...]
+        dot = jnp.mean(scaled * v, axis=-1, keepdims=True)
+        d_middle = inv * scaled - v * (inv * inv * inv * dot)
+        d_gate = active * gate * (1.0 - gate) * jnp.sum(
+            gradient * both_ref[...], axis=-1, keepdims=True
+        )
+        d_router_ref[...] = jnp.sum(state_ref[...] * d_gate, axis=0, keepdims=True)
+        grad_ref[...] = gradient + d_gate * router_ref[...] + d_middle
+        d_att_ref[...] = (active * gate * gradient + d_middle).astype(BF)
+        out_back_kernel(d_att_ref, w_out_ref, d_mixed_ref)
+
+
+def feed_back(gradient, both, gate, active, state, router, middle, gain, w_out, gated, upward,
+              w_gate, w_up, w_down):
+    n, model = state.shape
+    ff = w_gate.shape[1]
+    tile = 512 if ff % 512 == 0 else ff
+    across = pl.BlockSpec((model, tile), lambda i: (0, i))
+    made = pl.BlockSpec((n, tile), lambda i: (0, i))
+    wide = whole(n, model)
+    flat = lambda dtype: jax.ShapeDtypeStruct((n, model), dtype)
+    tall = jax.ShapeDtypeStruct((n, ff), BF)
+    row = jax.ShapeDtypeStruct((1, model), F32)
     return pl.pallas_call(
-        outer_rows_kernel,
+        feed_back_kernel,
+        grid=(ff // tile,),
+        in_specs=[
+            wide, wide, whole(n, 1), whole(n, 1), wide, whole(1, model), wide, whole(1, model),
+            whole(*w_out.shape), made, made, across, across,
+            pl.BlockSpec((tile, model), lambda i: (i, 0)),
+        ],
+        out_specs=[
+            wide, made, made, wide, wide, whole(CHUNKS, n, LANES), whole(1, model),
+            whole(1, model),
+        ],
+        out_shape=[
+            flat(BF), tall, tall, flat(BF), flat(F32),
+            jax.ShapeDtypeStruct((CHUNKS, n, LANES), BF), row, row,
+        ],
+        scratch_shapes=[pltpu.VMEM((n, model), F32)],
+        compiler_params=pltpu.CompilerParams(vmem_limit_bytes=ROOM),
+        name="feed_back",
+    )(gradient, both, gate, active, state, router, middle, gain, w_out, gated, upward, w_gate,
+      w_up, w_down)
+
+
+def outer_rows_kernel(count, *refs):
+    xs, ds, out_ref = refs[:count], refs[count:2 * count], refs[2 * count]
+    total = None
+    for x_ref, d_ref in zip(xs, ds):
+        part = jnp.dot(jnp.transpose(x_ref[...]), d_ref[...], preferred_element_type=F32)
+        total = part if total is None else total + part
+    out_ref[...] = total.astype(BF)
+
+
+def outer_rows(xs, ds, tile):
+    rows, columns = xs[0].shape[1], ds[0].shape[1]
+    tokens = sum(x.shape[0] for x in xs)
+    return pl.pallas_call(
+        functools.partial(outer_rows_kernel, len(xs)),
         grid=(rows // tile,),
-        in_specs=[pl.BlockSpec((n, tile), lambda i: (0, i)), whole(n, columns)],
+        in_specs=[pl.BlockSpec((x.shape[0], tile), lambda i: (0, i)) for x in xs]
+        + [whole(*d.shape) for d in ds],
         out_specs=pl.BlockSpec((tile, columns), lambda i: (i, 0)),
         out_shape=jax.ShapeDtypeStruct((rows, columns), BF),
         compiler_params=pltpu.CompilerParams(vmem_limit_bytes=ROOM),
         cost_estimate=pl.CostEstimate(
-            flops=2 * n * rows * columns, transcendentals=0,
-            bytes_accessed=2 * (n * columns + n * rows + rows * columns),
+            flops=2 * tokens * rows * columns, transcendentals=0,
+            bytes_accessed=2 * (tokens * (columns + rows) + rows * columns),
         ),
         name="outer_rows",
-    )(x, d)
+    )(*xs, *ds)
 
 
 def mm(a, b):
     return jnp.dot(a, b, preferred_element_type=F32)
 
 
-def mm_nt(a, b):
-    return lax.dot_general(a, b, NT, preferred_element_type=F32)
-
-
 def mm_tn(a, b):
     return lax.dot_general(a, b, TN, preferred_element_type=F32)
-
-
-def inverse_rms(v):
-    return lax.rsqrt(jnp.mean(v * v, axis=-1, keepdims=True) + EPS)
-
-
-def norm_back(grad, v, inv, gain):
-    scaled = grad * gain
-    dot = jnp.mean(scaled * v, axis=-1, keepdims=True)
-    return (inv * scaled - v * (inv * inv * inv * dot), jnp.sum(grad * v * inv, axis=0))
 
 
 def per_device(topo, *args):
@@ -1313,14 +1426,16 @@
     turns = jnp.stack([jnp.cos(angles), jnp.sin(angles)])
     turns = jnp.tile(turns, (1, 1, LANES * 2 // HD))
 
-    def forward(state, recursion, labels_all=None):
+    routers = [small[:, r][None] for r in range(RECS)]
+
+    def forward(state, projected, recursion, labels_all=None):
         n = state.shape[0]
         extra = None
-        n1, q, kv = project(state, gain_one, weight_qkv, turns[:, :n])
+        n1, q, kv = projected
         if recursion == 0:
             kv_all, labels_all = collect([kv, labels], 2)
             kv_all, later = lax.optimization_barrier((kv_all, cotangent))
-            extra = (labels_all, lax.ppermute(later, AXES, swap).astype(F32))
+            later = lax.ppermute(later, AXES, swap)
         else:
             kv_all, = collect([kv], 3)
         kv_all = kv_all.reshape(topo.T * n, 2 * kv_cols)
@@ -1331,52 +1446,43 @@
         query_labels = jnp.stack([labels[1, :n], labels[0, :n]])
         query_labels = jnp.pad(jnp.tile(query_labels, (1, SHARES)), ((0, 6), (0, 0)))
         mixed, out, stat = attend(n, span, key_labels, query_labels, kv_all, q)
-        attended = mm(mixed, weight_o)
-        middle = state + attended
-        inv_two = inverse_rms(middle)
-        n2 = (middle * inv_two * gain_two).astype(BF)
-        gated, upward = mm(n2, weight_g), mm(n2, weight_u)
-        hidden = (jax.nn.silu(gated) * upward).astype(BF)
-        both = attended + mm(hidden, weight_d)
-        gate = jax.nn.sigmoid(jnp.sum(state * small[:, recursion], axis=-1, keepdims=True))
+        if recursion == 0:
+            mixed, later = lax.optimization_barrier((mixed, later))
+            extra = (labels_all, later.astype(F32))
         active = (labels[2, :n] > recursion).astype(F32)[:, None]
-        new = state + active * gate * both
+        following = deep_rows if recursion + 1 < RECS else 0
+        new, middle, n2, gated, upward, hidden, both, gate, *projected = feed(
+            mixed, state, weight_o, gain_two, routers[recursion], active, weight_g, weight_u,
+            weight_d, following, (gain_one, weight_qkv, turns) if following else (),
+        )
         kept = (state, n1, q, kv_all, key_labels, query_labels, out, stat, mixed, middle,
-                inv_two, n2, gated, upward, hidden, both, gate, active)
-        return (new, kept, extra)
+                n2, gated, upward, hidden, both, gate, active)
+        return (new, projected, kept, extra)
 
     def backward(gradient, recursion, kept):
         (state, n1, q, kv_all, key_labels, query_labels, out, stat, mixed, middle,
-         inv_two, n2, gated, upward, hidden, both, gate, active) = kept
+         n2, gated, upward, hidden, both, gate, active) = kept
         n = state.shape[0]
-        d_both = active * gate * gradient
-        d_fed = d_both.astype(BF)
-        d_gate = active * gate * (1.0 - gate) * jnp.sum(gradient * both, axis=-1, keepdims=True)
-        d_router = jnp.sum(state * d_gate, axis=0)
-        d_hidden = mm_nt(d_fed, weight_d)
-        sig = jax.nn.sigmoid(gated)
-        d_up = (d_hidden * gated * sig).astype(BF)
-        d_gated = (d_hidden * upward * sig * (1.0 + gated * (1.0 - sig))).astype(BF)
-        d_middle, d_gain_two = norm_back(
-            mm_nt(d_gated, weight_g) + mm_nt(d_up, weight_u), middle, inv_two, gain_two)
-        d_att = (d_both + d_middle).astype(BF)
-        gradient = gradient + d_gate * small[:, recursion] + d_middle
+        d_fed, d_gated, d_up, d_att, gradient, d_mixed, d_router, d_gain_two = feed_back(
+            gradient, both, gate, active, state, routers[recursion], middle, gain_two, weight_o,
+            gated, upward, weight_g, weight_u, weight_d,
+        )
         dq, dkv = attend_back(
-            n, span, key_labels, query_labels, kv_all, q, out_back(d_att, weight_o), out, stat,
-            turns[:, :n],
+            n, span, key_labels, query_labels, kv_all, q, d_mixed, out, stat, turns[:, :n]
         )
         dkv = distribute(dkv.reshape(topo.T, n, 2 * kv_cols), 5 if recursion else 4)
-        gradient, dkv, d_gain_one = project_back(
+        gradient, dqkv, d_gain_one = project_back(
             gradient, state, gain_one, weight_qkv, turns[:, :n], dq, dkv
         )
-        left = (n1, dq, dkv, mixed, d_att, n2, d_gated, d_up, hidden, d_fed)
-        return (gradient, left, (d_router, d_gain_one[0], d_gain_two))
-
-    whole_state, kept, (labels_all, gradient) = forward(state, 0)
+        left = (n1, dqkv, mixed, d_att, n2, d_gated, d_up, hidden, d_fed)
+        return (gradient, left, (d_router[0], d_gain_one[0], d_gain_two[0]))
+
+    projected = project(state, gain_one, weight_qkv, turns)
+    whole_state, projected, kept, (labels_all, gradient) = forward(state, projected, 0)
     deep = whole_state[:deep_rows]
     all_kept = [kept]
     for recursion in range(1, RECS):
-        deep, kept, _ = forward(deep, recursion, labels_all)
+        deep, projected, kept, _ = forward(deep, projected, recursion, labels_all)
         all_kept.append(kept)
     final = jnp.concatenate([deep, whole_state[deep_rows:]], axis=0).astype(BF)
 
@@ -1394,11 +1500,11 @@
     final = lax.ppermute(final, AXES, swap)
     gradient = lax.ppermute(gradient, AXES, swap)
 
-    n1, dq, dkv, mixed, d_att, n2, d_gated, d_up, hidden, d_fed = (
-        jnp.concatenate(parts, axis=0) for parts in zip(*lefts)
-    )
-    dqkv = jnp.concatenate([dq, dkv], axis=1)
-    dqkv = jnp.pad(dqkv, ((0, 0), (0, -dqkv.shape[1] % 256)))
+    n1, dqkv, mixed, d_att, n2, d_gated, d_up, hidden, d_fed = zip(*lefts)
+
+    def outer(xs, ds):
+        return mm_tn(jnp.concatenate(xs, axis=0), jnp.concatenate(ds, axis=0))
+
     cut = lambda v: v.astype(BF).reshape(topo.T, -1, v.shape[-1])
     tiny = jnp.stack(
         [smalls[2][0], smalls[1][0], smalls[0][0],
@@ -1408,10 +1514,11 @@
     wide_out = -(-(model + tiny.shape[1]) // 256) * 256
     tiny = jnp.pad(tiny, ((0, 0), (0, wide_out - model - tiny.shape[1])))
     grad_qkv, grad_o, grad_gu, grad_down = reduce_gradients(topo, [
-        cut(outer_columns(n1, [dqkv], 256)[0]),
-        cut(jnp.concatenate([mm_tn(mixed, d_att), tiny], axis=1)),
-        outer_columns(n2, [d_gated, d_up], 512).reshape(2, topo.T, -1, ff),
+        cut(outer(n1, dqkv)),
+        cut(jnp.concatenate([outer(mixed, d_att), tiny], axis=1)),
+        cut(outer(n2, d_gated)),
         outer_rows(hidden, d_fed, 640).reshape(topo.T, -1, model),
+        cut(outer(n2, d_up)),
     ])
     grad_query = grad_qkv[:, :model].astype(F32)
     pair = grad_qkv[:, model + HD:model + HD + 2 * kv_cols].astype(F32)

time: 661 us -> 635 us (0.961)
  Pallas kernels: 469 us -> 521 us
  matrix products: 70.5 us -> 23.6 us
  other arithmetic: 44.4 us -> 22.4 us
  waiting for transfers between devices: 15.6 us -> 7.78 us
    pallas_call x6 -> x7, Pallas kernels: 41.8 us -> 100 us  [the longest x3 46.5 us: feed_back(): pl.pallas_call(feed_back_kernel, grid=(ff // tile,), in_specs=[wide, wide...]
    dot_general x15 -> x3, matrix products: 33.8 us -> 0.82 us  [mm(): return jnp.dot(a, b, preferred_element_type=F32)]
    dot_general x9 -> x0, matrix products: 29.1 us -> none  [mm_nt(): return lax.dot_general(a, b, NT, preferred_element_type=F32)]
    dot_general x3 -> x6, matrix products: 7.49 us -> 22.8 us  [mm_tn(): return lax.dot_general(a, b, TN, preferred_element_type=F32)]
    concatenate x7 -> x2, other arithmetic: 15.4 us -> 3.81 us  [the longest x1 2.25 us: per_device(): gradient = jnp.concatenate([deep_grad, gradient[deep_rows:]], axis=0)]
    pallas_call x3 -> x1, Pallas kernels: 12.4 us -> 4.37 us  [project(): pl.pallas_call(project_kernel, grid=(1,), in_specs=[whole(n, model), whol...]
    ppermute x1, waiting for transfers between devices: 15.6 us -> 7.77 us  [forward(): later = lax.ppermute(later, AXES, swap)]
    convert_element_type x9 -> x2, other arithmetic: 6.66 us -> 0.01 us  [forward(): active = (labels[2, :n] > recursion).astype(F32)[:, None]]
  transfers between devices with their start and end apart: 5 -> 5, of which waited for: 1 -> 1; matrix products, arithmetic and copies ran while one was open for 5% -> 7% of each run, Pallas kernels for 38% -> 38%
where the time goes in v6:
time: 635 us; the launch traced here: 624 us
  Pallas kernels  521 us (82%)
  local copies, waits for them, and re-layouts  29.3 us (5%)
  matrix products  23.6 us (4%)
  other arithmetic  22.4 us (4%)
  starting transfers between devices  15 us (2%)
  waiting for transfers between devices  7.78 us (1%)
    pallas_call x1, Pallas kernels, reduce_gradients(): pl.pallas_call(functools.partial(reduce_kernel, topo, shares), in_specs=[...  113 us
    pallas_call x1, Pallas kernels, gather_weights(): pl.pallas_call(functools.partial(gather_kernel, topo, pieces), in_specs=[...  105 us
    pallas_call x3, Pallas kernels, reduce_layer(): pl.pallas_call(functools.partial(group_reduce_kernel, topo), in_specs=[pl...  62.4 us
    pallas_call x3, Pallas kernels, gather_layer(): pl.pallas_call(functools.partial(group_gather_kernel, topo, n), in_specs=...  53.8 us
    pallas_call x3, Pallas kernels, feed_back(): pl.pallas_call(feed_back_kernel, grid=(ff // tile,), in_specs=[wide, wide...  46.5 us
    pallas_call x3, Pallas kernels, feed(): pl.pallas_call(functools.partial(feed_kernel, following), grid=(ff // til...  45.3 us
    pallas_call x3, Pallas kernels, attend_back(): pl.pallas_call(functools.partial(attend_back_kernel, rows), grid_spec=plt...  40.4 us
    pallas_call x3, Pallas kernels, attend(): pl.pallas_call(functools.partial(attend_kernel, rows), grid_spec=pltpu.Pr...  27.4 us
  transfers between devices with their start and end apart: 5, of which 1 were waited for; matrix products, arithmetic and copies ran while one was open for 7% of the time, Pallas kernels for 38%

profile of v6, /device:TPU:17, one launch (start us, length us, event | category | flops | bytes accessed | tf_op | source)
XLA Modules:
  0.0 623.7 jit_solution(3902648076494049275)
XLA Ops:
  5.5 3.6 collective-permute-start
  13.8 105.4 %gather_weights.1 = (bf16[8,120,1664]{2,1,0:T(8,128)(2,1)}, bf16[8,120,2560]{2,1,0:T(8,128)(2,1)}, bf16[8,120,2560]{2,1,0:T(8,128)(2,1)}, bf16[8,320,960]{2,1,0:T(8,128)(2,1)}, bf16[8,120,960]{2,1,0:T(8,128)(2,1)}) custom-call(bf16[120,1664]{1,0:T(8,128)(2,1)} %concatenate.48.refs_0_, bf16[120,2560]{1,0:T(8,128)(2,1)} %refs_1_.1, bf16[120,2560]{1,0:T(8,128)(2,1)} %refs_2_.1, ...), custom_call_target="tpu_custom_call" | custom-call | tf_op jit(solution)/shard_map/gather_weights/pallas_call | solution.py:298
  132.4 4.4 project.1
  136.7 20.0 %gather_layer.3 = (bf16[8,256,640]{2,1,0:T(8,128)(2,1)}, s32[8,8,256]{2,1,0:T(8,128)}) custom-call(bf16[256,640]{1,0:T(8,128)(2,1)} %get-tuple-element.111.refs_0_, s32[8,256]{1,0:T(8,128)} %copy-done.22), custom_call_target="tpu_custom_call" | custom-call | tf_op jit(solution)/shard_map/gather_layer/pallas_call | solution.py:782
  166.4 11.0 %attend.3 = (bf16[256,960]{1,0:T(8,128)(2,1)}, f32[8,256,128]{2,1,0:T(8,128)}, f32[5,8,768]{2,1,0:T(8,128)}) custom-call(s32[2]{0:T(128)} %pad_add_fusion.6.span, s32[2048,8]{1,0:T(8,128)} %pad.38.key_ref, s32[8,768]{1,0:T(8,128)} %pad.39.query_ref, bf16[2048,640]{1,0:T(8,128)(2,1)} %bitcast.122, bf16[8,256,128]{2,1,0:T(8,128)(2,1)} %get-tuple-element.115.q_ref), custom_call_target="tpu_custom_call" | custom-call | flops 8053063680 | bytes 5242880 | tf_op jit(solution)/shard_map/attend/pallas_call | solution.py:993
  177.4 7.8 %collective-permute-done.2 = bf16[256,960]{1,0:T(8,128)(2,1)S(1)} collective-permute-done((bf16[256,960]{1,0:T(8,128)(2,1)S(1)}, bf16[256,960]{1,0:T(8,128)(2,1)S(1)}, u32[]{:S(2)}, u32[]{:S(2)}) %collective-permute-start.2) | collective-permute-done | bytes 491552 | tf_op jit(solution)/shard_map/ppermute | solution.py:1438
  185.2 16.5 %feed.3 = (f32[256,960]{1,0:T(8,128)}, f32[256,960]{1,0:T(8,128)}, bf16[256,960]{1,0:T(8,128)(2,1)}, bf16[256,2560]{1,0:T(8,128)(2,1)}, bf16[256,2560]{1,0:T(8,1...) custom-call(bf16[256,960]{1,0:T(8,128)(2,1)} %get-tuple-element.118., ...), custom_call_target="tpu_custom_call" | custom-call | tf_op jit(solution)/shard_map/feed/pallas_call | solution.py:1237
  205.8 13.4 %gather_layer.4 = bf16[8,192,640]{2,1,0:T(8,128)(2,1)} custom-call(bf16[192,640]{1,0:T(8,128)(2,1)} %get-tuple-element.123.refs_0_), custom_call_target="tpu_custom_call" | custom-call | tf_op jit(solution)/shard_map/gather_layer/pallas_call | solution.py:782
  219.3 8.1 %attend.4 = (bf16[192,960]{1,0:T(8,128)(2,1)}, f32[8,192,128]{2,1,0:T(8,128)}, f32[5,8,576]{2,1,0:T(8,128)}) custom-call(s32[2]{0:T(128)} %pad_add_fusion.6.span, s32[1536,8]{1,0:T(8,128)} %pad.37.key_ref, s32[8,576]{1,0:T(8,128)} %pad.36.query_ref, bf16[1536,640]{1,0:T(8,128)(2,1)} %bitcast.114, bf16[8,192,128]{2,1,0:T(8,128)(2,1)} %get-tuple-element.124.q_ref), custom_call_target="tpu_custom_call" | custom-call | flops 4529848320 | bytes 3932160 | tf_op jit(solution)/shard_map/attend/pallas_call | solution.py:993
  227.3 15.5 %feed.4 = (f32[192,960]{1,0:T(8,128)}, f32[192,960]{1,0:T(8,128)}, bf16[192,960]{1,0:T(8,128)(2,1)}, bf16[192,2560]{1,0:T(8,128)(2,1)}, bf16[192,2560]{1,0:T(8,1...) custom-call(bf16[192,960]{1,0:T(8,128)(2,1)} %get-tuple-element.125., ...), custom_call_target="tpu_custom_call" | custom-call | tf_op jit(solution)/shard_map/feed/pallas_call | solution.py:1237
  242.9 20.3 %gather_layer.5 = bf16[8,192,640]{2,1,0:T(8,128)(2,1)} custom-call(bf16[192,640]{1,0:T(8,128)(2,1)} %get-tuple-element.127.refs_0_), custom_call_target="tpu_custom_call" | custom-call | tf_op jit(solution)/shard_map/gather_layer/pallas_call | solution.py:782
  263.2 8.3 %attend.5 = (bf16[192,960]{1,0:T(8,128)(2,1)}, f32[8,192,128]{2,1,0:T(8,128)}, f32[5,8,576]{2,1,0:T(8,128)}) custom-call(s32[2]{0:T(128)} %pad_add_fusion.6.span, s32[1536,8]{1,0:T(8,128)} %pad.35.key_ref, s32[8,576]{1,0:T(8,128)} %pad.36.query_ref, bf16[1536,640]{1,0:T(8,128)(2,1)} %bitcast.116, bf16[8,192,128]{2,1,0:T(8,128)(2,1)} %get-tuple-element.128.q_ref), custom_call_target="tpu_custom_call" | custom-call | flops 4529848320 | bytes 3932160 | tf_op jit(solution)/shard_map/attend/pallas_call | solution.py:993
  271.5 13.2 %feed.5 = (f32[192,960]{1,0:T(8,128)}, f32[192,960]{1,0:T(8,128)}, bf16[192,960]{1,0:T(8,128)(2,1)}, bf16[192,2560]{1,0:T(8,128)(2,1)}, bf16[192,2560]{1,0:T(8,1...) custom-call(bf16[192,960]{1,0:T(8,128)(2,1)} %get-tuple-element.129.mixed_ref, ...), custom_call_target="tpu_custom_call" | custom-call | tf_op jit(solution)/shard_map/feed/pallas_call | solution.py:1237
  286.0 15.1 %feed_back.3 = (bf16[192,960]{1,0:T(8,128)(2,1)}, bf16[192,2560]{1,0:T(8,128)(2,1)}, bf16[192,2560]{1,0:T(8,128)(2,1)}, bf16[192,960]{1,0:T(8,128)(2,1)}, f32[19...) custom-call(f32[192,960]{1,0:T(8,128)} %slice.168.gradient_ref, ...), custom_call_target="tpu_custom_call" | custom-call | tf_op jit(solution)/shard_map/feed_back/pallas_call | solution.py:1305
  301.1 13.0 %attend_back.3 = (bf16[192,1024]{1,0:T(8,128)(2,1)}, bf16[1536,640]{1,0:T(8,128)(2,1)}) custom-call(s32[2]{0:T(128)} %pad_add_fusion.6.span, s32[1536,8]{1,0:T(8,128)} %pad.35.key_ref, s32[8,576]{1,0:T(8,128)} %pad.36.query_ref, bf16[1536,640]{1,0:T(8,128)(2,1)} %bitcast.117, bf16[8,192,128]{2,1,0:T(8,128)(2,1)} %get-tuple-element.128.q_ref, ...), custom_call_target="tpu_custom_call" | custom-call | tf_op jit(solution)/shard_map/attend_back/pallas_call | solution.py:1079
  315.6 20.4 %reduce_layer.3.raw_ref = bf16[192,640]{1,0:T(8,128)(2,1)S(1)} custom-call(bf16[8,192,640]{2,1,0:T(8,128)(2,1)S(1)} %bitcast.82), custom_call_target="tpu_custom_call" | custom-call | tf_op jit(solution)/shard_map/reduce_layer/pallas_call | solution.py:852
  336.7 4.7 project_back.3
  341.4 15.1 %feed_back.4 = (bf16[192,960]{1,0:T(8,128)(2,1)}, bf16[192,2560]{1,0:T(8,128)(2,1)}, bf16[192,2560]{1,0:T(8,128)(2,1)}, bf16[192,960]{1,0:T(8,128)(2,1)}, f32[19...) custom-call(f32[192,960]{1,0:T(8,128)} %get-tuple-element.144.gradient_ref, ...), custom_call_target="tpu_custom_call" | custom-call | tf_op jit(solution)/shard_map/feed_back/pallas_call | solution.py:1305
  356.5 12.7 %attend_back.4 = (bf16[192,1024]{1,0:T(8,128)(2,1)}, bf16[1536,640]{1,0:T(8,128)(2,1)}) custom-call(s32[2]{0:T(128)} %pad_add_fusion.6.span, s32[1536,8]{1,0:T(8,128)} %pad.37.key_ref, s32[8,576]{1,0:T(8,128)} %pad.36.query_ref, bf16[1536,640]{1,0:T(8,128)(2,1)} %bitcast.115, bf16[8,192,128]{2,1,0:T(8,128)(2,1)} %get-tuple-element.124.q_ref, ...), custom_call_target="tpu_custom_call" | custom-call | tf_op jit(solution)/shard_map/attend_back/pallas_call | solution.py:1079
  370.8 17.9 %reduce_layer.4.raw_ref = bf16[192,640]{1,0:T(8,128)(2,1)S(1)} custom-call(bf16[8,192,640]{2,1,0:T(8,128)(2,1)S(1)} %bitcast.81), custom_call_target="tpu_custom_call" | custom-call | tf_op jit(solution)/shard_map/reduce_layer/pallas_call | solution.py:852
  389.4 4.7 project_back.4
  396.4 16.3 %feed_back.5 = (bf16[256,960]{1,0:T(8,128)(2,1)}, bf16[256,2560]{1,0:T(8,128)(2,1)}, bf16[256,2560]{1,0:T(8,128)(2,1)}, bf16[256,960]{1,0:T(8,128)(2,1)}, f32[25...) custom-call(f32[256,960]{1,0:T(8,128)} %pad_maximum_fusion.1.gradient_ref, ...), custom_call_target="tpu_custom_call" | custom-call | tf_op jit(solution)/shard_map/feed_back/pallas_call | solution.py:1305
  412.6 14.8 %attend_back.5 = (bf16[256,1024]{1,0:T(8,128)(2,1)}, bf16[2048,640]{1,0:T(8,128)(2,1)}) custom-call(s32[2]{0:T(128)} %pad_add_fusion.6.span, s32[2048,8]{1,0:T(8,128)} %pad.38.key_ref, s32[8,768]{1,0:T(8,128)} %pad.39.query_ref, bf16[2048,640]{1,0:T(8,128)(2,1)} %bitcast.123, bf16[8,256,128]{2,1,0:T(8,128)(2,1)} %get-tuple-element.115.q_ref, ...), custom_call_target="tpu_custom_call" | custom-call | tf_op jit(solution)/shard_map/attend_back/pallas_call | solution.py:1079
  429.2 24.1 %reduce_layer.5.raw_ref = bf16[256,640]{1,0:T(8,128)(2,1)S(1)} custom-call(bf16[8,256,640]{2,1,0:T(8,128)(2,1)S(1)} %bitcast.80), custom_call_target="tpu_custom_call" | custom-call | tf_op jit(solution)/shard_map/reduce_layer/pallas_call | solution.py:852
  453.9 5.2 project_back.5
  463.4 4.8 collective-permute-start.4
  468.6 3.2 convolution_convert_fusion.3
  474.7 5.9 convolution_convert_fusion.1
  480.7 5.8 convolution_convert_fusion
  486.5 4.7 convolution_convert_fusion.2
  491.2 8.2 %outer_rows.1 = bf16[2560,960]{1,0:T(8,128)(2,1)} custom-call(bf16[192,2560]{1,0:T(8,128)(2,1)} %get-tuple-element.195.refs_0_, bf16[192,2560]{1,0:T(8,128)(2,1)} %get-tuple-element.196.refs_1_, bf16[256,2560]{1,0:T(8,128)(2,1)} %get-tuple-element.197.refs_2_, bf16[192,960]{1,0:T(8,128)(2,1)} %get-tuple-element.198.refs_3_, ...), custom_call_target="tpu_custom_call" | custom-call | flops 3145728000 | bytes 9420800 | tf_op jit(solution)/shard_map/outer_rows/pallas_call | solution.py:1340
  499.4 112.5 %reduce_gradients.1 = (bf16[120,1792]{1,0:T(8,128)(2,1)}, bf16[120,1024]{1,0:T(8,128)(2,1)}, bf16[2,120,2560]{2,1,0:T(8,128)(2,1)}, bf16[320,960]{1,0:T(8,128)(2,1)}) custom-call(bf16[8,120,1792]{2,1,0:T(8,128)(2,1)} %bitcast.121, bf16[8,120,1024]{2,1,0:T(8,128)(2,1)} %pad_maximum_fusion.refs_1_, bf16[8,120,2560]{2,1,0:T(8,128)(2,1)} %bitcast.119, ...), custom_call_target="tpu_custom_call" | custom-call | tf_op jit(solution)/shard_map/reduce_gradients/pallas_call | solution.py:646
  (198 shorter events, 62.5 us)
Async XLA Ops:
  0.6 8.5 %copy-start = (bf16[256,960]{0,1:T(8,128)(2,1)S(1)}, bf16[256,960]{0,1:T(8,128)(2,1)}, u32[]{:S(2)}) copy-start(bf16[256,960]{0,1:T(8,128)(2,1)} %param.15) | copy-start | bytes 1474564
  0.7 11.9 %copy-start.33 = (bf16[120]{0:T(256)(128)(2,1)S(1)}, bf16[120]{0:T(256)(128)(2,1)}, u32[]{:S(2)}) copy-start(bf16[120]{0:T(256)(128)(2,1)} %param.25) | copy-start | bytes 724
  0.7 11.9 %copy-start.34 = (bf16[120]{0:T(256)(128)(2,1)S(1)}, bf16[120]{0:T(256)(128)(2,1)}, u32[]{:S(2)}) copy-start(bf16[120]{0:T(256)(128)(2,1)} %param.24) | copy-start | bytes 724
  0.7 11.9 %copy-start.32 = (bf16[120,3]{0,1:T(4,128)(2,1)S(1)}, bf16[120,3]{0,1:T(4,128)(2,1)}, u32[]{:S(2)}) copy-start(bf16[120,3]{0,1:T(4,128)(2,1)} %param.23) | copy-start | bytes 2164
  0.7 12.1 %copy-start.20 = (bf16[120,320]{0,1:T(8,128)(2,1)S(1)}, bf16[120,320]{0,1:T(8,128)(2,1)}, u32[]{:S(2)}) copy-start(bf16[120,320]{0,1:T(8,128)(2,1)} %param.18) | copy-start | bytes 230404
  0.7 12.1 %copy-start.21 = (bf16[120,320]{0,1:T(8,128)(2,1)S(1)}, bf16[120,320]{0,1:T(8,128)(2,1)}, u32[]{:S(2)}) copy-start(bf16[120,320]{0,1:T(8,128)(2,1)} %param.17) | copy-start | bytes 230404
  0.7 12.3 %copy-start.19 = (bf16[120,960]{1,0:T(8,128)(2,1)S(1)}, bf16[120,960]{1,0:T(8,128)(2,1)}, u32[]{:S(2)}) copy-start(bf16[120,960]{1,0:T(8,128)(2,1)} %param.16) | copy-start | bytes 691204
  5.5 117.1 %collective-permute-start = (s32[8,256]{1,0:T(8,128)S(1)}, s32[8,256]{1,0:T(8,128)S(1)}, u32[]{:S(2)}, u32[]{:S(2)}) collective-permute-start(s32[8,256]{1,0:T(8,128)S(1)} %pad.33), channel_id=1, source_target_pairs={{0,0},{1,1},{2,8},{3,9},{4,16},{5,17},{6,24},{7,25},{8,2},{9,3},{1... | collective-permute-start | bytes 24584 | tf_op jit(solution)/shard_map/ppermute | solution.py:1402
  9.7 121.6 %collective-permute-start.1 = (bf16[256,960]{1,0:T(8,128)(2,1)S(1)}, bf16[256,960]{1,0:T(8,128)(2,1)S(1)}, u32[]{:S(2)}, u32[]{:S(2)}) collective-permute-start(bf16[256,960]{1,0:T(8,128)(2,1)S(1)} %copy.117), channel_id=1, source_target_pairs={{0,0},{1,1},{2,8},{3,9},{4,16},{5,17},{6,24},{7,25},{8,2},{9,3},{1... | collective-permute-start | bytes 1474568 | tf_op jit(solution)/shard_map/ppermute | solution.py:1401
  13.8 108.4 %copy-start.13 = (bf16[256,960]{0,1:T(8,128)(2,1)S(1)}, bf16[256,960]{0,1:T(8,128)(2,1)}, u32[]{:S(2)}) copy-start(bf16[256,960]{0,1:T(8,128)(2,1)} %param.29) | copy-start | bytes 1474564
  122.6 14.1 %copy-start.22 = (s32[8,256]{1,0:T(8,128)}, s32[8,256]{1,0:T(8,128)S(1)}, u32[]{:S(2)}) copy-start(s32[8,256]{1,0:T(8,128)S(1)} %collective-permute-done.refs_1_) | copy-start | bytes 24580
  126.3 6.1 copy-start.8
  161.7 23.5 %collective-permute-start.2 = (bf16[256,960]{1,0:T(8,128)(2,1)S(1)}, bf16[256,960]{1,0:T(8,128)(2,1)S(1)}, u32[]{:S(2)}, u32[]{:S(2)}) collective-permute-start(bf16[256,960]{1,0:T(8,128)(2,1)S(1)} %convolution_convert_fusion.4), channel_id=1, source_target_pairs={{0,0},{1,1},{2,8},{3,9},{4,16},{5,17},{6,24},{7,25},{8,2},{9,3},{1... | collective-permute-start | bytes 1474568 | tf_op jit(solution)/shard_map/ppermute | solution.py:1438
  459.1 9.0 %copy-start.23 = (f32[1,960]{1,0:T(1,128)S(1)}, f32[1,960]{1,0:T(1,128)}, u32[]{:S(2)}) copy-start(f32[1,960]{1,0:T(1,128)} %get-tuple-element.180) | copy-start | bytes 11524
  459.1 9.0 %copy-start.26 = (f32[1,960]{1,0:T(1,128)S(1)}, f32[1,960]{1,0:T(1,128)}, u32[]{:S(2)}) copy-start(f32[1,960]{1,0:T(1,128)} %get-tuple-element.183) | copy-start | bytes 11524
  459.1 9.0 %copy-start.28 = (f32[1,960]{1,0:T(1,128)S(1)}, f32[1,960]{1,0:T(1,128)}, u32[]{:S(2)}) copy-start(f32[1,960]{1,0:T(1,128)} %get-tuple-element.181) | copy-start | bytes 11524
  459.1 9.1 %copy-start.29 = (f32[1,960]{1,0:T(1,128)S(1)}, f32[1,960]{1,0:T(1,128)}, u32[]{:S(2)}) copy-start(f32[1,960]{1,0:T(1,128)} %get-tuple-element.184) | copy-start | bytes 11524
  459.1 9.1 %copy-start.31 = (f32[1,960]{1,0:T(1,128)S(1)}, f32[1,960]{1,0:T(1,128)}, u32[]{:S(2)}) copy-start(f32[1,960]{1,0:T(1,128)} %get-tuple-element.185) | copy-start | bytes 11524
  459.1 9.1 %copy-start.24 = (f32[1,960]{1,0:T(1,128)S(1)}, f32[1,960]{1,0:T(1,128)}, u32[]{:S(2)}) copy-start(f32[1,960]{1,0:T(1,128)} %get-tuple-element.182) | copy-start | bytes 11524
  459.1 9.1 %copy-start.25 = (f32[1,960]{1,0:T(1,128)S(1)}, f32[1,960]{1,0:T(1,128)}, u32[]{:S(2)}) copy-start(f32[1,960]{1,0:T(1,128)} %get-tuple-element.186) | copy-start | bytes 11524
  459.2 9.1 %copy-start.27 = (f32[1,960]{1,0:T(1,128)S(1)}, f32[1,960]{1,0:T(1,128)}, u32[]{:S(2)}) copy-start(f32[1,960]{1,0:T(1,128)} %get-tuple-element.187) | copy-start | bytes 11524
  459.2 9.1 %copy-start.30 = (f32[1,960]{1,0:T(1,128)S(1)}, f32[1,960]{1,0:T(1,128)}, u32[]{:S(2)}) copy-start(f32[1,960]{1,0:T(1,128)} %get-tuple-element.188) | copy-start | bytes 11524
  459.2 9.4 %copy-start.15 = (bf16[192,960]{1,0:T(8,128)(2,1)S(1)}, bf16[192,960]{1,0:T(8,128)(2,1)}, u32[]{:S(2)}) copy-start(bf16[192,960]{1,0:T(8,128)(2,1)} %get-tuple-element.189) | copy-start | bytes 1105924
  459.2 9.4 %copy-start.11 = (bf16[256,960]{1,0:T(8,128)(2,1)S(1)}, bf16[256,960]{1,0:T(8,128)(2,1)}, u32[]{:S(2)}) copy-start(bf16[256,960]{1,0:T(8,128)(2,1)} %get-tuple-element.118.mixed_ref) | copy-start | bytes 1474564
  459.2 9.4 %copy-start.16 = (bf16[192,960]{1,0:T(8,128)(2,1)S(1)}, bf16[192,960]{1,0:T(8,128)(2,1)}, u32[]{:S(2)}) copy-start(bf16[192,960]{1,0:T(8,128)(2,1)} %get-tuple-element.125.mixed_ref) | copy-start | bytes 1105924
  461.4 158.5 %collective-permute-start.3 = (bf16[256,960]{1,0:T(8,128)(2,1)}, bf16[256,960]{1,0:T(8,128)(2,1)}, u32[]{:S(2)}, u32[]{:S(2)}) collective-permute-start(bf16[256,960]{1,0:T(8,128)(2,1)} %pad_maximum_fusion.2), channel_id=1, source_target_pairs={{0,0},{1,1},{2,8},{3,9},{4,16},{5,17},{6,24},{7,25},{8,2},{9,3},{1... | collective-permute-start | bytes 1474568 | tf_op jit(solution)/shard_map/ppermute | solution.py:1500
  463.4 158.8 %collective-permute-start.4 = (bf16[256,960]{1,0:T(8,128)(2,1)S(1)}, bf16[256,960]{1,0:T(8,128)(2,1)S(1)}, u32[]{:S(2)}, u32[]{:S(2)}) collective-permute-start(bf16[256,960]{1,0:T(8,128)(2,1)S(1)} %convert_element_type.134), channel_id=1, source_target_pairs={{0,0},{1,1},{2,8},{3,9},{4,16},{5,17},{6,24},{7,25},{8,2},{9,3},{1... | collective-permute-start | bytes 1474568 | tf_op jit(solution)/shard_map/ppermute | solution.py:1501
  474.7 5.9 copy-start.35
  474.7 5.9 copy-start.37
  474.7 5.9 copy-start.39
  480.6 5.9 copy-start.41
  616.4 6.8 %copy-start.1 = (bf16[256,960]{0,1:T(8,128)(2,1)S(1)}, bf16[256,960]{0,1:T(8,128)(2,1)}, u32[]{:S(2)}) copy-start(bf16[256,960]{0,1:T(8,128)(2,1)} %param.15) | copy-start | bytes 1474564
  (20 other events, 59.3 us)

commit v7 on v6

--- a/solution.py
+++ b/solution.py
@@ -890,28 +890,37 @@
     return v * lax.rsqrt(jnp.mean(v * v, axis=-1, keepdims=True) + EPS) * gain
 
 
-def project_kernel(state_ref, gain_ref, w_ref, turn_ref, n1_ref, q_ref, kv_ref):
-    project_into(state_ref[...], gain_ref[...], w_ref, turn_ref, n1_ref, q_ref, kv_ref)
-
-
-def project(state, gain, w, turns):
+def project_kernel(state_ref, w_ref, turn_ref, n1_ref, q_ref, kv_ref, small_ref):
+    start = (CHUNKS - 1) * LANES
+    small = jnp.transpose(w_ref[:, start:start + LANES].astype(F32))[HD:HD + 8]
+    small_ref[...] = small
+    project_into(
+        state_ref[...].astype(F32), small[RECS:RECS + 1], w_ref, turn_ref, n1_ref, q_ref, kv_ref
+    )
+
+
+def project(state, w, turns):
     n, model = state.shape
     return pl.pallas_call(
         project_kernel,
         grid=(1,),
-        in_specs=[whole(n, model), whole(1, model), whole(*w.shape), whole(*turns.shape)],
-        out_specs=[whole(n, model), whole(CHUNKS, n, LANES), whole(n, KV_HEADS * LANES)],
+        in_specs=[whole(n, model), whole(*w.shape), whole(*turns.shape)],
+        out_specs=[
+            whole(n, model), whole(CHUNKS, n, LANES), whole(n, KV_HEADS * LANES),
+            whole(8, model),
+        ],
         out_shape=[
             jax.ShapeDtypeStruct((n, model), BF),
             jax.ShapeDtypeStruct((CHUNKS, n, LANES), BF),
             jax.ShapeDtypeStruct((n, KV_HEADS * LANES), BF),
+            jax.ShapeDtypeStruct((8, model), F32),
         ],
         compiler_params=pltpu.CompilerParams(vmem_limit_bytes=ROOM),
         name="project",
-    )(state, gain, w, turns)
-
-
-def attend_kernel(rows, span, key_ref, query_ref, kv_ref, q_ref, mixed_ref, out_ref, stat_ref,
+    )(state, w, turns)
+
+
+def attend_kernel(rows, recursion, span, key_ref, query_ref, kv_ref, q_ref, mixed_ref, out_ref, stat_ref,
                   stacked, mixing, tops, sums):
     low = lanes_of(rows) < HD
     wide = SHARES * rows
@@ -928,7 +937,7 @@
 
     def body(t, carry):
         at = pl.ds(pl.multiple_of(t * rows, rows), rows)
-        bias = block_bias(key_ref[at, :], query_ref)
+        bias = block_bias(key_ref[t], query_ref, recursion, rows)
         def score(h):
             kv = kv_ref[at, h * LANES:(h + 1) * LANES]
             return lax.dot_general(kv, stacked[h], NT, preferred_element_type=F32) + bias
@@ -970,9 +979,11 @@
         mixed_ref[:, j * LANES:j * LANES + size] = both.astype(BF)[:, :size]
 
 
-def block_bias(keys, query_ref):
-    live, order = keys[:, 0:1], keys[:, 1:2]
-    begin, place = query_ref[0:1, :], query_ref[1:2, :]
+def block_bias(labels, query_ref, recursion, rows):
+    keys = jnp.transpose(labels.astype(F32))[:rows]
+    order, level = keys[:, 0:1], keys[:, 2:3]
+    live = jnp.where(level > recursion, order, -1.0)
+    place, begin = query_ref[0:1, :].astype(F32), query_ref[1:2, :].astype(F32)
     allowed = ((live >= begin) & (live <= place)) | (order == place)
     return jnp.where(allowed, 0.0, BIG)
 
@@ -987,16 +998,16 @@
     return jnp.transpose(jnp.concatenate([one(2 * j), one(2 * j + 1)], axis=0))
 
 
-def attend(rows, span, key_labels, query_labels, kv_all, q):
+def attend(rows, recursion, span, key_labels, query_labels, kv_all, q):
     count, columns = kv_all.shape
     wide = SHARES * rows
     return pl.pallas_call(
-        functools.partial(attend_kernel, rows),
+        functools.partial(attend_kernel, rows, recursion),
         grid_spec=pltpu.PrefetchScalarGridSpec(
             num_scalar_prefetch=1,
             grid=(1,),
             in_specs=[
-                whole(count, 8), whole(8, wide), whole(count, columns),
+                whole(*key_labels.shape), whole(8, wide), whole(count, columns),
                 whole(CHUNKS, rows, LANES),
             ],
             out_specs=[
@@ -1021,7 +1032,7 @@
     )(span, key_labels, query_labels, kv_all, q)
 
 
-def attend_back_kernel(rows, span, key_ref, query_ref, kv_ref, q_ref, d_ref, out_ref, stat_ref,
+def attend_back_kernel(rows, recursion, span, key_ref, query_ref, kv_ref, q_ref, d_ref, out_ref, stat_ref,
                        turn_ref, dq_ref, dkv_ref, stacked, part, mixing, deltas):
     low = lanes_of(rows) < HD
     wide = SHARES * rows
@@ -1050,7 +1061,7 @@
 
     def body(t, carry):
         at = pl.ds(pl.multiple_of(t * rows, rows), rows)
-        bias = block_bias(key_ref[at, :], query_ref)
+        bias = block_bias(key_ref[t], query_ref, recursion, rows)
         for h in range(KV_HEADS):
             kv = kv_ref[at, h * LANES:(h + 1) * LANES]
             zero = jnp.zeros_like(kv)
@@ -1073,18 +1084,18 @@
         dq_ref[:, j * LANES:(j + 1) * LANES] = both.astype(BF)
 
 
-def attend_back(rows, span, key_labels, query_labels, kv_all, q, d_mixed, out, stat, turns):
+def attend_back(rows, recursion, span, key_labels, query_labels, kv_all, q, d_mixed, out, stat, turns):
     count, columns = kv_all.shape
     wide = SHARES * rows
     return pl.pallas_call(
-        functools.partial(attend_back_kernel, rows),
+        functools.partial(attend_back_kernel, rows, recursion),
         grid_spec=pltpu.PrefetchScalarGridSpec(
             num_scalar_prefetch=1,
             grid=(1,),
             in_specs=[
-                whole(count, 8), whole(8, wide), whole(count, columns),
+                whole(*key_labels.shape), whole(8, wide), whole(count, columns),
                 whole(CHUNKS, rows, LANES), whole(CHUNKS, rows, LANES),
-                whole(CHUNKS, rows, LANES), whole(KV_HEADS, 8, wide), whole(*turns.shape),
+                whole(CHUNKS, rows, LANES), whole(KV_HEADS, 8, wide), whole(2, rows, LANES),
             ],
             out_specs=[whole(rows, CHUNKS * LANES), whole(count, columns)],
             scratch_shapes=[
@@ -1113,7 +1124,7 @@
         out_ref[j] = v
 
 
-def project_back_kernel(gradient_ref, state_ref, gain_ref, w_ref, turn_ref, dq_ref, raw_ref,
+def project_back_kernel(gradient_ref, state_ref, small_ref, w_ref, turn_ref, dq_ref, raw_ref,
                         grad_ref, joint_ref, dgain_ref):
     cosine, sine = turn_ref[0], turn_ref[1]
     key = lanes_of(dq_ref.shape[0]) < HD
@@ -1127,23 +1138,23 @@
     if joint_ref.shape[1] > full:
         joint_ref[:, full:] = jnp.zeros((key.shape[0], joint_ref.shape[1] - full), BF)
     d = lax.dot_general(joint_ref[:, :full], w_ref[...], NT, preferred_element_type=F32)
-    v = state_ref[...]
+    v = state_ref[...].astype(F32)
     inv = lax.rsqrt(jnp.mean(v * v, axis=-1, keepdims=True) + EPS)
-    scaled = d * gain_ref[...]
+    scaled = d * small_ref[RECS:RECS + 1, :]
     dot = jnp.mean(scaled * v, axis=-1, keepdims=True)
     grad_ref[...] = gradient_ref[...] + inv * scaled - v * (inv * inv * inv * dot)
     dgain_ref[...] = jnp.sum(d * v * inv, axis=0, keepdims=True)
 
 
-def project_back(gradient, state, gain, w, turns, dq, dkv):
-    n, model = state.shape
+def project_back(gradient, state, small, w, turns, dq, dkv):
+    n, model = dq.shape[0], state.shape[1]
     joint = -(-w.shape[1] // 256) * 256
     return pl.pallas_call(
         project_back_kernel,
         grid=(1,),
         in_specs=[
-            whole(n, model), whole(n, model), whole(1, model), whole(*w.shape),
-            whole(*turns.shape), whole(*dq.shape), whole(*dkv.shape),
+            whole(n, model), whole(n, model), whole(8, model), whole(*w.shape),
+            whole(2, n, LANES), whole(*dq.shape), whole(*dkv.shape),
         ],
         out_specs=[whole(n, model), whole(n, joint), whole(1, model)],
         out_shape=[
@@ -1153,7 +1164,7 @@
         ],
         compiler_params=pltpu.CompilerParams(vmem_limit_bytes=ROOM),
         name="project_back",
-    )(gradient, state, gain, w, turns, dq, dkv)
+    )(gradient, state, small, w, turns, dq, dkv)
 
 
 def project_into(state, gain, w_ref, turn_ref, n1_ref, q_ref, kv_ref):
@@ -1177,20 +1188,25 @@
                 kv_ref[:, j * LANES:(j + 1) * LANES] = jnp.where(key, turned, v).astype(BF)
 
 
-def feed_kernel(following, mixed_ref, state_ref, w_out_ref, gain_ref, router_ref, active_ref,
+def active_column(label_ref, recursion, rows):
+    level = jnp.transpose(label_ref[...].astype(F32))[:rows, 2:3]
+    return jnp.where(level > recursion, 1.0, 0.0)
+
+
+def feed_kernel(recursion, following, mixed_ref, state_ref, w_out_ref, small_ref, label_ref,
                 w_gate_ref, w_up_ref, w_down_ref, *refs):
     if following:
-        next_gain_ref, w_ref, turn_ref = refs[:3]
-        refs = refs[3:]
+        w_ref, turn_ref = refs[:2]
+        refs = refs[2:]
     (new_ref, middle_ref, n2_ref, gated_ref, up_ref, hidden_ref, both_ref, gate_ref) = refs[:8]
     step = pl.program_id(0)
 
     @pl.when(step == 0)
     def _():
         att = jnp.dot(mixed_ref[...], w_out_ref[...], preferred_element_type=F32)
-        middle = state_ref[...] + att
+        middle = state_ref[...].astype(F32) + att
         middle_ref[...] = middle
-        n2_ref[...] = normed(middle, gain_ref[...]).astype(BF)
+        n2_ref[...] = normed(middle, small_ref[RECS + 1:RECS + 2, :]).astype(BF)
         both_ref[...] = att
 
     n2 = n2_ref[...]
@@ -1204,18 +1220,20 @@
 
     @pl.when(step == pl.num_programs(0) - 1)
     def _():
-        state = state_ref[...]
-        gate = jax.nn.sigmoid(jnp.sum(state * router_ref[...], axis=-1, keepdims=True))
+        state = state_ref[...].astype(F32)
+        router = small_ref[recursion:recursion + 1, :]
+        gate = jax.nn.sigmoid(jnp.sum(state * router, axis=-1, keepdims=True))
+        active = active_column(label_ref, recursion, state.shape[0])
         gate_ref[...] = gate
-        new_ref[...] = state + active_ref[...] * gate * both_ref[...]
+        new_ref[...] = state + active * gate * both_ref[...]
         if following:
             project_into(
-                new_ref[:following, :], next_gain_ref[...], w_ref, turn_ref, *refs[8:11]
+                new_ref[:following, :], small_ref[RECS:RECS + 1, :], w_ref, turn_ref, *refs[8:11]
             )
 
 
-def feed(mixed, state, w_out, gain, router, active, w_gate, w_up, w_down, following, then=()):
-    n, model = state.shape
+def feed(recursion, mixed, state, w_out, small, labels, w_gate, w_up, w_down, following, then=()):
+    n, model = mixed.shape
     ff = w_gate.shape[1]
     tile = 512 if ff % 512 == 0 else ff
     across = pl.BlockSpec((model, tile), lambda i: (0, i))
@@ -1235,29 +1253,30 @@
         out_specs += [whole(*s) for s in shapes]
         out_shape += [jax.ShapeDtypeStruct(s, BF) for s in shapes]
     return pl.pallas_call(
-        functools.partial(feed_kernel, following),
+        functools.partial(feed_kernel, recursion, following),
         grid=(ff // tile,),
         in_specs=[
-            whole(n, model), whole(n, model), whole(*w_out.shape), whole(1, model),
-            whole(1, model), whole(n, 1), across, across,
+            whole(n, model), whole(n, model), whole(*w_out.shape), whole(8, model),
+            whole(*labels.shape), across, across,
             pl.BlockSpec((tile, model), lambda i: (i, 0)),
-        ] + [whole(*v.shape) for v in then],
+        ] + ([whole(*then[0].shape), whole(2, following, LANES)] if following else []),
         out_specs=out_specs,
         out_shape=out_shape,
         compiler_params=pltpu.CompilerParams(vmem_limit_bytes=ROOM),
         name="feed",
-    )(mixed, state, w_out, gain, router, active, w_gate, w_up, w_down, *then)
-
-
-def feed_back_kernel(gradient_ref, both_ref, gate_ref, active_ref, state_ref, router_ref,
-                     middle_ref, gain_ref, w_out_ref, gated_ref, up_ref, w_gate_ref, w_up_ref,
+    )(mixed, state, w_out, small, labels, w_gate, w_up, w_down, *then)
+
+
+def feed_back_kernel(recursion, gradient_ref, both_ref, gate_ref, label_ref, state_ref,
+                     small_ref, middle_ref, w_out_ref, gated_ref, up_ref, w_gate_ref, w_up_ref,
                      w_down_ref, d_fed_ref, d_gated_ref, d_up_ref, d_att_ref, grad_ref,
                      d_mixed_ref, d_router_ref, d_gain_ref, total):
     step = pl.program_id(0)
 
     @pl.when(step == 0)
     def _():
-        d_fed_ref[...] = (active_ref[...] * gate_ref[...] * gradient_ref[...]).astype(BF)
+        active = active_column(label_ref, recursion, gate_ref.shape[0])
+        d_fed_ref[...] = (active * gate_ref[...] * gradient_ref[...].astype(F32)).astype(BF)
         total[...] = jnp.zeros(total.shape, F32)
 
     d_hidden = lax.dot_general(d_fed_ref[...], w_down_ref[...], NT, preferred_element_type=F32)
@@ -1274,26 +1293,28 @@
 
     @pl.when(step == pl.num_programs(0) - 1)
     def _():
-        gradient, gate, active = gradient_ref[...], gate_ref[...], active_ref[...]
+        gradient, gate = gradient_ref[...].astype(F32), gate_ref[...]
+        active = active_column(label_ref, recursion, gate.shape[0])
+        router = small_ref[recursion:recursion + 1, :]
         d = total[...]
         v = middle_ref[...]
         inv = lax.rsqrt(jnp.mean(v * v, axis=-1, keepdims=True) + EPS)
         d_gain_ref[...] = jnp.sum(d * v * inv, axis=0, keepdims=True)
-        scaled = d * gain_ref[...]
+        scaled = d * small_ref[RECS + 1:RECS + 2, :]
         dot = jnp.mean(scaled * v, axis=-1, keepdims=True)
         d_middle = inv * scaled - v * (inv * inv * inv * dot)
         d_gate = active * gate * (1.0 - gate) * jnp.sum(
             gradient * both_ref[...], axis=-1, keepdims=True
         )
-        d_router_ref[...] = jnp.sum(state_ref[...] * d_gate, axis=0, keepdims=True)
-        grad_ref[...] = gradient + d_gate * router_ref[...] + d_middle
+        d_router_ref[...] = jnp.sum(state_ref[...].astype(F32) * d_gate, axis=0, keepdims=True)
+        grad_ref[...] = gradient + d_gate * router + d_middle
         d_att_ref[...] = (active * gate * gradient + d_middle).astype(BF)
         out_back_kernel(d_att_ref, w_out_ref, d_mixed_ref)
 
 
-def feed_back(gradient, both, gate, active, state, router, middle, gain, w_out, gated, upward,
+def feed_back(recursion, gradient, both, gate, labels, state, small, middle, w_out, gated, upward,
               w_gate, w_up, w_down):
-    n, model = state.shape
+    n, model = both.shape
     ff = w_gate.shape[1]
     tile = 512 if ff % 512 == 0 else ff
     across = pl.BlockSpec((model, tile), lambda i: (0, i))
@@ -1303,10 +1324,10 @@
     tall = jax.ShapeDtypeStruct((n, ff), BF)
     row = jax.ShapeDtypeStruct((1, model), F32)
     return pl.pallas_call(
-        feed_back_kernel,
+        functools.partial(feed_back_kernel, recursion),
         grid=(ff // tile,),
         in_specs=[
-            wide, wide, whole(n, 1), whole(n, 1), wide, whole(1, model), wide, whole(1, model),
+            wide, wide, whole(n, 1), whole(*labels.shape), wide, whole(8, model), wide,
             whole(*w_out.shape), made, made, across, across,
             pl.BlockSpec((tile, model), lambda i: (i, 0)),
         ],
@@ -1321,8 +1342,8 @@
         scratch_shapes=[pltpu.VMEM((n, model), F32)],
         compiler_params=pltpu.CompilerParams(vmem_limit_bytes=ROOM),
         name="feed_back",
-    )(gradient, both, gate, active, state, router, middle, gain, w_out, gated, upward, w_gate,
-      w_up, w_down)
+    )(gradient, both, gate, labels, state, small, middle, w_out, gated, upward, w_gate, w_up,
+      w_down)
 
 
 def outer_rows_kernel(count, *refs):
@@ -1398,7 +1419,7 @@
     labels = jnp.sum(jnp.where(chosen[None], labels[:, None, :], 0), axis=2)
     labels = jnp.pad(labels, ((0, 5), (0, 0)))
     swap = topo.swap_pairs()
-    state = lax.ppermute(mm(onehot, tokens).astype(BF), AXES, swap).astype(F32)
+    state = lax.ppermute(mm(onehot, tokens).astype(BF), AXES, swap)
     labels = lax.ppermute(labels, AXES, swap)
     cotangent = mm(onehot, cotangent).astype(BF)
 
@@ -1413,25 +1434,22 @@
         return group_scatter(topo, grads, ck + yk + xk)
 
 
-    small = weight_qkv[:, model:model + HD].astype(F32)
-    gain_one, gain_two = small[:, RECS][None], small[:, RECS + 1][None]
-
     pack = (lax.axis_index("grp") * topo.X) + lax.axis_index("tok") % topo.X
-    begin_all, level_mine = labels[1], labels[2]
     lowest = jnp.min(labels[1])
     span = jnp.stack([lowest // rows, pack + 1]).astype(jnp.int32)
     places = (labels[0] - labels[1]).astype(F32)
-    freqs = 10000.0 ** (-(jnp.arange(HD // 2, dtype=F32) * 2.0 / HD))
+    turn = (jnp.arange(LANES) % (HD // 2)).astype(F32)
+    freqs = 10000.0 ** (-(turn * 2.0 / HD))
     angles = places[:, None] * freqs[None, :]
     turns = jnp.stack([jnp.cos(angles), jnp.sin(angles)])
-    turns = jnp.tile(turns, (1, 1, LANES * 2 // HD))
-
-    routers = [small[:, r][None] for r in range(RECS)]
+    query_labels = {
+        n: jnp.concatenate([labels[:, :n]] * SHARES, axis=1) for n in (rows, deep_rows)
+    }
 
     def forward(state, projected, recursion, labels_all=None):
-        n = state.shape[0]
         extra = None
         n1, q, kv = projected
+        n = n1.shape[0]
         if recursion == 0:
             kv_all, labels_all = collect([kv, labels], 2)
             kv_all, later = lax.optimization_barrier((kv_all, cotangent))
@@ -1439,60 +1457,53 @@
         else:
             kv_all, = collect([kv], 3)
         kv_all = kv_all.reshape(topo.T * n, 2 * kv_cols)
-        live = labels_all[:, 2, :n] > recursion
-        order = labels_all[:, 0, :n]
-        key_labels = jnp.stack([jnp.where(live, order, -1), order], axis=-1).reshape(-1, 2)
-        key_labels = jnp.pad(key_labels, ((0, 0), (0, 6)))
-        query_labels = jnp.stack([labels[1, :n], labels[0, :n]])
-        query_labels = jnp.pad(jnp.tile(query_labels, (1, SHARES)), ((0, 6), (0, 0)))
-        mixed, out, stat = attend(n, span, key_labels, query_labels, kv_all, q)
+        mixed, out, stat = attend(n, recursion, span, labels_all, query_labels[n], kv_all, q)
         if recursion == 0:
             mixed, later = lax.optimization_barrier((mixed, later))
-            extra = (labels_all, later.astype(F32))
-        active = (labels[2, :n] > recursion).astype(F32)[:, None]
+            extra = (labels_all, later)
         following = deep_rows if recursion + 1 < RECS else 0
         new, middle, n2, gated, upward, hidden, both, gate, *projected = feed(
-            mixed, state, weight_o, gain_two, routers[recursion], active, weight_g, weight_u,
-            weight_d, following, (gain_one, weight_qkv, turns) if following else (),
-        )
-        kept = (state, n1, q, kv_all, key_labels, query_labels, out, stat, mixed, middle,
-                n2, gated, upward, hidden, both, gate, active)
+            recursion, mixed, state, weight_o, small, labels, weight_g, weight_u, weight_d,
+            following, (weight_qkv, turns) if following else (),
+        )
+        kept = (state, n1, q, kv_all, labels_all, out, stat, mixed, middle, n2, gated, upward,
+                hidden, both, gate)
         return (new, projected, kept, extra)
 
     def backward(gradient, recursion, kept):
-        (state, n1, q, kv_all, key_labels, query_labels, out, stat, mixed, middle,
-         n2, gated, upward, hidden, both, gate, active) = kept
-        n = state.shape[0]
+        (state, n1, q, kv_all, labels_all, out, stat, mixed, middle, n2, gated, upward, hidden,
+         both, gate) = kept
+        n = n1.shape[0]
         d_fed, d_gated, d_up, d_att, gradient, d_mixed, d_router, d_gain_two = feed_back(
-            gradient, both, gate, active, state, routers[recursion], middle, gain_two, weight_o,
-            gated, upward, weight_g, weight_u, weight_d,
+            recursion, gradient, both, gate, labels, state, small, middle, weight_o, gated,
+            upward, weight_g, weight_u, weight_d,
         )
         dq, dkv = attend_back(
-            n, span, key_labels, query_labels, kv_all, q, d_mixed, out, stat, turns[:, :n]
+            n, recursion, span, labels_all, query_labels[n], kv_all, q, d_mixed, out, stat, turns
         )
         dkv = distribute(dkv.reshape(topo.T, n, 2 * kv_cols), 5 if recursion else 4)
         gradient, dqkv, d_gain_one = project_back(
-            gradient, state, gain_one, weight_qkv, turns[:, :n], dq, dkv
+            gradient, state, small, weight_qkv, turns, dq, dkv
         )
         left = (n1, dqkv, mixed, d_att, n2, d_gated, d_up, hidden, d_fed)
         return (gradient, left, (d_router[0], d_gain_one[0], d_gain_two[0]))
 
-    projected = project(state, gain_one, weight_qkv, turns)
+    *projected, small = project(state, weight_qkv, turns)
     whole_state, projected, kept, (labels_all, gradient) = forward(state, projected, 0)
-    deep = whole_state[:deep_rows]
+    deep = whole_state
     all_kept = [kept]
     for recursion in range(1, RECS):
         deep, projected, kept, _ = forward(deep, projected, recursion, labels_all)
         all_kept.append(kept)
     final = jnp.concatenate([deep, whole_state[deep_rows:]], axis=0).astype(BF)
 
-    deep_grad = gradient[:deep_rows]
+    deep_grad = gradient
     lefts, smalls = [], []
     for recursion in reversed(range(1, RECS)):
         deep_grad, left, tiny = backward(deep_grad, recursion, all_kept[recursion])
         lefts.append(left)
         smalls.append(tiny)
-    gradient = jnp.concatenate([deep_grad, gradient[deep_rows:]], axis=0)
+    gradient = jnp.concatenate([deep_grad, gradient[deep_rows:].astype(F32)], axis=0)
     gradient, left, tiny = backward(gradient, 0, all_kept[0])
     lefts.append(left)
     smalls.append(tiny)

time: 635 us -> 624 us (0.983)
  local copies, waits for them, and re-layouts: 29.3 us -> 18 us
    pallas_call x3, Pallas kernels: 62.4 us -> 53.8 us  [reduce_layer(): pl.pallas_call(functools.partial(group_reduce_kernel, topo), in_specs=[pl...]
    slice x8 -> x0, local copies, waits for them, and re-layouts: 7.38 us -> none  [the longest x1 2.12 us: per_device(): deep = whole_state[:deep_rows]]
  transfers between devices with their start and end apart: 5 -> 5, of which waited for: 1 -> 1; matrix products, arithmetic and copies ran while one was open for 7% -> 6% of each run, Pallas kernels for 38% -> 39%
where the time goes in v7:
time: 624 us; the launch traced here: 613 us
  Pallas kernels  516 us (83%)
  matrix products  24.7 us (4%)
  other arithmetic  20.9 us (3%)
  local copies, waits for them, and re-layouts  18 us (3%)
  starting transfers between devices  17.7 us (3%)
  waiting for transfers between devices  10.6 us (2%)
    pallas_call x1, Pallas kernels, reduce_gradients(): pl.pallas_call(functools.partial(reduce_kernel, topo, shares), in_specs=[...  118 us
    pallas_call x1, Pallas kernels, gather_weights(): pl.pallas_call(functools.partial(gather_kernel, topo, pieces), in_specs=[...  105 us
    pallas_call x3, Pallas kernels, reduce_layer(): pl.pallas_call(functools.partial(group_reduce_kernel, topo), in_specs=[pl...  53.8 us
    pallas_call x3, Pallas kernels, gather_layer(): pl.pallas_call(functools.partial(group_gather_kernel, topo, n), in_specs=...  52.9 us
    pallas_call x3, Pallas kernels, feed_back(): pl.pallas_call(functools.partial(feed_back_kernel, recursion), grid=(ff /...  46.6 us
    pallas_call x3, Pallas kernels, feed(): pl.pallas_call(functools.partial(feed_kernel, recursion, following), grid...  44.8 us
    pallas_call x3, Pallas kernels, attend_back(): pl.pallas_call(functools.partial(attend_back_kernel, rows, recursion), gr...  41 us
    pallas_call x3, Pallas kernels, attend(): pl.pallas_call(functools.partial(attend_kernel, rows, recursion), grid_sp...  27.3 us
  transfers between devices with their start and end apart: 5, of which 1 were waited for; matrix products, arithmetic and copies ran while one was open for 6% of the time, Pallas kernels for 39%

profile of v7, /device:TPU:17, one launch (start us, length us, event | category | flops | bytes accessed | tf_op | source)
XLA Modules:
  0.0 612.8 jit_solution(9217367044954827652)
XLA Ops:
  5.5 3.6 collective-permute-start
  14.2 105.0 %gather_weights.1 = (bf16[8,120,1664]{2,1,0:T(8,128)(2,1)}, bf16[8,120,2560]{2,1,0:T(8,128)(2,1)}, bf16[8,120,2560]{2,1,0:T(8,128)(2,1)}, bf16[8,320,960]{2,1,0:T(8,128)(2,1)}, bf16[8,120,960]{2,1,0:T(8,128)(2,1)}) custom-call(bf16[120,1664]{1,0:T(8,128)(2,1)} %concatenate.51.refs_0_, bf16[120,2560]{1,0:T(8,128)(2,1)} %refs_1_.1, bf16[120,2560]{1,0:T(8,128)(2,1)} %refs_2_.1, ...), custom_call_target="tpu_custom_call" | custom-call | tf_op jit(solution)/shard_map/gather_weights/pallas_call | solution.py:298
  126.0 4.3 project.1
  130.3 20.1 %gather_layer.3 = (bf16[8,256,640]{2,1,0:T(8,128)(2,1)}, s32[8,8,256]{2,1,0:T(8,128)}) custom-call(bf16[256,640]{1,0:T(8,128)(2,1)} %get-tuple-element.112.refs_0_, s32[8,256]{1,0:T(8,128)} %copy-done.10), custom_call_target="tpu_custom_call" | custom-call | tf_op jit(solution)/shard_map/gather_layer/pallas_call | solution.py:782
  152.3 10.8 %attend.3 = (bf16[256,960]{1,0:T(8,128)(2,1)}, f32[8,256,128]{2,1,0:T(8,128)}, f32[5,8,768]{2,1,0:T(8,128)}) custom-call(s32[2]{0:T(128)} %pad_add_fusion.2.span, s32[8,8,256]{2,1,0:T(8,128)} %get-tuple-element.113.key_ref, s32[8,768]{1,0:T(8,128)} %copy-done.24, bf16[2048,640]{1,0:T(8,128)(2,1)} %bitcast.105, bf16[8,256,128]{2,1,0:T(8,128)(2,1)} %get-tuple-element.116.q_ref), custom_call_target="tpu_custom_call" | custom-call | flops 8053063680 | bytes 5242880 | tf_op jit(solution)/shard_map/attend/pallas_call | solution.py:1004
  163.1 10.6 %collective-permute-done.2.gradient_ref = bf16[256,960]{1,0:T(8,128)(2,1)S(1)} collective-permute-done((bf16[256,960]{1,0:T(8,128)(2,1)S(1)}, bf16[256,960]{1,0:T(8,128)(2,1)S(1)}, u32[]{:S(2)}, u32[]{:S(2)}) %collective-permute-start.2) | collective-permute-done | bytes 491552 | tf_op jit(solution)/shard_map/ppermute | solution.py:1456
  173.8 16.3 %feed.3 = (f32[256,960]{1,0:T(8,128)}, f32[256,960]{1,0:T(8,128)}, bf16[256,960]{1,0:T(8,128)(2,1)}, bf16[256,2560]{1,0:T(8,128)(2,1)}, bf16[256,2560]{1,0:T(8,1...) custom-call(bf16[256,960]{1,0:T(8,128)(2,1)} %get-tuple-element.119., ...), custom_call_target="tpu_custom_call" | custom-call | tf_op jit(solution)/shard_map/feed/pallas_call | solution.py:1255
  191.1 12.0 %gather_layer.4 = bf16[8,192,640]{2,1,0:T(8,128)(2,1)} custom-call(bf16[192,640]{1,0:T(8,128)(2,1)} %get-tuple-element.125.refs_0_), custom_call_target="tpu_custom_call" | custom-call | tf_op jit(solution)/shard_map/gather_layer/pallas_call | solution.py:782
  203.0 8.1 %attend.4 = (bf16[192,960]{1,0:T(8,128)(2,1)}, f32[8,192,128]{2,1,0:T(8,128)}, f32[5,8,576]{2,1,0:T(8,128)}) custom-call(s32[2]{0:T(128)} %pad_add_fusion.2.span, s32[8,8,256]{2,1,0:T(8,128)} %get-tuple-element.113.key_ref, s32[8,576]{1,0:T(8,128)} %pad_add_fusion.query_ref, bf16[1536,640]{1,0:T(8,128)(2,1)} %bitcast.97, ...), custom_call_target="tpu_custom_call" | custom-call | flops 4529848320 | bytes 3932160 | tf_op jit(solution)/shard_map/attend/pallas_call | solution.py:1004
  211.2 15.3 %feed.4 = (f32[192,960]{1,0:T(8,128)}, f32[192,960]{1,0:T(8,128)}, bf16[192,960]{1,0:T(8,128)(2,1)}, bf16[192,2560]{1,0:T(8,128)(2,1)}, bf16[192,2560]{1,0:T(8,1...) custom-call(bf16[192,960]{1,0:T(8,128)(2,1)} %get-tuple-element.127., ...), custom_call_target="tpu_custom_call" | custom-call | tf_op jit(solution)/shard_map/feed/pallas_call | solution.py:1255
  226.4 20.8 %gather_layer.5 = bf16[8,192,640]{2,1,0:T(8,128)(2,1)} custom-call(bf16[192,640]{1,0:T(8,128)(2,1)} %get-tuple-element.129.refs_0_), custom_call_target="tpu_custom_call" | custom-call | tf_op jit(solution)/shard_map/gather_layer/pallas_call | solution.py:782
  247.2 8.4 %attend.5 = (bf16[192,960]{1,0:T(8,128)(2,1)}, f32[8,192,128]{2,1,0:T(8,128)}, f32[5,8,576]{2,1,0:T(8,128)}) custom-call(s32[2]{0:T(128)} %pad_add_fusion.2.span, s32[8,8,256]{2,1,0:T(8,128)} %get-tuple-element.113.key_ref, s32[8,576]{1,0:T(8,128)} %pad_add_fusion.query_ref, bf16[1536,640]{1,0:T(8,128)(2,1)} %bitcast.99, ...), custom_call_target="tpu_custom_call" | custom-call | flops 4529848320 | bytes 3932160 | tf_op jit(solution)/shard_map/attend/pallas_call | solution.py:1004
  255.6 13.2 %feed.5 = (f32[192,960]{1,0:T(8,128)}, f32[192,960]{1,0:T(8,128)}, bf16[192,960]{1,0:T(8,128)(2,1)}, bf16[192,2560]{1,0:T(8,128)(2,1)}, bf16[192,2560]{1,0:T(8,1...) custom-call(bf16[192,960]{1,0:T(8,128)(2,1)} %get-tuple-element.131.mixed_ref, ...), custom_call_target="tpu_custom_call" | custom-call | tf_op jit(solution)/shard_map/feed/pallas_call | solution.py:1255
  271.8 15.2 %feed_back.3 = (bf16[192,960]{1,0:T(8,128)(2,1)}, bf16[192,2560]{1,0:T(8,128)(2,1)}, bf16[192,2560]{1,0:T(8,128)(2,1)}, bf16[192,960]{1,0:T(8,128)(2,1)}, f32[19...) custom-call(bf16[256,960]{1,0:T(8,128)(2,1)} %copy-done.11, ...), custom_call_target="tpu_custom_call" | custom-call | tf_op jit(solution)/shard_map/feed_back/pallas_call | solution.py:1326
  287.0 13.2 %attend_back.3 = (bf16[192,1024]{1,0:T(8,128)(2,1)}, bf16[1536,640]{1,0:T(8,128)(2,1)}) custom-call(s32[2]{0:T(128)} %pad_add_fusion.2.span, s32[8,8,256]{2,1,0:T(8,128)} %get-tuple-element.113.key_ref, s32[8,576]{1,0:T(8,128)} %pad_add_fusion.query_ref, bf16[1536,640]{1,0:T(8,128)(2,1)} %bitcast.100, bf16[8,192,128]{2,1,0:T(8,128)(2,1)} %get-tuple-element.130.q_ref, ...), custom_call_target="tpu_custom_call" | custom-call | tf_op jit(solution)/shard_map/attend_back/pallas_call | solution.py:1090
  301.7 16.8 %reduce_layer.3.raw_ref = bf16[192,640]{1,0:T(8,128)(2,1)S(1)} custom-call(bf16[8,192,640]{2,1,0:T(8,128)(2,1)S(1)} %bitcast.66), custom_call_target="tpu_custom_call" | custom-call | tf_op jit(solution)/shard_map/reduce_layer/pallas_call | solution.py:852
  319.2 4.7 project_back.3
  323.9 15.2 %feed_back.4 = (bf16[192,960]{1,0:T(8,128)(2,1)}, bf16[192,2560]{1,0:T(8,128)(2,1)}, bf16[192,2560]{1,0:T(8,128)(2,1)}, bf16[192,960]{1,0:T(8,128)(2,1)}, f32[19...) custom-call(f32[192,960]{1,0:T(8,128)} %get-tuple-element.146.gradient_ref, ...), custom_call_target="tpu_custom_call" | custom-call | tf_op jit(solution)/shard_map/feed_back/pallas_call | solution.py:1326
  339.1 13.0 %attend_back.4 = (bf16[192,1024]{1,0:T(8,128)(2,1)}, bf16[1536,640]{1,0:T(8,128)(2,1)}) custom-call(s32[2]{0:T(128)} %pad_add_fusion.2.span, s32[8,8,256]{2,1,0:T(8,128)} %get-tuple-element.113.key_ref, s32[8,576]{1,0:T(8,128)} %pad_add_fusion.query_ref, bf16[1536,640]{1,0:T(8,128)(2,1)} %bitcast.98, bf16[8,192,128]{2,1,0:T(8,128)(2,1)} %get-tuple-element.126.q_ref, ...), custom_call_target="tpu_custom_call" | custom-call | tf_op jit(solution)/shard_map/attend_back/pallas_call | solution.py:1090
  353.6 17.5 %reduce_layer.4.raw_ref = bf16[192,640]{1,0:T(8,128)(2,1)S(1)} custom-call(bf16[8,192,640]{2,1,0:T(8,128)(2,1)S(1)} %bitcast.65), custom_call_target="tpu_custom_call" | custom-call | tf_op jit(solution)/shard_map/reduce_layer/pallas_call | solution.py:852
  371.9 4.7 project_back.4
  378.9 16.3 %feed_back.5 = (bf16[256,960]{1,0:T(8,128)(2,1)}, bf16[256,2560]{1,0:T(8,128)(2,1)}, bf16[256,2560]{1,0:T(8,128)(2,1)}, bf16[256,960]{1,0:T(8,128)(2,1)}, f32[25...) custom-call(f32[256,960]{1,0:T(8,128)} %pad_maximum_fusion.1.gradient_ref, ...), custom_call_target="tpu_custom_call" | custom-call | tf_op jit(solution)/shard_map/feed_back/pallas_call | solution.py:1326
  395.1 14.8 %attend_back.5 = (bf16[256,1024]{1,0:T(8,128)(2,1)}, bf16[2048,640]{1,0:T(8,128)(2,1)}) custom-call(s32[2]{0:T(128)} %pad_add_fusion.2.span, s32[8,8,256]{2,1,0:T(8,128)} %get-tuple-element.113.key_ref, s32[8,768]{1,0:T(8,128)} %copy-done.24, bf16[2048,640]{1,0:T(8,128)(2,1)} %bitcast.106, bf16[8,256,128]{2,1,0:T(8,128)(2,1)} %get-tuple-element.116.q_ref, ...), custom_call_target="tpu_custom_call" | custom-call | tf_op jit(solution)/shard_map/attend_back/pallas_call | solution.py:1090
  411.7 19.5 %reduce_layer.5.raw_ref = bf16[256,640]{1,0:T(8,128)(2,1)S(1)} custom-call(bf16[8,256,640]{2,1,0:T(8,128)(2,1)S(1)} %bitcast.64), custom_call_target="tpu_custom_call" | custom-call | tf_op jit(solution)/shard_map/reduce_layer/pallas_call | solution.py:852
  431.9 5.1 project_back.5
  439.8 7.2 %collective-permute-start.3 = (bf16[256,960]{1,0:T(8,128)(2,1)}, bf16[256,960]{1,0:T(8,128)(2,1)}, u32[]{:S(2)}, u32[]{:S(2)}) collective-permute-start(bf16[256,960]{1,0:T(8,128)(2,1)} %pad_maximum_fusion.2), channel_id=1, source_target_pairs={{0,0},{1,1},{2,8},{3,9},{4,16},{5,17},{6,24},{7,25},{8,2},{9,3},{1... | collective-permute-start | bytes 1474568 | tf_op jit(solution)/shard_map/ppermute | solution.py:1511
  450.8 3.2 convolution_convert_fusion.3
  456.8 5.9 convolution_convert_fusion.1
  462.7 5.8 convolution_convert_fusion
  468.5 4.7 convolution_convert_fusion.2
  473.2 8.2 %outer_rows.1 = bf16[2560,960]{1,0:T(8,128)(2,1)} custom-call(bf16[192,2560]{1,0:T(8,128)(2,1)} %get-tuple-element.197.refs_0_, bf16[192,2560]{1,0:T(8,128)(2,1)} %get-tuple-element.198.refs_1_, bf16[256,2560]{1,0:T(8,128)(2,1)} %get-tuple-element.199.refs_2_, bf16[192,960]{1,0:T(8,128)(2,1)} %get-tuple-element.200.refs_3_, ...), custom_call_target="tpu_custom_call" | custom-call | flops 3145728000 | bytes 9420800 | tf_op jit(solution)/shard_map/outer_rows/pallas_call | solution.py:1361
  481.4 118.0 %reduce_gradients.1 = (bf16[120,1792]{1,0:T(8,128)(2,1)}, bf16[120,1024]{1,0:T(8,128)(2,1)}, bf16[2,120,2560]{2,1,0:T(8,128)(2,1)}, bf16[320,960]{1,0:T(8,128)(2,1)}) custom-call(bf16[8,120,1792]{2,1,0:T(8,128)(2,1)} %bitcast.104, bf16[8,120,1024]{2,1,0:T(8,128)(2,1)} %pad_maximum_fusion.refs_1_, bf16[8,120,2560]{2,1,0:T(8,128)(2,1)} %bitcast.102, ...), custom_call_target="tpu_custom_call" | custom-call | tf_op jit(solution)/shard_map/reduce_gradients/pallas_call | solution.py:646
  (167 shorter events, 51.0 us)
Async XLA Ops:
  0.6 8.5 %copy-start = (bf16[256,960]{0,1:T(8,128)(2,1)S(1)}, bf16[256,960]{0,1:T(8,128)(2,1)}, u32[]{:S(2)}) copy-start(bf16[256,960]{0,1:T(8,128)(2,1)} %param.15) | copy-start | bytes 1474564
  0.7 11.9 %copy-start.15 = (bf16[256,960]{0,1:T(8,128)(2,1)S(1)}, bf16[256,960]{0,1:T(8,128)(2,1)}, u32[]{:S(2)}) copy-start(bf16[256,960]{0,1:T(8,128)(2,1)} %param.29) | copy-start | bytes 1474564
  0.7 12.2 %copy-start.22 = (bf16[120,320]{0,1:T(8,128)(2,1)S(1)}, bf16[120,320]{0,1:T(8,128)(2,1)}, u32[]{:S(2)}) copy-start(bf16[120,320]{0,1:T(8,128)(2,1)} %param.18) | copy-start | bytes 230404
  0.7 12.2 %copy-start.23 = (bf16[120,320]{0,1:T(8,128)(2,1)S(1)}, bf16[120,320]{0,1:T(8,128)(2,1)}, u32[]{:S(2)}) copy-start(bf16[120,320]{0,1:T(8,128)(2,1)} %param.17) | copy-start | bytes 230404
  0.7 12.3 %copy-start.35 = (bf16[120]{0:T(256)(128)(2,1)S(1)}, bf16[120]{0:T(256)(128)(2,1)}, u32[]{:S(2)}) copy-start(bf16[120]{0:T(256)(128)(2,1)} %param.25) | copy-start | bytes 724
  0.7 12.3 %copy-start.36 = (bf16[120]{0:T(256)(128)(2,1)S(1)}, bf16[120]{0:T(256)(128)(2,1)}, u32[]{:S(2)}) copy-start(bf16[120]{0:T(256)(128)(2,1)} %param.24) | copy-start | bytes 724
  0.7 12.3 %copy-start.34 = (bf16[120,3]{0,1:T(4,128)(2,1)S(1)}, bf16[120,3]{0,1:T(4,128)(2,1)}, u32[]{:S(2)}) copy-start(bf16[120,3]{0,1:T(4,128)(2,1)} %param.23) | copy-start | bytes 2164
  0.7 12.6 %copy-start.20 = (bf16[120,960]{1,0:T(8,128)(2,1)S(1)}, bf16[120,960]{1,0:T(8,128)(2,1)}, u32[]{:S(2)}) copy-start(bf16[120,960]{1,0:T(8,128)(2,1)} %param.16) | copy-start | bytes 691204
  5.5 113.7 %collective-permute-start = (s32[8,256]{1,0:T(8,128)S(1)}, s32[8,256]{1,0:T(8,128)S(1)}, u32[]{:S(2)}, u32[]{:S(2)}) collective-permute-start(s32[8,256]{1,0:T(8,128)S(1)} %pad.13), channel_id=1, source_target_pairs={{0,0},{1,1},{2,8},{3,9},{4,16},{5,17},{6,24},{7,25},{8,2},{9,3},{1... | collective-permute-start | bytes 24584 | tf_op jit(solution)/shard_map/ppermute | solution.py:1423
  9.7 115.4 %collective-permute-start.1 = (bf16[256,960]{1,0:T(8,128)(2,1)S(1)}, bf16[256,960]{1,0:T(8,128)(2,1)S(1)}, u32[]{:S(2)}, u32[]{:S(2)}) collective-permute-start(bf16[256,960]{1,0:T(8,128)(2,1)S(1)} %copy.66), channel_id=1, source_target_pairs={{0,0},{1,1},{2,8},{3,9},{4,16},{5,17},{6,24},{7,25},{8,2},{9,3},{1... | collective-permute-start | bytes 1474568 | tf_op jit(solution)/shard_map/ppermute | solution.py:1422
  119.3 11.0 %copy-start.10 = (s32[8,256]{1,0:T(8,128)}, s32[8,256]{1,0:T(8,128)S(1)}, u32[]{:S(2)}) copy-start(s32[8,256]{1,0:T(8,128)S(1)} %collective-permute-done.refs_1_.label_ref) | copy-start | bytes 24580
  122.6 7.7 %copy-start.24 = (s32[8,768]{1,0:T(8,128)}, s32[8,768]{1,0:T(8,128)S(1)}, u32[]{:S(2)}) copy-start(s32[8,768]{1,0:T(8,128)S(1)} %constant_dynamic-update-slice_fusion.query_ref) | copy-start | bytes 73732
  150.4 23.4 %collective-permute-start.2 = (bf16[256,960]{1,0:T(8,128)(2,1)S(1)}, bf16[256,960]{1,0:T(8,128)(2,1)S(1)}, u32[]{:S(2)}, u32[]{:S(2)}) collective-permute-start(bf16[256,960]{1,0:T(8,128)(2,1)S(1)} %convolution_convert_fusion.4), channel_id=1, source_target_pairs={{0,0},{1,1},{2,8},{3,9},{4,16},{5,17},{6,24},{7,25},{8,2},{9,3},{1... | collective-permute-start | bytes 1474568 | tf_op jit(solution)/shard_map/ppermute | solution.py:1456
  173.7 16.4 %copy-start.11 = (bf16[256,960]{1,0:T(8,128)(2,1)}, bf16[256,960]{1,0:T(8,128)(2,1)S(1)}, u32[]{:S(2)}) copy-start(bf16[256,960]{1,0:T(8,128)(2,1)S(1)} %collective-permute-done.2.gradient_ref) | copy-start | bytes 1474564
  437.0 12.1 %copy-start.16 = (bf16[192,960]{1,0:T(8,128)(2,1)S(1)}, bf16[192,960]{1,0:T(8,128)(2,1)}, u32[]{:S(2)}) copy-start(bf16[192,960]{1,0:T(8,128)(2,1)} %get-tuple-element.192) | copy-start | bytes 1105924
  437.1 12.9 %copy-start.14 = (bf16[256,960]{1,0:T(8,128)(2,1)S(1)}, bf16[256,960]{1,0:T(8,128)(2,1)}, u32[]{:S(2)}) copy-start(bf16[256,960]{1,0:T(8,128)(2,1)} %get-tuple-element.193) | copy-start | bytes 1474564
  437.1 13.7 %copy-start.13 = (bf16[256,960]{1,0:T(8,128)(2,1)S(1)}, bf16[256,960]{1,0:T(8,128)(2,1)}, u32[]{:S(2)}) copy-start(bf16[256,960]{1,0:T(8,128)(2,1)} %get-tuple-element.119.mixed_ref) | copy-start | bytes 1474564
  437.1 13.7 %copy-start.17 = (bf16[192,960]{1,0:T(8,128)(2,1)S(1)}, bf16[192,960]{1,0:T(8,128)(2,1)}, u32[]{:S(2)}) copy-start(bf16[192,960]{1,0:T(8,128)(2,1)} %get-tuple-element.127.mixed_ref) | copy-start | bytes 1105924
  439.8 168.4 %collective-permute-start.3 = (bf16[256,960]{1,0:T(8,128)(2,1)}, bf16[256,960]{1,0:T(8,128)(2,1)}, u32[]{:S(2)}, u32[]{:S(2)}) collective-permute-start(bf16[256,960]{1,0:T(8,128)(2,1)} %pad_maximum_fusion.2), channel_id=1, source_target_pairs={{0,0},{1,1},{2,8},{3,9},{4,16},{5,17},{6,24},{7,25},{8,2},{9,3},{1... | collective-permute-start | bytes 1474568 | tf_op jit(solution)/shard_map/ppermute | solution.py:1511
  447.0 163.3 %collective-permute-start.4 = (bf16[256,960]{1,0:T(8,128)(2,1)S(1)}, bf16[256,960]{1,0:T(8,128)(2,1)}, u32[]{:S(2)}, u32[]{:S(2)}) collective-permute-start(bf16[256,960]{1,0:T(8,128)(2,1)S(1)} %convert_element_type.89), channel_id=1, source_target_pairs={{0,0},{1,1},{2,8},{3,9},{4,16},{5,17},{6,24},{7,25},{8,2},{9,3},{1... | collective-permute-start | bytes 1474568 | tf_op jit(solution)/shard_map/ppermute | solution.py:1512
  450.8 4.8 copy-start.42
  456.7 5.9 copy-start.37
  456.7 5.9 copy-start.39
  456.7 5.9 copy-start.41
  462.6 5.9 copy-start.43
  462.6 5.8 copy-start.44
  462.6 5.8 copy-start.45
  462.6 5.8 copy-start.46
  462.7 5.8 copy-start.47
  462.7 5.8 copy-start.48
  602.2 4.3 copy-start.19
  605.3 7.2 %copy-start.1 = (bf16[256,960]{0,1:T(8,128)(2,1)S(1)}, bf16[256,960]{0,1:T(8,128)(2,1)}, u32[]{:S(2)}) copy-start(bf16[256,960]{0,1:T(8,128)(2,1)} %param.15) | copy-start | bytes 1474564
  (22 other events, 46.4 us)

commit v8 on v7

--- a/solution.py
+++ b/solution.py
@@ -790,17 +790,12 @@
     )(*arrays)
 
 
-def group_reduce_kernel(topo, grads, out, held, from_c, from_b, from_a, load_sem, c_send, c_recv,
-                        send_sem, recv_sem):
+def group_reduce_kernel(topo, grads, out, held, from_c, from_b, from_a, c_send, c_recv, send_sem,
+                        recv_sem):
     layer = Layer(topo)
     c = layer.c
     a, b, sibling = layer.device(1, c), layer.device(2, c), layer.device(0, 1 - c)
     order = (3, 2, 1, 0)
-
-    def load(slot):
-        return pltpu.make_async_copy(
-            grads.at[layer.pack(slot, c)], held.at[slot], load_sem.at[slot]
-        )
 
     def c_copy(slot):
         theirs = (0, 2, 1, 3)[slot]
@@ -819,15 +814,12 @@
     direct = remote_copy(held.at[2], from_b.at[0], send_sem.at[1], recv_sem.at[1], b)
     passed = remote_copy(held.at[1], from_a, send_sem.at[2], recv_sem.at[2], a)
 
-    for slot in order:
-        load(slot).start()
     layer.meet()
     for slot in (3, 1, 2, 0):
         c_copy(slot).start()
     for slot in order:
-        load(slot).wait()
         c_arrived(slot)
-        held[slot] = held[slot] + from_c[slot]
+        held[slot] = grads[layer.pack(slot, c)] + from_c[slot]
         if slot == 3:
             across.start()
         if slot == 2:
@@ -851,13 +843,13 @@
     block = grads.shape[1:]
     return pl.pallas_call(
         functools.partial(group_reduce_kernel, topo),
-        in_specs=[pl.BlockSpec(memory_space=pl.ANY)],
+        in_specs=[pl.BlockSpec(memory_space=pltpu.VMEM)],
         out_specs=pl.BlockSpec(memory_space=pltpu.VMEM),
         out_shape=jax.ShapeDtypeStruct(block, BF),
         scratch_shapes=[
             pltpu.VMEM((4,) + block, BF), pltpu.VMEM((4,) + block, BF),
             pltpu.VMEM((2,) + block, BF), pltpu.VMEM(block, BF),
-            DMA((4,)), DMA((4,)), DMA((4,)), DMA((3,)), DMA((3,)),
+            DMA((4,)), DMA((4,)), DMA((3,)), DMA((3,)),
         ],
         compiler_params=pltpu.CompilerParams(
             collective_id=ident, has_side_effects=True, vmem_limit_bytes=32 << 20
@@ -1263,6 +1255,10 @@
         out_specs=out_specs,
         out_shape=out_shape,
         compiler_params=pltpu.CompilerParams(vmem_limit_bytes=ROOM),
+        cost_estimate=pl.CostEstimate(
+            flops=2 * n * model * (model + 3 * ff), transcendentals=n * ff,
+            bytes_accessed=2 * model * (model + 3 * ff) + 24 * n * model + 6 * n * ff,
+        ),
         name="feed",
     )(mixed, state, w_out, small, labels, w_gate, w_up, w_down, *then)
 
@@ -1341,6 +1337,10 @@
         ],
         scratch_shapes=[pltpu.VMEM((n, model), F32)],
         compiler_params=pltpu.CompilerParams(vmem_limit_bytes=ROOM),
+        cost_estimate=pl.CostEstimate(
+            flops=2 * n * model * (model + 3 * ff), transcendentals=n * ff,
+            bytes_accessed=2 * model * (model + 3 * ff) + 24 * n * model + 8 * n * ff,
+        ),
         name="feed_back",
     )(gradient, both, gate, labels, state, small, middle, w_out, gated, upward, w_gate, w_up,
       w_down)
@@ -1372,6 +1372,65 @@
         ),
         name="outer_rows",
     )(*xs, *ds)
+
+
+def finish_kernel(onehot_ref, final_ref, gradient_ref, qkv_ref, o_ref, gu_ref, down_ref,
+                  block_ref, token_ref, query_ref, key_ref, value_ref, out_ref, gate_ref, up_ref,
+                  gdown_ref, tiny_ref):
+    onehot = onehot_ref[...]
+    block_ref[...] = lax.dot_general(
+        final_ref[...], onehot, TN, preferred_element_type=F32
+    ).astype(BF)
+    token_ref[...] = lax.dot_general(
+        gradient_ref[...], onehot, TN, preferred_element_type=F32
+    ).astype(BF)
+    model = query_ref.shape[1]
+    query_ref[...] = qkv_ref[:, :model].astype(F32)
+    out_ref[...] = o_ref[:, :model].astype(F32)
+    rows = query_ref.shape[0]
+    room = jnp.zeros((-rows % LANES, LANES), F32)
+
+    def across(v):
+        return jnp.transpose(jnp.concatenate([v, room], axis=0))[:, :rows]
+
+    tiny = jnp.concatenate(
+        [o_ref[:, model:].astype(F32), jnp.zeros((rows, LANES - HD), F32)], axis=1
+    )
+    tiny_ref[...] = across(tiny)[:8]
+    gate_ref[...] = gu_ref[0].astype(F32)
+    up_ref[...] = gu_ref[1].astype(F32)
+    gdown_ref[...] = down_ref[...].astype(F32)
+    low = lanes_of(rows) < HD
+    heads = [
+        qkv_ref[:, (CHUNKS + h) * LANES:(CHUNKS + h + 1) * LANES].astype(F32)
+        for h in range(KV_HEADS)
+    ]
+    for h in range(0, KV_HEADS, 2):
+        even, odd = heads[h], heads[min(h + 1, KV_HEADS - 1)]
+        at = slice(h * HD, min(h + 2, KV_HEADS) * HD)
+        size = at.stop - at.start
+        key_ref[at, :] = across(jnp.where(low, even, pltpu.roll(odd, HD, 1)))[:size]
+        value_ref[at, :] = across(jnp.where(low, pltpu.roll(even, HD, 1), odd))[:size]
+
+
+def finish(onehot, final, gradient, qkv, o, gu, down):
+    rows, model = final.shape
+    shard, ff = gu.shape[1:]
+    kv = KV_HEADS * HD
+    shapes = [
+        (model, rows), (model, rows), (shard, model), (kv, shard), (kv, shard), (shard, model),
+        (shard, ff), (shard, ff), down.shape, (8, shard),
+    ]
+    args = (onehot, final, gradient, qkv, o, gu, down)
+    return pl.pallas_call(
+        finish_kernel,
+        grid=(1,),
+        in_specs=[whole(*v.shape) for v in args],
+        out_specs=[whole(*v) for v in shapes],
+        out_shape=[jax.ShapeDtypeStruct(v, BF if i < 2 else F32) for i, v in enumerate(shapes)],
+        compiler_params=pltpu.CompilerParams(vmem_limit_bytes=ROOM),
+        name="finish",
+    )(*args)
 
 
 def mm(a, b):
@@ -1459,7 +1518,6 @@
         kv_all = kv_all.reshape(topo.T * n, 2 * kv_cols)
         mixed, out, stat = attend(n, recursion, span, labels_all, query_labels[n], kv_all, q)
         if recursion == 0:
-            mixed, later = lax.optimization_barrier((mixed, later))
             extra = (labels_all, later)
         following = deep_rows if recursion + 1 < RECS else 0
         new, middle, n2, gated, upward, hidden, both, gate, *projected = feed(
@@ -1531,23 +1589,11 @@
         outer_rows(hidden, d_fed, 640).reshape(topo.T, -1, model),
         cut(outer(n2, d_up)),
     ])
-    grad_query = grad_qkv[:, :model].astype(F32)
-    pair = grad_qkv[:, model + HD:model + HD + 2 * kv_cols].astype(F32)
-    pair = pair.reshape(shard, KV_HEADS, 2, HD)
-    grad_key = pair[:, :, 0].reshape(shard, kv_cols)
-    grad_value = pair[:, :, 1].reshape(shard, kv_cols)
-    grad_out = grad_o[:, :model].astype(F32)
-    tiny = grad_o[:, model:].astype(F32)
-    grad_gate, grad_up = grad_gu[0].astype(F32), grad_gu[1].astype(F32)
-    grad_down = grad_down.astype(F32)
-
-    def unsort(v):
-        return mm_tn(onehot, v).astype(BF)
-
-    return (
-        unsort(final), unsort(gradient), grad_query, grad_key, grad_value, grad_out,
-        grad_gate, grad_up, grad_down, tiny[:, :RECS], tiny[:, RECS],
-        tiny[:, RECS + 1],
+    block, token, grad_query, grad_key, grad_value, *others, tiny = finish(
+        onehot, final, gradient, grad_qkv, grad_o, grad_gu, grad_down
+    )
+    return (block.T, token.T, grad_query, grad_key.T, grad_value.T) + tuple(others) + (
+        tiny[:RECS].T, tiny[RECS], tiny[RECS + 1]
     )
 
 

time: 624 us -> 613 us (0.982)
  Pallas kernels: 516 us -> 530 us
  waiting for transfers between devices: 10.6 us -> 0.01 us
    ppermute x1, waiting for transfers between devices: 10.6 us -> 0.01 us  [forward(): later = lax.ppermute(later, AXES, swap)]
    pallas_call x3, Pallas kernels: 53.8 us -> 63.6 us  [reduce_layer(): pl.pallas_call(functools.partial(group_reduce_kernel, topo), in_specs=[pl...]
    dot_general x6 -> x4, matrix products: 23.9 us -> 19.7 us  [mm_tn(): return lax.dot_general(a, b, TN, preferred_element_type=F32)]
    unnamed x104 -> x93, local copies, waits for them, and re-layouts: 12.5 us -> 12 us
  transfers between devices with their start and end apart: 5 -> 5, of which waited for: 1 -> 0; matrix products, arithmetic and copies ran while one was open for 6% -> 5% of each run, Pallas kernels for 39% -> 55%
where the time goes in v8:
time: 613 us; the launch traced here: 603 us
  Pallas kernels  530 us (86%)
  matrix products  20.6 us (3%)
  local copies, waits for them, and re-layouts  17.6 us (3%)
  other arithmetic  15.8 us (3%)
  starting transfers between devices  15.1 us (2%)
    pallas_call x1, Pallas kernels, reduce_gradients(): pl.pallas_call(functools.partial(reduce_kernel, topo, shares), in_specs=[...  112 us
    pallas_call x1, Pallas kernels, gather_weights(): pl.pallas_call(functools.partial(gather_kernel, topo, pieces), in_specs=[...  105 us
    pallas_call x3, Pallas kernels, reduce_layer(): pl.pallas_call(functools.partial(group_reduce_kernel, topo), in_specs=[pl...  63.6 us
    pallas_call x3, Pallas kernels, gather_layer(): pl.pallas_call(functools.partial(group_gather_kernel, topo, n), in_specs=...  57.2 us
    pallas_call x3, Pallas kernels, feed_back(): pl.pallas_call(functools.partial(feed_back_kernel, recursion), grid=(ff /...  46.8 us
    pallas_call x3, Pallas kernels, feed(): pl.pallas_call(functools.partial(feed_kernel, recursion, following), grid...  44.7 us
    pallas_call x3, Pallas kernels, attend_back(): pl.pallas_call(functools.partial(attend_back_kernel, rows, recursion), gr...  41 us
    pallas_call x3, Pallas kernels, attend(): pl.pallas_call(functools.partial(attend_kernel, rows, recursion), grid_sp...  27.3 us
  transfers between devices with their start and end apart: 5, of which 0 were waited for; matrix products, arithmetic and copies ran while one was open for 5% of the time, Pallas kernels for 55%

profile of v8, /device:TPU:17, one launch (start us, length us, event | category | flops | bytes accessed | tf_op | source)
XLA Modules:
  0.0 603.3 jit_solution(10250383631911006727)
XLA Ops:
  6.2 3.6 collective-permute-start
  14.9 105.0 %gather_weights.1 = (bf16[8,120,1664]{2,1,0:T(8,128)(2,1)}, bf16[8,120,2560]{2,1,0:T(8,128)(2,1)}, bf16[8,120,2560]{2,1,0:T(8,128)(2,1)}, bf16[8,320,960]{2,1,0:T(8,128)(2,1)}, bf16[8,120,960]{2,1,0:T(8,128)(2,1)}) custom-call(bf16[120,1664]{1,0:T(8,128)(2,1)} %concatenate.51.refs_0_, bf16[120,2560]{1,0:T(8,128)(2,1)} %refs_1_.1, bf16[120,2560]{1,0:T(8,128)(2,1)} %refs_2_.1, ...), custom_call_target="tpu_custom_call" | custom-call | tf_op jit(solution)/shard_map/gather_weights/pallas_call | solution.py:298
  126.6 4.3 project.1
  130.9 20.0 %gather_layer.3 = (bf16[8,256,640]{2,1,0:T(8,128)(2,1)}, s32[8,8,256]{2,1,0:T(8,128)}) custom-call(bf16[256,640]{1,0:T(8,128)(2,1)} %get-tuple-element.120.refs_0_, s32[8,256]{1,0:T(8,128)} %copy-done.9), custom_call_target="tpu_custom_call" | custom-call | tf_op jit(solution)/shard_map/gather_layer/pallas_call | solution.py:782
  152.9 10.7 %attend.3 = (bf16[256,960]{1,0:T(8,128)(2,1)}, f32[8,256,128]{2,1,0:T(8,128)}, f32[5,8,768]{2,1,0:T(8,128)}) custom-call(s32[2]{0:T(128)} %pad_add_fusion.2.span, s32[8,8,256]{2,1,0:T(8,128)} %get-tuple-element.121.key_ref, s32[8,768]{1,0:T(8,128)} %copy-done.20, bf16[2048,640]{1,0:T(8,128)(2,1)} %bitcast.103, bf16[8,256,128]{2,1,0:T(8,128)(2,1)} %get-tuple-element.124.q_ref), custom_call_target="tpu_custom_call" | custom-call | flops 8053063680 | bytes 5242880 | tf_op jit(solution)/shard_map/attend/pallas_call | solution.py:996
  163.6 16.2 %feed.3 = (f32[256,960]{1,0:T(8,128)}, f32[256,960]{1,0:T(8,128)}, bf16[256,960]{1,0:T(8,128)(2,1)}, bf16[256,2560]{1,0:T(8,128)(2,1)}, bf16[256,2560]{1,0:T(8,1...) custom-call(bf16[256,960]{1,0:T(8,128)(2,1)} %get-tuple-element.125., ...), custom_call_target="tpu_custom_call" | custom-call | flops 4246732800 | bytes 26419200 | tf_op jit(solution)/shard_map/feed/pallas_call | solution.py:1247
  180.7 21.2 %gather_layer.4 = bf16[8,192,640]{2,1,0:T(8,128)(2,1)} custom-call(bf16[192,640]{1,0:T(8,128)(2,1)} %get-tuple-element.131.refs_0_), custom_call_target="tpu_custom_call" | custom-call | tf_op jit(solution)/shard_map/gather_layer/pallas_call | solution.py:782
  201.9 8.2 %attend.4 = (bf16[192,960]{1,0:T(8,128)(2,1)}, f32[8,192,128]{2,1,0:T(8,128)}, f32[5,8,576]{2,1,0:T(8,128)}) custom-call(s32[2]{0:T(128)} %pad_add_fusion.2.span, s32[8,8,256]{2,1,0:T(8,128)} %get-tuple-element.121.key_ref, s32[8,576]{1,0:T(8,128)} %pad_add_fusion.query_ref, bf16[1536,640]{1,0:T(8,128)(2,1)} %bitcast.95, ...), custom_call_target="tpu_custom_call" | custom-call | flops 4529848320 | bytes 3932160 | tf_op jit(solution)/shard_map/attend/pallas_call | solution.py:996
  210.1 15.3 %feed.4 = (f32[192,960]{1,0:T(8,128)}, f32[192,960]{1,0:T(8,128)}, bf16[192,960]{1,0:T(8,128)(2,1)}, bf16[192,2560]{1,0:T(8,128)(2,1)}, bf16[192,2560]{1,0:T(8,1...) custom-call(bf16[192,960]{1,0:T(8,128)(2,1)} %get-tuple-element.133., ...), custom_call_target="tpu_custom_call" | custom-call | flops 3185049600 | bytes 23961600 | tf_op jit(solution)/shard_map/feed/pallas_call | solution.py:1247
  225.4 16.0 %gather_layer.5 = bf16[8,192,640]{2,1,0:T(8,128)(2,1)} custom-call(bf16[192,640]{1,0:T(8,128)(2,1)} %get-tuple-element.135.refs_0_), custom_call_target="tpu_custom_call" | custom-call | tf_op jit(solution)/shard_map/gather_layer/pallas_call | solution.py:782
  241.4 8.4 %attend.5 = (bf16[192,960]{1,0:T(8,128)(2,1)}, f32[8,192,128]{2,1,0:T(8,128)}, f32[5,8,576]{2,1,0:T(8,128)}) custom-call(s32[2]{0:T(128)} %pad_add_fusion.2.span, s32[8,8,256]{2,1,0:T(8,128)} %get-tuple-element.121.key_ref, s32[8,576]{1,0:T(8,128)} %pad_add_fusion.query_ref, bf16[1536,640]{1,0:T(8,128)(2,1)} %bitcast.97, ...), custom_call_target="tpu_custom_call" | custom-call | flops 4529848320 | bytes 3932160 | tf_op jit(solution)/shard_map/attend/pallas_call | solution.py:996
  249.9 13.3 %feed.5 = (f32[192,960]{1,0:T(8,128)}, f32[192,960]{1,0:T(8,128)}, bf16[192,960]{1,0:T(8,128)(2,1)}, bf16[192,2560]{1,0:T(8,128)(2,1)}, bf16[192,2560]{1,0:T(8,1...) custom-call(bf16[192,960]{1,0:T(8,128)(2,1)} %get-tuple-element.137.mixed_ref, ...), custom_call_target="tpu_custom_call" | custom-call | flops 3185049600 | bytes 23961600 | tf_op jit(solution)/shard_map/feed/pallas_call | solution.py:1247
  267.4 15.1 %feed_back.3 = (bf16[192,960]{1,0:T(8,128)(2,1)}, bf16[192,2560]{1,0:T(8,128)(2,1)}, bf16[192,2560]{1,0:T(8,128)(2,1)}, bf16[192,960]{1,0:T(8,128)(2,1)}, f32[19...) custom-call(bf16[256,960]{1,0:T(8,128)(2,1)} %copy-done.10, ...), custom_call_target="tpu_custom_call" | custom-call | flops 3185049600 | bytes 24944640 | tf_op jit(solution)/shard_map/feed_back/pallas_call | solution.py:1322
  282.6 13.2 %attend_back.3 = (bf16[192,1024]{1,0:T(8,128)(2,1)}, bf16[1536,640]{1,0:T(8,128)(2,1)}) custom-call(s32[2]{0:T(128)} %pad_add_fusion.2.span, s32[8,8,256]{2,1,0:T(8,128)} %get-tuple-element.121.key_ref, s32[8,576]{1,0:T(8,128)} %pad_add_fusion.query_ref, bf16[1536,640]{1,0:T(8,128)(2,1)} %bitcast.98, bf16[8,192,128]{2,1,0:T(8,128)(2,1)} %get-tuple-element.136.q_ref, ...), custom_call_target="tpu_custom_call" | custom-call | tf_op jit(solution)/shard_map/attend_back/pallas_call | solution.py:1082
  297.3 22.6 %reduce_layer.3.raw_ref = bf16[192,640]{1,0:T(8,128)(2,1)S(1)} custom-call(bf16[8,192,640]{2,1,0:T(8,128)(2,1)S(1)} %bitcast.64), custom_call_target="tpu_custom_call" | custom-call | tf_op jit(solution)/shard_map/reduce_layer/pallas_call | solution.py:844
  320.6 4.7 project_back.3
  325.3 15.3 %feed_back.4 = (bf16[192,960]{1,0:T(8,128)(2,1)}, bf16[192,2560]{1,0:T(8,128)(2,1)}, bf16[192,2560]{1,0:T(8,128)(2,1)}, bf16[192,960]{1,0:T(8,128)(2,1)}, f32[19...) custom-call(f32[192,960]{1,0:T(8,128)} %get-tuple-element.152.gradient_ref, ...), custom_call_target="tpu_custom_call" | custom-call | flops 3185049600 | bytes 24944640 | tf_op jit(solution)/shard_map/feed_back/pallas_call | solution.py:1322
  340.6 13.0 %attend_back.4 = (bf16[192,1024]{1,0:T(8,128)(2,1)}, bf16[1536,640]{1,0:T(8,128)(2,1)}) custom-call(s32[2]{0:T(128)} %pad_add_fusion.2.span, s32[8,8,256]{2,1,0:T(8,128)} %get-tuple-element.121.key_ref, s32[8,576]{1,0:T(8,128)} %pad_add_fusion.query_ref, bf16[1536,640]{1,0:T(8,128)(2,1)} %bitcast.96, bf16[8,192,128]{2,1,0:T(8,128)(2,1)} %get-tuple-element.132.q_ref, ...), custom_call_target="tpu_custom_call" | custom-call | tf_op jit(solution)/shard_map/attend_back/pallas_call | solution.py:1082
  355.1 17.5 %reduce_layer.4.raw_ref = bf16[192,640]{1,0:T(8,128)(2,1)S(1)} custom-call(bf16[8,192,640]{2,1,0:T(8,128)(2,1)S(1)} %bitcast.63), custom_call_target="tpu_custom_call" | custom-call | tf_op jit(solution)/shard_map/reduce_layer/pallas_call | solution.py:844
  373.4 4.7 project_back.4
  381.2 16.4 %feed_back.5 = (bf16[256,960]{1,0:T(8,128)(2,1)}, bf16[256,2560]{1,0:T(8,128)(2,1)}, bf16[256,2560]{1,0:T(8,128)(2,1)}, bf16[256,960]{1,0:T(8,128)(2,1)}, f32[25...) custom-call(f32[256,960]{1,0:T(8,128)} %pad_maximum_fusion.1.gradient_ref, ...), custom_call_target="tpu_custom_call" | custom-call | flops 4246732800 | bytes 27729920 | tf_op jit(solution)/shard_map/feed_back/pallas_call | solution.py:1322
  397.6 14.8 %attend_back.5 = (bf16[256,1024]{1,0:T(8,128)(2,1)}, bf16[2048,640]{1,0:T(8,128)(2,1)}) custom-call(s32[2]{0:T(128)} %pad_add_fusion.2.span, s32[8,8,256]{2,1,0:T(8,128)} %get-tuple-element.121.key_ref, s32[8,768]{1,0:T(8,128)} %copy-done.20, bf16[2048,640]{1,0:T(8,128)(2,1)} %bitcast.104, bf16[8,256,128]{2,1,0:T(8,128)(2,1)} %get-tuple-element.124.q_ref, ...), custom_call_target="tpu_custom_call" | custom-call | tf_op jit(solution)/shard_map/attend_back/pallas_call | solution.py:1082
  414.2 23.5 %reduce_layer.5.raw_ref = bf16[256,640]{1,0:T(8,128)(2,1)S(1)} custom-call(bf16[8,256,640]{2,1,0:T(8,128)(2,1)S(1)} %bitcast.62), custom_call_target="tpu_custom_call" | custom-call | tf_op jit(solution)/shard_map/reduce_layer/pallas_call | solution.py:844
  438.4 5.1 project_back.5
  447.9 4.8 collective-permute-start.4
  452.7 3.4 convolution_convert_fusion.3
  456.2 5.9 convolution_convert_fusion.1
  462.1 5.8 convolution_convert_fusion
  467.9 8.2 %outer_rows.1 = bf16[2560,960]{1,0:T(8,128)(2,1)} custom-call(bf16[192,2560]{1,0:T(8,128)(2,1)} %get-tuple-element.203.refs_0_, bf16[192,2560]{1,0:T(8,128)(2,1)} %get-tuple-element.204.refs_1_, bf16[256,2560]{1,0:T(8,128)(2,1)} %get-tuple-element.205.refs_2_, bf16[192,960]{1,0:T(8,128)(2,1)} %get-tuple-element.206.refs_3_, ...), custom_call_target="tpu_custom_call" | custom-call | flops 3145728000 | bytes 9420800 | tf_op jit(solution)/shard_map/outer_rows/pallas_call | solution.py:1361
  478.7 4.7 convolution_convert_fusion.2
  483.4 111.9 %reduce_gradients.1 = (bf16[120,1792]{1,0:T(8,128)(2,1)}, bf16[120,1024]{1,0:T(8,128)(2,1)}, bf16[2,120,2560]{2,1,0:T(8,128)(2,1)}, bf16[320,960]{1,0:T(8,128)(2,1)}) custom-call(bf16[8,120,1792]{2,1,0:T(8,128)(2,1)} %bitcast.102, bf16[8,120,1024]{2,1,0:T(8,128)(2,1)} %pad_maximum_fusion.refs_1_, bf16[8,120,2560]{2,1,0:T(8,128)(2,1)} %bitcast.100, ...), custom_call_target="tpu_custom_call" | custom-call | tf_op jit(solution)/shard_map/reduce_gradients/pallas_call | solution.py:646
  595.3 5.2 finish.1
  (148 shorter events, 41.0 us)
Async XLA Ops:
  0.6 9.1 %copy-start = (bf16[256,960]{0,1:T(8,128)(2,1)S(1)}, bf16[256,960]{0,1:T(8,128)(2,1)}, u32[]{:S(2)}) copy-start(bf16[256,960]{0,1:T(8,128)(2,1)} %param.15) | copy-start | bytes 1474564
  0.7 12.5 %copy-start.13 = (bf16[256,960]{0,1:T(8,128)(2,1)S(1)}, bf16[256,960]{0,1:T(8,128)(2,1)}, u32[]{:S(2)}) copy-start(bf16[256,960]{0,1:T(8,128)(2,1)} %param.29) | copy-start | bytes 1474564
  0.7 12.9 %copy-start.18 = (bf16[120,320]{0,1:T(8,128)(2,1)S(1)}, bf16[120,320]{0,1:T(8,128)(2,1)}, u32[]{:S(2)}) copy-start(bf16[120,320]{0,1:T(8,128)(2,1)} %param.18) | copy-start | bytes 230404
  0.7 12.9 %copy-start.19 = (bf16[120,320]{0,1:T(8,128)(2,1)S(1)}, bf16[120,320]{0,1:T(8,128)(2,1)}, u32[]{:S(2)}) copy-start(bf16[120,320]{0,1:T(8,128)(2,1)} %param.17) | copy-start | bytes 230404
  0.7 12.9 %copy-start.30 = (bf16[120]{0:T(256)(128)(2,1)S(1)}, bf16[120]{0:T(256)(128)(2,1)}, u32[]{:S(2)}) copy-start(bf16[120]{0:T(256)(128)(2,1)} %param.25) | copy-start | bytes 724
  0.7 12.9 %copy-start.31 = (bf16[120]{0:T(256)(128)(2,1)S(1)}, bf16[120]{0:T(256)(128)(2,1)}, u32[]{:S(2)}) copy-start(bf16[120]{0:T(256)(128)(2,1)} %param.24) | copy-start | bytes 724
  0.7 12.9 %copy-start.29 = (bf16[120,3]{0,1:T(4,128)(2,1)S(1)}, bf16[120,3]{0,1:T(4,128)(2,1)}, u32[]{:S(2)}) copy-start(bf16[120,3]{0,1:T(4,128)(2,1)} %param.23) | copy-start | bytes 2164
  0.7 13.3 %copy-start.15 = (bf16[120,960]{1,0:T(8,128)(2,1)S(1)}, bf16[120,960]{1,0:T(8,128)(2,1)}, u32[]{:S(2)}) copy-start(bf16[120,960]{1,0:T(8,128)(2,1)} %param.16) | copy-start | bytes 691204
  6.2 113.7 %collective-permute-start = (s32[8,256]{1,0:T(8,128)S(1)}, s32[8,256]{1,0:T(8,128)S(1)}, u32[]{:S(2)}, u32[]{:S(2)}) collective-permute-start(s32[8,256]{1,0:T(8,128)S(1)} %pad.13), channel_id=1, source_target_pairs={{0,0},{1,1},{2,8},{3,9},{4,16},{5,17},{6,24},{7,25},{8,2},{9,3},{1... | collective-permute-start | bytes 24584 | tf_op jit(solution)/shard_map/ppermute | solution.py:1482
  10.3 115.4 %collective-permute-start.1 = (bf16[256,960]{1,0:T(8,128)(2,1)S(1)}, bf16[256,960]{1,0:T(8,128)(2,1)S(1)}, u32[]{:S(2)}, u32[]{:S(2)}) collective-permute-start(bf16[256,960]{1,0:T(8,128)(2,1)S(1)} %copy.57), channel_id=1, source_target_pairs={{0,0},{1,1},{2,8},{3,9},{4,16},{5,17},{6,24},{7,25},{8,2},{9,3},{1... | collective-permute-start | bytes 1474568 | tf_op jit(solution)/shard_map/ppermute | solution.py:1481
  119.9 11.0 %copy-start.9 = (s32[8,256]{1,0:T(8,128)}, s32[8,256]{1,0:T(8,128)S(1)}, u32[]{:S(2)}) copy-start(s32[8,256]{1,0:T(8,128)S(1)} %collective-permute-done.refs_1_.label_ref) | copy-start | bytes 24580
  123.2 29.6 %copy-start.20 = (s32[8,768]{1,0:T(8,128)}, s32[8,768]{1,0:T(8,128)S(1)}, u32[]{:S(2)}) copy-start(s32[8,768]{1,0:T(8,128)S(1)} %constant_dynamic-update-slice_fusion.query_ref) | copy-start | bytes 73732
  150.9 114.6 %collective-permute-start.2 = (bf16[256,960]{1,0:T(8,128)(2,1)S(1)}, bf16[256,960]{1,0:T(8,128)(2,1)S(1)}, u32[]{:S(2)}, u32[]{:S(2)}) collective-permute-start(bf16[256,960]{1,0:T(8,128)(2,1)S(1)} %convolution_convert_fusion.4), channel_id=1, source_target_pairs={{0,0},{1,1},{2,8},{3,9},{4,16},{5,17},{6,24},{7,25},{8,2},{9,3},{1... | collective-permute-start | bytes 1474568 | tf_op jit(solution)/shard_map/ppermute | solution.py:1515
  249.9 15.5 %copy-start.14 = (bf16[192,960]{1,0:T(8,128)(2,1)S(1)}, bf16[192,960]{1,0:T(8,128)(2,1)}, u32[]{:S(2)}) copy-start(bf16[192,960]{1,0:T(8,128)(2,1)} %get-tuple-element.198) | copy-start | bytes 1105924
  438.4 6.5 %copy-start.21 = (f32[1,960]{1,0:T(1,128)S(1)}, f32[1,960]{1,0:T(1,128)}, u32[]{:S(2)}) copy-start(f32[1,960]{1,0:T(1,128)} %get-tuple-element.188) | copy-start | bytes 11524
  438.4 6.5 %copy-start.22 = (f32[1,960]{1,0:T(1,128)S(1)}, f32[1,960]{1,0:T(1,128)}, u32[]{:S(2)}) copy-start(f32[1,960]{1,0:T(1,128)} %get-tuple-element.190) | copy-start | bytes 11524
  438.4 6.5 %copy-start.23 = (f32[1,960]{1,0:T(1,128)S(1)}, f32[1,960]{1,0:T(1,128)}, u32[]{:S(2)}) copy-start(f32[1,960]{1,0:T(1,128)} %get-tuple-element.194) | copy-start | bytes 11524
  438.4 6.5 %copy-start.26 = (f32[1,960]{1,0:T(1,128)S(1)}, f32[1,960]{1,0:T(1,128)}, u32[]{:S(2)}) copy-start(f32[1,960]{1,0:T(1,128)} %get-tuple-element.195) | copy-start | bytes 11524
  438.4 6.5 %copy-start.28 = (f32[1,960]{1,0:T(1,128)S(1)}, f32[1,960]{1,0:T(1,128)}, u32[]{:S(2)}) copy-start(f32[1,960]{1,0:T(1,128)} %get-tuple-element.196) | copy-start | bytes 11524
  438.4 6.5 %copy-start.24 = (f32[1,960]{1,0:T(1,128)S(1)}, f32[1,960]{1,0:T(1,128)}, u32[]{:S(2)}) copy-start(f32[1,960]{1,0:T(1,128)} %get-tuple-element.191) | copy-start | bytes 11524
  438.4 6.5 %copy-start.25 = (f32[1,960]{1,0:T(1,128)S(1)}, f32[1,960]{1,0:T(1,128)}, u32[]{:S(2)}) copy-start(f32[1,960]{1,0:T(1,128)} %get-tuple-element.189) | copy-start | bytes 11524
  438.4 6.5 %copy-start.27 = (f32[1,960]{1,0:T(1,128)S(1)}, f32[1,960]{1,0:T(1,128)}, u32[]{:S(2)}) copy-start(f32[1,960]{1,0:T(1,128)} %get-tuple-element.192) | copy-start | bytes 11524
  438.4 14.3 %copy-start.11 = (bf16[256,960]{1,0:T(8,128)(2,1)S(1)}, bf16[256,960]{1,0:T(8,128)(2,1)}, u32[]{:S(2)}) copy-start(bf16[256,960]{1,0:T(8,128)(2,1)} %get-tuple-element.125.mixed_ref) | copy-start | bytes 1474564
  446.0 149.3 %collective-permute-start.3 = (bf16[256,960]{1,0:T(8,128)(2,1)S(1)}, bf16[256,960]{1,0:T(8,128)(2,1)}, u32[]{:S(2)}, u32[]{:S(2)}) collective-permute-start(bf16[256,960]{1,0:T(8,128)(2,1)S(1)} %pad_maximum_fusion.2), channel_id=1, source_target_pairs={{0,0},{1,1},{2,8},{3,9},{4,16},{5,17},{6,24},{7,25},{8,2},{9,3},{1... | collective-permute-start | bytes 1474568 | tf_op jit(solution)/shard_map/ppermute | solution.py:1569
  447.9 147.4 %collective-permute-start.4 = (bf16[256,960]{1,0:T(8,128)(2,1)S(1)}, bf16[256,960]{1,0:T(8,128)(2,1)}, u32[]{:S(2)}, u32[]{:S(2)}) collective-permute-start(bf16[256,960]{1,0:T(8,128)(2,1)S(1)} %convert_element_type.61), channel_id=1, source_target_pairs={{0,0},{1,1},{2,8},{3,9},{4,16},{5,17},{6,24},{7,25},{8,2},{9,3},{1... | collective-permute-start | bytes 1474568 | tf_op jit(solution)/shard_map/ppermute | solution.py:1570
  452.7 3.4 copy-start.17
  452.7 3.4 copy-start.33
  452.7 3.4 copy-start.35
  456.1 5.9 copy-start.32
  456.2 5.9 copy-start.34
  456.2 5.9 copy-start.36
  483.4 119.6 %copy-start.1 = (bf16[256,960]{0,1:T(8,128)(2,1)S(1)}, bf16[256,960]{0,1:T(8,128)(2,1)}, u32[]{:S(2)}) copy-start(bf16[256,960]{0,1:T(8,128)(2,1)} %param.15) | copy-start | bytes 1474564
  (17 other events, 28.7 us)

commit v9 on v8

--- a/solution.py
+++ b/solution.py
@@ -1227,7 +1227,7 @@
 def feed(recursion, mixed, state, w_out, small, labels, w_gate, w_up, w_down, following, then=()):
     n, model = mixed.shape
     ff = w_gate.shape[1]
-    tile = 512 if ff % 512 == 0 else ff
+    tile = ff // 2 if ff % 256 == 0 else ff
     across = pl.BlockSpec((model, tile), lambda i: (0, i))
     made = pl.BlockSpec((n, tile), lambda i: (0, i))
     out_specs = [
@@ -1312,7 +1312,7 @@
               w_gate, w_up, w_down):
     n, model = both.shape
     ff = w_gate.shape[1]
-    tile = 512 if ff % 512 == 0 else ff
+    tile = ff // 2 if ff % 256 == 0 else ff
     across = pl.BlockSpec((model, tile), lambda i: (0, i))
     made = pl.BlockSpec((n, tile), lambda i: (0, i))
     wide = whole(n, model)
@@ -1505,7 +1505,7 @@
         n: jnp.concatenate([labels[:, :n]] * SHARES, axis=1) for n in (rows, deep_rows)
     }
 
-    def forward(state, projected, recursion, labels_all=None):
+    def forward(state, projected, recursion, labels_all=None, pending=None):
         extra = None
         n1, q, kv = projected
         n = n1.shape[0]
@@ -1519,6 +1519,8 @@
         mixed, out, stat = attend(n, recursion, span, labels_all, query_labels[n], kv_all, q)
         if recursion == 0:
             extra = (labels_all, later)
+        if pending is not None:
+            mixed, extra = lax.optimization_barrier((mixed, pending))
         following = deep_rows if recursion + 1 < RECS else 0
         new, middle, n2, gated, upward, hidden, both, gate, *projected = feed(
             recursion, mixed, state, weight_o, small, labels, weight_g, weight_u, weight_d,
@@ -1551,7 +1553,9 @@
     deep = whole_state
     all_kept = [kept]
     for recursion in range(1, RECS):
-        deep, projected, kept, _ = forward(deep, projected, recursion, labels_all)
+        pending = gradient if recursion == 1 else None
+        deep, projected, kept, extra = forward(deep, projected, recursion, labels_all, pending)
+        gradient = extra if recursion == 1 else gradient
         all_kept.append(kept)
     final = jnp.concatenate([deep, whole_state[deep_rows:]], axis=0).astype(BF)
 
@@ -1561,13 +1565,12 @@
         deep_grad, left, tiny = backward(deep_grad, recursion, all_kept[recursion])
         lefts.append(left)
         smalls.append(tiny)
+    deep_grad, final = lax.optimization_barrier((deep_grad, lax.ppermute(final, AXES, swap)))
     gradient = jnp.concatenate([deep_grad, gradient[deep_rows:].astype(F32)], axis=0)
     gradient, left, tiny = backward(gradient, 0, all_kept[0])
     lefts.append(left)
     smalls.append(tiny)
-    final, gradient = lax.optimization_barrier((final, gradient.astype(BF)))
-    final = lax.ppermute(final, AXES, swap)
-    gradient = lax.ppermute(gradient, AXES, swap)
+    gradient = lax.ppermute(gradient.astype(BF), AXES, swap)
 
     n1, dqkv, mixed, d_att, n2, d_gated, d_up, hidden, d_fed = zip(*lefts)
 

time: 613 us -> 600 us (0.979)
  Pallas kernels: 530 us -> 520 us
  transfers between devices with their start and end apart: 5 -> 5, of which waited for: 0 -> 0; matrix products, arithmetic and copies ran while one was open for 5% -> 5% of each run, Pallas kernels for 55% -> 65%
where the time goes in v9:
time: 600 us; the launch traced here: 589 us
  Pallas kernels  520 us (87%)
  matrix products  20.8 us (3%)
  local copies, waits for them, and re-layouts  16.6 us (3%)
  other arithmetic  15 us (2%)
  starting transfers between devices  12.4 us (2%)
    pallas_call x1, Pallas kernels, reduce_gradients(): pl.pallas_call(functools.partial(reduce_kernel, topo, shares), in_specs=[...  109 us
    pallas_call x1, Pallas kernels, gather_weights(): pl.pallas_call(functools.partial(gather_kernel, topo, pieces), in_specs=[...  105 us
    pallas_call x3, Pallas kernels, reduce_layer(): pl.pallas_call(functools.partial(group_reduce_kernel, topo), in_specs=[pl...  63.9 us
    pallas_call x3, Pallas kernels, gather_layer(): pl.pallas_call(functools.partial(group_gather_kernel, topo, n), in_specs=...  57.2 us
    pallas_call x3, Pallas kernels, feed_back(): pl.pallas_call(functools.partial(feed_back_kernel, recursion), grid=(ff /...  44.8 us
    pallas_call x3, Pallas kernels, attend_back(): pl.pallas_call(functools.partial(attend_back_kernel, rows, recursion), gr...  41.2 us
    pallas_call x3, Pallas kernels, feed(): pl.pallas_call(functools.partial(feed_kernel, recursion, following), grid...  39.5 us
    pallas_call x3, Pallas kernels, attend(): pl.pallas_call(functools.partial(attend_kernel, rows, recursion), grid_sp...  27.6 us
  transfers between devices with their start and end apart: 5, of which 0 were waited for; matrix products, arithmetic and copies ran while one was open for 5% of the time, Pallas kernels for 65%

profile of v9, /device:TPU:17, one launch (start us, length us, event | category | flops | bytes accessed | tf_op | source)
XLA Modules:
  0.0 589.4 jit_solution(3503523822512374487)
XLA Ops:
  6.2 3.6 collective-permute-start
  10.4 2.9 collective-permute-start.1
  14.9 105.0 %gather_weights.1 = (bf16[8,120,1664]{2,1,0:T(8,128)(2,1)}, bf16[8,120,2560]{2,1,0:T(8,128)(2,1)}, bf16[8,120,2560]{2,1,0:T(8,128)(2,1)}, bf16[8,320,960]{2,1,0:T(8,128)(2,1)}, bf16[8,120,960]{2,1,0:T(8,128)(2,1)}) custom-call(bf16[120,1664]{1,0:T(8,128)(2,1)} %concatenate.51.refs_0_, bf16[120,2560]{1,0:T(8,128)(2,1)} %refs_1_.1, bf16[120,2560]{1,0:T(8,128)(2,1)} %refs_2_.1, ...), custom_call_target="tpu_custom_call" | custom-call | tf_op jit(solution)/shard_map/gather_weights/pallas_call | solution.py:298
  126.6 4.3 project.1
  130.9 20.0 %gather_layer.3 = (bf16[8,256,640]{2,1,0:T(8,128)(2,1)}, s32[8,8,256]{2,1,0:T(8,128)}) custom-call(bf16[256,640]{1,0:T(8,128)(2,1)} %get-tuple-element.122.refs_0_, s32[8,256]{1,0:T(8,128)} %copy-done.9), custom_call_target="tpu_custom_call" | custom-call | tf_op jit(solution)/shard_map/gather_layer/pallas_call | solution.py:782
  152.9 11.0 %attend.3 = (bf16[256,960]{1,0:T(8,128)(2,1)}, f32[8,256,128]{2,1,0:T(8,128)}, f32[5,8,768]{2,1,0:T(8,128)}) custom-call(s32[2]{0:T(128)} %pad_add_fusion.2.span, s32[8,8,256]{2,1,0:T(8,128)} %get-tuple-element.123.key_ref, s32[8,768]{1,0:T(8,128)} %copy-done.27, bf16[2048,640]{1,0:T(8,128)(2,1)} %bitcast.103, bf16[8,256,128]{2,1,0:T(8,128)(2,1)} %get-tuple-element.126.q_ref), custom_call_target="tpu_custom_call" | custom-call | flops 8053063680 | bytes 5242880 | tf_op jit(solution)/shard_map/attend/pallas_call | solution.py:996
  163.9 14.7 %feed.3 = (f32[256,960]{1,0:T(8,128)}, f32[256,960]{1,0:T(8,128)}, bf16[256,960]{1,0:T(8,128)(2,1)}, bf16[256,2560]{1,0:T(8,128)(2,1)}, bf16[256,2560]{1,0:T(8,1...) custom-call(bf16[256,960]{1,0:T(8,128)(2,1)} %get-tuple-element.127., ...), custom_call_target="tpu_custom_call" | custom-call | flops 4246732800 | bytes 26419200 | tf_op jit(solution)/shard_map/feed/pallas_call | solution.py:1247
  178.6 20.2 %gather_layer.4 = bf16[8,192,640]{2,1,0:T(8,128)(2,1)} custom-call(bf16[192,640]{1,0:T(8,128)(2,1)} %get-tuple-element.133.refs_0_), custom_call_target="tpu_custom_call" | custom-call | tf_op jit(solution)/shard_map/gather_layer/pallas_call | solution.py:782
  199.8 8.2 %attend.4 = (bf16[192,960]{1,0:T(8,128)(2,1)}, f32[8,192,128]{2,1,0:T(8,128)}, f32[5,8,576]{2,1,0:T(8,128)}) custom-call(s32[2]{0:T(128)} %pad_add_fusion.2.span, s32[8,8,256]{2,1,0:T(8,128)} %get-tuple-element.123.key_ref, s32[8,576]{1,0:T(8,128)} %pad_add_fusion.query_ref, bf16[1536,640]{1,0:T(8,128)(2,1)} %bitcast.95, ...), custom_call_target="tpu_custom_call" | custom-call | flops 4529848320 | bytes 3932160 | tf_op jit(solution)/shard_map/attend/pallas_call | solution.py:996
  208.0 13.3 %feed.4 = (f32[192,960]{1,0:T(8,128)}, f32[192,960]{1,0:T(8,128)}, bf16[192,960]{1,0:T(8,128)(2,1)}, bf16[192,2560]{1,0:T(8,128)(2,1)}, bf16[192,2560]{1,0:T(8,1...) custom-call(bf16[192,960]{1,0:T(8,128)(2,1)} %get-tuple-element.138., ...), custom_call_target="tpu_custom_call" | custom-call | flops 3185049600 | bytes 23961600 | tf_op jit(solution)/shard_map/feed/pallas_call | solution.py:1247
  221.3 16.9 %gather_layer.5 = bf16[8,192,640]{2,1,0:T(8,128)(2,1)} custom-call(bf16[192,640]{1,0:T(8,128)(2,1)} %get-tuple-element.140.refs_0_), custom_call_target="tpu_custom_call" | custom-call | tf_op jit(solution)/shard_map/gather_layer/pallas_call | solution.py:782
  238.3 8.4 %attend.5 = (bf16[192,960]{1,0:T(8,128)(2,1)}, f32[8,192,128]{2,1,0:T(8,128)}, f32[5,8,576]{2,1,0:T(8,128)}) custom-call(s32[2]{0:T(128)} %pad_add_fusion.2.span, s32[8,8,256]{2,1,0:T(8,128)} %get-tuple-element.123.key_ref, s32[8,576]{1,0:T(8,128)} %pad_add_fusion.query_ref, bf16[1536,640]{1,0:T(8,128)(2,1)} %bitcast.97, ...), custom_call_target="tpu_custom_call" | custom-call | flops 4529848320 | bytes 3932160 | tf_op jit(solution)/shard_map/attend/pallas_call | solution.py:996
  246.6 11.5 %feed.5 = (f32[192,960]{1,0:T(8,128)}, f32[192,960]{1,0:T(8,128)}, bf16[192,960]{1,0:T(8,128)(2,1)}, bf16[192,2560]{1,0:T(8,128)(2,1)}, bf16[192,2560]{1,0:T(8,1...) custom-call(bf16[192,960]{1,0:T(8,128)(2,1)} %get-tuple-element.142.mixed_ref, ...), custom_call_target="tpu_custom_call" | custom-call | flops 3185049600 | bytes 23961600 | tf_op jit(solution)/shard_map/feed/pallas_call | solution.py:1247
  261.3 14.6 %feed_back.3 = (bf16[192,960]{1,0:T(8,128)(2,1)}, bf16[192,2560]{1,0:T(8,128)(2,1)}, bf16[192,2560]{1,0:T(8,128)(2,1)}, bf16[192,960]{1,0:T(8,128)(2,1)}, f32[19...) custom-call(bf16[256,960]{1,0:T(8,128)(2,1)} %copy-done.10, ...), custom_call_target="tpu_custom_call" | custom-call | flops 3185049600 | bytes 24944640 | tf_op jit(solution)/shard_map/feed_back/pallas_call | solution.py:1322
  275.9 13.0 %attend_back.3 = (bf16[192,1024]{1,0:T(8,128)(2,1)}, bf16[1536,640]{1,0:T(8,128)(2,1)}) custom-call(s32[2]{0:T(128)} %pad_add_fusion.2.span, s32[8,8,256]{2,1,0:T(8,128)} %get-tuple-element.123.key_ref, s32[8,576]{1,0:T(8,128)} %pad_add_fusion.query_ref, bf16[1536,640]{1,0:T(8,128)(2,1)} %bitcast.98, bf16[8,192,128]{2,1,0:T(8,128)(2,1)} %get-tuple-element.141.q_ref, ...), custom_call_target="tpu_custom_call" | custom-call | tf_op jit(solution)/shard_map/attend_back/pallas_call | solution.py:1082
  290.5 21.7 %reduce_layer.3.raw_ref = bf16[192,640]{1,0:T(8,128)(2,1)S(1)} custom-call(bf16[8,192,640]{2,1,0:T(8,128)(2,1)S(1)} %bitcast.64), custom_call_target="tpu_custom_call" | custom-call | tf_op jit(solution)/shard_map/reduce_layer/pallas_call | solution.py:844
  312.9 4.7 project_back.3
  317.6 14.6 %feed_back.4 = (bf16[192,960]{1,0:T(8,128)(2,1)}, bf16[192,2560]{1,0:T(8,128)(2,1)}, bf16[192,2560]{1,0:T(8,128)(2,1)}, bf16[192,960]{1,0:T(8,128)(2,1)}, f32[19...) custom-call(f32[192,960]{1,0:T(8,128)} %get-tuple-element.155.gradient_ref, ...), custom_call_target="tpu_custom_call" | custom-call | flops 3185049600 | bytes 24944640 | tf_op jit(solution)/shard_map/feed_back/pallas_call | solution.py:1322
  333.0 13.2 %attend_back.4 = (bf16[192,1024]{1,0:T(8,128)(2,1)}, bf16[1536,640]{1,0:T(8,128)(2,1)}) custom-call(s32[2]{0:T(128)} %pad_add_fusion.2.span, s32[8,8,256]{2,1,0:T(8,128)} %get-tuple-element.123.key_ref, s32[8,576]{1,0:T(8,128)} %pad_add_fusion.query_ref, bf16[1536,640]{1,0:T(8,128)(2,1)} %bitcast.96, bf16[8,192,128]{2,1,0:T(8,128)(2,1)} %get-tuple-element.134.q_ref, ...), custom_call_target="tpu_custom_call" | custom-call | tf_op jit(solution)/shard_map/attend_back/pallas_call | solution.py:1082
  347.7 18.6 %reduce_layer.4.raw_ref = bf16[192,640]{1,0:T(8,128)(2,1)S(1)} custom-call(bf16[8,192,640]{2,1,0:T(8,128)(2,1)S(1)} %bitcast.63), custom_call_target="tpu_custom_call" | custom-call | tf_op jit(solution)/shard_map/reduce_layer/pallas_call | solution.py:844
  367.0 4.9 project_back.4
  374.7 15.6 %feed_back.5 = (bf16[256,960]{1,0:T(8,128)(2,1)}, bf16[256,2560]{1,0:T(8,128)(2,1)}, bf16[256,2560]{1,0:T(8,128)(2,1)}, bf16[256,960]{1,0:T(8,128)(2,1)}, f32[25...) custom-call(f32[256,960]{1,0:T(8,128)} %pad_maximum_fusion.1.gradient_ref, ...), custom_call_target="tpu_custom_call" | custom-call | flops 4246732800 | bytes 27729920 | tf_op jit(solution)/shard_map/feed_back/pallas_call | solution.py:1322
  390.3 14.9 %attend_back.5 = (bf16[256,1024]{1,0:T(8,128)(2,1)}, bf16[2048,640]{1,0:T(8,128)(2,1)}) custom-call(s32[2]{0:T(128)} %pad_add_fusion.2.span, s32[8,8,256]{2,1,0:T(8,128)} %get-tuple-element.123.key_ref, s32[8,768]{1,0:T(8,128)} %copy-done.27, bf16[2048,640]{1,0:T(8,128)(2,1)} %bitcast.104, bf16[8,256,128]{2,1,0:T(8,128)(2,1)} %get-tuple-element.126.q_ref, ...), custom_call_target="tpu_custom_call" | custom-call | tf_op jit(solution)/shard_map/attend_back/pallas_call | solution.py:1082
  407.0 23.6 %reduce_layer.5.raw_ref = bf16[256,640]{1,0:T(8,128)(2,1)S(1)} custom-call(bf16[8,256,640]{2,1,0:T(8,128)(2,1)S(1)} %bitcast.62), custom_call_target="tpu_custom_call" | custom-call | tf_op jit(solution)/shard_map/reduce_layer/pallas_call | solution.py:844
  431.4 5.2 project_back.5
  439.0 2.1 collective-permute-start.4
  441.2 7.7 %convolution_convert_fusion = bf16[960,2560]{1,0:T(8,128)(2,1)} fusion(bf16[640,960]{1,0:T(8,128)(2,1)S(1)} %copy-done.24, bf16[256,2560]{1,0:T(8,128)(2,1)} %get-tuple-element.215, bf16[192,2560]{1,0:T(8,128)(2,1)} %get-tuple-element.214, bf16[192,2560]{1,0:T(8,128)(2,1)S(1)} %copy-done.41), kind=kOutput, calls=%fused_computation | convolution fusion | flops 3158016000 | bytes 9420800 | tf_op jit(solution)/shard_map/dot_general | solution.py:1441
  448.9 5.8 convolution_convert_fusion.1
  456.6 8.2 %outer_rows.1 = bf16[2560,960]{1,0:T(8,128)(2,1)} custom-call(bf16[192,2560]{1,0:T(8,128)(2,1)} %get-tuple-element.207.refs_0_, bf16[192,2560]{1,0:T(8,128)(2,1)} %get-tuple-element.208.refs_1_, bf16[256,2560]{1,0:T(8,128)(2,1)} %get-tuple-element.209.refs_2_, bf16[192,960]{1,0:T(8,128)(2,1)} %get-tuple-element.210.refs_3_, ...), custom_call_target="tpu_custom_call" | custom-call | flops 3145728000 | bytes 9420800 | tf_op jit(solution)/shard_map/outer_rows/pallas_call | solution.py:1361
  467.5 4.7 convolution_convert_fusion.2
  472.1 108.5 %reduce_gradients.1 = (bf16[120,1792]{1,0:T(8,128)(2,1)}, bf16[120,1024]{1,0:T(8,128)(2,1)}, bf16[2,120,2560]{2,1,0:T(8,128)(2,1)}, bf16[320,960]{1,0:T(8,128)(2,1)}) custom-call(bf16[8,120,1792]{2,1,0:T(8,128)(2,1)} %bitcast.102, bf16[8,120,1024]{2,1,0:T(8,128)(2,1)} %pad_maximum_fusion.refs_1_, bf16[8,120,2560]{2,1,0:T(8,128)(2,1)} %bitcast.101, ...), custom_call_target="tpu_custom_call" | custom-call | tf_op jit(solution)/shard_map/reduce_gradients/pallas_call | solution.py:646
  581.5 5.1 finish.1
  (164 shorter events, 38.0 us)
Async XLA Ops:
  0.6 9.2 %copy-start = (bf16[256,960]{0,1:T(8,128)(2,1)S(1)}, bf16[256,960]{0,1:T(8,128)(2,1)}, u32[]{:S(2)}) copy-start(bf16[256,960]{0,1:T(8,128)(2,1)} %param.15) | copy-start | bytes 1474564
  0.7 12.6 %copy-start.16 = (bf16[256,960]{0,1:T(8,128)(2,1)S(1)}, bf16[256,960]{0,1:T(8,128)(2,1)}, u32[]{:S(2)}) copy-start(bf16[256,960]{0,1:T(8,128)(2,1)} %param.29) | copy-start | bytes 1474564
  0.7 12.9 %copy-start.26 = (bf16[120,320]{0,1:T(8,128)(2,1)S(1)}, bf16[120,320]{0,1:T(8,128)(2,1)}, u32[]{:S(2)}) copy-start(bf16[120,320]{0,1:T(8,128)(2,1)} %param.17) | copy-start | bytes 230404
  0.7 12.9 %copy-start.25 = (bf16[120,320]{0,1:T(8,128)(2,1)S(1)}, bf16[120,320]{0,1:T(8,128)(2,1)}, u32[]{:S(2)}) copy-start(bf16[120,320]{0,1:T(8,128)(2,1)} %param.18) | copy-start | bytes 230404
  0.7 13.0 %copy-start.38 = (bf16[120]{0:T(256)(128)(2,1)S(1)}, bf16[120]{0:T(256)(128)(2,1)}, u32[]{:S(2)}) copy-start(bf16[120]{0:T(256)(128)(2,1)} %param.24) | copy-start | bytes 724
  0.7 13.0 %copy-start.37 = (bf16[120]{0:T(256)(128)(2,1)S(1)}, bf16[120]{0:T(256)(128)(2,1)}, u32[]{:S(2)}) copy-start(bf16[120]{0:T(256)(128)(2,1)} %param.25) | copy-start | bytes 724
  0.7 13.0 %copy-start.36 = (bf16[120,3]{0,1:T(4,128)(2,1)S(1)}, bf16[120,3]{0,1:T(4,128)(2,1)}, u32[]{:S(2)}) copy-start(bf16[120,3]{0,1:T(4,128)(2,1)} %param.23) | copy-start | bytes 2164
  0.7 13.3 %copy-start.21 = (bf16[120,960]{1,0:T(8,128)(2,1)S(1)}, bf16[120,960]{1,0:T(8,128)(2,1)}, u32[]{:S(2)}) copy-start(bf16[120,960]{1,0:T(8,128)(2,1)} %param.16) | copy-start | bytes 691204
  6.2 113.8 %collective-permute-start = (s32[8,256]{1,0:T(8,128)S(1)}, s32[8,256]{1,0:T(8,128)S(1)}, u32[]{:S(2)}, u32[]{:S(2)}) collective-permute-start(s32[8,256]{1,0:T(8,128)S(1)} %pad.13), channel_id=1, source_target_pairs={{0,0},{1,1},{2,8},{3,9},{4,16},{5,17},{6,24},{7,25},{8,2},{9,3},{1... | collective-permute-start | bytes 24584 | tf_op jit(solution)/shard_map/ppermute | solution.py:1482
  10.4 115.4 %collective-permute-start.1 = (bf16[256,960]{1,0:T(8,128)(2,1)S(1)}, bf16[256,960]{1,0:T(8,128)(2,1)S(1)}, u32[]{:S(2)}, u32[]{:S(2)}) collective-permute-start(bf16[256,960]{1,0:T(8,128)(2,1)S(1)} %copy.57), channel_id=1, source_target_pairs={{0,0},{1,1},{2,8},{3,9},{4,16},{5,17},{6,24},{7,25},{8,2},{9,3},{1... | collective-permute-start | bytes 1474568 | tf_op jit(solution)/shard_map/ppermute | solution.py:1481
  120.0 11.0 %copy-start.9 = (s32[8,256]{1,0:T(8,128)}, s32[8,256]{1,0:T(8,128)S(1)}, u32[]{:S(2)}) copy-start(s32[8,256]{1,0:T(8,128)S(1)} %collective-permute-done.refs_1_.label_ref) | copy-start | bytes 24580
  123.2 29.7 %copy-start.27 = (s32[8,768]{1,0:T(8,128)}, s32[8,768]{1,0:T(8,128)S(1)}, u32[]{:S(2)}) copy-start(s32[8,768]{1,0:T(8,128)S(1)} %constant_dynamic-update-slice_fusion.query_ref) | copy-start | bytes 73732
  151.0 57.0 %collective-permute-start.2 = (bf16[256,960]{1,0:T(8,128)(2,1)S(1)}, bf16[256,960]{1,0:T(8,128)(2,1)S(1)}, u32[]{:S(2)}, u32[]{:S(2)}) collective-permute-start(bf16[256,960]{1,0:T(8,128)(2,1)S(1)} %convolution_convert_fusion.4), channel_id=1, source_target_pairs={{0,0},{1,1},{2,8},{3,9},{4,16},{5,17},{6,24},{7,25},{8,2},{9,3},{1... | collective-permute-start | bytes 1474568 | tf_op jit(solution)/shard_map/ppermute | solution.py:1515
  208.0 13.3 %copy-start.10 = (bf16[256,960]{1,0:T(8,128)(2,1)}, bf16[256,960]{1,0:T(8,128)(2,1)S(1)}, u32[]{:S(2)}) copy-start(bf16[256,960]{1,0:T(8,128)(2,1)S(1)} %collective-permute-done.2.gradient_ref) | copy-start | bytes 1474564
  259.4 114.0 %collective-permute-start.3 = (bf16[256,960]{1,0:T(8,128)(2,1)S(1)}, bf16[256,960]{1,0:T(8,128)(2,1)S(1)}, u32[]{:S(2)}, u32[]{:S(2)}) collective-permute-start(bf16[256,960]{1,0:T(8,128)(2,1)S(1)} %pad_maximum_fusion.2), channel_id=1, source_target_pairs={{0,0},{1,1},{2,8},{3,9},{4,16},{5,17},{6,24},{7,25},{8,2},{9,3},{1... | collective-permute-start | bytes 1474568 | tf_op jit(solution)/shard_map/ppermute | solution.py:1568
  317.6 14.6 %copy-start.18 = (bf16[192,960]{1,0:T(8,128)(2,1)S(1)}, bf16[192,960]{1,0:T(8,128)(2,1)}, u32[]{:S(2)}) copy-start(bf16[192,960]{1,0:T(8,128)(2,1)} %get-tuple-element.201) | copy-start | bytes 1105924
  372.1 18.2 %copy-start.23 = (bf16[640,960]{1,0:T(8,128)(2,1)}, bf16[640,960]{1,0:T(8,128)(2,1)S(1)}, u32[]{:S(2)}) copy-start(bf16[640,960]{1,0:T(8,128)(2,1)S(1)} %constant_dynamic-update-slice_fusion.3) | copy-start | bytes 3686404
  373.4 16.9 %copy-start.14 = (bf16[256,960]{1,0:T(8,128)(2,1)}, bf16[256,960]{1,0:T(8,128)(2,1)S(1)}, u32[]{:S(2)}) copy-start(bf16[256,960]{1,0:T(8,128)(2,1)S(1)} %collective-permute-done.3.final_ref) | copy-start | bytes 1474564
  390.3 41.0 %copy-start.32 = (f32[1,960]{1,0:T(1,128)S(1)}, f32[1,960]{1,0:T(1,128)}, u32[]{:S(2)}) copy-start(f32[1,960]{1,0:T(1,128)} %get-tuple-element.193) | copy-start | bytes 11524
  390.3 41.0 %copy-start.35 = (f32[1,960]{1,0:T(1,128)S(1)}, f32[1,960]{1,0:T(1,128)}, u32[]{:S(2)}) copy-start(f32[1,960]{1,0:T(1,128)} %get-tuple-element.192) | copy-start | bytes 11524
  431.4 6.0 %copy-start.28 = (f32[1,960]{1,0:T(1,128)S(1)}, f32[1,960]{1,0:T(1,128)}, u32[]{:S(2)}) copy-start(f32[1,960]{1,0:T(1,128)} %get-tuple-element.194) | copy-start | bytes 11524
  431.4 6.0 %copy-start.29 = (f32[1,960]{1,0:T(1,128)S(1)}, f32[1,960]{1,0:T(1,128)}, u32[]{:S(2)}) copy-start(f32[1,960]{1,0:T(1,128)} %get-tuple-element.198) | copy-start | bytes 11524
  431.4 6.0 %copy-start.31 = (f32[1,960]{1,0:T(1,128)S(1)}, f32[1,960]{1,0:T(1,128)}, u32[]{:S(2)}) copy-start(f32[1,960]{1,0:T(1,128)} %get-tuple-element.199) | copy-start | bytes 11524
  431.4 6.0 %copy-start.34 = (f32[1,960]{1,0:T(1,128)S(1)}, f32[1,960]{1,0:T(1,128)}, u32[]{:S(2)}) copy-start(f32[1,960]{1,0:T(1,128)} %get-tuple-element.200) | copy-start | bytes 11524
  431.4 9.7 %copy-start.24 = (bf16[640,960]{1,0:T(8,128)(2,1)S(1)}, bf16[640,960]{1,0:T(8,128)(2,1)}, u32[]{:S(2)}) copy-start(bf16[640,960]{1,0:T(8,128)(2,1)} %copy-done.23) | copy-start | bytes 3686404
  431.4 9.7 %copy-start.41 = (bf16[192,2560]{1,0:T(8,128)(2,1)S(1)}, bf16[192,2560]{1,0:T(8,128)(2,1)}, u32[]{:S(2)}) copy-start(bf16[192,2560]{1,0:T(8,128)(2,1)} %get-tuple-element.213) | copy-start | bytes 2949124
  439.0 141.7 %collective-permute-start.4 = (bf16[256,960]{1,0:T(8,128)(2,1)S(1)}, bf16[256,960]{1,0:T(8,128)(2,1)S(1)}, u32[]{:S(2)}, u32[]{:S(2)}) collective-permute-start(bf16[256,960]{1,0:T(8,128)(2,1)S(1)} %convert_element_type.61), channel_id=1, source_target_pairs={{0,0},{1,1},{2,8},{3,9},{4,16},{5,17},{6,24},{7,25},{8,2},{9,3},{1... | collective-permute-start | bytes 1474568 | tf_op jit(solution)/shard_map/ppermute | solution.py:1573
  441.1 7.7 %copy-start.39 = (bf16[256,2560]{1,0:T(8,128)(2,1)S(1)}, bf16[256,2560]{1,0:T(8,128)(2,1)}, u32[]{:S(2)}) copy-start(bf16[256,2560]{1,0:T(8,128)(2,1)} %get-tuple-element.206) | copy-start | bytes 3932164
  441.1 7.7 %copy-start.40 = (bf16[192,2560]{1,0:T(8,128)(2,1)S(1)}, bf16[192,2560]{1,0:T(8,128)(2,1)}, u32[]{:S(2)}) copy-start(bf16[192,2560]{1,0:T(8,128)(2,1)} %get-tuple-element.204) | copy-start | bytes 2949124
  441.2 7.7 %copy-start.42 = (bf16[192,2560]{1,0:T(8,128)(2,1)S(1)}, bf16[192,2560]{1,0:T(8,128)(2,1)}, u32[]{:S(2)}) copy-start(bf16[192,2560]{1,0:T(8,128)(2,1)} %get-tuple-element.205) | copy-start | bytes 2949124
  448.9 5.9 %copy-start.12 = (bf16[256,960]{1,0:T(8,128)(2,1)S(1)}, bf16[256,960]{1,0:T(8,128)(2,1)}, u32[]{:S(2)}) copy-start(bf16[256,960]{1,0:T(8,128)(2,1)} %get-tuple-element.127.mixed_ref) | copy-start | bytes 1474564
  472.1 117.1 %copy-start.1 = (bf16[256,960]{0,1:T(8,128)(2,1)S(1)}, bf16[256,960]{0,1:T(8,128)(2,1)}, u32[]{:S(2)}) copy-start(bf16[256,960]{0,1:T(8,128)(2,1)} %param.15) | copy-start | bytes 1474564
  (25 other events, 78.4 us)

commit v10 on v9

--- a/solution.py
+++ b/solution.py
@@ -1589,7 +1589,7 @@
         cut(outer(n1, dqkv)),
         cut(jnp.concatenate([outer(mixed, d_att), tiny], axis=1)),
         cut(outer(n2, d_gated)),
-        outer_rows(hidden, d_fed, 640).reshape(topo.T, -1, model),
+        outer_rows(hidden, d_fed, 1280).reshape(topo.T, -1, model),
         cut(outer(n2, d_up)),
     ])
     block, token, grad_query, grad_key, grad_value, *others, tiny = finish(

time: 600 us -> 599 us (level)
  transfers between devices with their start and end apart: 5 -> 5, of which waited for: 0 -> 0; matrix products, arithmetic and copies ran while one was open for 5% -> 5% of each run, Pallas kernels for 65% -> 64%
where the time goes in v10:
time: 599 us; the launch traced here: 589 us
  Pallas kernels  516 us (86%)
  matrix products  20.8 us (3%)
  local copies, waits for them, and re-layouts  16.6 us (3%)
  starting transfers between devices  16.5 us (3%)
  other arithmetic  15 us (3%)
    pallas_call x1, Pallas kernels, reduce_gradients(): pl.pallas_call(functools.partial(reduce_kernel, topo, shares), in_specs=[...  109 us
    pallas_call x1, Pallas kernels, gather_weights(): pl.pallas_call(functools.partial(gather_kernel, topo, pieces), in_specs=[...  105 us
    pallas_call x3, Pallas kernels, reduce_layer(): pl.pallas_call(functools.partial(group_reduce_kernel, topo), in_specs=[pl...  60 us
    pallas_call x3, Pallas kernels, gather_layer(): pl.pallas_call(functools.partial(group_gather_kernel, topo, n), in_specs=...  57.2 us
    pallas_call x3, Pallas kernels, feed_back(): pl.pallas_call(functools.partial(feed_back_kernel, recursion), grid=(ff /...  44.7 us
    pallas_call x3, Pallas kernels, attend_back(): pl.pallas_call(functools.partial(attend_back_kernel, rows, recursion), gr...  40.9 us
    pallas_call x3, Pallas kernels, feed(): pl.pallas_call(functools.partial(feed_kernel, recursion, following), grid...  39.6 us
    pallas_call x3, Pallas kernels, attend(): pl.pallas_call(functools.partial(attend_kernel, rows, recursion), grid_sp...  27.7 us
  transfers between devices with their start and end apart: 5, of which 0 were waited for; matrix products, arithmetic and copies ran while one was open for 5% of the time, Pallas kernels for 64%

profile of v10, /device:TPU:17, one launch (start us, length us, event | category | flops | bytes accessed | tf_op | source)
XLA Modules:
  0.0 589.3 jit_solution(6122897653998454198)
XLA Ops:
  6.2 3.6 collective-permute-start
  10.4 2.9 collective-permute-start.1
  14.9 105.0 %gather_weights.1 = (bf16[8,120,1664]{2,1,0:T(8,128)(2,1)}, bf16[8,120,2560]{2,1,0:T(8,128)(2,1)}, bf16[8,120,2560]{2,1,0:T(8,128)(2,1)}, bf16[8,320,960]{2,1,0:T(8,128)(2,1)}, bf16[8,120,960]{2,1,0:T(8,128)(2,1)}) custom-call(bf16[120,1664]{1,0:T(8,128)(2,1)} %concatenate.51.refs_0_, bf16[120,2560]{1,0:T(8,128)(2,1)} %refs_1_.1, bf16[120,2560]{1,0:T(8,128)(2,1)} %refs_2_.1, ...), custom_call_target="tpu_custom_call" | custom-call | tf_op jit(solution)/shard_map/gather_weights/pallas_call | solution.py:298
  126.6 4.3 project.1
  130.9 20.0 %gather_layer.3 = (bf16[8,256,640]{2,1,0:T(8,128)(2,1)}, s32[8,8,256]{2,1,0:T(8,128)}) custom-call(bf16[256,640]{1,0:T(8,128)(2,1)} %get-tuple-element.122.refs_0_, s32[8,256]{1,0:T(8,128)} %copy-done.9), custom_call_target="tpu_custom_call" | custom-call | tf_op jit(solution)/shard_map/gather_layer/pallas_call | solution.py:782
  152.9 10.8 %attend.3 = (bf16[256,960]{1,0:T(8,128)(2,1)}, f32[8,256,128]{2,1,0:T(8,128)}, f32[5,8,768]{2,1,0:T(8,128)}) custom-call(s32[2]{0:T(128)} %pad_add_fusion.2.span, s32[8,8,256]{2,1,0:T(8,128)} %get-tuple-element.123.key_ref, s32[8,768]{1,0:T(8,128)} %copy-done.27, bf16[2048,640]{1,0:T(8,128)(2,1)} %bitcast.103, bf16[8,256,128]{2,1,0:T(8,128)(2,1)} %get-tuple-element.126.q_ref), custom_call_target="tpu_custom_call" | custom-call | flops 8053063680 | bytes 5242880 | tf_op jit(solution)/shard_map/attend/pallas_call | solution.py:996
  163.7 14.7 %feed.3 = (f32[256,960]{1,0:T(8,128)}, f32[256,960]{1,0:T(8,128)}, bf16[256,960]{1,0:T(8,128)(2,1)}, bf16[256,2560]{1,0:T(8,128)(2,1)}, bf16[256,2560]{1,0:T(8,1...) custom-call(bf16[256,960]{1,0:T(8,128)(2,1)} %get-tuple-element.127., ...), custom_call_target="tpu_custom_call" | custom-call | flops 4246732800 | bytes 26419200 | tf_op jit(solution)/shard_map/feed/pallas_call | solution.py:1247
  178.5 20.2 %gather_layer.4 = bf16[8,192,640]{2,1,0:T(8,128)(2,1)} custom-call(bf16[192,640]{1,0:T(8,128)(2,1)} %get-tuple-element.133.refs_0_), custom_call_target="tpu_custom_call" | custom-call | tf_op jit(solution)/shard_map/gather_layer/pallas_call | solution.py:782
  199.6 8.2 %attend.4 = (bf16[192,960]{1,0:T(8,128)(2,1)}, f32[8,192,128]{2,1,0:T(8,128)}, f32[5,8,576]{2,1,0:T(8,128)}) custom-call(s32[2]{0:T(128)} %pad_add_fusion.2.span, s32[8,8,256]{2,1,0:T(8,128)} %get-tuple-element.123.key_ref, s32[8,576]{1,0:T(8,128)} %pad_add_fusion.query_ref, bf16[1536,640]{1,0:T(8,128)(2,1)} %bitcast.95, ...), custom_call_target="tpu_custom_call" | custom-call | flops 4529848320 | bytes 3932160 | tf_op jit(solution)/shard_map/attend/pallas_call | solution.py:996
  207.8 13.3 %feed.4 = (f32[192,960]{1,0:T(8,128)}, f32[192,960]{1,0:T(8,128)}, bf16[192,960]{1,0:T(8,128)(2,1)}, bf16[192,2560]{1,0:T(8,128)(2,1)}, bf16[192,2560]{1,0:T(8,1...) custom-call(bf16[192,960]{1,0:T(8,128)(2,1)} %get-tuple-element.138., ...), custom_call_target="tpu_custom_call" | custom-call | flops 3185049600 | bytes 23961600 | tf_op jit(solution)/shard_map/feed/pallas_call | solution.py:1247
  221.2 16.9 %gather_layer.5 = bf16[8,192,640]{2,1,0:T(8,128)(2,1)} custom-call(bf16[192,640]{1,0:T(8,128)(2,1)} %get-tuple-element.140.refs_0_), custom_call_target="tpu_custom_call" | custom-call | tf_op jit(solution)/shard_map/gather_layer/pallas_call | solution.py:782
  238.1 8.7 %attend.5 = (bf16[192,960]{1,0:T(8,128)(2,1)}, f32[8,192,128]{2,1,0:T(8,128)}, f32[5,8,576]{2,1,0:T(8,128)}) custom-call(s32[2]{0:T(128)} %pad_add_fusion.2.span, s32[8,8,256]{2,1,0:T(8,128)} %get-tuple-element.123.key_ref, s32[8,576]{1,0:T(8,128)} %pad_add_fusion.query_ref, bf16[1536,640]{1,0:T(8,128)(2,1)} %bitcast.97, ...), custom_call_target="tpu_custom_call" | custom-call | flops 4529848320 | bytes 3932160 | tf_op jit(solution)/shard_map/attend/pallas_call | solution.py:996
  246.8 11.5 %feed.5 = (f32[192,960]{1,0:T(8,128)}, f32[192,960]{1,0:T(8,128)}, bf16[192,960]{1,0:T(8,128)(2,1)}, bf16[192,2560]{1,0:T(8,128)(2,1)}, bf16[192,2560]{1,0:T(8,1...) custom-call(bf16[192,960]{1,0:T(8,128)(2,1)} %get-tuple-element.142.mixed_ref, ...), custom_call_target="tpu_custom_call" | custom-call | flops 3185049600 | bytes 23961600 | tf_op jit(solution)/shard_map/feed/pallas_call | solution.py:1247
  259.6 5.8 collective-permute-start.3
  265.4 14.6 %feed_back.3 = (bf16[192,960]{1,0:T(8,128)(2,1)}, bf16[192,2560]{1,0:T(8,128)(2,1)}, bf16[192,2560]{1,0:T(8,128)(2,1)}, bf16[192,960]{1,0:T(8,128)(2,1)}, f32[19...) custom-call(bf16[256,960]{1,0:T(8,128)(2,1)} %copy-done.10, ...), custom_call_target="tpu_custom_call" | custom-call | flops 3185049600 | bytes 24944640 | tf_op jit(solution)/shard_map/feed_back/pallas_call | solution.py:1322
  280.0 13.0 %attend_back.3 = (bf16[192,1024]{1,0:T(8,128)(2,1)}, bf16[1536,640]{1,0:T(8,128)(2,1)}) custom-call(s32[2]{0:T(128)} %pad_add_fusion.2.span, s32[8,8,256]{2,1,0:T(8,128)} %get-tuple-element.123.key_ref, s32[8,576]{1,0:T(8,128)} %pad_add_fusion.query_ref, bf16[1536,640]{1,0:T(8,128)(2,1)} %bitcast.98, bf16[8,192,128]{2,1,0:T(8,128)(2,1)} %get-tuple-element.141.q_ref, ...), custom_call_target="tpu_custom_call" | custom-call | tf_op jit(solution)/shard_map/attend_back/pallas_call | solution.py:1082
  294.5 17.9 %reduce_layer.3.raw_ref = bf16[192,640]{1,0:T(8,128)(2,1)S(1)} custom-call(bf16[8,192,640]{2,1,0:T(8,128)(2,1)S(1)} %bitcast.64), custom_call_target="tpu_custom_call" | custom-call | tf_op jit(solution)/shard_map/reduce_layer/pallas_call | solution.py:844
  313.1 4.7 project_back.3
  317.8 14.6 %feed_back.4 = (bf16[192,960]{1,0:T(8,128)(2,1)}, bf16[192,2560]{1,0:T(8,128)(2,1)}, bf16[192,2560]{1,0:T(8,128)(2,1)}, bf16[192,960]{1,0:T(8,128)(2,1)}, f32[19...) custom-call(f32[192,960]{1,0:T(8,128)} %get-tuple-element.155.gradient_ref, ...), custom_call_target="tpu_custom_call" | custom-call | flops 3185049600 | bytes 24944640 | tf_op jit(solution)/shard_map/feed_back/pallas_call | solution.py:1322
  333.2 13.0 %attend_back.4 = (bf16[192,1024]{1,0:T(8,128)(2,1)}, bf16[1536,640]{1,0:T(8,128)(2,1)}) custom-call(s32[2]{0:T(128)} %pad_add_fusion.2.span, s32[8,8,256]{2,1,0:T(8,128)} %get-tuple-element.123.key_ref, s32[8,576]{1,0:T(8,128)} %pad_add_fusion.query_ref, bf16[1536,640]{1,0:T(8,128)(2,1)} %bitcast.96, bf16[8,192,128]{2,1,0:T(8,128)(2,1)} %get-tuple-element.134.q_ref, ...), custom_call_target="tpu_custom_call" | custom-call | tf_op jit(solution)/shard_map/attend_back/pallas_call | solution.py:1082
  347.7 18.6 %reduce_layer.4.raw_ref = bf16[192,640]{1,0:T(8,128)(2,1)S(1)} custom-call(bf16[8,192,640]{2,1,0:T(8,128)(2,1)S(1)} %bitcast.63), custom_call_target="tpu_custom_call" | custom-call | tf_op jit(solution)/shard_map/reduce_layer/pallas_call | solution.py:844
  367.0 4.9 project_back.4
  374.6 15.6 %feed_back.5 = (bf16[256,960]{1,0:T(8,128)(2,1)}, bf16[256,2560]{1,0:T(8,128)(2,1)}, bf16[256,2560]{1,0:T(8,128)(2,1)}, bf16[256,960]{1,0:T(8,128)(2,1)}, f32[25...) custom-call(f32[256,960]{1,0:T(8,128)} %pad_maximum_fusion.1.gradient_ref, ...), custom_call_target="tpu_custom_call" | custom-call | flops 4246732800 | bytes 27729920 | tf_op jit(solution)/shard_map/feed_back/pallas_call | solution.py:1322
  390.3 14.9 %attend_back.5 = (bf16[256,1024]{1,0:T(8,128)(2,1)}, bf16[2048,640]{1,0:T(8,128)(2,1)}) custom-call(s32[2]{0:T(128)} %pad_add_fusion.2.span, s32[8,8,256]{2,1,0:T(8,128)} %get-tuple-element.123.key_ref, s32[8,768]{1,0:T(8,128)} %copy-done.27, bf16[2048,640]{1,0:T(8,128)(2,1)} %bitcast.104, bf16[8,256,128]{2,1,0:T(8,128)(2,1)} %get-tuple-element.126.q_ref, ...), custom_call_target="tpu_custom_call" | custom-call | tf_op jit(solution)/shard_map/attend_back/pallas_call | solution.py:1082
  407.0 23.5 %reduce_layer.5.raw_ref = bf16[256,640]{1,0:T(8,128)(2,1)S(1)} custom-call(bf16[8,256,640]{2,1,0:T(8,128)(2,1)S(1)} %bitcast.62), custom_call_target="tpu_custom_call" | custom-call | tf_op jit(solution)/shard_map/reduce_layer/pallas_call | solution.py:844
  431.4 5.2 project_back.5
  441.4 7.7 %convolution_convert_fusion = bf16[960,2560]{1,0:T(8,128)(2,1)} fusion(bf16[640,960]{1,0:T(8,128)(2,1)S(1)} %copy-done.24, bf16[256,2560]{1,0:T(8,128)(2,1)} %get-tuple-element.215, bf16[192,2560]{1,0:T(8,128)(2,1)} %get-tuple-element.214, bf16[192,2560]{1,0:T(8,128)(2,1)S(1)} %copy-done.41), kind=kOutput, calls=%fused_computation | convolution fusion | flops 3158016000 | bytes 9420800 | tf_op jit(solution)/shard_map/dot_general | solution.py:1441
  449.1 5.8 convolution_convert_fusion.1
  456.8 8.0 %outer_rows.1 = bf16[2560,960]{1,0:T(8,128)(2,1)} custom-call(bf16[192,2560]{1,0:T(8,128)(2,1)} %get-tuple-element.207.refs_0_, bf16[192,2560]{1,0:T(8,128)(2,1)} %get-tuple-element.208.refs_1_, bf16[256,2560]{1,0:T(8,128)(2,1)} %get-tuple-element.209.refs_2_, bf16[192,960]{1,0:T(8,128)(2,1)} %get-tuple-element.210.refs_3_, ...), custom_call_target="tpu_custom_call" | custom-call | flops 3145728000 | bytes 9420800 | tf_op jit(solution)/shard_map/outer_rows/pallas_call | solution.py:1361
  467.4 4.7 convolution_convert_fusion.2
  472.1 108.5 %reduce_gradients.1 = (bf16[120,1792]{1,0:T(8,128)(2,1)}, bf16[120,1024]{1,0:T(8,128)(2,1)}, bf16[2,120,2560]{2,1,0:T(8,128)(2,1)}, bf16[320,960]{1,0:T(8,128)(2,1)}) custom-call(bf16[8,120,1792]{2,1,0:T(8,128)(2,1)} %bitcast.102, bf16[8,120,1024]{2,1,0:T(8,128)(2,1)} %pad_maximum_fusion.refs_1_, bf16[8,120,2560]{2,1,0:T(8,128)(2,1)} %bitcast.101, ...), custom_call_target="tpu_custom_call" | custom-call | tf_op jit(solution)/shard_map/reduce_gradients/pallas_call | solution.py:646
  581.5 5.1 finish.1
  (164 shorter events, 38.4 us)
Async XLA Ops:
  0.6 9.2 %copy-start = (bf16[256,960]{0,1:T(8,128)(2,1)S(1)}, bf16[256,960]{0,1:T(8,128)(2,1)}, u32[]{:S(2)}) copy-start(bf16[256,960]{0,1:T(8,128)(2,1)} %param.15) | copy-start | bytes 1474564
  0.7 12.6 %copy-start.16 = (bf16[256,960]{0,1:T(8,128)(2,1)S(1)}, bf16[256,960]{0,1:T(8,128)(2,1)}, u32[]{:S(2)}) copy-start(bf16[256,960]{0,1:T(8,128)(2,1)} %param.29) | copy-start | bytes 1474564
  0.7 12.9 %copy-start.26 = (bf16[120,320]{0,1:T(8,128)(2,1)S(1)}, bf16[120,320]{0,1:T(8,128)(2,1)}, u32[]{:S(2)}) copy-start(bf16[120,320]{0,1:T(8,128)(2,1)} %param.17) | copy-start | bytes 230404
  0.7 12.9 %copy-start.25 = (bf16[120,320]{0,1:T(8,128)(2,1)S(1)}, bf16[120,320]{0,1:T(8,128)(2,1)}, u32[]{:S(2)}) copy-start(bf16[120,320]{0,1:T(8,128)(2,1)} %param.18) | copy-start | bytes 230404
  0.7 13.0 %copy-start.38 = (bf16[120]{0:T(256)(128)(2,1)S(1)}, bf16[120]{0:T(256)(128)(2,1)}, u32[]{:S(2)}) copy-start(bf16[120]{0:T(256)(128)(2,1)} %param.24) | copy-start | bytes 724
  0.7 13.0 %copy-start.37 = (bf16[120]{0:T(256)(128)(2,1)S(1)}, bf16[120]{0:T(256)(128)(2,1)}, u32[]{:S(2)}) copy-start(bf16[120]{0:T(256)(128)(2,1)} %param.25) | copy-start | bytes 724
  0.7 13.0 %copy-start.36 = (bf16[120,3]{0,1:T(4,128)(2,1)S(1)}, bf16[120,3]{0,1:T(4,128)(2,1)}, u32[]{:S(2)}) copy-start(bf16[120,3]{0,1:T(4,128)(2,1)} %param.23) | copy-start | bytes 2164
  0.7 13.3 %copy-start.21 = (bf16[120,960]{1,0:T(8,128)(2,1)S(1)}, bf16[120,960]{1,0:T(8,128)(2,1)}, u32[]{:S(2)}) copy-start(bf16[120,960]{1,0:T(8,128)(2,1)} %param.16) | copy-start | bytes 691204
  6.2 113.8 %collective-permute-start = (s32[8,256]{1,0:T(8,128)S(1)}, s32[8,256]{1,0:T(8,128)S(1)}, u32[]{:S(2)}, u32[]{:S(2)}) collective-permute-start(s32[8,256]{1,0:T(8,128)S(1)} %pad.13), channel_id=1, source_target_pairs={{0,0},{1,1},{2,8},{3,9},{4,16},{5,17},{6,24},{7,25},{8,2},{9,3},{1... | collective-permute-start | bytes 24584 | tf_op jit(solution)/shard_map/ppermute | solution.py:1482
  10.4 115.4 %collective-permute-start.1 = (bf16[256,960]{1,0:T(8,128)(2,1)S(1)}, bf16[256,960]{1,0:T(8,128)(2,1)S(1)}, u32[]{:S(2)}, u32[]{:S(2)}) collective-permute-start(bf16[256,960]{1,0:T(8,128)(2,1)S(1)} %copy.57), channel_id=1, source_target_pairs={{0,0},{1,1},{2,8},{3,9},{4,16},{5,17},{6,24},{7,25},{8,2},{9,3},{1... | collective-permute-start | bytes 1474568 | tf_op jit(solution)/shard_map/ppermute | solution.py:1481
  120.0 11.0 %copy-start.9 = (s32[8,256]{1,0:T(8,128)}, s32[8,256]{1,0:T(8,128)S(1)}, u32[]{:S(2)}) copy-start(s32[8,256]{1,0:T(8,128)S(1)} %collective-permute-done.refs_1_.label_ref) | copy-start | bytes 24580
  123.2 29.7 %copy-start.27 = (s32[8,768]{1,0:T(8,128)}, s32[8,768]{1,0:T(8,128)S(1)}, u32[]{:S(2)}) copy-start(s32[8,768]{1,0:T(8,128)S(1)} %constant_dynamic-update-slice_fusion.query_ref) | copy-start | bytes 73732
  151.0 56.9 %collective-permute-start.2 = (bf16[256,960]{1,0:T(8,128)(2,1)S(1)}, bf16[256,960]{1,0:T(8,128)(2,1)S(1)}, u32[]{:S(2)}, u32[]{:S(2)}) collective-permute-start(bf16[256,960]{1,0:T(8,128)(2,1)S(1)} %convolution_convert_fusion.4), channel_id=1, source_target_pairs={{0,0},{1,1},{2,8},{3,9},{4,16},{5,17},{6,24},{7,25},{8,2},{9,3},{1... | collective-permute-start | bytes 1474568 | tf_op jit(solution)/shard_map/ppermute | solution.py:1515
  207.8 13.3 %copy-start.10 = (bf16[256,960]{1,0:T(8,128)(2,1)}, bf16[256,960]{1,0:T(8,128)(2,1)S(1)}, u32[]{:S(2)}) copy-start(bf16[256,960]{1,0:T(8,128)(2,1)S(1)} %collective-permute-done.2.gradient_ref) | copy-start | bytes 1474564
  259.6 113.8 %collective-permute-start.3 = (bf16[256,960]{1,0:T(8,128)(2,1)S(1)}, bf16[256,960]{1,0:T(8,128)(2,1)S(1)}, u32[]{:S(2)}, u32[]{:S(2)}) collective-permute-start(bf16[256,960]{1,0:T(8,128)(2,1)S(1)} %pad_maximum_fusion.2), channel_id=1, source_target_pairs={{0,0},{1,1},{2,8},{3,9},{4,16},{5,17},{6,24},{7,25},{8,2},{9,3},{1... | collective-permute-start | bytes 1474568 | tf_op jit(solution)/shard_map/ppermute | solution.py:1568
  317.8 14.6 %copy-start.18 = (bf16[192,960]{1,0:T(8,128)(2,1)S(1)}, bf16[192,960]{1,0:T(8,128)(2,1)}, u32[]{:S(2)}) copy-start(bf16[192,960]{1,0:T(8,128)(2,1)} %get-tuple-element.201) | copy-start | bytes 1105924
  372.1 18.2 %copy-start.23 = (bf16[640,960]{1,0:T(8,128)(2,1)}, bf16[640,960]{1,0:T(8,128)(2,1)S(1)}, u32[]{:S(2)}) copy-start(bf16[640,960]{1,0:T(8,128)(2,1)S(1)} %constant_dynamic-update-slice_fusion.3) | copy-start | bytes 3686404
  373.4 16.9 %copy-start.14 = (bf16[256,960]{1,0:T(8,128)(2,1)}, bf16[256,960]{1,0:T(8,128)(2,1)S(1)}, u32[]{:S(2)}) copy-start(bf16[256,960]{1,0:T(8,128)(2,1)S(1)} %collective-permute-done.3.final_ref) | copy-start | bytes 1474564
  390.3 41.0 %copy-start.32 = (f32[1,960]{1,0:T(1,128)S(1)}, f32[1,960]{1,0:T(1,128)}, u32[]{:S(2)}) copy-start(f32[1,960]{1,0:T(1,128)} %get-tuple-element.193) | copy-start | bytes 11524
  390.3 41.0 %copy-start.35 = (f32[1,960]{1,0:T(1,128)S(1)}, f32[1,960]{1,0:T(1,128)}, u32[]{:S(2)}) copy-start(f32[1,960]{1,0:T(1,128)} %get-tuple-element.192) | copy-start | bytes 11524
  431.3 6.0 %copy-start.28 = (f32[1,960]{1,0:T(1,128)S(1)}, f32[1,960]{1,0:T(1,128)}, u32[]{:S(2)}) copy-start(f32[1,960]{1,0:T(1,128)} %get-tuple-element.194) | copy-start | bytes 11524
  431.3 6.0 %copy-start.29 = (f32[1,960]{1,0:T(1,128)S(1)}, f32[1,960]{1,0:T(1,128)}, u32[]{:S(2)}) copy-start(f32[1,960]{1,0:T(1,128)} %get-tuple-element.198) | copy-start | bytes 11524
  431.4 6.0 %copy-start.31 = (f32[1,960]{1,0:T(1,128)S(1)}, f32[1,960]{1,0:T(1,128)}, u32[]{:S(2)}) copy-start(f32[1,960]{1,0:T(1,128)} %get-tuple-element.199) | copy-start | bytes 11524
  431.4 6.0 %copy-start.34 = (f32[1,960]{1,0:T(1,128)S(1)}, f32[1,960]{1,0:T(1,128)}, u32[]{:S(2)}) copy-start(f32[1,960]{1,0:T(1,128)} %get-tuple-element.200) | copy-start | bytes 11524
  431.4 9.9 %copy-start.24 = (bf16[640,960]{1,0:T(8,128)(2,1)S(1)}, bf16[640,960]{1,0:T(8,128)(2,1)}, u32[]{:S(2)}) copy-start(bf16[640,960]{1,0:T(8,128)(2,1)} %copy-done.23) | copy-start | bytes 3686404
  431.4 9.9 %copy-start.41 = (bf16[192,2560]{1,0:T(8,128)(2,1)S(1)}, bf16[192,2560]{1,0:T(8,128)(2,1)}, u32[]{:S(2)}) copy-start(bf16[192,2560]{1,0:T(8,128)(2,1)} %get-tuple-element.213) | copy-start | bytes 2949124
  439.0 141.7 %collective-permute-start.4 = (bf16[256,960]{1,0:T(8,128)(2,1)S(1)}, bf16[256,960]{1,0:T(8,128)(2,1)S(1)}, u32[]{:S(2)}, u32[]{:S(2)}) collective-permute-start(bf16[256,960]{1,0:T(8,128)(2,1)S(1)} %convert_element_type.61), channel_id=1, source_target_pairs={{0,0},{1,1},{2,8},{3,9},{4,16},{5,17},{6,24},{7,25},{8,2},{9,3},{1... | collective-permute-start | bytes 1474568 | tf_op jit(solution)/shard_map/ppermute | solution.py:1573
  441.3 7.7 %copy-start.39 = (bf16[256,2560]{1,0:T(8,128)(2,1)S(1)}, bf16[256,2560]{1,0:T(8,128)(2,1)}, u32[]{:S(2)}) copy-start(bf16[256,2560]{1,0:T(8,128)(2,1)} %get-tuple-element.206) | copy-start | bytes 3932164
  441.3 7.7 %copy-start.40 = (bf16[192,2560]{1,0:T(8,128)(2,1)S(1)}, bf16[192,2560]{1,0:T(8,128)(2,1)}, u32[]{:S(2)}) copy-start(bf16[192,2560]{1,0:T(8,128)(2,1)} %get-tuple-element.204) | copy-start | bytes 2949124
  441.4 7.7 %copy-start.42 = (bf16[192,2560]{1,0:T(8,128)(2,1)S(1)}, bf16[192,2560]{1,0:T(8,128)(2,1)}, u32[]{:S(2)}) copy-start(bf16[192,2560]{1,0:T(8,128)(2,1)} %get-tuple-element.205) | copy-start | bytes 2949124
  449.1 5.9 %copy-start.12 = (bf16[256,960]{1,0:T(8,128)(2,1)S(1)}, bf16[256,960]{1,0:T(8,128)(2,1)}, u32[]{:S(2)}) copy-start(bf16[256,960]{1,0:T(8,128)(2,1)} %get-tuple-element.127.mixed_ref) | copy-start | bytes 1474564
  472.1 117.1 %copy-start.1 = (bf16[256,960]{0,1:T(8,128)(2,1)S(1)}, bf16[256,960]{0,1:T(8,128)(2,1)}, u32[]{:S(2)}) copy-start(bf16[256,960]{0,1:T(8,128)(2,1)} %param.15) | copy-start | bytes 1474564
  (25 other events, 78.4 us)
